TPU v7x, 32 devices: a whole 2x2x4 slice. The times are simulated.
32 devices in a mesh: sec: 8 (over z, x), op: 4 (over y, core).
Axes of the slice: x: 2, y: 2, z: 4, core: 2. Of those that a mesh axis runs over, the one named last changes fastest.
Arguments:
- wavefunction: bfloat16 [64, 384, 384], P('sec'), may hold values from -6 to 6
- left_ops: bfloat16 [32, 384, 384], P('op'), may hold values from -0.3125 to 0.3125
- right_ops: bfloat16 [32, 384, 384], P('op'), may hold values from -0.3125 to 0.3125
- charge: int32 [32], P('op'), may hold values from -1 to 1
- couple: int32 [32, 64], P('op', 'sec'), may hold values from 0 to 1, as said below
- amplitude: float32 [32, 64], P('op', 'sec'), may hold values from -0.6 to 0.6
Outputs:
- sigma: float32 [64, 384, 384], P('sec', 'op')
Inputs may be any that keep to these rules, and one draw needn't show every extreme that they name: `couple`: 1 where operator k acts into target sector t, else 0.
All inputs are finite; a program needn't handle non-finite values.
Results may differ from a plain program's by a relative error of at most 0.0029.
Values may be sent and summed in bfloat16 or wider, within the bound.
No kernel may reach another device: no remote copies, remote signals or barrier semaphores. Data moves between devices by JAX's collectives and lax.ppermute only.
A program may use at most 64 MiB of HBM per device.

v0:
```python
import jax
import jax.numpy as jnp
from jax import lax
from jax.sharding import PartitionSpec as P


def padded(cells, sides, width):
    for axis, dim in sides:
        count = lax.axis_size(axis)
        head = lax.slice_in_dim(cells, 0, width, axis=dim)
        tail = lax.slice_in_dim(cells, cells.shape[dim] - width, cells.shape[dim], axis=dim)
        cells = jnp.concatenate(
            [
                lax.ppermute(tail, axis, [(i, (i + 1) % count) for i in range(count)]),
                cells,
                lax.ppermute(head, axis, [((i + 1) % count, i) for i in range(count)]),
            ],
            axis=dim,
        )
    return cells


def batched(left_op, sources, right_op, factor_values):
    middle = jnp.einsum("ij,sjk->sik", left_op, sources, preferred_element_type=jnp.float32).astype(
        jnp.bfloat16
    )
    contribution = jnp.einsum("sik,lk->sil", middle, right_op, preferred_element_type=jnp.float32)
    return contribution * factor_values[:, None, None]


def shards(wavefunction, left_ops, right_ops, charge, couple, amplitude):
    factor = amplitude * couple.astype(jnp.float32)
    sectors = wavefunction.shape[0]
    states = wavefunction.shape[1]
    extended = padded(wavefunction, (("sec", 0),), 1)

    def accumulate(accumulated, operands):
        left_op, right_op, sector_shift, factor_row = operands
        start = 1 - sector_shift
        sources = lax.dynamic_slice_in_dim(extended, start, sectors, 0)
        return (accumulated + batched(left_op, sources, right_op, factor_row), None)

    initial = jnp.zeros((sectors, states, states), jnp.float32)
    accumulated, unused = lax.scan(accumulate, initial, (left_ops, right_ops, charge, factor))
    return lax.psum_scatter(accumulated, "op", scatter_dimension=1, tiled=True)


def solution(mesh):
    placed = (
        P("sec", None, None),
        P("op", None, None),
        P("op", None, None),
        P("op"),
        P("op", "sec"),
        P("op", "sec"),
    )
    return jax.shard_map(
        shards, mesh=mesh, in_specs=placed, out_specs=P("sec", "op", None), check_vma=False
    )
```

profile of v0, /device:TPU:0, one launch (start us, length us, event | category | flops | bytes accessed | tf_op | source)
XLA Modules:
  0.0 156.6 jit_solution(3473044227460174080)
XLA Ops:
  6.5 0.0 reduce-scatter.2.cloned.1.call-start
  6.5 1.1 fusion.20
  7.7 3.0 %collective-permute-start = (bf16[1,384,384]{2,1,0:T(8,128)(2,1)S(1)}, bf16[1,384,384]{2,1,0:T(8,128)(2,1)S(1)}, u32[]{:S(2)}, u32[]{:S(2)}) collective-permute-start(bf16[1,384,384]{2,1,0:T(8,128)(2,1)S(1)} %get-tuple-element.133), channel_id=1, source_target_pairs={{0,4},{4,8},{8,12},{12,16},{16,20},{20,24},{24,28},{28,0},{1,5},{5... | collective-permute-start | bytes 884744 | tf_op jit(solution)/shard_map/ppermute | solution.py:14
  10.7 3.1 %collective-permute-start.1 = (bf16[1,384,384]{2,1,0:T(8,128)(2,1)S(1)}, bf16[1,384,384]{2,1,0:T(8,128)(2,1)S(1)}, u32[]{:S(2)}, u32[]{:S(2)}) collective-permute-start(bf16[1,384,384]{2,1,0:T(8,128)(2,1)S(1)} %get-tuple-element.134), channel_id=1, source_target_pairs={{4,0},{8,4},{12,8},{16,12},{20,16},{24,20},{28,24},{0,28},{5,1},{9... | collective-permute-start | bytes 884744 | tf_op jit(solution)/shard_map/ppermute | solution.py:16
  13.8 0.7 convert_multiply_fusion
  14.5 0.0 copy-start
  14.5 8.8 %collective-permute-done = bf16[1,384,384]{2,1,0:T(8,128)(2,1)S(1)} collective-permute-done((bf16[1,384,384]{2,1,0:T(8,128)(2,1)S(1)}, bf16[1,384,384]{2,1,0:T(8,128)(2,1)S(1)}, u32[]{:S(2)}, u32[]{:S(2)}) %collective-permute-start) | collective-permute-done | bytes 294944 | tf_op jit(solution)/shard_map/ppermute | solution.py:14
  23.3 2.2 %collective-permute-done.1 = bf16[1,384,384]{2,1,0:T(8,128)(2,1)S(1)} collective-permute-done((bf16[1,384,384]{2,1,0:T(8,128)(2,1)S(1)}, bf16[1,384,384]{2,1,0:T(8,128)(2,1)S(1)}, u32[]{:S(2)}, u32[]{:S(2)}) %collective-permute-start.1) | collective-permute-done | bytes 294944 | tf_op jit(solution)/shard_map/ppermute | solution.py:16
  25.5 2.1 %pad_maximum_fusion = bf16[10,384,384]{2,1,0:T(8,128)(2,1)S(1)} fusion(bf16[1,384,384]{2,1,0:T(8,128)(2,1)S(1)} %collective-permute-done.1, bf16[8,384,384]{2,1,0:T(8,128)(2,1)} %param.8, bf16[1,384,384]{2,1,0:T(8,128)(2,1)S(1)} %collective-permute-done), kind=kLoop, calls=%fused_computation.13 | loop fusion | flops 2949120 | bytes 5898240 | tf_op jit(solution)/shard_map/concatenate | solution.py:12
  27.6 0.0 copy-done
  27.6 74.0 %while.13 = (s32[]{:T(128)}, f32[8,384,384]{2,1,0:T(8,128)}, s32[8]{0:T(128)S(1)}, bf16[10,384,384]{2,1,0:T(8,128)(2,1)S(1)}, bf16[8,384,384]{2,1,0:T(8,128)(2,1...) while((s32[]{:T(128)}, f32[8,384,384]{2,1,0:T(8,128)}, ...), condition=%wide.region_1.2_spmd.clone, body=%wide.region_0.1_spmd.clone.sunk | while | flops 1816657920 | bytes 12388089 | solution.py:44
  27.6 0.7 dynamic_slice.65
  29.5 6.0 %select_add_fusion.2 = f32[8,384,384]{2,1,0:T(8,128)} fusion(f32[8,384,384]{2,1,0:T(8,128)} %get-tuple-element.190, f32[8]{0:T(128)S(1)} %fusion.30, pred[]{:T(512)S(6)} %compare.3, bf16[10,384,384]{2,1,0:T(8,128)(2,1)S(1)} %get-tuple-element.203, s32[]{:T(128)S(6)} %select_n.8, bf16[8,384,384]{2,1,0:T(8,128)(2,1)} %get-tuple-element.205, ...), kind=kOutput, calls=%fused_computation.clone.1 | convolution fusion | flops 1816657920 | bytes 12387845 | tf_op jit(solution)/shard_map/while/body/eval_jaxpr/sik,lk->sil/dot_general | solution.py:27
  35.5 0.6 dynamic_slice.65
  37.5 7.5 %select_add_fusion.2 = f32[8,384,384]{2,1,0:T(8,128)} fusion(f32[8,384,384]{2,1,0:T(8,128)} %get-tuple-element.190, f32[8]{0:T(128)S(1)} %fusion.30, pred[]{:T(512)S(6)} %compare.3, bf16[10,384,384]{2,1,0:T(8,128)(2,1)S(1)} %get-tuple-element.203, s32[]{:T(128)S(6)} %select_n.8, bf16[8,384,384]{2,1,0:T(8,128)(2,1)} %get-tuple-element.205, ...), kind=kOutput, calls=%fused_computation.clone.1 | convolution fusion | flops 1816657920 | bytes 12387845 | tf_op jit(solution)/shard_map/while/body/eval_jaxpr/sik,lk->sil/dot_general | solution.py:27
  45.0 0.6 dynamic_slice.65
  46.9 7.5 %select_add_fusion.2 = f32[8,384,384]{2,1,0:T(8,128)} fusion(f32[8,384,384]{2,1,0:T(8,128)} %get-tuple-element.190, f32[8]{0:T(128)S(1)} %fusion.30, pred[]{:T(512)S(6)} %compare.3, bf16[10,384,384]{2,1,0:T(8,128)(2,1)S(1)} %get-tuple-element.203, s32[]{:T(128)S(6)} %select_n.8, bf16[8,384,384]{2,1,0:T(8,128)(2,1)} %get-tuple-element.205, ...), kind=kOutput, calls=%fused_computation.clone.1 | convolution fusion | flops 1816657920 | bytes 12387845 | tf_op jit(solution)/shard_map/while/body/eval_jaxpr/sik,lk->sil/dot_general | solution.py:27
  54.4 0.6 dynamic_slice.65
  56.4 7.5 %select_add_fusion.2 = f32[8,384,384]{2,1,0:T(8,128)} fusion(f32[8,384,384]{2,1,0:T(8,128)} %get-tuple-element.190, f32[8]{0:T(128)S(1)} %fusion.30, pred[]{:T(512)S(6)} %compare.3, bf16[10,384,384]{2,1,0:T(8,128)(2,1)S(1)} %get-tuple-element.203, s32[]{:T(128)S(6)} %select_n.8, bf16[8,384,384]{2,1,0:T(8,128)(2,1)} %get-tuple-element.205, ...), kind=kOutput, calls=%fused_computation.clone.1 | convolution fusion | flops 1816657920 | bytes 12387845 | tf_op jit(solution)/shard_map/while/body/eval_jaxpr/sik,lk->sil/dot_general | solution.py:27
  63.9 0.6 dynamic_slice.65
  65.8 7.5 %select_add_fusion.2 = f32[8,384,384]{2,1,0:T(8,128)} fusion(f32[8,384,384]{2,1,0:T(8,128)} %get-tuple-element.190, f32[8]{0:T(128)S(1)} %fusion.30, pred[]{:T(512)S(6)} %compare.3, bf16[10,384,384]{2,1,0:T(8,128)(2,1)S(1)} %get-tuple-element.203, s32[]{:T(128)S(6)} %select_n.8, bf16[8,384,384]{2,1,0:T(8,128)(2,1)} %get-tuple-element.205, ...), kind=kOutput, calls=%fused_computation.clone.1 | convolution fusion | flops 1816657920 | bytes 12387845 | tf_op jit(solution)/shard_map/while/body/eval_jaxpr/sik,lk->sil/dot_general | solution.py:27
  73.3 0.6 dynamic_slice.65
  75.2 7.5 %select_add_fusion.2 = f32[8,384,384]{2,1,0:T(8,128)} fusion(f32[8,384,384]{2,1,0:T(8,128)} %get-tuple-element.190, f32[8]{0:T(128)S(1)} %fusion.30, pred[]{:T(512)S(6)} %compare.3, bf16[10,384,384]{2,1,0:T(8,128)(2,1)S(1)} %get-tuple-element.203, s32[]{:T(128)S(6)} %select_n.8, bf16[8,384,384]{2,1,0:T(8,128)(2,1)} %get-tuple-element.205, ...), kind=kOutput, calls=%fused_computation.clone.1 | convolution fusion | flops 1816657920 | bytes 12387845 | tf_op jit(solution)/shard_map/while/body/eval_jaxpr/sik,lk->sil/dot_general | solution.py:27
  82.7 0.6 dynamic_slice.65
  84.7 7.5 %select_add_fusion.2 = f32[8,384,384]{2,1,0:T(8,128)} fusion(f32[8,384,384]{2,1,0:T(8,128)} %get-tuple-element.190, f32[8]{0:T(128)S(1)} %fusion.30, pred[]{:T(512)S(6)} %compare.3, bf16[10,384,384]{2,1,0:T(8,128)(2,1)S(1)} %get-tuple-element.203, s32[]{:T(128)S(6)} %select_n.8, bf16[8,384,384]{2,1,0:T(8,128)(2,1)} %get-tuple-element.205, ...), kind=kOutput, calls=%fused_computation.clone.1 | convolution fusion | flops 1816657920 | bytes 12387845 | tf_op jit(solution)/shard_map/while/body/eval_jaxpr/sik,lk->sil/dot_general | solution.py:27
  92.2 0.6 dynamic_slice.65
  94.1 7.5 %select_add_fusion.2 = f32[8,384,384]{2,1,0:T(8,128)} fusion(f32[8,384,384]{2,1,0:T(8,128)} %get-tuple-element.190, f32[8]{0:T(128)S(1)} %fusion.30, pred[]{:T(512)S(6)} %compare.3, bf16[10,384,384]{2,1,0:T(8,128)(2,1)S(1)} %get-tuple-element.203, s32[]{:T(128)S(6)} %select_n.8, bf16[8,384,384]{2,1,0:T(8,128)(2,1)} %get-tuple-element.205, ...), kind=kOutput, calls=%fused_computation.clone.1 | convolution fusion | flops 1816657920 | bytes 12387845 | tf_op jit(solution)/shard_map/while/body/eval_jaxpr/sik,lk->sil/dot_general | solution.py:27
  101.6 0.0 reduce-scatter.2.cloned.1.call-update
  101.6 48.2 %reduce-scatter.2.cloned.1.call-done = f32[8,96,384]{2,1,0:T(8,128)} async-done(((f32[8,384,384]{2,1,0:T(8,128)}), f32[8,96,384]{2,1,0:T(8,128)}) %reduce-scatter.2.cloned.1.call-update) | async-done | bytes 1179664 | tf_op jit(solution)/shard_map/reduce_scatter | solution.py:45
  (9 shorter events, 0.1 us)
Async XLA Ops:
  6.5 143.3 %reduce-scatter.2.cloned.1.call-start = ((), (), s32[]{:S(2)}) async-start(), calls=%async_computation.1 | async-start | bytes 5898240 | tf_op jit(solution)/shard_map/reduce_scatter | solution.py:45
  7.7 15.6 %collective-permute-start = (bf16[1,384,384]{2,1,0:T(8,128)(2,1)S(1)}, bf16[1,384,384]{2,1,0:T(8,128)(2,1)S(1)}, u32[]{:S(2)}, u32[]{:S(2)}) collective-permute-start(bf16[1,384,384]{2,1,0:T(8,128)(2,1)S(1)} %get-tuple-element.133), channel_id=1, source_target_pairs={{0,4},{4,8},{8,12},{12,16},{16,20},{20,24},{24,28},{28,0},{1,5},{5... | collective-permute-start | bytes 884744 | tf_op jit(solution)/shard_map/ppermute | solution.py:14
  10.7 14.8 %collective-permute-start.1 = (bf16[1,384,384]{2,1,0:T(8,128)(2,1)S(1)}, bf16[1,384,384]{2,1,0:T(8,128)(2,1)S(1)}, u32[]{:S(2)}, u32[]{:S(2)}) collective-permute-start(bf16[1,384,384]{2,1,0:T(8,128)(2,1)S(1)} %get-tuple-element.134), channel_id=1, source_target_pairs={{4,0},{8,4},{12,8},{16,12},{20,16},{24,20},{28,24},{0,28},{5,1},{9... | collective-permute-start | bytes 884744 | tf_op jit(solution)/shard_map/ppermute | solution.py:16
  14.5 13.1 %copy-start = (s32[8]{0:T(128)S(1)}, s32[8]{0:T(128)}, u32[]{:S(2)}) copy-start(s32[8]{0:T(128)} %param.11) | copy-start | bytes 100
Sparse Core Ops, SparseCore 0:
  101.8 47.9 reduce-scatter.1
where the time goes:
time: 157 us
  waiting for transfers between devices  59.1 us (38%)
  matrix products  58.5 us (37%)
  between operations  13.4 us (9%)
  loops' own time  10.3 us (7%)
  local copies, waits for them, and re-layouts  6.36 us (4%)
  starting transfers between devices  6.13 us (4%)
  other arithmetic  2.8 us (2%)
    dot_general x8, matrix products, batched(): jnp.einsum('sik,lk->sil', middle, right_op, preferred_element_type=jnp.fl...  58.5 us
    reduce_scatter x1, waiting for transfers between devices, shards(): return lax.psum_scatter(accumulated, 'op', scatter_dimension=1, tiled=True)  48.2 us
    another operation x1, loops' own time, shards(): lax.scan(accumulate, initial, (left_ops, right_ops, charge, factor))  10.3 us
    ppermute x1, waiting for transfers between devices, padded(): lax.ppermute(tail, axis, [(i, (i + 1) % count) for i in range(count)])  8.77 us
    dynamic_slice x8, local copies, waits for them, and re-layouts, shards(): lax.scan(accumulate, initial, (left_ops, right_ops, charge, factor))  5.17 us
  transfers between devices with their start and end apart: 3, of which 3 were waited for; matrix products, arithmetic and copies ran while one was open for 0% of the time, Pallas kernels for 0%

commit v1 on v0

--- a/solution.py
+++ b/solution.py
@@ -1,7 +1,14 @@
+import functools
+
 import jax
 import jax.numpy as jnp
 from jax import lax
+from jax.experimental import pallas as pl
+from jax.experimental.pallas import tpu as pltpu
 from jax.sharding import PartitionSpec as P
+
+CORES = 2
+EDGE = 2
 
 
 def padded(cells, sides, width):
@@ -28,7 +35,7 @@
     return contribution * factor_values[:, None, None]
 
 
-def shards(wavefunction, left_ops, right_ops, charge, couple, amplitude):
+def plain_shards(wavefunction, left_ops, right_ops, charge, couple, amplitude):
     factor = amplitude * couple.astype(jnp.float32)
     sectors = wavefunction.shape[0]
     states = wavefunction.shape[1]
@@ -43,6 +50,261 @@
     initial = jnp.zeros((sectors, states, states), jnp.float32)
     accumulated, unused = lax.scan(accumulate, initial, (left_ops, right_ops, charge, factor))
     return lax.psum_scatter(accumulated, "op", scatter_dimension=1, tiled=True)
+
+
+def products(groups, sources, lefts, middles, rights, first_target, targets, waits, results):
+    operators, rows, states = lefts.shape
+    half = rows // CORES
+    per_group = operators // len(groups)
+    for k in range(operators):
+        charge, couple, amplitude = groups[k // per_group]
+        own = k % per_group
+        waits(k)
+        shift = 1 - charge[own]
+        wide = jnp.concatenate([sources[shift + t] for t in range(targets)], axis=1)
+        middle = jnp.dot(lefts[k], wide, preferred_element_type=jnp.float32)
+        for t in range(targets):
+            at = first_target + t
+            factor = amplitude[own, at] * couple[own, at].astype(jnp.float32)
+            block = middle[:, t * states : (t + 1) * states].astype(jnp.bfloat16)
+            block = (block.astype(jnp.float32) * factor).astype(jnp.bfloat16)
+            for core in range(CORES):
+                row = (core * targets + t) * half
+                middles[row : row + half, k * states : (k + 1) * states] = block[
+                    core * half : (core + 1) * half
+                ]
+    waits(operators)
+    right = jnp.concatenate([rights[k] for k in range(operators)], axis=1)
+    width = targets * half
+    step = 256
+    for low in range(0, CORES * width, step):
+        high = min(low + step, CORES * width)
+        total = lax.dot_general(
+            right, middles[low:high, :], (((1,), (1,)), ((), ())), preferred_element_type=jnp.float32
+        ).T
+        for core in range(CORES):
+            begin, end = max(low, core * width), min(high, (core + 1) * width)
+            if begin < end:
+                results[core][begin - core * width : end - core * width, :] = total[
+                    begin - low : end - low, :
+                ].astype(results[core].dtype)
+
+
+def position():
+    place = lax.axis_index("op")
+    return place // CORES, place % CORES
+
+
+def row_of(chip, core, half):
+    return pl.multiple_of((chip * CORES + core) * half, 16)
+
+
+def inner_kernel(
+    remote, charge, couple, amplitude, left, right, cells, keep, send, lefts, rights, sources, middles,
+    cell_sem, left_sem, right_sem,
+):
+    chip, core = position()
+    chip = 1 - chip if remote else chip
+    operators, rows, states = lefts.shape
+    half = rows // CORES
+    slabs = sources.shape[0]
+    targets = slabs - 2
+    first = EDGE - 1
+    cell_copy = pltpu.make_async_copy(cells.at[pl.ds(first, slabs)], sources, cell_sem)
+    cell_copy.start()
+    left_copies = []
+    right_copies = []
+    for k in range(operators):
+        for part, owner in enumerate((core, 1 - core)):
+            copy = pltpu.make_async_copy(
+                left.at[k, pl.ds(row_of(chip, owner, half), half)],
+                lefts.at[k, pl.ds(part * half, half)],
+                left_sem.at[k, part],
+            )
+            copy.start()
+            left_copies.append(copy)
+    for k in range(operators):
+        copy = pltpu.make_async_copy(right.at[k], rights.at[k], right_sem.at[k])
+        copy.start()
+        right_copies.append(copy)
+
+    def waits(k):
+        if k == 0:
+            cell_copy.wait()
+            for copy in left_copies[: 2 * CORES]:
+                copy.wait()
+        elif k == 2:
+            for copy in left_copies[2 * CORES :]:
+                copy.wait()
+        elif k == operators:
+            for copy in right_copies:
+                copy.wait()
+
+    products(
+        [(charge, couple, amplitude)], sources, lefts, middles, rights, EDGE, targets, waits, (keep, send)
+    )
+
+
+def edge_kernel(
+    remote, charge, couple, amplitude, charge_in, couple_in, amplitude_in, left, right, left_in, right_in,
+    cells, low_halo, high_halo, keep, send, lefts, rights, sources, middles,
+    cell_sem, left_sem, right_sem,
+):
+    chip, core = position()
+    chip = 1 - chip if remote else chip
+    operators, rows, states = lefts.shape
+    half = rows // CORES
+    sectors = cells.shape[0]
+    inside = EDGE + 1
+    cell_copy = pltpu.make_async_copy(
+        cells.at[pl.ds((sectors - inside) * core, inside)], sources.at[pl.ds(1 - core, inside)], cell_sem.at[0]
+    )
+    cell_copy.start()
+
+    @pl.when(core == 0)
+    def low():
+        pltpu.make_async_copy(low_halo.at[0], sources.at[0], cell_sem.at[1]).start()
+
+    @pl.when(core != 0)
+    def high():
+        pltpu.make_async_copy(high_halo.at[0], sources.at[inside], cell_sem.at[1]).start()
+
+    left_copies = []
+    right_copies = []
+    per_group = operators // CORES
+    for k in range(operators):
+        origin = left if k < per_group else left_in
+        for part, owner in enumerate((core, 1 - core)):
+            copy = pltpu.make_async_copy(
+                origin.at[k % per_group, pl.ds(row_of(chip, owner, half), half)],
+                lefts.at[k, pl.ds(part * half, half)],
+                left_sem.at[k, part],
+            )
+            copy.start()
+            left_copies.append(copy)
+    for k in range(operators):
+        origin = right if k < per_group else right_in
+        copy = pltpu.make_async_copy(origin.at[k % per_group], rights.at[k], right_sem.at[k])
+        copy.start()
+        right_copies.append(copy)
+
+    def waits(k):
+        if k == 0:
+            cell_copy.wait()
+            pltpu.make_async_copy(low_halo.at[0], sources.at[0], cell_sem.at[1]).wait()
+            for copy in left_copies[: 2 * CORES]:
+                copy.wait()
+        elif k == 2:
+            for copy in left_copies[2 * CORES :]:
+                copy.wait()
+        elif k == operators:
+            for copy in right_copies:
+                copy.wait()
+
+    products(
+        [(charge, couple, amplitude), (charge_in, couple_in, amplitude_in)],
+        sources, lefts, middles, rights, (sectors - EDGE) * core, EDGE, waits, (keep, send),
+    )
+
+
+def sum_kernel(inner_own, inner_chip, inner_far, near_own, near_far, other_chip, other_far, sigma):
+    core = lax.axis_index("op") % CORES
+    sectors = sigma.shape[0]
+    far = sectors - EDGE
+    sigma[EDGE:far] = inner_own[...] + inner_chip[...] + inner_far[...].astype(jnp.float32)
+    sigma[pl.ds(far * core, EDGE)] = near_own[...] + near_far[...].astype(jnp.float32)
+    sigma[pl.ds(far * (1 - core), EDGE)] = other_chip[...] + other_far[...].astype(jnp.float32)
+
+
+SMALL = pl.BlockSpec(memory_space=pltpu.SMEM)
+LARGE = pl.BlockSpec(memory_space=pl.ANY)
+BLOCK = pl.BlockSpec(memory_space=pltpu.VMEM)
+
+
+def call(kernel, name, small, large, operators, slabs, targets, half, states, dtypes, cell_sems):
+    rows = CORES * half
+    flops = operators * targets * rows * states * states * 4
+    results = [jax.ShapeDtypeStruct((targets * half, states), dtype) for dtype in dtypes]
+    outs = pl.pallas_call(
+        kernel,
+        out_shape=results,
+        in_specs=[SMALL] * len(small) + [LARGE] * len(large),
+        out_specs=[BLOCK] * len(results),
+        scratch_shapes=[
+            pltpu.VMEM((operators, rows, states), jnp.bfloat16),
+            pltpu.VMEM((operators, states, states), jnp.bfloat16),
+            pltpu.VMEM((slabs, states, states), jnp.bfloat16),
+            pltpu.VMEM((targets * rows, operators * states), jnp.bfloat16),
+            pltpu.SemaphoreType.DMA(cell_sems),
+            pltpu.SemaphoreType.DMA((operators, CORES)),
+            pltpu.SemaphoreType.DMA((operators,)),
+        ],
+        compiler_params=pltpu.CompilerParams(vmem_limit_bytes=40 * 1024 * 1024),
+        cost_estimate=pl.CostEstimate(flops=flops, bytes_accessed=operators * states * states * 4, transcendentals=0),
+        name=name,
+    )(*small, *large)
+    return [out.reshape(targets, half, states) for out in outs]
+
+
+def shards(wavefunction, left_ops, right_ops, charge, couple, amplitude):
+    sec = lax.axis_size("sec")
+    op = lax.axis_size("op")
+    sectors, states = wavefunction.shape[:2]
+    operators = left_ops.shape[0]
+    half = states // op
+    inner = sectors - 2 * EDGE
+
+    across = [(i, i ^ 1) for i in range(op)]
+    far = [(i, i ^ CORES) for i in range(op)]
+    far_across = [(i, i ^ (CORES + 1)) for i in range(op)]
+
+    def chip_mate(value):
+        return lax.ppermute(value, "op", across)
+
+    up = [
+        (s * op + o, ((s + 1) % sec) * op + o) for s in range(sec) for o in range(op) if o % CORES == 0
+    ]
+    down = [
+        (s * op + o, ((s - 1) % sec) * op + o) for s in range(sec) for o in range(op) if o % CORES != 0
+    ]
+    low_halo = lax.ppermute(wavefunction[sectors - 1 :], ("sec", "op"), up)
+    high_halo = lax.ppermute(wavefunction[:1], ("sec", "op"), down)
+    left_in = chip_mate(left_ops)
+    right_in = chip_mate(right_ops)
+    small = (charge, couple, amplitude)
+    small_in = tuple(chip_mate(value) for value in small)
+
+    def inner_part(remote, name):
+        return call(
+            functools.partial(inner_kernel, remote), name, small, (left_ops, right_ops, wavefunction),
+            operators, inner + 2, inner, half, states, (jnp.float32, jnp.float32), (),
+        )
+
+    def edge_part(remote, name, dtype):
+        return call(
+            functools.partial(edge_kernel, remote), name, small + small_in,
+            (left_ops, right_ops, left_in, right_in, wavefunction, low_halo, high_halo),
+            CORES * operators, EDGE + 2, EDGE, half, states, (dtype, dtype), (2,),
+        )
+
+    inner_far_keep, inner_far_send = inner_part(True, "inner_far")
+    inner_far_in = chip_mate(inner_far_send)
+    inner_own, inner_send = inner_part(False, "inner_own")
+    inner_chip = chip_mate(inner_send)
+    inner_far = lax.ppermute((inner_far_keep + inner_far_in).astype(jnp.bfloat16), "op", far)
+    near_send, other_send = edge_part(True, "edge_far", jnp.bfloat16)
+    near_far = lax.ppermute(near_send, "op", far)
+    other_far = lax.ppermute(other_send, "op", far_across)
+    near_own, near_mate = edge_part(False, "edge_own", jnp.float32)
+    other_chip = chip_mate(near_mate)
+    return pl.pallas_call(
+        sum_kernel,
+        out_shape=jax.ShapeDtypeStruct((sectors, half, states), jnp.float32),
+        in_specs=[BLOCK] * 7,
+        out_specs=BLOCK,
+        compiler_params=pltpu.CompilerParams(vmem_limit_bytes=16 * 1024 * 1024),
+        name="total",
+    )(inner_own, inner_chip, inner_far, near_own, near_far, other_chip, other_far)
 
 
 def solution(mesh):
@@ -54,6 +316,7 @@
         P("op", "sec"),
         P("op", "sec"),
     )
+    body = shards if mesh.shape["op"] == CORES * CORES else plain_shards
     return jax.shard_map(
-        shards, mesh=mesh, in_specs=placed, out_specs=P("sec", "op", None), check_vma=False
-    )
+        body, mesh=mesh, in_specs=placed, out_specs=P("sec", "op", None), check_vma=False
+    )

time: 157 us -> 70.5 us (0.45)
  matrix products: 58.5 us -> 0 us
  waiting for transfers between devices: 59.1 us -> 8.9 us
  Pallas kernels: 0 us -> 40.2 us
  between operations: 13.4 us -> 0.1 us
  loops' own time: 10.3 us -> 0 us
  starting transfers between devices: 6.13 us -> 13.8 us
  other arithmetic: 2.8 us -> 0.08 us
    dot_general x8 -> x0, matrix products: 58.5 us -> none  [batched(): jnp.einsum('sik,lk->sil', middle, right_op, preferred_element_type=jnp.fl...]
    reduce_scatter x1 -> x0, waiting for transfers between devices: 48.2 us -> none  [shards(): return lax.psum_scatter(accumulated, 'op', scatter_dimension=1, tiled=True)]
    pallas_call x0 -> x5, Pallas kernels: none -> 40.2 us  [the longest x4 39.1 us: call(): pl.pallas_call(kernel, out_shape=results, in_specs=[SMALL] * len(small) +...]
    another operation x1 -> x0, loops' own time: 10.3 us -> none  [shards(): lax.scan(accumulate, initial, (left_ops, right_ops, charge, factor))]
    ppermute x2 -> x13, starting transfers between devices: 6.12 us -> 13.8 us  [the longest x8 4.95 us: chip_mate(): return lax.ppermute(value, 'op', across)]
    unnamed x2 -> x12, local copies, waits for them, and re-layouts: 0.01 us -> 7.02 us
    dynamic_slice x8 -> x0, local copies, waits for them, and re-layouts: 5.17 us -> none  [shards(): lax.scan(accumulate, initial, (left_ops, right_ops, charge, factor))]
    concatenate x1 -> x0, other arithmetic: 2.09 us -> none  [padded(): jnp.concatenate([lax.ppermute(tail, axis, [(i, (i + 1) % count) for i in...]
  transfers between devices with their start and end apart: 3 -> 13, of which waited for: 3 -> 4; matrix products, arithmetic and copies ran while one was open for 0% -> 0% of each run, Pallas kernels for 0% -> 56%
where the time goes in v1:
time: 70.5 us; the launch traced here: 70.2 us
  Pallas kernels  40.2 us (57%)
  starting transfers between devices  13.8 us (20%)
  waiting for transfers between devices  8.9 us (13%)
  local copies, waits for them, and re-layouts  7.08 us (10%)
    pallas_call x4, Pallas kernels, call(): pl.pallas_call(kernel, out_shape=results, in_specs=[SMALL] * len(small) +...  39.1 us
    unnamed x12, local copies, waits for them, and re-layouts  7.02 us
    ppermute x8, starting transfers between devices, chip_mate(): return lax.ppermute(value, 'op', across)  4.95 us
    ppermute x1, waiting for transfers between devices, shards(): near_far = lax.ppermute(near_send, 'op', far)  4.87 us
    ppermute x1, starting transfers between devices, shards(): low_halo = lax.ppermute(wavefunction[sectors - 1:], ('sec', 'op'), up)  4.74 us
    ppermute x1, waiting for transfers between devices, shards(): other_far = lax.ppermute(other_send, 'op', far_across)  2.2 us
    ppermute x8, waiting for transfers between devices, chip_mate(): return lax.ppermute(value, 'op', across)  1.82 us
    ppermute x1, starting transfers between devices, shards(): lax.ppermute((inner_far_keep + inner_far_in).astype(jnp.bfloat16), 'op',...  1.52 us
  transfers between devices with their start and end apart: 13, of which 4 were waited for; matrix products, arithmetic and copies ran while one was open for 0% of the time, Pallas kernels for 56%

profile of v1, /device:TPU:0, one launch (start us, length us, event | category | flops | bytes accessed | tf_op | source)
XLA Modules:
  0.0 70.2 jit_solution(2809454537825646739)
XLA Ops:
  0.0 0.5 collective-permute-start.6
  0.5 0.0 collective-permute-start.7
  0.5 0.0 copy-start
  0.5 1.7 %copy-done = bf16[8,384,384]{2,1,0:T(8,128)(2,1)S(1)} copy-done((bf16[8,384,384]{2,1,0:T(8,128)(2,1)S(1)}, bf16[8,384,384]{2,1,0:T(8,128)(2,1)}, u32[]{:S(2)}) %copy-start) | copy-done | bytes 2359320
  2.2 0.0 copy-start.1
  2.2 1.7 %copy-done.1 = bf16[8,384,384]{2,1,0:T(8,128)(2,1)S(1)} copy-done((bf16[8,384,384]{2,1,0:T(8,128)(2,1)S(1)}, bf16[8,384,384]{2,1,0:T(8,128)(2,1)}, u32[]{:S(2)}) %copy-start.1) | copy-done | bytes 2359320
  3.8 0.0 copy-start.2
  3.8 1.7 %copy-done.2 = bf16[8,384,384]{2,1,0:T(8,128)(2,1)S(1)} copy-done((bf16[8,384,384]{2,1,0:T(8,128)(2,1)S(1)}, bf16[8,384,384]{2,1,0:T(8,128)(2,1)}, u32[]{:S(2)}) %copy-start.2) | copy-done | bytes 2359320
  5.5 0.0 copy-start.3
  5.5 0.7 copy-done.3
  6.2 0.0 copy-start.4
  6.2 0.7 copy-done.4
  6.9 0.0 copy-start.5
  6.9 0.7 copy-done.5
  7.5 8.3 %inner_far.1 = (f32[384,384]{1,0:T(8,128)S(1)}, f32[384,384]{1,0:T(8,128)S(1)}) custom-call(s32[8]{0:T(128)S(1)} %copy-done.5, s32[8,8]{1,0:T(8,128)S(1)} %copy-done.3, f32[8,8]{1,0:T(8,128)S(1)} %copy-done.4, bf16[8,384,384]{2,1,0:T(8,128)(2,1)S(1)} %copy-done.1, bf16[8,384,384]{2,1,0:T(8,128)(2,1)S(1)} %copy-done.2, bf16[8,384,384]{2,1,0:T(8,128)(2,1)S(1)} %copy-done), custom_call_target="tpu_custom_call" | custom-call | flops 3623878656 | bytes 4718592 | tf_op jit(solution)/shard_map/inner_far/pallas_call | solution.py:228
  15.9 0.6 collective-permute-start.1
  16.4 0.1 collective-permute-start.4
  16.5 0.4 collective-permute-start.3
  16.9 0.1 fusion
  17.0 1.1 %collective-permute-done.3.charge_in = s32[8]{0:T(128)S(1)} collective-permute-done((s32[8]{0:T(128)S(1)}, s32[8]{0:T(128)S(1)}, u32[]{:S(2)}, u32[]{:S(2)}) %collective-permute-start.3) | collective-permute-done | bytes 64 | tf_op jit(solution)/shard_map/ppermute | solution.py:262
  18.1 4.7 %collective-permute-start.8 = (bf16[1,384,384]{2,1,0:T(8,128)(2,1)S(1)}, bf16[1,384,384]{2,1,0:T(8,128)(2,1)S(1)}, u32[]{:S(2)}, u32[]{:S(2)}) collective-permute-start(bf16[1,384,384]{2,1,0:T(8,128)(2,1)S(1)} %get-tuple-element.22), channel_id=1, source_target_pairs={{0,4},{2,6},{4,8},{6,10},{8,12},{10,14},{12,16},{14,18},{16,20},{1... | collective-permute-start | bytes 884744 | tf_op jit(solution)/shard_map/ppermute | solution.py:270
  22.8 0.0 collective-permute-done.4.couple_in
  22.8 0.7 collective-permute-start.9
  23.5 8.3 %inner_own.1 = (f32[384,384]{1,0:T(8,128)S(1)}, f32[384,384]{1,0:T(8,128)S(1)}) custom-call(s32[8]{0:T(128)S(1)} %copy-done.5, s32[8,8]{1,0:T(8,128)S(1)} %copy-done.3, f32[8,8]{1,0:T(8,128)S(1)} %copy-done.4, bf16[8,384,384]{2,1,0:T(8,128)(2,1)S(1)} %copy-done.1, bf16[8,384,384]{2,1,0:T(8,128)(2,1)S(1)} %copy-done.2, bf16[8,384,384]{2,1,0:T(8,128)(2,1)S(1)} %copy-done), custom_call_target="tpu_custom_call" | custom-call | flops 3623878656 | bytes 4718592 | tf_op jit(solution)/shard_map/inner_own/pallas_call | solution.py:228
  31.8 0.0 collective-permute-done.1
  31.8 3.0 %collective-permute-start.5 = (f32[8,8]{1,0:T(8,128)S(1)}, f32[8,8]{1,0:T(8,128)S(1)}, u32[]{:S(2)}, u32[]{:S(2)}) collective-permute-start(f32[8,8]{1,0:T(8,128)S(1)} %copy-done.4), channel_id=1, source_target_pairs={{0,1},{1,0},{2,3},{3,2},{4,5},{5,4},{6,7},{7,6},{8,9},{9,8},{10,11... | collective-permute-start | bytes 776 | tf_op jit(solution)/shard_map/ppermute | solution.py:262
  34.8 0.1 add_convert_fusion
  34.9 0.7 %collective-permute-done.5.amplitude_in = f32[8,8]{1,0:T(8,128)S(1)} collective-permute-done((f32[8,8]{1,0:T(8,128)S(1)}, f32[8,8]{1,0:T(8,128)S(1)}, u32[]{:S(2)}, u32[]{:S(2)}) %collective-permute-start.5) | collective-permute-done | bytes 288 | tf_op jit(solution)/shard_map/ppermute | solution.py:262
  35.6 0.3 collective-permute-start
  36.0 0.0 collective-permute-done.8.low_halo
  36.0 1.5 %collective-permute-start.2 = (bf16[4,96,384]{2,1,0:T(8,128)(2,1)S(1)}, bf16[4,96,384]{2,1,0:T(8,128)(2,1)S(1)}, u32[]{:S(2)}, u32[]{:S(2)}) collective-permute-start(bf16[4,96,384]{2,1,0:T(8,128)(2,1)S(1)} %add_convert_fusion), channel_id=1, source_target_pairs={{0,2},{1,3},{2,0},{3,1},{4,6},{5,7},{6,4},{7,5},{8,10},{9,11},{10,... | collective-permute-start | bytes 884744 | tf_op jit(solution)/shard_map/ppermute | solution.py:294
  37.5 0.0 collective-permute-done.9.high_halo
  37.5 0.0 collective-permute-done.6.left_in
  37.5 0.0 collective-permute-done.7.right_in
  37.5 11.3 %edge_own.1 = (f32[192,384]{1,0:T(8,128)S(1)}, f32[192,384]{1,0:T(8,128)S(1)}) custom-call(s32[8]{0:T(128)S(1)} %copy-done.5, s32[8,8]{1,0:T(8,128)S(1)} %copy-done.3, f32[8,8]{1,0:T(8,128)S(1)} %copy-done.4, s32[8]{0:T(128)S(1)} %collective-permute-done.3.charge_in, s32[8,8]{1,0:T(8,128)S(1)} %collective-permute-done.4.couple_in, ...), custom_call_target="tpu_custom_call" | custom-call | flops 3623878656 | bytes 9437184 | tf_op jit(solution)/shard_map/edge_own/pallas_call | solution.py:228
  48.8 0.1 collective-permute-start.11
  48.9 11.1 %edge_far.1 = (bf16[192,384]{1,0:T(8,128)(2,1)S(1)}, bf16[192,384]{1,0:T(8,128)(2,1)S(1)}) custom-call(s32[8]{0:T(128)S(1)} %copy-done.5, s32[8,8]{1,0:T(8,128)S(1)} %copy-done.3, f32[8,8]{1,0:T(8,128)S(1)} %copy-done.4, s32[8]{0:T(128)S(1)} %collective-permute-done.3.charge_in, s32[8,8]{1,0:T(8,128)S(1)} %collective-permute-done.4.couple_in, ...), custom_call_target="tpu_custom_call" | custom-call | flops 3623878656 | bytes 9437184 | tf_op jit(solution)/shard_map/edge_far/pallas_call | solution.py:228
  60.0 0.6 collective-permute-start.10
  60.6 1.3 %collective-permute-start.12 = (bf16[2,96,384]{2,1,0:T(8,128)(2,1)S(1)}, bf16[2,96,384]{2,1,0:T(8,128)(2,1)S(1)}, u32[]{:S(2)}, u32[]{:S(2)}) collective-permute-start(bf16[2,96,384]{2,1,0:T(8,128)(2,1)S(1)} %bitcast.14), channel_id=1, source_target_pairs={{0,3},{1,2},{2,1},{3,0},{4,7},{5,6},{6,5},{7,4},{8,11},{9,10},{10,... | collective-permute-start | bytes 442376 | tf_op jit(solution)/shard_map/ppermute | solution.py:297
  61.9 0.0 collective-permute-done.inner_chip
  61.9 0.0 collective-permute-done.2.inner_far
  61.9 4.9 %collective-permute-done.10.near_far = bf16[2,96,384]{2,1,0:T(8,128)(2,1)S(1)} collective-permute-done((bf16[2,96,384]{2,1,0:T(8,128)(2,1)S(1)}, bf16[2,96,384]{2,1,0:T(8,128)(2,1)S(1)}, u32[]{:S(2)}, u32[]{:S(2)}) %collective-permute-start.10) | collective-permute-done | bytes 147488 | tf_op jit(solution)/shard_map/ppermute | solution.py:296
  66.8 2.2 %collective-permute-done.12.other_far = bf16[2,96,384]{2,1,0:T(8,128)(2,1)S(1)} collective-permute-done((bf16[2,96,384]{2,1,0:T(8,128)(2,1)S(1)}, bf16[2,96,384]{2,1,0:T(8,128)(2,1)S(1)}, u32[]{:S(2)}, u32[]{:S(2)}) %collective-permute-start.12) | collective-permute-done | bytes 147488 | tf_op jit(solution)/shard_map/ppermute | solution.py:297
  69.0 0.0 collective-permute-done.11.other_chip
  69.0 1.2 %total.1 = f32[8,96,384]{2,1,0:T(8,128)} custom-call(f32[4,96,384]{2,1,0:T(8,128)S(1)} %bitcast.8, f32[4,96,384]{2,1,0:T(8,128)S(1)} %collective-permute-done.inner_chip, bf16[4,96,384]{2,1,0:T(8,128)(2,1)S(1)} %collective-permute-done.2.inner_far, f32[2,96,384]{2,1,0:T(8,128)S(1)} %bitcast.10, bf16[2,96,384]{2,1,0:T(8,128)(2,1)S(1)} %collective-permute-done.10.near_far, ...), custom_call_target="tpu_custom_call" | custom-call | tf_op jit(solution)/shard_map/total/pallas_call | solution.py:300
Async XLA Ops:
  0.0 37.5 %collective-permute-start.6 = (bf16[8,384,384]{2,1,0:T(8,128)(2,1)}, bf16[8,384,384]{2,1,0:T(8,128)(2,1)S(1)}, u32[]{:S(2)}, u32[]{:S(2)}) collective-permute-start(bf16[8,384,384]{2,1,0:T(8,128)(2,1)} %left.7), channel_id=1, source_target_pairs={{0,1},{1,0},{2,3},{3,2},{4,5},{5,4},{6,7},{7,6},{8,9},{9,8},{10,11... | collective-permute-start | bytes 7077896 | tf_op jit(solution)/shard_map/ppermute | solution.py:262
  0.5 37.0 %collective-permute-start.7 = (bf16[8,384,384]{2,1,0:T(8,128)(2,1)}, bf16[8,384,384]{2,1,0:T(8,128)(2,1)S(1)}, u32[]{:S(2)}, u32[]{:S(2)}) collective-permute-start(bf16[8,384,384]{2,1,0:T(8,128)(2,1)} %right.7), channel_id=1, source_target_pairs={{0,1},{1,0},{2,3},{3,2},{4,5},{5,4},{6,7},{7,6},{8,9},{9,8},{10,11... | collective-permute-start | bytes 7077896 | tf_op jit(solution)/shard_map/ppermute | solution.py:262
  0.5 1.7 %copy-start = (bf16[8,384,384]{2,1,0:T(8,128)(2,1)S(1)}, bf16[8,384,384]{2,1,0:T(8,128)(2,1)}, u32[]{:S(2)}) copy-start(bf16[8,384,384]{2,1,0:T(8,128)(2,1)} %cells.7) | copy-start | bytes 7077892
  2.2 1.7 %copy-start.1 = (bf16[8,384,384]{2,1,0:T(8,128)(2,1)S(1)}, bf16[8,384,384]{2,1,0:T(8,128)(2,1)}, u32[]{:S(2)}) copy-start(bf16[8,384,384]{2,1,0:T(8,128)(2,1)} %left.7) | copy-start | bytes 7077892
  3.8 1.7 %copy-start.2 = (bf16[8,384,384]{2,1,0:T(8,128)(2,1)S(1)}, bf16[8,384,384]{2,1,0:T(8,128)(2,1)}, u32[]{:S(2)}) copy-start(bf16[8,384,384]{2,1,0:T(8,128)(2,1)} %right.7) | copy-start | bytes 7077892
  5.5 0.7 copy-start.3
  6.2 0.7 copy-start.4
  6.9 0.7 copy-start.5
  15.9 16.0 %collective-permute-start.1 = (f32[4,96,384]{2,1,0:T(8,128)S(1)}, f32[4,96,384]{2,1,0:T(8,128)S(1)}, u32[]{:S(2)}, u32[]{:S(2)}) collective-permute-start(f32[4,96,384]{2,1,0:T(8,128)S(1)} %bitcast.12), channel_id=1, source_target_pairs={{0,1},{1,0},{2,3},{3,2},{4,5},{5,4},{6,7},{7,6},{8,9},{9,8},{10,11... | collective-permute-start | bytes 1769480 | tf_op jit(solution)/shard_map/ppermute | solution.py:262
  16.4 6.4 %collective-permute-start.4 = (s32[8,8]{1,0:T(8,128)S(1)}, s32[8,8]{1,0:T(8,128)S(1)}, u32[]{:S(2)}, u32[]{:S(2)}) collective-permute-start(s32[8,8]{1,0:T(8,128)S(1)} %copy-done.3), channel_id=1, source_target_pairs={{0,1},{1,0},{2,3},{3,2},{4,5},{5,4},{6,7},{7,6},{8,9},{9,8},{10,11... | collective-permute-start | bytes 776 | tf_op jit(solution)/shard_map/ppermute | solution.py:262
  16.5 1.6 %collective-permute-start.3 = (s32[8]{0:T(128)S(1)}, s32[8]{0:T(128)S(1)}, u32[]{:S(2)}, u32[]{:S(2)}) collective-permute-start(s32[8]{0:T(128)S(1)} %copy-done.5), channel_id=1, source_target_pairs={{0,1},{1,0},{2,3},{3,2},{4,5},{5,4},{6,7},{7,6},{8,9},{9,8},{10,11... | collective-permute-start | bytes 104 | tf_op jit(solution)/shard_map/ppermute | solution.py:262
  18.1 17.9 %collective-permute-start.8 = (bf16[1,384,384]{2,1,0:T(8,128)(2,1)S(1)}, bf16[1,384,384]{2,1,0:T(8,128)(2,1)S(1)}, u32[]{:S(2)}, u32[]{:S(2)}) collective-permute-start(bf16[1,384,384]{2,1,0:T(8,128)(2,1)S(1)} %get-tuple-element.22), channel_id=1, source_target_pairs={{0,4},{2,6},{4,8},{6,10},{8,12},{10,14},{12,16},{14,18},{16,20},{1... | collective-permute-start | bytes 884744 | tf_op jit(solution)/shard_map/ppermute | solution.py:270
  22.8 14.7 %collective-permute-start.9 = (bf16[1,384,384]{2,1,0:T(8,128)(2,1)S(1)}, bf16[1,384,384]{2,1,0:T(8,128)(2,1)S(1)}, u32[]{:S(2)}, u32[]{:S(2)}) collective-permute-start(bf16[1,384,384]{2,1,0:T(8,128)(2,1)S(1)} %get-tuple-element.21), channel_id=1, source_target_pairs={{1,29},{3,31},{5,1},{7,3},{9,5},{11,7},{13,9},{15,11},{17,13},{19,... | collective-permute-start | bytes 884744 | tf_op jit(solution)/shard_map/ppermute | solution.py:271
  31.8 3.8 %collective-permute-start.5 = (f32[8,8]{1,0:T(8,128)S(1)}, f32[8,8]{1,0:T(8,128)S(1)}, u32[]{:S(2)}, u32[]{:S(2)}) collective-permute-start(f32[8,8]{1,0:T(8,128)S(1)} %copy-done.4), channel_id=1, source_target_pairs={{0,1},{1,0},{2,3},{3,2},{4,5},{5,4},{6,7},{7,6},{8,9},{9,8},{10,11... | collective-permute-start | bytes 776 | tf_op jit(solution)/shard_map/ppermute | solution.py:262
  35.6 26.3 %collective-permute-start = (f32[4,96,384]{2,1,0:T(8,128)S(1)}, f32[4,96,384]{2,1,0:T(8,128)S(1)}, u32[]{:S(2)}, u32[]{:S(2)}) collective-permute-start(f32[4,96,384]{2,1,0:T(8,128)S(1)} %bitcast.11), channel_id=1, source_target_pairs={{0,1},{1,0},{2,3},{3,2},{4,5},{5,4},{6,7},{7,6},{8,9},{9,8},{10,11... | collective-permute-start | bytes 1769480 | tf_op jit(solution)/shard_map/ppermute | solution.py:262
  36.0 26.0 %collective-permute-start.2 = (bf16[4,96,384]{2,1,0:T(8,128)(2,1)S(1)}, bf16[4,96,384]{2,1,0:T(8,128)(2,1)S(1)}, u32[]{:S(2)}, u32[]{:S(2)}) collective-permute-start(bf16[4,96,384]{2,1,0:T(8,128)(2,1)S(1)} %add_convert_fusion), channel_id=1, source_target_pairs={{0,2},{1,3},{2,0},{3,1},{4,6},{5,7},{6,4},{7,5},{8,10},{9,11},{10,... | collective-permute-start | bytes 884744 | tf_op jit(solution)/shard_map/ppermute | solution.py:294
  48.8 20.2 %collective-permute-start.11 = (f32[2,96,384]{2,1,0:T(8,128)S(1)}, f32[2,96,384]{2,1,0:T(8,128)S(1)}, u32[]{:S(2)}, u32[]{:S(2)}) collective-permute-start(f32[2,96,384]{2,1,0:T(8,128)S(1)} %bitcast.13), channel_id=1, source_target_pairs={{0,1},{1,0},{2,3},{3,2},{4,5},{5,4},{6,7},{7,6},{8,9},{9,8},{10,11... | collective-permute-start | bytes 884744 | tf_op jit(solution)/shard_map/ppermute | solution.py:262
  60.0 6.8 %collective-permute-start.10 = (bf16[2,96,384]{2,1,0:T(8,128)(2,1)S(1)}, bf16[2,96,384]{2,1,0:T(8,128)(2,1)S(1)}, u32[]{:S(2)}, u32[]{:S(2)}) collective-permute-start(bf16[2,96,384]{2,1,0:T(8,128)(2,1)S(1)} %bitcast.15), channel_id=1, source_target_pairs={{0,2},{1,3},{2,0},{3,1},{4,6},{5,7},{6,4},{7,5},{8,10},{9,11},{10,... | collective-permute-start | bytes 442376 | tf_op jit(solution)/shard_map/ppermute | solution.py:296
  60.6 8.4 %collective-permute-start.12 = (bf16[2,96,384]{2,1,0:T(8,128)(2,1)S(1)}, bf16[2,96,384]{2,1,0:T(8,128)(2,1)S(1)}, u32[]{:S(2)}, u32[]{:S(2)}) collective-permute-start(bf16[2,96,384]{2,1,0:T(8,128)(2,1)S(1)} %bitcast.14), channel_id=1, source_target_pairs={{0,3},{1,2},{2,1},{3,0},{4,7},{5,6},{6,5},{7,4},{8,11},{9,10},{10,... | collective-permute-start | bytes 442376 | tf_op jit(solution)/shard_map/ppermute | solution.py:297

commit v2 on v0

--- a/solution.py
+++ b/solution.py
@@ -1,7 +1,13 @@
 import jax
 import jax.numpy as jnp
 from jax import lax
+from jax.experimental import pallas as pl
+from jax.experimental.pallas import tpu as pltpu
 from jax.sharding import PartitionSpec as P
+
+
+CORES = 2
+EDGE = 2
 
 
 def padded(cells, sides, width):
@@ -28,7 +34,7 @@
     return contribution * factor_values[:, None, None]
 
 
-def shards(wavefunction, left_ops, right_ops, charge, couple, amplitude):
+def plain_shards(wavefunction, left_ops, right_ops, charge, couple, amplitude):
     factor = amplitude * couple.astype(jnp.float32)
     sectors = wavefunction.shape[0]
     states = wavefunction.shape[1]
@@ -41,8 +47,296 @@
         return (accumulated + batched(left_op, sources, right_op, factor_row), None)
 
     initial = jnp.zeros((sectors, states, states), jnp.float32)
-    accumulated, unused = lax.scan(accumulate, initial, (left_ops, right_ops, charge, factor))
+    accumulated, _ = lax.scan(accumulate, initial, (left_ops, right_ops, charge, factor))
     return lax.psum_scatter(accumulated, "op", scatter_dimension=1, tiled=True)
+
+
+def middle_of(k, factors, own, left, sources, middles, first_target, targets, chip, core):
+    states = sources.shape[-1]
+    half = middles.shape[0] // (CORES * targets)
+    shift = 1 - factors[own, factors.shape[1] - 1].astype(jnp.int32)
+    wide = jnp.concatenate([sources[shift + t] for t in range(targets)], axis=1)
+    rows = jnp.concatenate(
+        [left[own, pl.ds(row_of(chip, owner, half), half)] for owner in (core, 1 - core)], axis=0
+    )
+    middle = jnp.dot(rows, wide, preferred_element_type=jnp.float32)
+    for t in range(targets):
+        factor = factors[own, first_target + t]
+        block = middle[:, t * states : (t + 1) * states].astype(jnp.bfloat16)
+        block = (block.astype(jnp.float32) * factor).astype(jnp.bfloat16)
+        for part in range(CORES):
+            row = (part * targets + t) * half
+            middles[row : row + half, k * states : (k + 1) * states] = block[part * half : (part + 1) * half]
+
+
+def summed(right, middles, results):
+    width = middles.shape[0] // CORES
+    step = 256
+    for low in range(0, CORES * width, step):
+        high = min(low + step, CORES * width)
+        total = lax.dot_general(
+            right, middles[low:high, :], (((1,), (1,)), ((), ())), preferred_element_type=jnp.float32
+        ).T
+        for part in range(CORES):
+            begin, end = max(low, part * width), min(high, (part + 1) * width)
+            if begin < end:
+                results[part][begin - part * width : end - part * width, :] = total[
+                    begin - low : end - low, :
+                ].astype(results[part].dtype)
+
+
+def position():
+    place = lax.axis_index("op")
+    return place // CORES, place % CORES
+
+
+def row_of(chip, core, half):
+    return pl.multiple_of((chip * CORES + core) * half, 32)
+
+
+def inner_far_kernel(
+    charge, couple, amplitude, left_far, right_far, cells_far, keep, send, factors, left, right, cells,
+    middles, charge_here, couple_here, amplitude_here, small_sem, cell_sem, left_sem, right_sem,
+):
+    chip, core = position()
+    operators, _ = left.shape[:2]
+    sectors = cells.shape[0]
+    targets = sectors - 2 * EDGE
+    half = keep.shape[0] // targets
+    first = EDGE - 1
+    slabs = targets + 2
+    chip_rows = CORES * half
+
+    def rows(k, place):
+        at = pl.ds(pl.multiple_of(place * chip_rows, 64), chip_rows)
+        return left_far.at[k, at], left.at[k, at]
+
+    def begin(source, target, sem):
+        copy = pltpu.make_async_copy(source, target, sem)
+        copy.start()
+        return copy
+
+    small = [
+        begin(charge, charge_here, small_sem.at[0]),
+        begin(couple, couple_here, small_sem.at[1]),
+        begin(amplitude, amplitude_here, small_sem.at[2]),
+    ]
+    inside = pl.ds(first, slabs)
+    cell = begin(cells_far.at[inside], cells.at[inside], cell_sem.at[0])
+    lefts = [begin(*rows(k, 1 - chip), left_sem.at[0, k]) for k in range(operators)]
+    rights = [begin(right_far.at[k], right.at[k], right_sem.at[k]) for k in range(operators)]
+    later = [begin(*rows(k, chip), left_sem.at[1, k]) for k in range(operators)]
+    later.append(begin(cells_far.at[pl.ds(0, first)], cells.at[pl.ds(0, first)], cell_sem.at[1]))
+    last = pl.ds(first + slabs, first)
+    later.append(begin(cells_far.at[last], cells.at[last], cell_sem.at[2]))
+    for copy in small:
+        copy.wait()
+    for k in range(operators):
+        for t in range(sectors):
+            factors[k, t] = amplitude_here[k, t] * couple_here[k, t].astype(jnp.float32)
+        factors[k, sectors] = charge_here[k].astype(jnp.float32)
+    cell.wait()
+    for k in range(operators):
+        if k == 0:
+            for copy in lefts[:2]:
+                copy.wait()
+        elif k == 2:
+            for copy in lefts[2:]:
+                copy.wait()
+        middle_of(k, factors, k, left, cells.at[inside], middles, EDGE, targets, 1 - chip, core)
+    for copy in rights:
+        copy.wait()
+    summed(jnp.concatenate([right[k] for k in range(operators)], axis=1), middles, (keep, send))
+    for copy in later:
+        copy.wait()
+
+
+def inner_own_kernel(factors, left, right, cells, keep, send, middles):
+    chip, core = position()
+    operators = left.shape[0]
+    targets = cells.shape[0] - 2 * EDGE
+    inside = cells.at[pl.ds(EDGE - 1, targets + 2)]
+    for k in range(operators):
+        middle_of(k, factors, k, left, inside, middles, EDGE, targets, chip, core)
+    summed(jnp.concatenate([right[k] for k in range(operators)], axis=1), middles, (keep, send))
+
+
+def edge_products(groups, sources, middles, results, first_target, chip, core):
+    k = 0
+    for factors, left, right in groups:
+        for own in range(left.shape[0]):
+            middle_of(k, factors, own, left, sources, middles, first_target, EDGE, chip, core)
+            k += 1
+    wide = jnp.concatenate([right[own] for _, _, right in groups for own in range(right.shape[0])], axis=1)
+    summed(wide, middles, results)
+
+
+def edge_far_kernel(
+    factors, factors_in, left, right, left_in, right_in, cells, halo, keep, send, sources, middles, sem
+):
+    chip, core = position()
+    sectors = cells.shape[0]
+    inside = EDGE + 1
+    copies = [
+        pltpu.make_async_copy(
+            cells.at[pl.ds((sectors - inside) * core, inside)], sources.at[pl.ds(1 - core, inside)], sem.at[0]
+        ),
+        pltpu.make_async_copy(halo.at[0], sources.at[inside * core], sem.at[1]),
+    ]
+    for copy in copies:
+        copy.start()
+    for copy in copies:
+        copy.wait()
+    groups = ((factors, left, right), (factors_in, left_in, right_in))
+    edge_products(groups, sources, middles, (keep, send), (sectors - EDGE) * core, 1 - chip, core)
+
+
+def edge_own_kernel(factors, factors_in, left, right, left_in, right_in, sources, keep, send, middles):
+    chip, core = position()
+    sectors = factors.shape[1] - 1
+    groups = ((factors, left, right), (factors_in, left_in, right_in))
+    edge_products(groups, sources, middles, (keep, send), (sectors - EDGE) * core, chip, core)
+
+
+def sum_kernel(inner_own, inner_chip, inner_far, near_own, near_far, other_chip, other_far, sigma):
+    core = lax.axis_index("op") % CORES
+    sectors = sigma.shape[0]
+    far = sectors - EDGE
+    sigma[EDGE:far] = inner_own[...] + inner_chip[...] + inner_far[...].astype(jnp.float32)
+    sigma[pl.ds(far * core, EDGE)] = near_own[...] + near_far[...].astype(jnp.float32)
+    sigma[pl.ds(far * (1 - core), EDGE)] = other_chip[...] + other_far[...].astype(jnp.float32)
+
+
+SMALL = pl.BlockSpec(memory_space=pltpu.SMEM)
+LARGE = pl.BlockSpec(memory_space=pl.ANY)
+BLOCK = pl.BlockSpec(memory_space=pltpu.VMEM)
+MIB = 1024 * 1024
+
+
+def shards(wavefunction, left_ops, right_ops, charge, couple, amplitude):
+    sec = lax.axis_size("sec")
+    op = lax.axis_size("op")
+    sectors, states = wavefunction.shape[:2]
+    operators = left_ops.shape[0]
+    half = states // op
+    inner = sectors - 2 * EDGE
+    wide, narrow = jnp.float32, jnp.bfloat16
+
+    def shape(*dims, dtype=wide):
+        return jax.ShapeDtypeStruct(dims, dtype)
+
+    def run(kernel, ops, targets, operands, in_specs, outs, out_specs, scratch):
+        return pl.pallas_call(
+            kernel,
+            out_shape=outs,
+            in_specs=in_specs,
+            out_specs=out_specs,
+            scratch_shapes=[pltpu.VMEM((targets * CORES * half, ops * states), narrow)] + scratch,
+            compiler_params=pltpu.CompilerParams(vmem_limit_bytes=20 * MIB),
+            cost_estimate=pl.CostEstimate(
+                flops=ops * targets * CORES * half * states * states * 4,
+                bytes_accessed=ops * states * states * 4,
+                transcendentals=0,
+            ),
+        )(*operands)
+
+    def over_op(value, flip):
+        return lax.ppermute(value, "op", [(i, i ^ flip) for i in range(op)])
+
+
+    def per_target(value):
+        return value.reshape(-1, half, states)
+
+    core = lax.axis_index("op") & (CORES - 1)
+    ring = []
+    for s in range(sec):
+        for o in range(op):
+            ring.append((s * op + o, (s + 1 if o % CORES == 0 else s - 1) % sec * op + o))
+    border = lax.dynamic_slice_in_dim(wavefunction, (sectors - 1) * (1 - core), 1, 0)
+    halo = lax.ppermute(border, ("sec", "op"), ring)
+    left_in = over_op(left_ops, 1)
+    right_in = over_op(right_ops, 1)
+
+    block = shape(inner * half, states)
+    far_keep, far_send, factors, left, right, cells = run(
+        inner_far_kernel,
+        operators,
+        inner,
+        [
+            pltpu.with_memory_space_constraint(value, pltpu.HBM)
+            for value in (charge, couple, amplitude, left_ops, right_ops, wavefunction)
+        ],
+        [LARGE] * 6,
+        [
+            block,
+            block,
+            shape(operators, sectors + 1),
+            pltpu.VMEM(left_ops.shape, narrow),
+            pltpu.VMEM(right_ops.shape, narrow),
+            pltpu.VMEM(wavefunction.shape, narrow),
+        ],
+        [BLOCK, BLOCK, SMALL, BLOCK, BLOCK, BLOCK],
+        [
+            pltpu.SMEM(charge.shape, charge.dtype),
+            pltpu.SMEM(couple.shape, couple.dtype),
+            pltpu.SMEM(amplitude.shape, amplitude.dtype),
+            pltpu.SemaphoreType.DMA((3,)),
+            pltpu.SemaphoreType.DMA((3,)),
+            pltpu.SemaphoreType.DMA((2, operators)),
+            pltpu.SemaphoreType.DMA((operators,)),
+        ],
+    )
+    far_in = over_op(far_send, 1)
+    factors_in = over_op(factors, 1)
+    inner_own, inner_send = run(
+        inner_own_kernel,
+        operators,
+        inner,
+        [factors, left, right, cells],
+        [SMALL, BLOCK, BLOCK, BLOCK],
+        [block, block],
+        [BLOCK, BLOCK],
+        [],
+    )
+    inner_chip = over_op(inner_send, 1)
+    inner_far = over_op((far_keep + far_in).astype(narrow), CORES)
+
+    held = [factors, factors_in, left, right, left_in, right_in]
+    held_specs = [SMALL, SMALL, BLOCK, BLOCK, BLOCK, BLOCK]
+    edge_narrow = shape(EDGE * half, states, dtype=narrow)
+    near_send, other_send, sources = run(
+        edge_far_kernel,
+        CORES * operators,
+        EDGE,
+        held + [cells, halo],
+        held_specs + [BLOCK, LARGE],
+        [edge_narrow, edge_narrow, shape(EDGE + 2, states, states, dtype=narrow)],
+        [BLOCK, BLOCK, BLOCK],
+        [pltpu.SemaphoreType.DMA((2,))],
+    )
+    near_far = over_op(near_send, CORES)
+    other_far = over_op(other_send, CORES + 1)
+    edge_wide = shape(EDGE * half, states)
+    near_own, near_mate = run(
+        edge_own_kernel,
+        CORES * operators,
+        EDGE,
+        held + [sources],
+        held_specs + [BLOCK],
+        [edge_wide, edge_wide],
+        [BLOCK, BLOCK],
+        [],
+    )
+    other_chip = over_op(near_mate, 1)
+    parts = (inner_own, inner_chip, inner_far, near_own, near_far, other_chip, other_far)
+    return pl.pallas_call(
+        sum_kernel,
+        out_shape=shape(sectors, half, states),
+        in_specs=[BLOCK] * len(parts),
+        out_specs=BLOCK,
+        compiler_params=pltpu.CompilerParams(vmem_limit_bytes=16 * MIB),
+        name="total",
+    )(*[per_target(part) for part in parts])
 
 
 def solution(mesh):
@@ -54,6 +348,8 @@
         P("op", "sec"),
         P("op", "sec"),
     )
+    two_chips = mesh.shape["op"] == CORES * CORES
     return jax.shard_map(
-        shards, mesh=mesh, in_specs=placed, out_specs=P("sec", "op", None), check_vma=False
-    )
+        shards if two_chips else plain_shards,
+        mesh=mesh, in_specs=placed, out_specs=P("sec", "op", None), check_vma=False,
+    )

time: 157 us -> 58.7 us (0.37)
  matrix products: 58.5 us -> 0 us
  waiting for transfers between devices: 59.1 us -> 7.01 us
  Pallas kernels: 0 us -> 29.4 us
  between operations: 13.4 us -> 0.07 us
  loops' own time: 10.3 us -> 0 us
  starting transfers between devices: 6.13 us -> 10.4 us
  local copies, waits for them, and re-layouts: 6.36 us -> 10.3 us
  other arithmetic: 2.8 us -> 1.12 us
    dot_general x8 -> x0, matrix products: 58.5 us -> none  [batched(): jnp.einsum('sik,lk->sil', middle, right_op, preferred_element_type=jnp.fl...]
    reduce_scatter x1 -> x0, waiting for transfers between devices: 48.2 us -> none  [shards(): return lax.psum_scatter(accumulated, 'op', scatter_dimension=1, tiled=True)]
    pallas_call x0 -> x5, Pallas kernels: none -> 29.4 us  [the longest x4 28.3 us: run(): pl.pallas_call(kernel, out_shape=outs, in_specs=in_specs, out_specs=out_s...]
    another operation x1 -> x0, loops' own time: 10.3 us -> none  [shards(): lax.scan(accumulate, initial, (left_ops, right_ops, charge, factor))]
    unnamed x2 -> x12, local copies, waits for them, and re-layouts: 0.01 us -> 9.32 us
    ppermute x2 -> x10, starting transfers between devices: 6.12 us -> 10.4 us  [the longest x9 7.89 us: over_op(): return lax.ppermute(value, 'op', [(i, i ^ flip) for i in range(op)])]
    dynamic_slice x8 -> x1, local copies, waits for them, and re-layouts: 5.17 us -> 0.99 us  [shards(): lax.dynamic_slice_in_dim(wavefunction, (sectors - 1) * (1 - core), 1, 0)]
    ppermute x2 -> x10, waiting for transfers between devices: 11 us -> 7.01 us  [the longest x9 7.01 us: over_op(): return lax.ppermute(value, 'op', [(i, i ^ flip) for i in range(op)])]
  transfers between devices with their start and end apart: 3 -> 10, of which waited for: 3 -> 2; matrix products, arithmetic and copies ran while one was open for 0% -> 4% of each run, Pallas kernels for 0% -> 48%
where the time goes in v2:
time: 58.7 us; the launch traced here: 58.3 us
  Pallas kernels  29.4 us (50%)
  starting transfers between devices  10.4 us (18%)
  local copies, waits for them, and re-layouts  10.3 us (18%)
  waiting for transfers between devices  7.01 us (12%)
  other arithmetic  1.12 us (2%)
    pallas_call x4, Pallas kernels, run(): pl.pallas_call(kernel, out_shape=outs, in_specs=in_specs, out_specs=out_s...  28.3 us
    unnamed x12, local copies, waits for them, and re-layouts  9.32 us
    ppermute x9, starting transfers between devices, over_op(): return lax.ppermute(value, 'op', [(i, i ^ flip) for i in range(op)])  7.89 us
    ppermute x9, waiting for transfers between devices, over_op(): return lax.ppermute(value, 'op', [(i, i ^ flip) for i in range(op)])  7.01 us
    ppermute x1, starting transfers between devices, shards(): halo = lax.ppermute(border, ('sec', 'op'), ring)  2.53 us
  transfers between devices with their start and end apart: 10, of which 2 were waited for; matrix products, arithmetic and copies ran while one was open for 4% of the time, Pallas kernels for 48%

profile of v2, /device:TPU:0, one launch (start us, length us, event | category | flops | bytes accessed | tf_op | source)
XLA Modules:
  0.0 58.3 jit_solution(10390728497394378749)
XLA Ops:
  0.0 0.5 collective-permute-start.4
  0.5 0.0 collective-permute-start.5
  0.5 8.5 %shard_map.64 = (f32[384,384]{1,0:T(8,128)S(1)}, f32[384,384]{1,0:T(8,128)S(1)}, f32[8,9]{1,0:T(8,128)S(1)}, bf16[8,384,384]{2,1,0:T(8,128)(2,1)S(1)}, bf16[8,38...) custom-call(s32[8]{0:T(128)} %charge.1, s32[8,8]{1,0:T(8,128)} %couple.1, f32[8,8]{1,0:T(8,128)} %amplitude.1, ...), custom_call_target="tpu_custom_call" | custom-call | flops 3623878656 | bytes 4718592 | tf_op jit(solution)/shard_map/pallas_call | solution.py:229
  9.0 0.0 copy-start
  9.0 1.4 %copy-done = bf16[8,384,384]{2,1,0:T(8,128)(2,1)} copy-done((bf16[8,384,384]{2,1,0:T(8,128)(2,1)}, bf16[8,384,384]{2,1,0:T(8,128)(2,1)S(1)}, u32[]{:S(2)}) %copy-start) | copy-done | bytes 2359320
  10.4 0.0 copy-start.2
  10.4 1.4 %copy-done.2 = bf16[8,384,384]{2,1,0:T(8,128)(2,1)} copy-done((bf16[8,384,384]{2,1,0:T(8,128)(2,1)}, bf16[8,384,384]{2,1,0:T(8,128)(2,1)S(1)}, u32[]{:S(2)}) %copy-start.2) | copy-done | bytes 2359320
  11.9 0.0 copy-start.4
  11.9 1.5 %copy-done.4 = bf16[8,384,384]{2,1,0:T(8,128)(2,1)} copy-done((bf16[8,384,384]{2,1,0:T(8,128)(2,1)}, bf16[8,384,384]{2,1,0:T(8,128)(2,1)S(1)}, u32[]{:S(2)}) %copy-start.4) | copy-done | bytes 2359320
  13.3 0.5 collective-permute-start.1
  13.9 1.0 %constant_dynamic-slice_fusion = bf16[1,384,384]{2,1,0:T(8,128)(2,1)S(1)} fusion(bf16[8,384,384]{2,1,0:T(8,128)(2,1)} %cells_far.1, s32[]{:T(128)S(6)} %select_n.3), kind=kLoop, calls=%fused_computation.1 | loop fusion | bytes 589828 | tf_op jit(solution)/shard_map/dynamic_slice | solution.py:255
  14.9 2.5 %collective-permute-start.6 = (bf16[1,384,384]{2,1,0:T(8,128)(2,1)S(1)}, bf16[1,384,384]{2,1,0:T(8,128)(2,1)S(1)}, u32[]{:S(2)}, u32[]{:S(2)}) collective-permute-start(bf16[1,384,384]{2,1,0:T(8,128)(2,1)S(1)} %constant_dynamic-slice_fusion), channel_id=1, source_target_pairs={{0,4},{1,29},{2,6},{3,31},{4,8},{5,1},{6,10},{7,3},{8,12},{9,5},{1... | collective-permute-start | bytes 884744 | tf_op jit(solution)/shard_map/ppermute | solution.py:256
  17.4 3.2 %collective-permute-start.3 = (f32[8,9]{1,0:T(8,128)S(1)}, f32[8,9]{1,0:T(8,128)S(1)}, u32[]{:S(2)}, u32[]{:S(2)}) collective-permute-start(f32[8,9]{1,0:T(8,128)S(1)} %get-tuple-element.18.factors), channel_id=1, source_target_pairs={{0,1},{1,0},{2,3},{3,2},{4,5},{5,4},{6,7},{7,6},{8,9},{9,8},{10,11... | collective-permute-start | bytes 872 | tf_op jit(solution)/shard_map/ppermute | solution.py:244
  20.6 0.0 copy-start.1
  20.6 1.7 %copy-done.1 = bf16[8,384,384]{2,1,0:T(8,128)(2,1)S(1)} copy-done((bf16[8,384,384]{2,1,0:T(8,128)(2,1)S(1)}, bf16[8,384,384]{2,1,0:T(8,128)(2,1)}, u32[]{:S(2)}) %copy-start.1) | copy-done | bytes 2359320
  22.3 0.0 copy-start.3
  22.3 1.7 %copy-done.3 = bf16[8,384,384]{2,1,0:T(8,128)(2,1)S(1)} copy-done((bf16[8,384,384]{2,1,0:T(8,128)(2,1)S(1)}, bf16[8,384,384]{2,1,0:T(8,128)(2,1)}, u32[]{:S(2)}) %copy-start.3) | copy-done | bytes 2359320
  24.0 0.0 copy-start.5
  24.0 1.7 %copy-done.5 = bf16[8,384,384]{2,1,0:T(8,128)(2,1)S(1)} copy-done((bf16[8,384,384]{2,1,0:T(8,128)(2,1)S(1)}, bf16[8,384,384]{2,1,0:T(8,128)(2,1)}, u32[]{:S(2)}) %copy-start.5) | copy-done | bytes 2359320
  25.6 5.3 %shard_map.65 = (f32[384,384]{1,0:T(8,128)S(1)}, f32[384,384]{1,0:T(8,128)S(1)}) custom-call(f32[8,9]{1,0:T(8,128)S(1)} %get-tuple-element.18.factors, bf16[8,384,384]{2,1,0:T(8,128)(2,1)S(1)} %copy-done.1, bf16[8,384,384]{2,1,0:T(8,128)(2,1)S(1)} %copy-done.3, bf16[8,384,384]{2,1,0:T(8,128)(2,1)S(1)} %copy-done.5), custom_call_target="tpu_custom_call" | custom-call | flops 3623878656 | bytes 4718592 | tf_op jit(solution)/shard_map/pallas_call | solution.py:229
  31.0 0.0 collective-permute-done.1
  31.0 0.1 collective-permute-start
  31.1 1.1 %add_convert_fusion = bf16[384,384]{1,0:T(8,128)(2,1)S(1)} fusion(f32[384,384]{1,0:T(8,128)S(1)} %get-tuple-element.24, f32[384,384]{1,0:T(8,128)} %collective-permute-done.1), kind=kLoop, calls=%fused_computation | loop fusion | flops 294912 | bytes 1474560 | tf_op jit(solution)/shard_map/convert_element_type | solution.py:302
  32.2 0.0 collective-permute-done.3.factors_in
  32.2 1.6 %collective-permute-start.2 = (bf16[384,384]{1,0:T(8,128)(2,1)S(1)}, bf16[384,384]{1,0:T(8,128)(2,1)S(1)}, u32[]{:S(2)}, u32[]{:S(2)}) collective-permute-start(bf16[384,384]{1,0:T(8,128)(2,1)S(1)} %add_convert_fusion), channel_id=1, source_target_pairs={{0,2},{1,3},{2,0},{3,1},{4,6},{5,7},{6,4},{7,5},{8,10},{9,11},{10,... | collective-permute-start | bytes 884744 | tf_op jit(solution)/shard_map/ppermute | solution.py:244
  33.8 0.0 collective-permute-done.6.halo
  33.8 0.0 collective-permute-done.4.left_in
  33.8 0.0 collective-permute-done.5.right_in
  33.8 7.4 %shard_map.66 = (bf16[192,384]{1,0:T(8,128)(2,1)S(1)}, bf16[192,384]{1,0:T(8,128)(2,1)S(1)}, bf16[4,384,384]{2,1,0:T(8,128)(2,1)S(1)}) custom-call(f32[8,9]{1,0:T(8,128)S(1)} %get-tuple-element.18.factors, f32[8,9]{1,0:T(8,128)S(1)} %collective-permute-done.3.factors_in, bf16[8,384,384]{2,1,0:T(8,128)(2,1)S(1)} %copy-done.1, ...), custom_call_target="tpu_custom_call" | custom-call | flops 3623878656 | bytes 9437184 | tf_op jit(solution)/shard_map/pallas_call | solution.py:229
  41.3 7.0 %shard_map.67 = (f32[192,384]{1,0:T(8,128)S(1)}, f32[192,384]{1,0:T(8,128)S(1)}) custom-call(f32[8,9]{1,0:T(8,128)S(1)} %get-tuple-element.18.factors, f32[8,9]{1,0:T(8,128)S(1)} %collective-permute-done.3.factors_in, bf16[8,384,384]{2,1,0:T(8,128)(2,1)S(1)} %copy-done.1, bf16[8,384,384]{2,1,0:T(8,128)(2,1)S(1)} %copy-done.3, ...), custom_call_target="tpu_custom_call" | custom-call | flops 3623878656 | bytes 9437184 | tf_op jit(solution)/shard_map/pallas_call | solution.py:229
  48.3 0.2 collective-permute-start.8
  48.4 0.5 collective-permute-start.7
  49.0 1.2 %collective-permute-start.9 = (bf16[192,384]{1,0:T(8,128)(2,1)S(1)}, bf16[192,384]{1,0:T(8,128)(2,1)S(1)}, u32[]{:S(2)}, u32[]{:S(2)}) collective-permute-start(bf16[192,384]{1,0:T(8,128)(2,1)S(1)} %get-tuple-element.30), channel_id=1, source_target_pairs={{0,3},{1,2},{2,1},{3,0},{4,7},{5,6},{6,5},{7,4},{8,11},{9,10},{10,... | collective-permute-start | bytes 442376 | tf_op jit(solution)/shard_map/ppermute | solution.py:244
  50.2 0.0 collective-permute-done
  50.2 0.0 collective-permute-done.2
  50.2 5.0 %collective-permute-done.7 = bf16[192,384]{1,0:T(8,128)(2,1)S(1)} collective-permute-done((bf16[192,384]{1,0:T(8,128)(2,1)S(1)}, bf16[192,384]{1,0:T(8,128)(2,1)S(1)}, u32[]{:S(2)}, u32[]{:S(2)}) %collective-permute-start.7) | collective-permute-done | bytes 147488 | tf_op jit(solution)/shard_map/ppermute | solution.py:244
  55.2 2.0 %collective-permute-done.9 = bf16[192,384]{1,0:T(8,128)(2,1)S(1)} collective-permute-done((bf16[192,384]{1,0:T(8,128)(2,1)S(1)}, bf16[192,384]{1,0:T(8,128)(2,1)S(1)}, u32[]{:S(2)}, u32[]{:S(2)}) %collective-permute-start.9) | collective-permute-done | bytes 147488 | tf_op jit(solution)/shard_map/ppermute | solution.py:244
  57.2 0.0 collective-permute-done.8
  57.2 1.1 %total.1 = f32[8,96,384]{2,1,0:T(8,128)} custom-call(f32[4,96,384]{2,1,0:T(8,128)S(1)} %bitcast.7, f32[4,96,384]{2,1,0:T(8,128)S(1)} %bitcast.8, bf16[4,96,384]{2,1,0:T(8,128)(2,1)S(1)} %bitcast.9, f32[2,96,384]{2,1,0:T(8,128)S(1)} %bitcast.10, bf16[2,96,384]{2,1,0:T(8,128)(2,1)S(1)} %bitcast.12, f32[2,96,384]{2,1,0:T(8,128)S(1)} %bitcast.11, ...), custom_call_target="tpu_custom_call" | custom-call | tf_op jit(solution)/shard_map/total/pallas_call | solution.py:332
Async XLA Ops:
  0.0 33.8 %collective-permute-start.4 = (bf16[8,384,384]{2,1,0:T(8,128)(2,1)}, bf16[8,384,384]{2,1,0:T(8,128)(2,1)S(1)}, u32[]{:S(2)}, u32[]{:S(2)}) collective-permute-start(bf16[8,384,384]{2,1,0:T(8,128)(2,1)} %left_far.1), channel_id=1, source_target_pairs={{0,1},{1,0},{2,3},{3,2},{4,5},{5,4},{6,7},{7,6},{8,9},{9,8},{10,11... | collective-permute-start | bytes 7077896 | tf_op jit(solution)/shard_map/ppermute | solution.py:244
  0.5 33.3 %collective-permute-start.5 = (bf16[8,384,384]{2,1,0:T(8,128)(2,1)}, bf16[8,384,384]{2,1,0:T(8,128)(2,1)}, u32[]{:S(2)}, u32[]{:S(2)}) collective-permute-start(bf16[8,384,384]{2,1,0:T(8,128)(2,1)} %right_far.1), channel_id=1, source_target_pairs={{0,1},{1,0},{2,3},{3,2},{4,5},{5,4},{6,7},{7,6},{8,9},{9,8},{10,11... | collective-permute-start | bytes 7077896 | tf_op jit(solution)/shard_map/ppermute | solution.py:244
  9.0 1.4 %copy-start = (bf16[8,384,384]{2,1,0:T(8,128)(2,1)}, bf16[8,384,384]{2,1,0:T(8,128)(2,1)S(1)}, u32[]{:S(2)}) copy-start(bf16[8,384,384]{2,1,0:T(8,128)(2,1)S(1)} %get-tuple-element.19.left) | copy-start | bytes 7077892
  10.4 1.4 %copy-start.2 = (bf16[8,384,384]{2,1,0:T(8,128)(2,1)}, bf16[8,384,384]{2,1,0:T(8,128)(2,1)S(1)}, u32[]{:S(2)}) copy-start(bf16[8,384,384]{2,1,0:T(8,128)(2,1)S(1)} %get-tuple-element.20.right) | copy-start | bytes 7077892
  11.9 1.5 %copy-start.4 = (bf16[8,384,384]{2,1,0:T(8,128)(2,1)}, bf16[8,384,384]{2,1,0:T(8,128)(2,1)S(1)}, u32[]{:S(2)}) copy-start(bf16[8,384,384]{2,1,0:T(8,128)(2,1)S(1)} %get-tuple-element.21.cells) | copy-start | bytes 7077892
  13.3 17.6 %collective-permute-start.1 = (f32[384,384]{1,0:T(8,128)S(1)}, f32[384,384]{1,0:T(8,128)}, u32[]{:S(2)}, u32[]{:S(2)}) collective-permute-start(f32[384,384]{1,0:T(8,128)S(1)} %get-tuple-element.25), channel_id=1, source_target_pairs={{0,1},{1,0},{2,3},{3,2},{4,5},{5,4},{6,7},{7,6},{8,9},{9,8},{10,11... | collective-permute-start | bytes 1769480 | tf_op jit(solution)/shard_map/ppermute | solution.py:244
  14.9 18.9 %collective-permute-start.6 = (bf16[1,384,384]{2,1,0:T(8,128)(2,1)S(1)}, bf16[1,384,384]{2,1,0:T(8,128)(2,1)S(1)}, u32[]{:S(2)}, u32[]{:S(2)}) collective-permute-start(bf16[1,384,384]{2,1,0:T(8,128)(2,1)S(1)} %constant_dynamic-slice_fusion), channel_id=1, source_target_pairs={{0,4},{1,29},{2,6},{3,31},{4,8},{5,1},{6,10},{7,3},{8,12},{9,5},{1... | collective-permute-start | bytes 884744 | tf_op jit(solution)/shard_map/ppermute | solution.py:256
  17.4 14.8 %collective-permute-start.3 = (f32[8,9]{1,0:T(8,128)S(1)}, f32[8,9]{1,0:T(8,128)S(1)}, u32[]{:S(2)}, u32[]{:S(2)}) collective-permute-start(f32[8,9]{1,0:T(8,128)S(1)} %get-tuple-element.18.factors), channel_id=1, source_target_pairs={{0,1},{1,0},{2,3},{3,2},{4,5},{5,4},{6,7},{7,6},{8,9},{9,8},{10,11... | collective-permute-start | bytes 872 | tf_op jit(solution)/shard_map/ppermute | solution.py:244
  20.6 1.7 %copy-start.1 = (bf16[8,384,384]{2,1,0:T(8,128)(2,1)S(1)}, bf16[8,384,384]{2,1,0:T(8,128)(2,1)}, u32[]{:S(2)}) copy-start(bf16[8,384,384]{2,1,0:T(8,128)(2,1)} %copy-done) | copy-start | bytes 7077892
  22.3 1.7 %copy-start.3 = (bf16[8,384,384]{2,1,0:T(8,128)(2,1)S(1)}, bf16[8,384,384]{2,1,0:T(8,128)(2,1)}, u32[]{:S(2)}) copy-start(bf16[8,384,384]{2,1,0:T(8,128)(2,1)} %copy-done.2) | copy-start | bytes 7077892
  24.0 1.7 %copy-start.5 = (bf16[8,384,384]{2,1,0:T(8,128)(2,1)S(1)}, bf16[8,384,384]{2,1,0:T(8,128)(2,1)}, u32[]{:S(2)}) copy-start(bf16[8,384,384]{2,1,0:T(8,128)(2,1)} %copy-done.4) | copy-start | bytes 7077892
  31.0 19.2 %collective-permute-start = (f32[384,384]{1,0:T(8,128)S(1)}, f32[384,384]{1,0:T(8,128)S(1)}, u32[]{:S(2)}, u32[]{:S(2)}) collective-permute-start(f32[384,384]{1,0:T(8,128)S(1)} %get-tuple-element.23), channel_id=1, source_target_pairs={{0,1},{1,0},{2,3},{3,2},{4,5},{5,4},{6,7},{7,6},{8,9},{9,8},{10,11... | collective-permute-start | bytes 1769480 | tf_op jit(solution)/shard_map/ppermute | solution.py:244
  32.2 18.0 %collective-permute-start.2 = (bf16[384,384]{1,0:T(8,128)(2,1)S(1)}, bf16[384,384]{1,0:T(8,128)(2,1)S(1)}, u32[]{:S(2)}, u32[]{:S(2)}) collective-permute-start(bf16[384,384]{1,0:T(8,128)(2,1)S(1)} %add_convert_fusion), channel_id=1, source_target_pairs={{0,2},{1,3},{2,0},{3,1},{4,6},{5,7},{6,4},{7,5},{8,10},{9,11},{10,... | collective-permute-start | bytes 884744 | tf_op jit(solution)/shard_map/ppermute | solution.py:244
  48.3 8.9 %collective-permute-start.8 = (f32[192,384]{1,0:T(8,128)S(1)}, f32[192,384]{1,0:T(8,128)S(1)}, u32[]{:S(2)}, u32[]{:S(2)}) collective-permute-start(f32[192,384]{1,0:T(8,128)S(1)} %get-tuple-element.29), channel_id=1, source_target_pairs={{0,1},{1,0},{2,3},{3,2},{4,5},{5,4},{6,7},{7,6},{8,9},{9,8},{10,11... | collective-permute-start | bytes 884744 | tf_op jit(solution)/shard_map/ppermute | solution.py:244
  48.4 6.7 %collective-permute-start.7 = (bf16[192,384]{1,0:T(8,128)(2,1)S(1)}, bf16[192,384]{1,0:T(8,128)(2,1)S(1)}, u32[]{:S(2)}, u32[]{:S(2)}) collective-permute-start(bf16[192,384]{1,0:T(8,128)(2,1)S(1)} %get-tuple-element.28), channel_id=1, source_target_pairs={{0,2},{1,3},{2,0},{3,1},{4,6},{5,7},{6,4},{7,5},{8,10},{9,11},{10,... | collective-permute-start | bytes 442376 | tf_op jit(solution)/shard_map/ppermute | solution.py:244
  49.0 8.2 %collective-permute-start.9 = (bf16[192,384]{1,0:T(8,128)(2,1)S(1)}, bf16[192,384]{1,0:T(8,128)(2,1)S(1)}, u32[]{:S(2)}, u32[]{:S(2)}) collective-permute-start(bf16[192,384]{1,0:T(8,128)(2,1)S(1)} %get-tuple-element.30), channel_id=1, source_target_pairs={{0,3},{1,2},{2,1},{3,0},{4,7},{5,6},{6,5},{7,4},{8,11},{9,10},{10,... | collective-permute-start | bytes 442376 | tf_op jit(solution)/shard_map/ppermute | solution.py:244

commit v3 on v2

--- a/solution.py
+++ b/solution.py
@@ -7,6 +7,8 @@
 
 
 CORES = 2
+AHEAD = 2
+LANES = 128
 EDGE = 2
 
 
@@ -51,10 +53,10 @@
     return lax.psum_scatter(accumulated, "op", scatter_dimension=1, tiled=True)
 
 
-def middle_of(k, factors, own, left, sources, middles, first_target, targets, chip, core):
+def middle_of(k, factors, own, left, sources, middles, sectors, first_target, targets, chip, core):
     states = sources.shape[-1]
     half = middles.shape[0] // (CORES * targets)
-    shift = 1 - factors[own, factors.shape[1] - 1].astype(jnp.int32)
+    shift = 1 - factors[own, sectors].astype(jnp.int32)
     wide = jnp.concatenate([sources[shift + t] for t in range(targets)], axis=1)
     rows = jnp.concatenate(
         [left[own, pl.ds(row_of(chip, owner, half), half)] for owner in (core, 1 - core)], axis=0
@@ -87,7 +89,7 @@
 
 def position():
     place = lax.axis_index("op")
-    return place // CORES, place % CORES
+    return lax.shift_right_logical(place, CORES - 1), place & (CORES - 1)
 
 
 def row_of(chip, core, half):
@@ -95,11 +97,12 @@
 
 
 def inner_far_kernel(
-    charge, couple, amplitude, left_far, right_far, cells_far, keep, send, factors, left, right, cells,
+    charge, couple, amplitude, left_far, right_far, cells_far,
+    keep, send, factors, left, right, cells, border,
     middles, charge_here, couple_here, amplitude_here, small_sem, cell_sem, left_sem, right_sem,
 ):
     chip, core = position()
-    operators, _ = left.shape[:2]
+    operators, states = left.shape[:2]
     sectors = cells.shape[0]
     targets = sectors - 2 * EDGE
     half = keep.shape[0] // targets
@@ -123,27 +126,39 @@
     ]
     inside = pl.ds(first, slabs)
     cell = begin(cells_far.at[inside], cells.at[inside], cell_sem.at[0])
-    lefts = [begin(*rows(k, 1 - chip), left_sem.at[0, k]) for k in range(operators)]
+    lefts = [begin(*rows(k, 1 - chip), left_sem.at[0, k]) for k in range(AHEAD)]
+    for copy in small:
+        copy.wait()
+    lefts += [begin(*rows(k, 1 - chip), left_sem.at[0, k]) for k in range(AHEAD, operators)]
+    row = lax.broadcasted_iota(jnp.int32, (operators, LANES), 0)
+    column = lax.broadcasted_iota(jnp.int32, (operators, LANES), 1)
+    table = jnp.zeros((operators, LANES), jnp.float32)
+    for k in range(operators):
+        for t in range(sectors + 1):
+            if t < sectors:
+                entry = amplitude_here[k, t] * couple_here[k, t].astype(jnp.float32)
+            else:
+                entry = charge_here[k].astype(jnp.float32)
+            factors[k, t] = entry
+            table = jnp.where((row == k) & (column == t), entry, table)
+    width = keep.shape[0]
+    send[width:, :] = jnp.concatenate(
+        [table, jnp.zeros((operators, states - LANES), jnp.float32)], axis=1
+    )
+    cell.wait()
+    for copy in lefts[:AHEAD]:
+        copy.wait()
     rights = [begin(right_far.at[k], right.at[k], right_sem.at[k]) for k in range(operators)]
     later = [begin(*rows(k, chip), left_sem.at[1, k]) for k in range(operators)]
     later.append(begin(cells_far.at[pl.ds(0, first)], cells.at[pl.ds(0, first)], cell_sem.at[1]))
     last = pl.ds(first + slabs, first)
     later.append(begin(cells_far.at[last], cells.at[last], cell_sem.at[2]))
-    for copy in small:
-        copy.wait()
+    later.append(begin(cells_far.at[(sectors - 1) * (1 - core)], border.at[0], cell_sem.at[3]))
     for k in range(operators):
-        for t in range(sectors):
-            factors[k, t] = amplitude_here[k, t] * couple_here[k, t].astype(jnp.float32)
-        factors[k, sectors] = charge_here[k].astype(jnp.float32)
-    cell.wait()
-    for k in range(operators):
-        if k == 0:
-            for copy in lefts[:2]:
+        if k == AHEAD:
+            for copy in lefts[AHEAD:]:
                 copy.wait()
-        elif k == 2:
-            for copy in lefts[2:]:
-                copy.wait()
-        middle_of(k, factors, k, left, cells.at[inside], middles, EDGE, targets, 1 - chip, core)
+        middle_of(k, factors, k, left, cells.at[inside], middles, sectors, EDGE, targets, 1 - chip, core)
     for copy in rights:
         copy.wait()
     summed(jnp.concatenate([right[k] for k in range(operators)], axis=1), middles, (keep, send))
@@ -157,22 +172,29 @@
     targets = cells.shape[0] - 2 * EDGE
     inside = cells.at[pl.ds(EDGE - 1, targets + 2)]
     for k in range(operators):
-        middle_of(k, factors, k, left, inside, middles, EDGE, targets, chip, core)
+        middle_of(k, factors, k, left, inside, middles, cells.shape[0], EDGE, targets, chip, core)
     summed(jnp.concatenate([right[k] for k in range(operators)], axis=1), middles, (keep, send))
 
 
-def edge_products(groups, sources, middles, results, first_target, chip, core):
+def edge_products(groups, sources, middles, results, sectors, chip, core):
     k = 0
+    first_target = (sectors - EDGE) * core
     for factors, left, right in groups:
         for own in range(left.shape[0]):
-            middle_of(k, factors, own, left, sources, middles, first_target, EDGE, chip, core)
+            middle_of(k, factors, own, left, sources, middles, sectors, first_target, EDGE, chip, core)
             k += 1
     wide = jnp.concatenate([right[own] for _, _, right in groups for own in range(right.shape[0])], axis=1)
     summed(wide, middles, results)
 
 
+def table_copy(mate, factors_in, sem):
+    operators = factors_in.shape[0]
+    place = mate.at[pl.ds(mate.shape[0] - operators, operators), pl.ds(0, LANES)]
+    return pltpu.make_async_copy(place, factors_in, sem)
+
+
 def edge_far_kernel(
-    factors, factors_in, left, right, left_in, right_in, cells, halo, keep, send, sources, middles, sem
+    factors, mate, left, right, left_in, right_in, cells, halo, send, sources, middles, factors_in, sem
 ):
     chip, core = position()
     sectors = cells.shape[0]
@@ -182,29 +204,37 @@
             cells.at[pl.ds((sectors - inside) * core, inside)], sources.at[pl.ds(1 - core, inside)], sem.at[0]
         ),
         pltpu.make_async_copy(halo.at[0], sources.at[inside * core], sem.at[1]),
+        table_copy(mate, factors_in, sem.at[2]),
     ]
     for copy in copies:
         copy.start()
     for copy in copies:
         copy.wait()
     groups = ((factors, left, right), (factors_in, left_in, right_in))
-    edge_products(groups, sources, middles, (keep, send), (sectors - EDGE) * core, 1 - chip, core)
-
-
-def edge_own_kernel(factors, factors_in, left, right, left_in, right_in, sources, keep, send, middles):
+    width = send.shape[0] // CORES
+    halves = [send.at[pl.ds(part * width, width)] for part in range(CORES)]
+    edge_products(groups, sources, middles, halves, sectors, 1 - chip, core)
+
+
+def edge_own_kernel(
+    factors, mate, left, right, left_in, right_in, sources, keep, send, middles, factors_in, sem
+):
     chip, core = position()
     sectors = factors.shape[1] - 1
+    copy = table_copy(mate, factors_in, sem)
+    copy.start()
+    copy.wait()
     groups = ((factors, left, right), (factors_in, left_in, right_in))
-    edge_products(groups, sources, middles, (keep, send), (sectors - EDGE) * core, chip, core)
-
-
-def sum_kernel(inner_own, inner_chip, inner_far, near_own, near_far, other_chip, other_far, sigma):
-    core = lax.axis_index("op") % CORES
+    edge_products(groups, sources, middles, (keep, send), sectors, chip, core)
+
+
+def sum_kernel(inner_own, inner_chip, inner_far, near_own, edge_far, other, sigma):
+    core = lax.axis_index("op") & (CORES - 1)
     sectors = sigma.shape[0]
     far = sectors - EDGE
     sigma[EDGE:far] = inner_own[...] + inner_chip[...] + inner_far[...].astype(jnp.float32)
-    sigma[pl.ds(far * core, EDGE)] = near_own[...] + near_far[...].astype(jnp.float32)
-    sigma[pl.ds(far * (1 - core), EDGE)] = other_chip[...] + other_far[...].astype(jnp.float32)
+    sigma[pl.ds(far * core, EDGE)] = near_own[...] + edge_far[:EDGE].astype(jnp.float32)
+    sigma[pl.ds(far * (1 - core), EDGE)] = other[...]
 
 
 SMALL = pl.BlockSpec(memory_space=pltpu.SMEM)
@@ -247,18 +277,16 @@
     def per_target(value):
         return value.reshape(-1, half, states)
 
-    core = lax.axis_index("op") & (CORES - 1)
     ring = []
     for s in range(sec):
         for o in range(op):
             ring.append((s * op + o, (s + 1 if o % CORES == 0 else s - 1) % sec * op + o))
-    border = lax.dynamic_slice_in_dim(wavefunction, (sectors - 1) * (1 - core), 1, 0)
-    halo = lax.ppermute(border, ("sec", "op"), ring)
     left_in = over_op(left_ops, 1)
     right_in = over_op(right_ops, 1)
 
     block = shape(inner * half, states)
-    far_keep, far_send, factors, left, right, cells = run(
+    block_and_table = shape(inner * half + operators, states)
+    far_keep, far_send, factors, left, right, cells, border = run(
         inner_far_kernel,
         operators,
         inner,
@@ -269,25 +297,26 @@
         [LARGE] * 6,
         [
             block,
-            block,
+            block_and_table,
             shape(operators, sectors + 1),
             pltpu.VMEM(left_ops.shape, narrow),
             pltpu.VMEM(right_ops.shape, narrow),
             pltpu.VMEM(wavefunction.shape, narrow),
+            pltpu.VMEM((1, states, states), narrow),
         ],
-        [BLOCK, BLOCK, SMALL, BLOCK, BLOCK, BLOCK],
+        [BLOCK, BLOCK, SMALL, BLOCK, BLOCK, BLOCK, BLOCK],
         [
             pltpu.SMEM(charge.shape, charge.dtype),
             pltpu.SMEM(couple.shape, couple.dtype),
             pltpu.SMEM(amplitude.shape, amplitude.dtype),
             pltpu.SemaphoreType.DMA((3,)),
-            pltpu.SemaphoreType.DMA((3,)),
+            pltpu.SemaphoreType.DMA((4,)),
             pltpu.SemaphoreType.DMA((2, operators)),
             pltpu.SemaphoreType.DMA((operators,)),
         ],
     )
     far_in = over_op(far_send, 1)
-    factors_in = over_op(factors, 1)
+    halo = lax.ppermute(border, ("sec", "op"), ring)
     inner_own, inner_send = run(
         inner_own_kernel,
         operators,
@@ -299,23 +328,22 @@
         [],
     )
     inner_chip = over_op(inner_send, 1)
-    inner_far = over_op((far_keep + far_in).astype(narrow), CORES)
-
-    held = [factors, factors_in, left, right, left_in, right_in]
-    held_specs = [SMALL, SMALL, BLOCK, BLOCK, BLOCK, BLOCK]
-    edge_narrow = shape(EDGE * half, states, dtype=narrow)
-    near_send, other_send, sources = run(
+    inner_far = over_op((far_keep + far_in[: inner * half]).astype(narrow), CORES)
+
+    held = [factors, far_in, left, right, left_in, right_in]
+    held_specs = [SMALL, BLOCK, BLOCK, BLOCK, BLOCK, BLOCK]
+    table = pltpu.SMEM((operators, LANES), wide)
+    edge_send, sources = run(
         edge_far_kernel,
         CORES * operators,
         EDGE,
         held + [cells, halo],
-        held_specs + [BLOCK, LARGE],
-        [edge_narrow, edge_narrow, shape(EDGE + 2, states, states, dtype=narrow)],
-        [BLOCK, BLOCK, BLOCK],
-        [pltpu.SemaphoreType.DMA((2,))],
-    )
-    near_far = over_op(near_send, CORES)
-    other_far = over_op(other_send, CORES + 1)
+        held_specs + [BLOCK, BLOCK],
+        [shape(CORES * EDGE * half, states, dtype=narrow), shape(EDGE + 2, states, states, dtype=narrow)],
+        [BLOCK, BLOCK],
+        [table, pltpu.SemaphoreType.DMA((3,))],
+    )
+    edge_far = over_op(edge_send, CORES)
     edge_wide = shape(EDGE * half, states)
     near_own, near_mate = run(
         edge_own_kernel,
@@ -325,10 +353,10 @@
         held_specs + [BLOCK],
         [edge_wide, edge_wide],
         [BLOCK, BLOCK],
-        [],
-    )
-    other_chip = over_op(near_mate, 1)
-    parts = (inner_own, inner_chip, inner_far, near_own, near_far, other_chip, other_far)
+        [table, pltpu.SemaphoreType.DMA],
+    )
+    other = over_op(near_mate + edge_far[EDGE * half :].astype(wide), 1)
+    parts = (inner_own, inner_chip, inner_far, near_own, edge_far, other)
     return pl.pallas_call(
         sum_kernel,
         out_shape=shape(sectors, half, states),

time: 58.7 us -> 40.1 us (0.68)
  local copies, waits for them, and re-layouts: 10.3 us -> 0 us
  waiting for transfers between devices: 7.01 us -> 3.11 us
  Pallas kernels: 29.4 us -> 27.5 us
  starting transfers between devices: 10.4 us -> 9.11 us
  other arithmetic: 1.12 us -> 0.08 us
    unnamed x12 -> x0, local copies, waits for them, and re-layouts: 9.32 us -> none
    ppermute x9 -> x7, waiting for transfers between devices: 7.01 us -> 3.11 us  [over_op(): return lax.ppermute(value, 'op', [(i, i ^ flip) for i in range(op)])]
    pallas_call x4, Pallas kernels: 28.3 us -> 26.4 us  [run(): pl.pallas_call(kernel, out_shape=outs, in_specs=in_specs, out_specs=out_s...]
    ppermute x9 -> x7, starting transfers between devices: 7.89 us -> 6.59 us  [over_op(): return lax.ppermute(value, 'op', [(i, i ^ flip) for i in range(op)])]
    convert_element_type x1, other arithmetic: 1.12 us -> 0.06 us  [shards(): (far_keep + far_in[:inner * half]).astype(narrow)]
    dynamic_slice x1 -> x0, local copies, waits for them, and re-layouts: 0.99 us -> none  [shards(): lax.dynamic_slice_in_dim(wavefunction, (sectors - 1) * (1 - core), 1, 0)]
  transfers between devices with their start and end apart: 10 -> 8, of which waited for: 2 -> 2; matrix products, arithmetic and copies ran while one was open for 4% -> 0% of each run, Pallas kernels for 48% -> 66%
where the time goes in v3:
time: 40.1 us; the launch traced here: 39.9 us
  Pallas kernels  27.5 us (69%)
  starting transfers between devices  9.11 us (23%)
  waiting for transfers between devices  3.11 us (8%)
    pallas_call x4, Pallas kernels, run(): pl.pallas_call(kernel, out_shape=outs, in_specs=in_specs, out_specs=out_s...  26.4 us
    ppermute x7, starting transfers between devices, over_op(): return lax.ppermute(value, 'op', [(i, i ^ flip) for i in range(op)])  6.59 us
    ppermute x7, waiting for transfers between devices, over_op(): return lax.ppermute(value, 'op', [(i, i ^ flip) for i in range(op)])  3.11 us
    ppermute x1, starting transfers between devices, shards(): halo = lax.ppermute(border, ('sec', 'op'), ring)  2.52 us
    pallas_call x1, Pallas kernels, shards(): pl.pallas_call(sum_kernel, out_shape=shape(sectors, half, states), in_spe...  1.15 us
  transfers between devices with their start and end apart: 8, of which 2 were waited for; matrix products, arithmetic and copies ran while one was open for 0% of the time, Pallas kernels for 66%

profile of v3, /device:TPU:0, one launch (start us, length us, event | category | flops | bytes accessed | tf_op | source)
XLA Modules:
  0.0 39.9 jit_solution(9952193383107409708)
XLA Ops:
  0.0 0.5 %collective-permute-start.3 = (bf16[8,384,384]{2,1,0:T(8,128)(2,1)}, bf16[8,384,384]{2,1,0:T(8,128)(2,1)S(1)}, u32[]{:S(2)}, u32[]{:S(2)}) collective-permute-start(bf16[8,384,384]{2,1,0:T(8,128)(2,1)} %left_far.1), channel_id=1, source_target_pairs={{0,1},{1,0},{2,3},{3,2},{4,5},{5,4},{6,7},{7,6},{8,9},{9,8},{10,11... | collective-permute-start | bytes 7077896 | tf_op jit(solution)/shard_map/ppermute | solution.py:274
  0.5 0.0 collective-permute-start.4
  0.5 7.5 %shard_map.64 = (f32[384,384]{1,0:T(8,128)S(1)}, f32[392,384]{1,0:T(8,128)S(1)}, f32[8,9]{1,0:T(8,128)S(1)}, bf16[8,384,384]{2,1,0:T(8,128)(2,1)S(1)}, bf16[8,38...) custom-call(s32[8]{0:T(128)} %charge.1, s32[8,8]{1,0:T(8,128)} %couple.1, ...), custom_call_target="tpu_custom_call" | custom-call | flops 3623878656 | bytes 4718592 | tf_op jit(solution)/shard_map/pallas_call | solution.py:259
  8.0 0.6 %collective-permute-start.1 = (f32[392,384]{1,0:T(8,128)S(1)}, f32[392,384]{1,0:T(8,128)S(1)}, u32[]{:S(2)}, u32[]{:S(2)}) collective-permute-start(f32[392,384]{1,0:T(8,128)S(1)} %get-tuple-element.25), channel_id=1, source_target_pairs={{0,1},{1,0},{2,3},{3,2},{4,5},{5,4},{6,7},{7,6},{8,9},{9,8},{10,11... | collective-permute-start | bytes 1806344 | tf_op jit(solution)/shard_map/ppermute | solution.py:274
  8.6 2.5 %collective-permute-start.5 = (bf16[1,384,384]{2,1,0:T(8,128)(2,1)S(1)}, bf16[1,384,384]{2,1,0:T(8,128)(2,1)S(1)}, u32[]{:S(2)}, u32[]{:S(2)}) collective-permute-start(bf16[1,384,384]{2,1,0:T(8,128)(2,1)S(1)} %get-tuple-element.26), channel_id=1, source_target_pairs={{0,4},{1,29},{2,6},{3,31},{4,8},{5,1},{6,10},{7,3},{8,12},{9,5},{1... | collective-permute-start | bytes 884744 | tf_op jit(solution)/shard_map/ppermute | solution.py:319
  11.1 5.4 %shard_map.65 = (f32[384,384]{1,0:T(8,128)S(1)}, f32[384,384]{1,0:T(8,128)S(1)}) custom-call(f32[8,9]{1,0:T(8,128)S(1)} %get-tuple-element.18.factors, bf16[8,384,384]{2,1,0:T(8,128)(2,1)S(1)} %get-tuple-element.19.left, bf16[8,384,384]{2,1,0:T(8,128)(2,1)S(1)} %get-tuple-element.20.right, bf16[8,384,384]{2,1,0:T(8,128)(2,1)S(1)} %get-tuple-element.21.cells), custom_call_target="tpu_custom_call" | custom-call | flops 3623878656 | bytes 4718592 | tf_op jit(solution)/shard_map/pallas_call | solution.py:259
  16.5 3.3 %collective-permute-start = (f32[384,384]{1,0:T(8,128)S(1)}, f32[384,384]{1,0:T(8,128)S(1)}, u32[]{:S(2)}, u32[]{:S(2)}) collective-permute-start(f32[384,384]{1,0:T(8,128)S(1)} %get-tuple-element.23), channel_id=1, source_target_pairs={{0,1},{1,0},{2,3},{3,2},{4,5},{5,4},{6,7},{7,6},{8,9},{9,8},{10,11... | collective-permute-start | bytes 1769480 | tf_op jit(solution)/shard_map/ppermute | solution.py:274
  19.8 0.0 collective-permute-done.1.mate
  19.8 0.1 fusion
  19.8 1.6 %collective-permute-start.2 = (bf16[384,384]{1,0:T(8,128)(2,1)S(1)}, bf16[384,384]{1,0:T(8,128)(2,1)S(1)}, u32[]{:S(2)}, u32[]{:S(2)}) collective-permute-start(bf16[384,384]{1,0:T(8,128)(2,1)S(1)} %fusion), channel_id=1, source_target_pairs={{0,2},{1,3},{2,0},{3,1},{4,6},{5,7},{6,4},{7,5},{8,10},{9,11},{10,... | collective-permute-start | bytes 884744 | tf_op jit(solution)/shard_map/ppermute | solution.py:274
  21.4 0.0 collective-permute-done.5.halo
  21.4 0.0 collective-permute-done.3.left_in
  21.4 0.0 collective-permute-done.4.right_in
  21.4 7.0 %shard_map.66 = (bf16[384,384]{1,0:T(8,128)(2,1)S(1)}, bf16[4,384,384]{2,1,0:T(8,128)(2,1)S(1)}) custom-call(f32[8,9]{1,0:T(8,128)S(1)} %get-tuple-element.18.factors, f32[392,384]{1,0:T(8,128)S(1)} %collective-permute-done.1.mate, bf16[8,384,384]{2,1,0:T(8,128)(2,1)S(1)} %get-tuple-element.19.left, bf16[8,384,384]{2,1,0:T(8,128)(2,1)S(1)} %get-tuple-element.20.right, ...), custom_call_target="tpu_custom_call" | custom-call | flops 3623878656 | bytes 9437184 | tf_op jit(solution)/shard_map/pallas_call | solution.py:259
  28.4 0.6 %collective-permute-start.6 = (bf16[384,384]{1,0:T(8,128)(2,1)S(1)}, bf16[384,384]{1,0:T(8,128)(2,1)S(1)}, u32[]{:S(2)}, u32[]{:S(2)}) collective-permute-start(bf16[384,384]{1,0:T(8,128)(2,1)S(1)} %get-tuple-element.29), channel_id=1, source_target_pairs={{0,2},{1,3},{2,0},{3,1},{4,6},{5,7},{6,4},{7,5},{8,10},{9,11},{10,... | collective-permute-start | bytes 884744 | tf_op jit(solution)/shard_map/ppermute | solution.py:274
  29.0 6.5 %shard_map.67 = (f32[192,384]{1,0:T(8,128)S(1)}, f32[192,384]{1,0:T(8,128)S(1)}) custom-call(f32[8,9]{1,0:T(8,128)S(1)} %get-tuple-element.18.factors, f32[392,384]{1,0:T(8,128)S(1)} %collective-permute-done.1.mate, bf16[8,384,384]{2,1,0:T(8,128)(2,1)S(1)} %get-tuple-element.19.left, bf16[8,384,384]{2,1,0:T(8,128)(2,1)S(1)} %get-tuple-element.20.right, ...), custom_call_target="tpu_custom_call" | custom-call | flops 3623878656 | bytes 9437184 | tf_op jit(solution)/shard_map/pallas_call | solution.py:259
  35.5 1.5 %collective-permute-done.6 = bf16[384,384]{1,0:T(8,128)(2,1)S(1)} collective-permute-done((bf16[384,384]{1,0:T(8,128)(2,1)S(1)}, bf16[384,384]{1,0:T(8,128)(2,1)S(1)}, u32[]{:S(2)}, u32[]{:S(2)}) %collective-permute-start.6) | collective-permute-done | bytes 294944 | tf_op jit(solution)/shard_map/ppermute | solution.py:274
  37.1 0.1 collective-permute-start.7
  37.2 0.0 collective-permute-done
  37.2 0.0 collective-permute-done.2
  37.2 1.5 %collective-permute-done.7 = f32[192,384]{1,0:T(8,128)S(1)} collective-permute-done((f32[192,384]{1,0:T(8,128)S(1)}, f32[192,384]{1,0:T(8,128)S(1)}, u32[]{:S(2)}, u32[]{:S(2)}) %collective-permute-start.7) | collective-permute-done | bytes 294944 | tf_op jit(solution)/shard_map/ppermute | solution.py:274
  38.8 1.1 %total.1 = f32[8,96,384]{2,1,0:T(8,128)} custom-call(f32[4,96,384]{2,1,0:T(8,128)S(1)} %bitcast.7, f32[4,96,384]{2,1,0:T(8,128)S(1)} %bitcast.8, bf16[4,96,384]{2,1,0:T(8,128)(2,1)S(1)} %bitcast.9, f32[2,96,384]{2,1,0:T(8,128)S(1)} %bitcast.10, bf16[4,96,384]{2,1,0:T(8,128)(2,1)S(1)} %bitcast.6, f32[2,96,384]{2,1,0:T(8,128)S(1)} %bitcast.11), custom_call_target="tpu_custom_call" | custom-call | tf_op jit(solution)/shard_map/total/pallas_call | solution.py:360
  (1 shorter events, 0.0 us)
Async XLA Ops:
  0.0 21.4 %collective-permute-start.3 = (bf16[8,384,384]{2,1,0:T(8,128)(2,1)}, bf16[8,384,384]{2,1,0:T(8,128)(2,1)S(1)}, u32[]{:S(2)}, u32[]{:S(2)}) collective-permute-start(bf16[8,384,384]{2,1,0:T(8,128)(2,1)} %left_far.1), channel_id=1, source_target_pairs={{0,1},{1,0},{2,3},{3,2},{4,5},{5,4},{6,7},{7,6},{8,9},{9,8},{10,11... | collective-permute-start | bytes 7077896 | tf_op jit(solution)/shard_map/ppermute | solution.py:274
  0.5 20.9 %collective-permute-start.4 = (bf16[8,384,384]{2,1,0:T(8,128)(2,1)}, bf16[8,384,384]{2,1,0:T(8,128)(2,1)S(1)}, u32[]{:S(2)}, u32[]{:S(2)}) collective-permute-start(bf16[8,384,384]{2,1,0:T(8,128)(2,1)} %right_far.1), channel_id=1, source_target_pairs={{0,1},{1,0},{2,3},{3,2},{4,5},{5,4},{6,7},{7,6},{8,9},{9,8},{10,11... | collective-permute-start | bytes 7077896 | tf_op jit(solution)/shard_map/ppermute | solution.py:274
  8.0 11.8 %collective-permute-start.1 = (f32[392,384]{1,0:T(8,128)S(1)}, f32[392,384]{1,0:T(8,128)S(1)}, u32[]{:S(2)}, u32[]{:S(2)}) collective-permute-start(f32[392,384]{1,0:T(8,128)S(1)} %get-tuple-element.25), channel_id=1, source_target_pairs={{0,1},{1,0},{2,3},{3,2},{4,5},{5,4},{6,7},{7,6},{8,9},{9,8},{10,11... | collective-permute-start | bytes 1806344 | tf_op jit(solution)/shard_map/ppermute | solution.py:274
  8.6 12.8 %collective-permute-start.5 = (bf16[1,384,384]{2,1,0:T(8,128)(2,1)S(1)}, bf16[1,384,384]{2,1,0:T(8,128)(2,1)S(1)}, u32[]{:S(2)}, u32[]{:S(2)}) collective-permute-start(bf16[1,384,384]{2,1,0:T(8,128)(2,1)S(1)} %get-tuple-element.26), channel_id=1, source_target_pairs={{0,4},{1,29},{2,6},{3,31},{4,8},{5,1},{6,10},{7,3},{8,12},{9,5},{1... | collective-permute-start | bytes 884744 | tf_op jit(solution)/shard_map/ppermute | solution.py:319
  16.5 20.7 %collective-permute-start = (f32[384,384]{1,0:T(8,128)S(1)}, f32[384,384]{1,0:T(8,128)S(1)}, u32[]{:S(2)}, u32[]{:S(2)}) collective-permute-start(f32[384,384]{1,0:T(8,128)S(1)} %get-tuple-element.23), channel_id=1, source_target_pairs={{0,1},{1,0},{2,3},{3,2},{4,5},{5,4},{6,7},{7,6},{8,9},{9,8},{10,11... | collective-permute-start | bytes 1769480 | tf_op jit(solution)/shard_map/ppermute | solution.py:274
  19.8 17.4 %collective-permute-start.2 = (bf16[384,384]{1,0:T(8,128)(2,1)S(1)}, bf16[384,384]{1,0:T(8,128)(2,1)S(1)}, u32[]{:S(2)}, u32[]{:S(2)}) collective-permute-start(bf16[384,384]{1,0:T(8,128)(2,1)S(1)} %fusion), channel_id=1, source_target_pairs={{0,2},{1,3},{2,0},{3,1},{4,6},{5,7},{6,4},{7,5},{8,10},{9,11},{10,... | collective-permute-start | bytes 884744 | tf_op jit(solution)/shard_map/ppermute | solution.py:274
  28.4 8.7 %collective-permute-start.6 = (bf16[384,384]{1,0:T(8,128)(2,1)S(1)}, bf16[384,384]{1,0:T(8,128)(2,1)S(1)}, u32[]{:S(2)}, u32[]{:S(2)}) collective-permute-start(bf16[384,384]{1,0:T(8,128)(2,1)S(1)} %get-tuple-element.29), channel_id=1, source_target_pairs={{0,2},{1,3},{2,0},{3,1},{4,6},{5,7},{6,4},{7,5},{8,10},{9,11},{10,... | collective-permute-start | bytes 884744 | tf_op jit(solution)/shard_map/ppermute | solution.py:274
  37.1 1.6 %collective-permute-start.7 = (f32[192,384]{1,0:T(8,128)S(1)}, f32[192,384]{1,0:T(8,128)S(1)}, u32[]{:S(2)}, u32[]{:S(2)}) collective-permute-start(f32[192,384]{1,0:T(8,128)S(1)} %convert_add_fusion), channel_id=1, source_target_pairs={{0,1},{1,0},{2,3},{3,2},{4,5},{5,4},{6,7},{7,6},{8,9},{9,8},{10,11... | collective-permute-start | bytes 884744 | tf_op jit(solution)/shard_map/ppermute | solution.py:274

commit v4 on v3

--- a/solution.py
+++ b/solution.py
@@ -8,7 +8,6 @@
 
 CORES = 2
 AHEAD = 2
-LANES = 128
 EDGE = 2
 
 
@@ -96,69 +95,60 @@
     return pl.multiple_of((chip * CORES + core) * half, 32)
 
 
-def inner_far_kernel(
-    charge, couple, amplitude, left_far, right_far, cells_far,
-    keep, send, factors, left, right, cells, border,
-    middles, charge_here, couple_here, amplitude_here, small_sem, cell_sem, left_sem, right_sem,
+def begin(source, target, sem):
+    copy = pltpu.make_async_copy(source, target, sem)
+    copy.start()
+    return copy
+
+
+def load_kernel(
+    charge, couple, amplitude, cells_far, factors, cells, border,
+    charge_here, couple_here, amplitude_here, small_sem, cell_sem,
 ):
-    chip, core = position()
-    operators, states = left.shape[:2]
-    sectors = cells.shape[0]
-    targets = sectors - 2 * EDGE
-    half = keep.shape[0] // targets
-    first = EDGE - 1
-    slabs = targets + 2
-    chip_rows = CORES * half
-
-    def rows(k, place):
-        at = pl.ds(pl.multiple_of(place * chip_rows, 64), chip_rows)
-        return left_far.at[k, at], left.at[k, at]
-
-    def begin(source, target, sem):
-        copy = pltpu.make_async_copy(source, target, sem)
-        copy.start()
-        return copy
-
+    _, core = position()
+    operators, sectors = couple.shape
     small = [
         begin(charge, charge_here, small_sem.at[0]),
         begin(couple, couple_here, small_sem.at[1]),
         begin(amplitude, amplitude_here, small_sem.at[2]),
     ]
-    inside = pl.ds(first, slabs)
-    cell = begin(cells_far.at[inside], cells.at[inside], cell_sem.at[0])
-    lefts = [begin(*rows(k, 1 - chip), left_sem.at[0, k]) for k in range(AHEAD)]
+    large = [begin(cells_far.at[(sectors - 1) * (1 - core)], border.at[0], cell_sem.at[sectors])]
+    large += [begin(cells_far.at[s], cells.at[s], cell_sem.at[s]) for s in range(sectors)]
     for copy in small:
         copy.wait()
-    lefts += [begin(*rows(k, 1 - chip), left_sem.at[0, k]) for k in range(AHEAD, operators)]
-    row = lax.broadcasted_iota(jnp.int32, (operators, LANES), 0)
-    column = lax.broadcasted_iota(jnp.int32, (operators, LANES), 1)
-    table = jnp.zeros((operators, LANES), jnp.float32)
     for k in range(operators):
-        for t in range(sectors + 1):
-            if t < sectors:
-                entry = amplitude_here[k, t] * couple_here[k, t].astype(jnp.float32)
-            else:
-                entry = charge_here[k].astype(jnp.float32)
-            factors[k, t] = entry
-            table = jnp.where((row == k) & (column == t), entry, table)
-    width = keep.shape[0]
-    send[width:, :] = jnp.concatenate(
-        [table, jnp.zeros((operators, states - LANES), jnp.float32)], axis=1
-    )
-    cell.wait()
-    for copy in lefts[:AHEAD]:
-        copy.wait()
+        for t in range(sectors):
+            factors[k, t] = amplitude_here[k, t] * couple_here[k, t].astype(jnp.float32)
+        factors[k, sectors] = charge_here[k].astype(jnp.float32)
+    for copy in large:
+        copy.wait()
+
+
+def inner_far_kernel(
+    factors, left_far, right_far, cells, keep, send, left, right, middles, left_sem, right_sem
+):
+    chip, core = position()
+    operators = left.shape[0]
+    sectors = cells.shape[0]
+    targets = sectors - 2 * EDGE
+    chip_rows = keep.shape[0] // targets * CORES
+
+    def rows(k, place):
+        at = pl.ds(pl.multiple_of(place * chip_rows, 64), chip_rows)
+        return left_far.at[k, at], left.at[k, at]
+
+    lefts = [begin(*rows(k, 1 - chip), left_sem.at[0, k]) for k in range(operators)]
     rights = [begin(right_far.at[k], right.at[k], right_sem.at[k]) for k in range(operators)]
     later = [begin(*rows(k, chip), left_sem.at[1, k]) for k in range(operators)]
-    later.append(begin(cells_far.at[pl.ds(0, first)], cells.at[pl.ds(0, first)], cell_sem.at[1]))
-    last = pl.ds(first + slabs, first)
-    later.append(begin(cells_far.at[last], cells.at[last], cell_sem.at[2]))
-    later.append(begin(cells_far.at[(sectors - 1) * (1 - core)], border.at[0], cell_sem.at[3]))
+    inside = cells.at[pl.ds(EDGE - 1, targets + 2)]
     for k in range(operators):
+        if k == 0:
+            for copy in lefts[:AHEAD]:
+                copy.wait()
         if k == AHEAD:
             for copy in lefts[AHEAD:]:
                 copy.wait()
-        middle_of(k, factors, k, left, cells.at[inside], middles, sectors, EDGE, targets, 1 - chip, core)
+        middle_of(k, factors, k, left, inside, middles, sectors, EDGE, targets, 1 - chip, core)
     for copy in rights:
         copy.wait()
     summed(jnp.concatenate([right[k] for k in range(operators)], axis=1), middles, (keep, send))
@@ -187,14 +177,8 @@
     summed(wide, middles, results)
 
 
-def table_copy(mate, factors_in, sem):
-    operators = factors_in.shape[0]
-    place = mate.at[pl.ds(mate.shape[0] - operators, operators), pl.ds(0, LANES)]
-    return pltpu.make_async_copy(place, factors_in, sem)
-
-
 def edge_far_kernel(
-    factors, mate, left, right, left_in, right_in, cells, halo, send, sources, middles, factors_in, sem
+    factors, factors_in, left, right, left_in, right_in, cells, halo, send, sources, middles, sem
 ):
     chip, core = position()
     sectors = cells.shape[0]
@@ -204,7 +188,6 @@
             cells.at[pl.ds((sectors - inside) * core, inside)], sources.at[pl.ds(1 - core, inside)], sem.at[0]
         ),
         pltpu.make_async_copy(halo.at[0], sources.at[inside * core], sem.at[1]),
-        table_copy(mate, factors_in, sem.at[2]),
     ]
     for copy in copies:
         copy.start()
@@ -217,13 +200,10 @@
 
 
 def edge_own_kernel(
-    factors, mate, left, right, left_in, right_in, sources, keep, send, middles, factors_in, sem
+    factors, factors_in, left, right, left_in, right_in, sources, keep, send, middles
 ):
     chip, core = position()
     sectors = factors.shape[1] - 1
-    copy = table_copy(mate, factors_in, sem)
-    copy.start()
-    copy.wait()
     groups = ((factors, left, right), (factors_in, left_in, right_in))
     edge_products(groups, sources, middles, (keep, send), sectors, chip, core)
 
@@ -284,39 +264,58 @@
     left_in = over_op(left_ops, 1)
     right_in = over_op(right_ops, 1)
 
-    block = shape(inner * half, states)
-    block_and_table = shape(inner * half + operators, states)
-    far_keep, far_send, factors, left, right, cells, border = run(
-        inner_far_kernel,
-        operators,
-        inner,
-        [
-            pltpu.with_memory_space_constraint(value, pltpu.HBM)
-            for value in (charge, couple, amplitude, left_ops, right_ops, wavefunction)
-        ],
-        [LARGE] * 6,
-        [
-            block,
-            block_and_table,
+    def in_hbm(*values):
+        return [pltpu.with_memory_space_constraint(value, pltpu.HBM) for value in values]
+
+    factors, cells, border = pl.pallas_call(
+        load_kernel,
+        out_shape=[
             shape(operators, sectors + 1),
-            pltpu.VMEM(left_ops.shape, narrow),
-            pltpu.VMEM(right_ops.shape, narrow),
             pltpu.VMEM(wavefunction.shape, narrow),
             pltpu.VMEM((1, states, states), narrow),
         ],
-        [BLOCK, BLOCK, SMALL, BLOCK, BLOCK, BLOCK, BLOCK],
-        [
+        in_specs=[LARGE] * 4,
+        out_specs=[SMALL, BLOCK, BLOCK],
+        scratch_shapes=[
             pltpu.SMEM(charge.shape, charge.dtype),
             pltpu.SMEM(couple.shape, couple.dtype),
             pltpu.SMEM(amplitude.shape, amplitude.dtype),
             pltpu.SemaphoreType.DMA((3,)),
-            pltpu.SemaphoreType.DMA((4,)),
-            pltpu.SemaphoreType.DMA((2, operators)),
-            pltpu.SemaphoreType.DMA((operators,)),
+            pltpu.SemaphoreType.DMA((sectors + 1,)),
         ],
+        compiler_params=pltpu.CompilerParams(vmem_limit_bytes=4 * MIB),
+        name="load_kernel",
+    )(*in_hbm(charge, couple, amplitude, wavefunction))
+    halo = lax.ppermute(border, ("sec", "op"), ring)
+    factors_in = over_op(factors, 1)
+
+    block = shape(inner * half, states)
+    far_keep, far_send, left, right = run(
+        inner_far_kernel,
+        operators,
+        inner,
+        [factors, *in_hbm(left_ops, right_ops), cells],
+        [SMALL, LARGE, LARGE, BLOCK],
+        [block, block, pltpu.VMEM(left_ops.shape, narrow), pltpu.VMEM(right_ops.shape, narrow)],
+        [BLOCK] * 4,
+        [pltpu.SemaphoreType.DMA((2, operators)), pltpu.SemaphoreType.DMA((operators,))],
     )
     far_in = over_op(far_send, 1)
-    halo = lax.ppermute(border, ("sec", "op"), ring)
+
+    held = [factors, factors_in, left, right, left_in, right_in]
+    held_specs = [SMALL, SMALL, BLOCK, BLOCK, BLOCK, BLOCK]
+    edge_send, sources = run(
+        edge_far_kernel,
+        CORES * operators,
+        EDGE,
+        held + [cells, halo],
+        held_specs + [BLOCK, BLOCK],
+        [shape(CORES * EDGE * half, states, dtype=narrow), shape(EDGE + 2, states, states, dtype=narrow)],
+        [BLOCK, BLOCK],
+        [pltpu.SemaphoreType.DMA((2,))],
+    )
+    edge_far = over_op(edge_send, CORES)
+    inner_far = over_op((far_keep + far_in).astype(narrow), CORES)
     inner_own, inner_send = run(
         inner_own_kernel,
         operators,
@@ -328,22 +327,6 @@
         [],
     )
     inner_chip = over_op(inner_send, 1)
-    inner_far = over_op((far_keep + far_in[: inner * half]).astype(narrow), CORES)
-
-    held = [factors, far_in, left, right, left_in, right_in]
-    held_specs = [SMALL, BLOCK, BLOCK, BLOCK, BLOCK, BLOCK]
-    table = pltpu.SMEM((operators, LANES), wide)
-    edge_send, sources = run(
-        edge_far_kernel,
-        CORES * operators,
-        EDGE,
-        held + [cells, halo],
-        held_specs + [BLOCK, BLOCK],
-        [shape(CORES * EDGE * half, states, dtype=narrow), shape(EDGE + 2, states, states, dtype=narrow)],
-        [BLOCK, BLOCK],
-        [table, pltpu.SemaphoreType.DMA((3,))],
-    )
-    edge_far = over_op(edge_send, CORES)
     edge_wide = shape(EDGE * half, states)
     near_own, near_mate = run(
         edge_own_kernel,
@@ -353,7 +336,7 @@
         held_specs + [BLOCK],
         [edge_wide, edge_wide],
         [BLOCK, BLOCK],
-        [table, pltpu.SemaphoreType.DMA],
+        [],
     )
     other = over_op(near_mate + edge_far[EDGE * half :].astype(wide), 1)
     parts = (inner_own, inner_chip, inner_far, near_own, edge_far, other)

time: 40.1 us -> 41.7 us (1.040)
  Pallas kernels: 27.5 us -> 28.4 us
  waiting for transfers between devices: 3.11 us -> 3.72 us
    pallas_call x0 -> x1, Pallas kernels: none -> 2.43 us  [shards(): pl.pallas_call(load_kernel, out_shape=[shape(operators, sectors + 1), plt...]
    pallas_call x4, Pallas kernels: 26.4 us -> 24.9 us  [run(): pl.pallas_call(kernel, out_shape=outs, in_specs=in_specs, out_specs=out_s...]
    ppermute x7 -> x8, waiting for transfers between devices: 3.11 us -> 3.72 us  [over_op(): return lax.ppermute(value, 'op', [(i, i ^ flip) for i in range(op)])]
    ppermute x1, starting transfers between devices: 2.52 us -> 2.94 us  [shards(): halo = lax.ppermute(border, ('sec', 'op'), ring)]
    ppermute x7 -> x8, starting transfers between devices: 6.59 us -> 6.26 us  [over_op(): return lax.ppermute(value, 'op', [(i, i ^ flip) for i in range(op)])]
  transfers between devices with their start and end apart: 8 -> 9, of which waited for: 2 -> 2; matrix products, arithmetic and copies ran while one was open for 0% -> 0% of each run, Pallas kernels for 66% -> 66%
where the time goes in v4:
time: 41.7 us; the launch traced here: 41.5 us
  Pallas kernels  28.4 us (68%)
  starting transfers between devices  9.2 us (22%)
  waiting for transfers between devices  3.72 us (9%)
    pallas_call x4, Pallas kernels, run(): pl.pallas_call(kernel, out_shape=outs, in_specs=in_specs, out_specs=out_s...  24.9 us
    ppermute x8, starting transfers between devices, over_op(): return lax.ppermute(value, 'op', [(i, i ^ flip) for i in range(op)])  6.26 us
    ppermute x8, waiting for transfers between devices, over_op(): return lax.ppermute(value, 'op', [(i, i ^ flip) for i in range(op)])  3.72 us
    ppermute x1, starting transfers between devices, shards(): halo = lax.ppermute(border, ('sec', 'op'), ring)  2.94 us
    pallas_call x1, Pallas kernels, shards(): pl.pallas_call(load_kernel, out_shape=[shape(operators, sectors + 1), plt...  2.43 us
    pallas_call x1, Pallas kernels, shards(): pl.pallas_call(sum_kernel, out_shape=shape(sectors, half, states), in_spe...  1.13 us
  transfers between devices with their start and end apart: 9, of which 2 were waited for; matrix products, arithmetic and copies ran while one was open for 0% of the time, Pallas kernels for 66%

profile of v4, /device:TPU:0, one launch (start us, length us, event | category | flops | bytes accessed | tf_op | source)
XLA Modules:
  0.0 41.5 jit_solution(13984839329575300214)
XLA Ops:
  0.0 0.5 %collective-permute-start.4 = (bf16[8,384,384]{2,1,0:T(8,128)(2,1)}, bf16[8,384,384]{2,1,0:T(8,128)(2,1)S(1)}, u32[]{:S(2)}, u32[]{:S(2)}) collective-permute-start(bf16[8,384,384]{2,1,0:T(8,128)(2,1)} %left_far.1), channel_id=1, source_target_pairs={{0,1},{1,0},{2,3},{3,2},{4,5},{5,4},{6,7},{7,6},{8,9},{9,8},{10,11... | collective-permute-start | bytes 7077896 | tf_op jit(solution)/shard_map/ppermute | solution.py:254
  0.5 0.0 collective-permute-start.5
  0.5 2.4 %load_kernel.1 = (f32[8,9]{1,0:T(8,128)S(1)}, bf16[8,384,384]{2,1,0:T(8,128)(2,1)S(1)}, bf16[1,384,384]{2,1,0:T(8,128)(2,1)S(1)}) custom-call(s32[8]{0:T(128)} %charge.1, s32[8,8]{1,0:T(8,128)} %couple.1, f32[8,8]{1,0:T(8,128)} %amplitude.1, bf16[8,384,384]{2,1,0:T(8,128)(2,1)} %cells_far.1), custom_call_target="tpu_custom_call" | custom-call | tf_op jit(solution)/shard_map/load_kernel/pallas_call | solution.py:270
  2.9 7.1 %shard_map.64 = (f32[384,384]{1,0:T(8,128)S(1)}, f32[384,384]{1,0:T(8,128)S(1)}, bf16[8,384,384]{2,1,0:T(8,128)(2,1)S(1)}, bf16[8,384,384]{2,1,0:T(8,128)(2,1)S(1)}) custom-call(f32[8,9]{1,0:T(8,128)S(1)} %get-tuple-element.18.factors, bf16[8,384,384]{2,1,0:T(8,128)(2,1)} %left_far.1, bf16[8,384,384]{2,1,0:T(8,128)(2,1)} %right_far.1, ...), custom_call_target="tpu_custom_call" | custom-call | flops 3623878656 | bytes 4718592 | tf_op jit(solution)/shard_map/pallas_call | solution.py:239
  10.0 0.5 %collective-permute-start.1 = (f32[384,384]{1,0:T(8,128)S(1)}, f32[384,384]{1,0:T(8,128)S(1)}, u32[]{:S(2)}, u32[]{:S(2)}) collective-permute-start(f32[384,384]{1,0:T(8,128)S(1)} %get-tuple-element.25), channel_id=1, source_target_pairs={{0,1},{1,0},{2,3},{3,2},{4,5},{5,4},{6,7},{7,6},{8,9},{9,8},{10,11... | collective-permute-start | bytes 1769480 | tf_op jit(solution)/shard_map/ppermute | solution.py:254
  10.6 0.1 collective-permute-start.3
  10.6 2.9 %collective-permute-start.6 = (bf16[1,384,384]{2,1,0:T(8,128)(2,1)S(1)}, bf16[1,384,384]{2,1,0:T(8,128)(2,1)S(1)}, u32[]{:S(2)}, u32[]{:S(2)}) collective-permute-start(bf16[1,384,384]{2,1,0:T(8,128)(2,1)S(1)} %get-tuple-element.26), channel_id=1, source_target_pairs={{0,4},{1,29},{2,6},{3,31},{4,8},{5,1},{6,10},{7,3},{8,12},{9,5},{1... | collective-permute-start | bytes 884744 | tf_op jit(solution)/shard_map/ppermute | solution.py:289
  13.6 5.4 %shard_map.65 = (f32[384,384]{1,0:T(8,128)S(1)}, f32[384,384]{1,0:T(8,128)S(1)}) custom-call(f32[8,9]{1,0:T(8,128)S(1)} %get-tuple-element.18.factors, bf16[8,384,384]{2,1,0:T(8,128)(2,1)S(1)} %get-tuple-element.20.left, bf16[8,384,384]{2,1,0:T(8,128)(2,1)S(1)} %get-tuple-element.21.right, bf16[8,384,384]{2,1,0:T(8,128)(2,1)S(1)} %get-tuple-element.19.cells), custom_call_target="tpu_custom_call" | custom-call | flops 3623878656 | bytes 4718592 | tf_op jit(solution)/shard_map/pallas_call | solution.py:239
  18.9 0.0 collective-permute-done.1
  19.0 2.9 %collective-permute-start = (f32[384,384]{1,0:T(8,128)S(1)}, f32[384,384]{1,0:T(8,128)S(1)}, u32[]{:S(2)}, u32[]{:S(2)}) collective-permute-start(f32[384,384]{1,0:T(8,128)S(1)} %get-tuple-element.23), channel_id=1, source_target_pairs={{0,1},{1,0},{2,3},{3,2},{4,5},{5,4},{6,7},{7,6},{8,9},{9,8},{10,11... | collective-permute-start | bytes 1769480 | tf_op jit(solution)/shard_map/ppermute | solution.py:254
  21.9 0.1 add_convert_fusion
  22.0 0.0 collective-permute-done.3.factors_in
  22.0 1.6 %collective-permute-start.2 = (bf16[384,384]{1,0:T(8,128)(2,1)S(1)}, bf16[384,384]{1,0:T(8,128)(2,1)S(1)}, u32[]{:S(2)}, u32[]{:S(2)}) collective-permute-start(bf16[384,384]{1,0:T(8,128)(2,1)S(1)} %add_convert_fusion), channel_id=1, source_target_pairs={{0,2},{1,3},{2,0},{3,1},{4,6},{5,7},{6,4},{7,5},{8,10},{9,11},{10,... | collective-permute-start | bytes 884744 | tf_op jit(solution)/shard_map/ppermute | solution.py:254
  23.6 0.0 collective-permute-done.6.halo
  23.6 0.0 collective-permute-done.4.left_in
  23.6 0.0 collective-permute-done.5.right_in
  23.6 6.4 %shard_map.66 = (bf16[384,384]{1,0:T(8,128)(2,1)S(1)}, bf16[4,384,384]{2,1,0:T(8,128)(2,1)S(1)}) custom-call(f32[8,9]{1,0:T(8,128)S(1)} %get-tuple-element.18.factors, f32[8,9]{1,0:T(8,128)S(1)} %collective-permute-done.3.factors_in, bf16[8,384,384]{2,1,0:T(8,128)(2,1)S(1)} %get-tuple-element.20.left, bf16[8,384,384]{2,1,0:T(8,128)(2,1)S(1)} %get-tuple-element.21.right, ...), custom_call_target="tpu_custom_call" | custom-call | flops 3623878656 | bytes 9437184 | tf_op jit(solution)/shard_map/pallas_call | solution.py:239
  30.0 0.6 %collective-permute-start.7 = (bf16[384,384]{1,0:T(8,128)(2,1)S(1)}, bf16[384,384]{1,0:T(8,128)(2,1)S(1)}, u32[]{:S(2)}, u32[]{:S(2)}) collective-permute-start(bf16[384,384]{1,0:T(8,128)(2,1)S(1)} %get-tuple-element.29), channel_id=1, source_target_pairs={{0,2},{1,3},{2,0},{3,1},{4,6},{5,7},{6,4},{7,5},{8,10},{9,11},{10,... | collective-permute-start | bytes 884744 | tf_op jit(solution)/shard_map/ppermute | solution.py:254
  30.6 6.0 %shard_map.67 = (f32[192,384]{1,0:T(8,128)S(1)}, f32[192,384]{1,0:T(8,128)S(1)}) custom-call(f32[8,9]{1,0:T(8,128)S(1)} %get-tuple-element.18.factors, f32[8,9]{1,0:T(8,128)S(1)} %collective-permute-done.3.factors_in, bf16[8,384,384]{2,1,0:T(8,128)(2,1)S(1)} %get-tuple-element.20.left, bf16[8,384,384]{2,1,0:T(8,128)(2,1)S(1)} %get-tuple-element.21.right, ...), custom_call_target="tpu_custom_call" | custom-call | flops 3623878656 | bytes 9437184 | tf_op jit(solution)/shard_map/pallas_call | solution.py:239
  36.6 2.2 %collective-permute-done.7 = bf16[384,384]{1,0:T(8,128)(2,1)S(1)} collective-permute-done((bf16[384,384]{1,0:T(8,128)(2,1)S(1)}, bf16[384,384]{1,0:T(8,128)(2,1)S(1)}, u32[]{:S(2)}, u32[]{:S(2)}) %collective-permute-start.7) | collective-permute-done | bytes 294944 | tf_op jit(solution)/shard_map/ppermute | solution.py:254
  38.7 0.1 collective-permute-start.8
  38.8 0.0 collective-permute-done
  38.8 0.0 collective-permute-done.2
  38.8 1.5 %collective-permute-done.8 = f32[192,384]{1,0:T(8,128)S(1)} collective-permute-done((f32[192,384]{1,0:T(8,128)S(1)}, f32[192,384]{1,0:T(8,128)S(1)}, u32[]{:S(2)}, u32[]{:S(2)}) %collective-permute-start.8) | collective-permute-done | bytes 294944 | tf_op jit(solution)/shard_map/ppermute | solution.py:254
  40.4 1.1 %total.1 = f32[8,96,384]{2,1,0:T(8,128)} custom-call(f32[4,96,384]{2,1,0:T(8,128)S(1)} %bitcast.7, f32[4,96,384]{2,1,0:T(8,128)S(1)} %bitcast.8, bf16[4,96,384]{2,1,0:T(8,128)(2,1)S(1)} %bitcast.9, f32[2,96,384]{2,1,0:T(8,128)S(1)} %bitcast.10, bf16[4,96,384]{2,1,0:T(8,128)(2,1)S(1)} %bitcast.6, f32[2,96,384]{2,1,0:T(8,128)S(1)} %bitcast.11), custom_call_target="tpu_custom_call" | custom-call | tf_op jit(solution)/shard_map/total/pallas_call | solution.py:343
  (1 shorter events, 0.0 us)
Async XLA Ops:
  0.0 23.6 %collective-permute-start.4 = (bf16[8,384,384]{2,1,0:T(8,128)(2,1)}, bf16[8,384,384]{2,1,0:T(8,128)(2,1)S(1)}, u32[]{:S(2)}, u32[]{:S(2)}) collective-permute-start(bf16[8,384,384]{2,1,0:T(8,128)(2,1)} %left_far.1), channel_id=1, source_target_pairs={{0,1},{1,0},{2,3},{3,2},{4,5},{5,4},{6,7},{7,6},{8,9},{9,8},{10,11... | collective-permute-start | bytes 7077896 | tf_op jit(solution)/shard_map/ppermute | solution.py:254
  0.5 23.1 %collective-permute-start.5 = (bf16[8,384,384]{2,1,0:T(8,128)(2,1)}, bf16[8,384,384]{2,1,0:T(8,128)(2,1)S(1)}, u32[]{:S(2)}, u32[]{:S(2)}) collective-permute-start(bf16[8,384,384]{2,1,0:T(8,128)(2,1)} %right_far.1), channel_id=1, source_target_pairs={{0,1},{1,0},{2,3},{3,2},{4,5},{5,4},{6,7},{7,6},{8,9},{9,8},{10,11... | collective-permute-start | bytes 7077896 | tf_op jit(solution)/shard_map/ppermute | solution.py:254
  10.0 8.9 %collective-permute-start.1 = (f32[384,384]{1,0:T(8,128)S(1)}, f32[384,384]{1,0:T(8,128)S(1)}, u32[]{:S(2)}, u32[]{:S(2)}) collective-permute-start(f32[384,384]{1,0:T(8,128)S(1)} %get-tuple-element.25), channel_id=1, source_target_pairs={{0,1},{1,0},{2,3},{3,2},{4,5},{5,4},{6,7},{7,6},{8,9},{9,8},{10,11... | collective-permute-start | bytes 1769480 | tf_op jit(solution)/shard_map/ppermute | solution.py:254
  10.6 11.4 %collective-permute-start.3 = (f32[8,9]{1,0:T(8,128)S(1)}, f32[8,9]{1,0:T(8,128)S(1)}, u32[]{:S(2)}, u32[]{:S(2)}) collective-permute-start(f32[8,9]{1,0:T(8,128)S(1)} %get-tuple-element.18.factors), channel_id=1, source_target_pairs={{0,1},{1,0},{2,3},{3,2},{4,5},{5,4},{6,7},{7,6},{8,9},{9,8},{10,11... | collective-permute-start | bytes 872 | tf_op jit(solution)/shard_map/ppermute | solution.py:254
  10.6 12.9 %collective-permute-start.6 = (bf16[1,384,384]{2,1,0:T(8,128)(2,1)S(1)}, bf16[1,384,384]{2,1,0:T(8,128)(2,1)S(1)}, u32[]{:S(2)}, u32[]{:S(2)}) collective-permute-start(bf16[1,384,384]{2,1,0:T(8,128)(2,1)S(1)} %get-tuple-element.26), channel_id=1, source_target_pairs={{0,4},{1,29},{2,6},{3,31},{4,8},{5,1},{6,10},{7,3},{8,12},{9,5},{1... | collective-permute-start | bytes 884744 | tf_op jit(solution)/shard_map/ppermute | solution.py:289
  19.0 19.9 %collective-permute-start = (f32[384,384]{1,0:T(8,128)S(1)}, f32[384,384]{1,0:T(8,128)S(1)}, u32[]{:S(2)}, u32[]{:S(2)}) collective-permute-start(f32[384,384]{1,0:T(8,128)S(1)} %get-tuple-element.23), channel_id=1, source_target_pairs={{0,1},{1,0},{2,3},{3,2},{4,5},{5,4},{6,7},{7,6},{8,9},{9,8},{10,11... | collective-permute-start | bytes 1769480 | tf_op jit(solution)/shard_map/ppermute | solution.py:254
  22.0 16.9 %collective-permute-start.2 = (bf16[384,384]{1,0:T(8,128)(2,1)S(1)}, bf16[384,384]{1,0:T(8,128)(2,1)S(1)}, u32[]{:S(2)}, u32[]{:S(2)}) collective-permute-start(bf16[384,384]{1,0:T(8,128)(2,1)S(1)} %add_convert_fusion), channel_id=1, source_target_pairs={{0,2},{1,3},{2,0},{3,1},{4,6},{5,7},{6,4},{7,5},{8,10},{9,11},{10,... | collective-permute-start | bytes 884744 | tf_op jit(solution)/shard_map/ppermute | solution.py:254
  30.0 8.7 %collective-permute-start.7 = (bf16[384,384]{1,0:T(8,128)(2,1)S(1)}, bf16[384,384]{1,0:T(8,128)(2,1)S(1)}, u32[]{:S(2)}, u32[]{:S(2)}) collective-permute-start(bf16[384,384]{1,0:T(8,128)(2,1)S(1)} %get-tuple-element.29), channel_id=1, source_target_pairs={{0,2},{1,3},{2,0},{3,1},{4,6},{5,7},{6,4},{7,5},{8,10},{9,11},{10,... | collective-permute-start | bytes 884744 | tf_op jit(solution)/shard_map/ppermute | solution.py:254
  38.7 1.6 %collective-permute-start.8 = (f32[192,384]{1,0:T(8,128)S(1)}, f32[192,384]{1,0:T(8,128)S(1)}, u32[]{:S(2)}, u32[]{:S(2)}) collective-permute-start(f32[192,384]{1,0:T(8,128)S(1)} %convert_add_fusion), channel_id=1, source_target_pairs={{0,1},{1,0},{2,3},{3,2},{4,5},{5,4},{6,7},{7,6},{8,9},{9,8},{10,11... | collective-permute-start | bytes 884744 | tf_op jit(solution)/shard_map/ppermute | solution.py:254

commit v5 on v4

--- a/solution.py
+++ b/solution.py
@@ -101,54 +101,49 @@
     return copy
 
 
-def load_kernel(
-    charge, couple, amplitude, cells_far, factors, cells, border,
-    charge_here, couple_here, amplitude_here, small_sem, cell_sem,
-):
-    _, core = position()
-    operators, sectors = couple.shape
-    small = [
-        begin(charge, charge_here, small_sem.at[0]),
-        begin(couple, couple_here, small_sem.at[1]),
-        begin(amplitude, amplitude_here, small_sem.at[2]),
-    ]
-    large = [begin(cells_far.at[(sectors - 1) * (1 - core)], border.at[0], cell_sem.at[sectors])]
-    large += [begin(cells_far.at[s], cells.at[s], cell_sem.at[s]) for s in range(sectors)]
-    for copy in small:
-        copy.wait()
-    for k in range(operators):
-        for t in range(sectors):
-            factors[k, t] = amplitude_here[k, t] * couple_here[k, t].astype(jnp.float32)
-        factors[k, sectors] = charge_here[k].astype(jnp.float32)
-    for copy in large:
-        copy.wait()
-
-
 def inner_far_kernel(
-    factors, left_far, right_far, cells, keep, send, left, right, middles, left_sem, right_sem
+    charge, couple, amplitude, left_far, right_far, cells_far,
+    keep, send, factors, left, right, cells,
+    middles, charge_here, couple_here, amplitude_here, small_sem, cell_sem, left_sem, right_sem,
 ):
     chip, core = position()
     operators = left.shape[0]
     sectors = cells.shape[0]
     targets = sectors - 2 * EDGE
     chip_rows = keep.shape[0] // targets * CORES
+    inside = range(EDGE - 1, sectors - EDGE + 1)
 
     def rows(k, place):
         at = pl.ds(pl.multiple_of(place * chip_rows, 64), chip_rows)
         return left_far.at[k, at], left.at[k, at]
 
+    def cell(s):
+        return begin(cells_far.at[s], cells.at[s], cell_sem.at[s])
+
+    small = [
+        begin(charge, charge_here, small_sem.at[0]),
+        begin(couple, couple_here, small_sem.at[1]),
+        begin(amplitude, amplitude_here, small_sem.at[2]),
+    ]
+    first = [cell(s) for s in inside]
     lefts = [begin(*rows(k, 1 - chip), left_sem.at[0, k]) for k in range(operators)]
+    for copy in small:
+        copy.wait()
+    for k in range(operators):
+        for t in range(sectors):
+            factors[k, t] = amplitude_here[k, t] * couple_here[k, t].astype(jnp.float32)
+        factors[k, sectors] = charge_here[k].astype(jnp.float32)
+    for copy in first + lefts[:AHEAD]:
+        copy.wait()
     rights = [begin(right_far.at[k], right.at[k], right_sem.at[k]) for k in range(operators)]
     later = [begin(*rows(k, chip), left_sem.at[1, k]) for k in range(operators)]
-    inside = cells.at[pl.ds(EDGE - 1, targets + 2)]
+    later += [cell(s) for s in range(sectors) if s not in inside]
+    sources = cells.at[pl.ds(EDGE - 1, targets + 2)]
     for k in range(operators):
-        if k == 0:
-            for copy in lefts[:AHEAD]:
-                copy.wait()
         if k == AHEAD:
             for copy in lefts[AHEAD:]:
                 copy.wait()
-        middle_of(k, factors, k, left, inside, middles, sectors, EDGE, targets, 1 - chip, core)
+        middle_of(k, factors, k, left, sources, middles, sectors, EDGE, targets, 1 - chip, core)
     for copy in rights:
         copy.wait()
     summed(jnp.concatenate([right[k] for k in range(operators)], axis=1), middles, (keep, send))
@@ -261,45 +256,42 @@
     for s in range(sec):
         for o in range(op):
             ring.append((s * op + o, (s + 1 if o % CORES == 0 else s - 1) % sec * op + o))
+    core = lax.axis_index("op") & (CORES - 1)
+    border = lax.dynamic_slice_in_dim(wavefunction, (sectors - 1) * (1 - core), 1, 0)
+    halo = lax.ppermute(border, ("sec", "op"), ring)
     left_in = over_op(left_ops, 1)
     right_in = over_op(right_ops, 1)
 
     def in_hbm(*values):
         return [pltpu.with_memory_space_constraint(value, pltpu.HBM) for value in values]
 
-    factors, cells, border = pl.pallas_call(
-        load_kernel,
-        out_shape=[
+    block = shape(inner * half, states)
+    far_keep, far_send, factors, left, right, cells = run(
+        inner_far_kernel,
+        operators,
+        inner,
+        in_hbm(charge, couple, amplitude, left_ops, right_ops, wavefunction),
+        [LARGE] * 6,
+        [
+            block,
+            block,
             shape(operators, sectors + 1),
+            pltpu.VMEM(left_ops.shape, narrow),
+            pltpu.VMEM(right_ops.shape, narrow),
             pltpu.VMEM(wavefunction.shape, narrow),
-            pltpu.VMEM((1, states, states), narrow),
         ],
-        in_specs=[LARGE] * 4,
-        out_specs=[SMALL, BLOCK, BLOCK],
-        scratch_shapes=[
+        [BLOCK, BLOCK, SMALL, BLOCK, BLOCK, BLOCK],
+        [
             pltpu.SMEM(charge.shape, charge.dtype),
             pltpu.SMEM(couple.shape, couple.dtype),
             pltpu.SMEM(amplitude.shape, amplitude.dtype),
             pltpu.SemaphoreType.DMA((3,)),
-            pltpu.SemaphoreType.DMA((sectors + 1,)),
+            pltpu.SemaphoreType.DMA((sectors,)),
+            pltpu.SemaphoreType.DMA((2, operators)),
+            pltpu.SemaphoreType.DMA((operators,)),
         ],
-        compiler_params=pltpu.CompilerParams(vmem_limit_bytes=4 * MIB),
-        name="load_kernel",
-    )(*in_hbm(charge, couple, amplitude, wavefunction))
-    halo = lax.ppermute(border, ("sec", "op"), ring)
+    )
     factors_in = over_op(factors, 1)
-
-    block = shape(inner * half, states)
-    far_keep, far_send, left, right = run(
-        inner_far_kernel,
-        operators,
-        inner,
-        [factors, *in_hbm(left_ops, right_ops), cells],
-        [SMALL, LARGE, LARGE, BLOCK],
-        [block, block, pltpu.VMEM(left_ops.shape, narrow), pltpu.VMEM(right_ops.shape, narrow)],
-        [BLOCK] * 4,
-        [pltpu.SemaphoreType.DMA((2, operators)), pltpu.SemaphoreType.DMA((operators,))],
-    )
     far_in = over_op(far_send, 1)
 
     held = [factors, factors_in, left, right, left_in, right_in]

time: 41.7 us -> 52.9 us (1.27)
  local copies, waits for them, and re-layouts: 0 us -> 10.3 us
  other arithmetic: 0.1 us -> 1.19 us
    unnamed x0 -> x12, local copies, waits for them, and re-layouts: none -> 9.3 us
    pallas_call x4, Pallas kernels: 24.9 us -> 27.5 us  [run(): pl.pallas_call(kernel, out_shape=outs, in_specs=in_specs, out_specs=out_s...]
    pallas_call x1 -> x0, Pallas kernels: 2.43 us -> none  [shards(): pl.pallas_call(load_kernel, out_shape=[shape(operators, sectors + 1), plt...]
    convert_element_type x1, other arithmetic: 0.07 us -> 1.17 us  [shards(): inner_far = over_op((far_keep + far_in).astype(narrow), CORES)]
    dynamic_slice x0 -> x1, local copies, waits for them, and re-layouts: none -> 0.99 us  [shards(): lax.dynamic_slice_in_dim(wavefunction, (sectors - 1) * (1 - core), 1, 0)]
  transfers between devices with their start and end apart: 9 -> 9, of which waited for: 2 -> 2; matrix products, arithmetic and copies ran while one was open for 0% -> 4% of each run, Pallas kernels for 66% -> 52%
where the time goes in v5:
time: 52.9 us; the launch traced here: 52.5 us
  Pallas kernels  28.6 us (54%)
  local copies, waits for them, and re-layouts  10.3 us (19%)
  starting transfers between devices  9.13 us (17%)
  waiting for transfers between devices  3.2 us (6%)
  other arithmetic  1.19 us (2%)
    pallas_call x4, Pallas kernels, run(): pl.pallas_call(kernel, out_shape=outs, in_specs=in_specs, out_specs=out_s...  27.5 us
    unnamed x12, local copies, waits for them, and re-layouts  9.3 us
    ppermute x8, starting transfers between devices, over_op(): return lax.ppermute(value, 'op', [(i, i ^ flip) for i in range(op)])  6.59 us
    ppermute x8, waiting for transfers between devices, over_op(): return lax.ppermute(value, 'op', [(i, i ^ flip) for i in range(op)])  3.19 us
    ppermute x1, starting transfers between devices, shards(): halo = lax.ppermute(border, ('sec', 'op'), ring)  2.54 us
    convert_element_type x1, other arithmetic, shards(): inner_far = over_op((far_keep + far_in).astype(narrow), CORES)  1.17 us
    pallas_call x1, Pallas kernels, shards(): pl.pallas_call(sum_kernel, out_shape=shape(sectors, half, states), in_spe...  1.13 us
  transfers between devices with their start and end apart: 9, of which 2 were waited for; matrix products, arithmetic and copies ran while one was open for 4% of the time, Pallas kernels for 52%

profile of v5, /device:TPU:0, one launch (start us, length us, event | category | flops | bytes accessed | tf_op | source)
XLA Modules:
  0.0 52.5 jit_solution(8916415928256598236)
XLA Ops:
  0.0 0.5 collective-permute-start.4
  0.5 0.0 collective-permute-start.5
  0.5 7.7 %shard_map.64 = (f32[384,384]{1,0:T(8,128)S(1)}, f32[384,384]{1,0:T(8,128)S(1)}, f32[8,9]{1,0:T(8,128)S(1)}, bf16[8,384,384]{2,1,0:T(8,128)(2,1)S(1)}, bf16[8,38...) custom-call(s32[8]{0:T(128)} %charge.1, s32[8,8]{1,0:T(8,128)} %couple.1, f32[8,8]{1,0:T(8,128)} %amplitude.1, ...), custom_call_target="tpu_custom_call" | custom-call | flops 3623878656 | bytes 4718592 | tf_op jit(solution)/shard_map/pallas_call | solution.py:234
  8.3 0.0 copy-start
  8.3 1.4 %copy-done = bf16[8,384,384]{2,1,0:T(8,128)(2,1)} copy-done((bf16[8,384,384]{2,1,0:T(8,128)(2,1)}, bf16[8,384,384]{2,1,0:T(8,128)(2,1)S(1)}, u32[]{:S(2)}) %copy-start) | copy-done | bytes 2359320
  9.7 0.0 copy-start.2
  9.7 1.4 %copy-done.2 = bf16[8,384,384]{2,1,0:T(8,128)(2,1)} copy-done((bf16[8,384,384]{2,1,0:T(8,128)(2,1)}, bf16[8,384,384]{2,1,0:T(8,128)(2,1)S(1)}, u32[]{:S(2)}) %copy-start.2) | copy-done | bytes 2359320
  11.1 0.0 copy-start.4
  11.1 1.5 %copy-done.4 = bf16[8,384,384]{2,1,0:T(8,128)(2,1)} copy-done((bf16[8,384,384]{2,1,0:T(8,128)(2,1)}, bf16[8,384,384]{2,1,0:T(8,128)(2,1)S(1)}, u32[]{:S(2)}) %copy-start.4) | copy-done | bytes 2359320
  12.6 0.5 %collective-permute-start.1 = (f32[384,384]{1,0:T(8,128)S(1)}, f32[384,384]{1,0:T(8,128)}, u32[]{:S(2)}, u32[]{:S(2)}) collective-permute-start(f32[384,384]{1,0:T(8,128)S(1)} %get-tuple-element.24), channel_id=1, source_target_pairs={{0,1},{1,0},{2,3},{3,2},{4,5},{5,4},{6,7},{7,6},{8,9},{9,8},{10,11... | collective-permute-start | bytes 1769480 | tf_op jit(solution)/shard_map/ppermute | solution.py:249
  13.1 1.0 %constant_dynamic-slice_fusion = bf16[1,384,384]{2,1,0:T(8,128)(2,1)S(1)} fusion(bf16[8,384,384]{2,1,0:T(8,128)(2,1)} %cells_far.1, s32[]{:T(128)S(6)} %select_n.3), kind=kLoop, calls=%fused_computation.2 | loop fusion | bytes 589828 | tf_op jit(solution)/shard_map/dynamic_slice | solution.py:260
  14.1 2.5 %collective-permute-start.6 = (bf16[1,384,384]{2,1,0:T(8,128)(2,1)S(1)}, bf16[1,384,384]{2,1,0:T(8,128)(2,1)S(1)}, u32[]{:S(2)}, u32[]{:S(2)}) collective-permute-start(bf16[1,384,384]{2,1,0:T(8,128)(2,1)S(1)} %constant_dynamic-slice_fusion), channel_id=1, source_target_pairs={{0,4},{1,29},{2,6},{3,31},{4,8},{5,1},{6,10},{7,3},{8,12},{9,5},{1... | collective-permute-start | bytes 884744 | tf_op jit(solution)/shard_map/ppermute | solution.py:261
  16.6 3.2 %collective-permute-start.3 = (f32[8,9]{1,0:T(8,128)S(1)}, f32[8,9]{1,0:T(8,128)S(1)}, u32[]{:S(2)}, u32[]{:S(2)}) collective-permute-start(f32[8,9]{1,0:T(8,128)S(1)} %get-tuple-element.17.factors), channel_id=1, source_target_pairs={{0,1},{1,0},{2,3},{3,2},{4,5},{5,4},{6,7},{7,6},{8,9},{9,8},{10,11... | collective-permute-start | bytes 872 | tf_op jit(solution)/shard_map/ppermute | solution.py:249
  19.9 0.0 copy-start.1
  19.9 1.7 %copy-done.1 = bf16[8,384,384]{2,1,0:T(8,128)(2,1)S(1)} copy-done((bf16[8,384,384]{2,1,0:T(8,128)(2,1)S(1)}, bf16[8,384,384]{2,1,0:T(8,128)(2,1)}, u32[]{:S(2)}) %copy-start.1) | copy-done | bytes 2359320
  21.5 0.0 copy-start.3
  21.5 1.7 %copy-done.3 = bf16[8,384,384]{2,1,0:T(8,128)(2,1)S(1)} copy-done((bf16[8,384,384]{2,1,0:T(8,128)(2,1)S(1)}, bf16[8,384,384]{2,1,0:T(8,128)(2,1)}, u32[]{:S(2)}) %copy-start.3) | copy-done | bytes 2359320
  23.2 0.0 copy-start.5
  23.2 1.7 %copy-done.5 = bf16[8,384,384]{2,1,0:T(8,128)(2,1)S(1)} copy-done((bf16[8,384,384]{2,1,0:T(8,128)(2,1)S(1)}, bf16[8,384,384]{2,1,0:T(8,128)(2,1)}, u32[]{:S(2)}) %copy-start.5) | copy-done | bytes 2359320
  24.9 5.3 %shard_map.65 = (f32[384,384]{1,0:T(8,128)S(1)}, f32[384,384]{1,0:T(8,128)S(1)}) custom-call(f32[8,9]{1,0:T(8,128)S(1)} %get-tuple-element.17.factors, bf16[8,384,384]{2,1,0:T(8,128)(2,1)S(1)} %copy-done.1, bf16[8,384,384]{2,1,0:T(8,128)(2,1)S(1)} %copy-done.3, bf16[8,384,384]{2,1,0:T(8,128)(2,1)S(1)} %copy-done.5), custom_call_target="tpu_custom_call" | custom-call | flops 3623878656 | bytes 4718592 | tf_op jit(solution)/shard_map/pallas_call | solution.py:234
  30.2 0.0 collective-permute-done.1
  30.2 0.1 collective-permute-start
  30.3 1.2 %add_convert_fusion = bf16[384,384]{1,0:T(8,128)(2,1)S(1)} fusion(f32[384,384]{1,0:T(8,128)S(1)} %get-tuple-element.23, f32[384,384]{1,0:T(8,128)} %collective-permute-done.1), kind=kLoop, calls=%fused_computation | loop fusion | flops 294912 | bytes 1474560 | tf_op jit(solution)/shard_map/convert_element_type | solution.py:310
  31.5 0.0 collective-permute-done.3.factors_in
  31.5 1.6 %collective-permute-start.2 = (bf16[384,384]{1,0:T(8,128)(2,1)S(1)}, bf16[384,384]{1,0:T(8,128)(2,1)S(1)}, u32[]{:S(2)}, u32[]{:S(2)}) collective-permute-start(bf16[384,384]{1,0:T(8,128)(2,1)S(1)} %add_convert_fusion), channel_id=1, source_target_pairs={{0,2},{1,3},{2,0},{3,1},{4,6},{5,7},{6,4},{7,5},{8,10},{9,11},{10,... | collective-permute-start | bytes 884744 | tf_op jit(solution)/shard_map/ppermute | solution.py:249
  33.1 0.0 collective-permute-done.6.halo
  33.1 0.0 collective-permute-done.4.left_in
  33.1 0.0 collective-permute-done.5.right_in
  33.1 7.4 %shard_map.66 = (bf16[384,384]{1,0:T(8,128)(2,1)S(1)}, bf16[4,384,384]{2,1,0:T(8,128)(2,1)S(1)}) custom-call(f32[8,9]{1,0:T(8,128)S(1)} %get-tuple-element.17.factors, f32[8,9]{1,0:T(8,128)S(1)} %collective-permute-done.3.factors_in, bf16[8,384,384]{2,1,0:T(8,128)(2,1)S(1)} %copy-done.1, bf16[8,384,384]{2,1,0:T(8,128)(2,1)S(1)} %copy-done.3, ...), custom_call_target="tpu_custom_call" | custom-call | flops 3623878656 | bytes 9437184 | tf_op jit(solution)/shard_map/pallas_call | solution.py:234
  40.5 0.6 %collective-permute-start.7 = (bf16[384,384]{1,0:T(8,128)(2,1)S(1)}, bf16[384,384]{1,0:T(8,128)(2,1)S(1)}, u32[]{:S(2)}, u32[]{:S(2)}) collective-permute-start(bf16[384,384]{1,0:T(8,128)(2,1)S(1)} %get-tuple-element.27), channel_id=1, source_target_pairs={{0,2},{1,3},{2,0},{3,1},{4,6},{5,7},{6,4},{7,5},{8,10},{9,11},{10,... | collective-permute-start | bytes 884744 | tf_op jit(solution)/shard_map/ppermute | solution.py:249
  41.1 7.0 %shard_map.67 = (f32[192,384]{1,0:T(8,128)S(1)}, f32[192,384]{1,0:T(8,128)S(1)}) custom-call(f32[8,9]{1,0:T(8,128)S(1)} %get-tuple-element.17.factors, f32[8,9]{1,0:T(8,128)S(1)} %collective-permute-done.3.factors_in, bf16[8,384,384]{2,1,0:T(8,128)(2,1)S(1)} %copy-done.1, bf16[8,384,384]{2,1,0:T(8,128)(2,1)S(1)} %copy-done.3, ...), custom_call_target="tpu_custom_call" | custom-call | flops 3623878656 | bytes 9437184 | tf_op jit(solution)/shard_map/pallas_call | solution.py:234
  48.0 1.6 %collective-permute-done.7 = bf16[384,384]{1,0:T(8,128)(2,1)S(1)} collective-permute-done((bf16[384,384]{1,0:T(8,128)(2,1)S(1)}, bf16[384,384]{1,0:T(8,128)(2,1)S(1)}, u32[]{:S(2)}, u32[]{:S(2)}) %collective-permute-start.7) | collective-permute-done | bytes 294944 | tf_op jit(solution)/shard_map/ppermute | solution.py:249
  49.7 0.1 collective-permute-start.8
  49.8 0.0 collective-permute-done
  49.8 0.0 collective-permute-done.2
  49.8 1.5 %collective-permute-done.8 = f32[192,384]{1,0:T(8,128)S(1)} collective-permute-done((f32[192,384]{1,0:T(8,128)S(1)}, f32[192,384]{1,0:T(8,128)S(1)}, u32[]{:S(2)}, u32[]{:S(2)}) %collective-permute-start.8) | collective-permute-done | bytes 294944 | tf_op jit(solution)/shard_map/ppermute | solution.py:249
  51.3 1.1 %total.1 = f32[8,96,384]{2,1,0:T(8,128)} custom-call(f32[4,96,384]{2,1,0:T(8,128)S(1)} %bitcast.7, f32[4,96,384]{2,1,0:T(8,128)S(1)} %bitcast.8, bf16[4,96,384]{2,1,0:T(8,128)(2,1)S(1)} %bitcast.9, f32[2,96,384]{2,1,0:T(8,128)S(1)} %bitcast.10, bf16[4,96,384]{2,1,0:T(8,128)(2,1)S(1)} %bitcast.6, f32[2,96,384]{2,1,0:T(8,128)S(1)} %bitcast.11), custom_call_target="tpu_custom_call" | custom-call | tf_op jit(solution)/shard_map/total/pallas_call | solution.py:335
  (1 shorter events, 0.0 us)
Async XLA Ops:
  0.0 33.1 %collective-permute-start.4 = (bf16[8,384,384]{2,1,0:T(8,128)(2,1)}, bf16[8,384,384]{2,1,0:T(8,128)(2,1)S(1)}, u32[]{:S(2)}, u32[]{:S(2)}) collective-permute-start(bf16[8,384,384]{2,1,0:T(8,128)(2,1)} %left_far.1), channel_id=1, source_target_pairs={{0,1},{1,0},{2,3},{3,2},{4,5},{5,4},{6,7},{7,6},{8,9},{9,8},{10,11... | collective-permute-start | bytes 7077896 | tf_op jit(solution)/shard_map/ppermute | solution.py:249
  0.5 32.6 %collective-permute-start.5 = (bf16[8,384,384]{2,1,0:T(8,128)(2,1)}, bf16[8,384,384]{2,1,0:T(8,128)(2,1)}, u32[]{:S(2)}, u32[]{:S(2)}) collective-permute-start(bf16[8,384,384]{2,1,0:T(8,128)(2,1)} %right_far.1), channel_id=1, source_target_pairs={{0,1},{1,0},{2,3},{3,2},{4,5},{5,4},{6,7},{7,6},{8,9},{9,8},{10,11... | collective-permute-start | bytes 7077896 | tf_op jit(solution)/shard_map/ppermute | solution.py:249
  8.3 1.4 %copy-start = (bf16[8,384,384]{2,1,0:T(8,128)(2,1)}, bf16[8,384,384]{2,1,0:T(8,128)(2,1)S(1)}, u32[]{:S(2)}) copy-start(bf16[8,384,384]{2,1,0:T(8,128)(2,1)S(1)} %get-tuple-element.18.left) | copy-start | bytes 7077892
  9.7 1.4 %copy-start.2 = (bf16[8,384,384]{2,1,0:T(8,128)(2,1)}, bf16[8,384,384]{2,1,0:T(8,128)(2,1)S(1)}, u32[]{:S(2)}) copy-start(bf16[8,384,384]{2,1,0:T(8,128)(2,1)S(1)} %get-tuple-element.19.right) | copy-start | bytes 7077892
  11.1 1.5 %copy-start.4 = (bf16[8,384,384]{2,1,0:T(8,128)(2,1)}, bf16[8,384,384]{2,1,0:T(8,128)(2,1)S(1)}, u32[]{:S(2)}) copy-start(bf16[8,384,384]{2,1,0:T(8,128)(2,1)S(1)} %get-tuple-element.20.cells) | copy-start | bytes 7077892
  12.6 17.6 %collective-permute-start.1 = (f32[384,384]{1,0:T(8,128)S(1)}, f32[384,384]{1,0:T(8,128)}, u32[]{:S(2)}, u32[]{:S(2)}) collective-permute-start(f32[384,384]{1,0:T(8,128)S(1)} %get-tuple-element.24), channel_id=1, source_target_pairs={{0,1},{1,0},{2,3},{3,2},{4,5},{5,4},{6,7},{7,6},{8,9},{9,8},{10,11... | collective-permute-start | bytes 1769480 | tf_op jit(solution)/shard_map/ppermute | solution.py:249
  14.1 19.0 %collective-permute-start.6 = (bf16[1,384,384]{2,1,0:T(8,128)(2,1)S(1)}, bf16[1,384,384]{2,1,0:T(8,128)(2,1)S(1)}, u32[]{:S(2)}, u32[]{:S(2)}) collective-permute-start(bf16[1,384,384]{2,1,0:T(8,128)(2,1)S(1)} %constant_dynamic-slice_fusion), channel_id=1, source_target_pairs={{0,4},{1,29},{2,6},{3,31},{4,8},{5,1},{6,10},{7,3},{8,12},{9,5},{1... | collective-permute-start | bytes 884744 | tf_op jit(solution)/shard_map/ppermute | solution.py:261
  16.6 14.8 %collective-permute-start.3 = (f32[8,9]{1,0:T(8,128)S(1)}, f32[8,9]{1,0:T(8,128)S(1)}, u32[]{:S(2)}, u32[]{:S(2)}) collective-permute-start(f32[8,9]{1,0:T(8,128)S(1)} %get-tuple-element.17.factors), channel_id=1, source_target_pairs={{0,1},{1,0},{2,3},{3,2},{4,5},{5,4},{6,7},{7,6},{8,9},{9,8},{10,11... | collective-permute-start | bytes 872 | tf_op jit(solution)/shard_map/ppermute | solution.py:249
  19.9 1.7 %copy-start.1 = (bf16[8,384,384]{2,1,0:T(8,128)(2,1)S(1)}, bf16[8,384,384]{2,1,0:T(8,128)(2,1)}, u32[]{:S(2)}) copy-start(bf16[8,384,384]{2,1,0:T(8,128)(2,1)} %copy-done) | copy-start | bytes 7077892
  21.5 1.7 %copy-start.3 = (bf16[8,384,384]{2,1,0:T(8,128)(2,1)S(1)}, bf16[8,384,384]{2,1,0:T(8,128)(2,1)}, u32[]{:S(2)}) copy-start(bf16[8,384,384]{2,1,0:T(8,128)(2,1)} %copy-done.2) | copy-start | bytes 7077892
  23.2 1.7 %copy-start.5 = (bf16[8,384,384]{2,1,0:T(8,128)(2,1)S(1)}, bf16[8,384,384]{2,1,0:T(8,128)(2,1)}, u32[]{:S(2)}) copy-start(bf16[8,384,384]{2,1,0:T(8,128)(2,1)} %copy-done.4) | copy-start | bytes 7077892
  30.2 19.6 %collective-permute-start = (f32[384,384]{1,0:T(8,128)S(1)}, f32[384,384]{1,0:T(8,128)S(1)}, u32[]{:S(2)}, u32[]{:S(2)}) collective-permute-start(f32[384,384]{1,0:T(8,128)S(1)} %get-tuple-element.22), channel_id=1, source_target_pairs={{0,1},{1,0},{2,3},{3,2},{4,5},{5,4},{6,7},{7,6},{8,9},{9,8},{10,11... | collective-permute-start | bytes 1769480 | tf_op jit(solution)/shard_map/ppermute | solution.py:249
  31.5 18.3 %collective-permute-start.2 = (bf16[384,384]{1,0:T(8,128)(2,1)S(1)}, bf16[384,384]{1,0:T(8,128)(2,1)S(1)}, u32[]{:S(2)}, u32[]{:S(2)}) collective-permute-start(bf16[384,384]{1,0:T(8,128)(2,1)S(1)} %add_convert_fusion), channel_id=1, source_target_pairs={{0,2},{1,3},{2,0},{3,1},{4,6},{5,7},{6,4},{7,5},{8,10},{9,11},{10,... | collective-permute-start | bytes 884744 | tf_op jit(solution)/shard_map/ppermute | solution.py:249
  40.5 9.2 %collective-permute-start.7 = (bf16[384,384]{1,0:T(8,128)(2,1)S(1)}, bf16[384,384]{1,0:T(8,128)(2,1)S(1)}, u32[]{:S(2)}, u32[]{:S(2)}) collective-permute-start(bf16[384,384]{1,0:T(8,128)(2,1)S(1)} %get-tuple-element.27), channel_id=1, source_target_pairs={{0,2},{1,3},{2,0},{3,1},{4,6},{5,7},{6,4},{7,5},{8,10},{9,11},{10,... | collective-permute-start | bytes 884744 | tf_op jit(solution)/shard_map/ppermute | solution.py:249
  49.7 1.6 %collective-permute-start.8 = (f32[192,384]{1,0:T(8,128)S(1)}, f32[192,384]{1,0:T(8,128)S(1)}, u32[]{:S(2)}, u32[]{:S(2)}) collective-permute-start(f32[192,384]{1,0:T(8,128)S(1)} %convert_add_fusion), channel_id=1, source_target_pairs={{0,1},{1,0},{2,3},{3,2},{4,5},{5,4},{6,7},{7,6},{8,9},{9,8},{10,11... | collective-permute-start | bytes 884744 | tf_op jit(solution)/shard_map/ppermute | solution.py:249

commit v6 on v5

--- a/solution.py
+++ b/solution.py
@@ -52,17 +52,19 @@
     return lax.psum_scatter(accumulated, "op", scatter_dimension=1, tiled=True)
 
 
-def middle_of(k, factors, own, left, sources, middles, sectors, first_target, targets, chip, core):
+def middle_of(k, small, own, left, sources, middles, first_target, targets, chip, core):
+    charge, couple, amplitude = small
     states = sources.shape[-1]
     half = middles.shape[0] // (CORES * targets)
-    shift = 1 - factors[own, sectors].astype(jnp.int32)
+    shift = 1 - charge[own]
     wide = jnp.concatenate([sources[shift + t] for t in range(targets)], axis=1)
     rows = jnp.concatenate(
         [left[own, pl.ds(row_of(chip, owner, half), half)] for owner in (core, 1 - core)], axis=0
     )
     middle = jnp.dot(rows, wide, preferred_element_type=jnp.float32)
     for t in range(targets):
-        factor = factors[own, first_target + t]
+        at = first_target + t
+        factor = amplitude[own, at] * couple[own, at].astype(jnp.float32)
         block = middle[:, t * states : (t + 1) * states].astype(jnp.bfloat16)
         block = (block.astype(jnp.float32) * factor).astype(jnp.bfloat16)
         for part in range(CORES):
@@ -86,6 +88,11 @@
                 ].astype(results[part].dtype)
 
 
+def halves(results):
+    width = results.shape[0] // CORES
+    return [results.at[pl.ds(part * width, width)] for part in range(CORES)]
+
+
 def position():
     place = lax.axis_index("op")
     return lax.shift_right_logical(place, CORES - 1), place & (CORES - 1)
@@ -102,15 +109,14 @@
 
 
 def inner_far_kernel(
-    charge, couple, amplitude, left_far, right_far, cells_far,
-    keep, send, factors, left, right, cells,
-    middles, charge_here, couple_here, amplitude_here, small_sem, cell_sem, left_sem, right_sem,
+    charge, couple, amplitude, left_far, right_far, cells_far, send, left, right, cells, middles,
+    charge_here, couple_here, amplitude_here, small_sem, cell_sem, left_sem, right_sem,
 ):
     chip, core = position()
     operators = left.shape[0]
     sectors = cells.shape[0]
     targets = sectors - 2 * EDGE
-    chip_rows = keep.shape[0] // targets * CORES
+    chip_rows = send.shape[0] // targets
     inside = range(EDGE - 1, sectors - EDGE + 1)
 
     def rows(k, place):
@@ -129,51 +135,49 @@
     lefts = [begin(*rows(k, 1 - chip), left_sem.at[0, k]) for k in range(operators)]
     for copy in small:
         copy.wait()
-    for k in range(operators):
-        for t in range(sectors):
-            factors[k, t] = amplitude_here[k, t] * couple_here[k, t].astype(jnp.float32)
-        factors[k, sectors] = charge_here[k].astype(jnp.float32)
     for copy in first + lefts[:AHEAD]:
         copy.wait()
     rights = [begin(right_far.at[k], right.at[k], right_sem.at[k]) for k in range(operators)]
     later = [begin(*rows(k, chip), left_sem.at[1, k]) for k in range(operators)]
     later += [cell(s) for s in range(sectors) if s not in inside]
     sources = cells.at[pl.ds(EDGE - 1, targets + 2)]
+    here = (charge_here, couple_here, amplitude_here)
     for k in range(operators):
         if k == AHEAD:
             for copy in lefts[AHEAD:]:
                 copy.wait()
-        middle_of(k, factors, k, left, sources, middles, sectors, EDGE, targets, 1 - chip, core)
+        middle_of(k, here, k, left, sources, middles, EDGE, targets, 1 - chip, core)
     for copy in rights:
         copy.wait()
-    summed(jnp.concatenate([right[k] for k in range(operators)], axis=1), middles, (keep, send))
+    summed(jnp.concatenate([right[k] for k in range(operators)], axis=1), middles, halves(send))
     for copy in later:
         copy.wait()
 
 
-def inner_own_kernel(factors, left, right, cells, keep, send, middles):
+def inner_own_kernel(charge, couple, amplitude, left, right, cells, keep, send, middles):
     chip, core = position()
     operators = left.shape[0]
     targets = cells.shape[0] - 2 * EDGE
     inside = cells.at[pl.ds(EDGE - 1, targets + 2)]
     for k in range(operators):
-        middle_of(k, factors, k, left, inside, middles, cells.shape[0], EDGE, targets, chip, core)
+        middle_of(k, (charge, couple, amplitude), k, left, inside, middles, EDGE, targets, chip, core)
     summed(jnp.concatenate([right[k] for k in range(operators)], axis=1), middles, (keep, send))
 
 
 def edge_products(groups, sources, middles, results, sectors, chip, core):
     k = 0
     first_target = (sectors - EDGE) * core
-    for factors, left, right in groups:
+    for small, left, right in groups:
         for own in range(left.shape[0]):
-            middle_of(k, factors, own, left, sources, middles, sectors, first_target, EDGE, chip, core)
+            middle_of(k, small, own, left, sources, middles, first_target, EDGE, chip, core)
             k += 1
     wide = jnp.concatenate([right[own] for _, _, right in groups for own in range(right.shape[0])], axis=1)
     summed(wide, middles, results)
 
 
 def edge_far_kernel(
-    factors, factors_in, left, right, left_in, right_in, cells, halo, send, sources, middles, sem
+    charge, couple, amplitude, charge_in, couple_in, amplitude_in, left, right, left_in, right_in,
+    cells, halo, send, sources, middles, sem,
 ):
     chip, core = position()
     sectors = cells.shape[0]
@@ -188,18 +192,23 @@
         copy.start()
     for copy in copies:
         copy.wait()
-    groups = ((factors, left, right), (factors_in, left_in, right_in))
-    width = send.shape[0] // CORES
-    halves = [send.at[pl.ds(part * width, width)] for part in range(CORES)]
-    edge_products(groups, sources, middles, halves, sectors, 1 - chip, core)
+    groups = (
+        ((charge, couple, amplitude), left, right),
+        ((charge_in, couple_in, amplitude_in), left_in, right_in),
+    )
+    edge_products(groups, sources, middles, halves(send), sectors, 1 - chip, core)
 
 
 def edge_own_kernel(
-    factors, factors_in, left, right, left_in, right_in, sources, keep, send, middles
+    charge, couple, amplitude, charge_in, couple_in, amplitude_in, left, right, left_in, right_in,
+    sources, keep, send, middles,
 ):
     chip, core = position()
-    sectors = factors.shape[1] - 1
-    groups = ((factors, left, right), (factors_in, left_in, right_in))
+    sectors = couple.shape[1]
+    groups = (
+        ((charge, couple, amplitude), left, right),
+        ((charge_in, couple_in, amplitude_in), left_in, right_in),
+    )
     edge_products(groups, sources, middles, (keep, send), sectors, chip, core)
 
 
@@ -207,7 +216,7 @@
     core = lax.axis_index("op") & (CORES - 1)
     sectors = sigma.shape[0]
     far = sectors - EDGE
-    sigma[EDGE:far] = inner_own[...] + inner_chip[...] + inner_far[...].astype(jnp.float32)
+    sigma[EDGE:far] = inner_own[...] + inner_chip[...] + inner_far[: far - EDGE].astype(jnp.float32)
     sigma[pl.ds(far * core, EDGE)] = near_own[...] + edge_far[:EDGE].astype(jnp.float32)
     sigma[pl.ds(far * (1 - core), EDGE)] = other[...]
 
@@ -262,25 +271,25 @@
     left_in = over_op(left_ops, 1)
     right_in = over_op(right_ops, 1)
 
+    small = (charge, couple, amplitude)
+    small_in = [over_op(value, 1) for value in small]
+
     def in_hbm(*values):
         return [pltpu.with_memory_space_constraint(value, pltpu.HBM) for value in values]
 
-    block = shape(inner * half, states)
-    far_keep, far_send, factors, left, right, cells = run(
+    far_send, left, right, cells = run(
         inner_far_kernel,
         operators,
         inner,
-        in_hbm(charge, couple, amplitude, left_ops, right_ops, wavefunction),
+        in_hbm(*small, left_ops, right_ops, wavefunction),
         [LARGE] * 6,
         [
-            block,
-            block,
-            shape(operators, sectors + 1),
+            shape(CORES * inner * half, states, dtype=narrow),
             pltpu.VMEM(left_ops.shape, narrow),
             pltpu.VMEM(right_ops.shape, narrow),
             pltpu.VMEM(wavefunction.shape, narrow),
         ],
-        [BLOCK, BLOCK, SMALL, BLOCK, BLOCK, BLOCK],
+        [BLOCK] * 4,
         [
             pltpu.SMEM(charge.shape, charge.dtype),
             pltpu.SMEM(couple.shape, couple.dtype),
@@ -291,11 +300,11 @@
             pltpu.SemaphoreType.DMA((operators,)),
         ],
     )
-    factors_in = over_op(factors, 1)
-    far_in = over_op(far_send, 1)
-
-    held = [factors, factors_in, left, right, left_in, right_in]
-    held_specs = [SMALL, SMALL, BLOCK, BLOCK, BLOCK, BLOCK]
+    inner_far = over_op(far_send, CORES)
+
+    here = in_hbm(*small)
+    held = [*here, *small_in, left, right, left_in, right_in]
+    held_specs = [SMALL] * 6 + [BLOCK] * 4
     edge_send, sources = run(
         edge_far_kernel,
         CORES * operators,
@@ -307,18 +316,18 @@
         [pltpu.SemaphoreType.DMA((2,))],
     )
     edge_far = over_op(edge_send, CORES)
-    inner_far = over_op((far_keep + far_in).astype(narrow), CORES)
+    block = shape(inner * half, states)
     inner_own, inner_send = run(
         inner_own_kernel,
         operators,
         inner,
-        [factors, left, right, cells],
-        [SMALL, BLOCK, BLOCK, BLOCK],
+        [*here, left, right, cells],
+        [SMALL] * 3 + [BLOCK] * 3,
         [block, block],
         [BLOCK, BLOCK],
         [],
     )
-    inner_chip = over_op(inner_send, 1)
+    inner_chip = over_op(inner_send + inner_far[inner * half :].astype(wide), 1)
     edge_wide = shape(EDGE * half, states)
     near_own, near_mate = run(
         edge_own_kernel,

time: 52.9 us -> 52.4 us (level)
  other arithmetic: 1.19 us -> 0.08 us
  waiting for transfers between devices: 3.2 us -> 3.95 us
  Pallas kernels: 28.6 us -> 27.9 us
  starting transfers between devices: 9.13 us -> 9.68 us
    ppermute x8 -> x9, starting transfers between devices: 6.59 us -> 7.96 us  [over_op(): return lax.ppermute(value, 'op', [(i, i ^ flip) for i in range(op)])]
    convert_element_type x1 -> x0, other arithmetic: 1.17 us -> none  [shards(): inner_far = over_op((far_keep + far_in).astype(narrow), CORES)]
    ppermute x1, starting transfers between devices: 2.54 us -> 1.72 us  [shards(): halo = lax.ppermute(border, ('sec', 'op'), ring)]
    ppermute x8 -> x9, waiting for transfers between devices: 3.19 us -> 3.95 us  [over_op(): return lax.ppermute(value, 'op', [(i, i ^ flip) for i in range(op)])]
    pallas_call x4, Pallas kernels: 27.5 us -> 26.7 us  [run(): pl.pallas_call(kernel, out_shape=outs, in_specs=in_specs, out_specs=out_s...]
    unnamed x12 -> x18, local copies, waits for them, and re-layouts: 9.3 us -> 9.36 us
  transfers between devices with their start and end apart: 9 -> 10, of which waited for: 2 -> 3; matrix products, arithmetic and copies ran while one was open for 4% -> 2% of each run, Pallas kernels for 52% -> 51%
where the time goes in v6:
time: 52.4 us; the launch traced here: 52 us
  Pallas kernels  27.9 us (53%)
  local copies, waits for them, and re-layouts  10.4 us (20%)
  starting transfers between devices  9.68 us (18%)
  waiting for transfers between devices  3.95 us (8%)
    pallas_call x4, Pallas kernels, run(): pl.pallas_call(kernel, out_shape=outs, in_specs=in_specs, out_specs=out_s...  26.7 us
    unnamed x18, local copies, waits for them, and re-layouts  9.36 us
    ppermute x9, starting transfers between devices, over_op(): return lax.ppermute(value, 'op', [(i, i ^ flip) for i in range(op)])  7.96 us
    ppermute x9, waiting for transfers between devices, over_op(): return lax.ppermute(value, 'op', [(i, i ^ flip) for i in range(op)])  3.95 us
    ppermute x1, starting transfers between devices, shards(): halo = lax.ppermute(border, ('sec', 'op'), ring)  1.72 us
    pallas_call x1, Pallas kernels, shards(): pl.pallas_call(sum_kernel, out_shape=shape(sectors, half, states), in_spe...  1.15 us
  transfers between devices with their start and end apart: 10, of which 3 were waited for; matrix products, arithmetic and copies ran while one was open for 2% of the time, Pallas kernels for 51%

profile of v6, /device:TPU:0, one launch (start us, length us, event | category | flops | bytes accessed | tf_op | source)
XLA Modules:
  0.0 52.0 jit_solution(8071915907121249271)
XLA Ops:
  0.0 0.0 copy-start.8
  0.0 0.5 collective-permute-start.5
  0.5 0.1 collective-permute-start.6
  0.6 7.0 %shard_map.64 = (bf16[768,384]{1,0:T(8,128)(2,1)S(1)}, bf16[8,384,384]{2,1,0:T(8,128)(2,1)S(1)}, bf16[8,384,384]{2,1,0:T(8,128)(2,1)S(1)}, bf16[8,384,384]{2,1,0:T(8,128)(2,1)S(1)}) custom-call(s32[8]{0:T(128)} %charge.7, s32[8,8]{1,0:T(8,128)} %couple.7, f32[8,8]{1,0:T(8,128)} %amplitude.7, bf16[8,384,384]{2,1,0:T(8,128)(2,1)} %left_far.1, ...), custom_call_target="tpu_custom_call" | custom-call | flops 3623878656 | bytes 4718592 | tf_op jit(solution)/shard_map/pallas_call | solution.py:243
  7.6 0.0 copy-start
  7.6 1.4 %copy-done = bf16[8,384,384]{2,1,0:T(8,128)(2,1)} copy-done((bf16[8,384,384]{2,1,0:T(8,128)(2,1)}, bf16[8,384,384]{2,1,0:T(8,128)(2,1)S(1)}, u32[]{:S(2)}) %copy-start) | copy-done | bytes 2359320
  9.0 0.0 copy-start.2
  9.0 1.4 %copy-done.2 = bf16[8,384,384]{2,1,0:T(8,128)(2,1)} copy-done((bf16[8,384,384]{2,1,0:T(8,128)(2,1)}, bf16[8,384,384]{2,1,0:T(8,128)(2,1)S(1)}, u32[]{:S(2)}) %copy-start.2) | copy-done | bytes 2359320
  10.5 0.0 copy-start.4
  10.5 1.5 %copy-done.4 = bf16[8,384,384]{2,1,0:T(8,128)(2,1)} copy-done((bf16[8,384,384]{2,1,0:T(8,128)(2,1)}, bf16[8,384,384]{2,1,0:T(8,128)(2,1)S(1)}, u32[]{:S(2)}) %copy-start.4) | copy-done | bytes 2359320
  11.9 3.0 %collective-permute-start = (bf16[768,384]{1,0:T(8,128)(2,1)S(1)}, bf16[768,384]{1,0:T(8,128)(2,1)S(1)}, u32[]{:S(2)}, u32[]{:S(2)}) collective-permute-start(bf16[768,384]{1,0:T(8,128)(2,1)S(1)} %get-tuple-element.20), channel_id=1, source_target_pairs={{0,2},{1,3},{2,0},{3,1},{4,6},{5,7},{6,4},{7,5},{8,10},{9,11},{10,... | collective-permute-start | bytes 1769480 | tf_op jit(solution)/shard_map/ppermute | solution.py:258
  14.9 0.0 copy-done.8
  14.9 0.0 collective-permute-start.2
  14.9 1.0 %constant_dynamic-slice_fusion = bf16[1,384,384]{2,1,0:T(8,128)(2,1)S(1)} fusion(bf16[8,384,384]{2,1,0:T(8,128)(2,1)} %cells_far.1, s32[]{:T(128)S(6)} %select_n.3), kind=kLoop, calls=%fused_computation.2 | loop fusion | bytes 589828 | tf_op jit(solution)/shard_map/dynamic_slice | solution.py:269
  15.9 1.7 %collective-permute-start.7 = (bf16[1,384,384]{2,1,0:T(8,128)(2,1)S(1)}, bf16[1,384,384]{2,1,0:T(8,128)(2,1)S(1)}, u32[]{:S(2)}, u32[]{:S(2)}) collective-permute-start(bf16[1,384,384]{2,1,0:T(8,128)(2,1)S(1)} %constant_dynamic-slice_fusion), channel_id=1, source_target_pairs={{0,4},{1,29},{2,6},{3,31},{4,8},{5,1},{6,10},{7,3},{8,12},{9,5},{1... | collective-permute-start | bytes 884744 | tf_op jit(solution)/shard_map/ppermute | solution.py:270
  17.6 0.0 copy-start.1
  17.6 1.7 %copy-done.1 = bf16[8,384,384]{2,1,0:T(8,128)(2,1)S(1)} copy-done((bf16[8,384,384]{2,1,0:T(8,128)(2,1)S(1)}, bf16[8,384,384]{2,1,0:T(8,128)(2,1)}, u32[]{:S(2)}) %copy-start.1) | copy-done | bytes 2359320
  19.3 0.0 copy-start.3
  19.3 1.7 %copy-done.3 = bf16[8,384,384]{2,1,0:T(8,128)(2,1)S(1)} copy-done((bf16[8,384,384]{2,1,0:T(8,128)(2,1)S(1)}, bf16[8,384,384]{2,1,0:T(8,128)(2,1)}, u32[]{:S(2)}) %copy-start.3) | copy-done | bytes 2359320
  21.0 0.0 copy-start.5
  21.0 1.7 %copy-done.5 = bf16[8,384,384]{2,1,0:T(8,128)(2,1)S(1)} copy-done((bf16[8,384,384]{2,1,0:T(8,128)(2,1)S(1)}, bf16[8,384,384]{2,1,0:T(8,128)(2,1)}, u32[]{:S(2)}) %copy-start.5) | copy-done | bytes 2359320
  22.6 0.0 copy-start.6
  22.6 0.0 copy-start.7
  22.6 5.6 %shard_map.65 = (f32[384,384]{1,0:T(8,128)S(1)}, f32[384,384]{1,0:T(8,128)S(1)}) custom-call(s32[8]{0:T(128)} %charge.7, s32[8,8]{1,0:T(8,128)} %couple.7, f32[8,8]{1,0:T(8,128)} %amplitude.7, bf16[8,384,384]{2,1,0:T(8,128)(2,1)S(1)} %copy-done.1, bf16[8,384,384]{2,1,0:T(8,128)(2,1)S(1)} %copy-done.3, bf16[8,384,384]{2,1,0:T(8,128)(2,1)S(1)} %copy-done.5), custom_call_target="tpu_custom_call" | custom-call | flops 3623878656 | bytes 4718592 | tf_op jit(solution)/shard_map/pallas_call | solution.py:243
  28.2 0.0 collective-permute-done.2.charge_in
  28.3 0.0 copy-done.6
  28.3 3.4 %collective-permute-start.3 = (s32[8,8]{1,0:T(8,128)S(1)}, s32[8,8]{1,0:T(8,128)S(1)}, u32[]{:S(2)}, u32[]{:S(2)}) collective-permute-start(s32[8,8]{1,0:T(8,128)S(1)} %copy-done.6), channel_id=1, source_target_pairs={{0,1},{1,0},{2,3},{3,2},{4,5},{5,4},{6,7},{7,6},{8,9},{9,8},{10,11... | collective-permute-start | bytes 776 | tf_op jit(solution)/shard_map/ppermute | solution.py:258
  31.6 0.0 collective-permute-done
  31.6 0.0 copy-done.7
  31.6 0.1 collective-permute-start.4
  31.7 0.1 convert_add_fusion
  31.8 0.7 %collective-permute-done.3.couple_in = s32[8,8]{1,0:T(8,128)S(1)} collective-permute-done((s32[8,8]{1,0:T(8,128)S(1)}, s32[8,8]{1,0:T(8,128)S(1)}, u32[]{:S(2)}, u32[]{:S(2)}) %collective-permute-start.3) | collective-permute-done | bytes 288 | tf_op jit(solution)/shard_map/ppermute | solution.py:258
  32.5 0.3 collective-permute-start.1
  32.8 0.0 collective-permute-done.4.amplitude_in
  32.8 0.0 collective-permute-done.7.halo
  32.8 0.0 collective-permute-done.5.left_in
  32.8 0.0 collective-permute-done.6.right_in
  32.8 7.2 %shard_map.66 = (bf16[384,384]{1,0:T(8,128)(2,1)S(1)}, bf16[4,384,384]{2,1,0:T(8,128)(2,1)S(1)}) custom-call(s32[8]{0:T(128)} %charge.7, s32[8,8]{1,0:T(8,128)} %couple.7, f32[8,8]{1,0:T(8,128)} %amplitude.7, s32[8]{0:T(128)S(1)} %collective-permute-done.2.charge_in, s32[8,8]{1,0:T(8,128)S(1)} %collective-permute-done.3.couple_in, ...), custom_call_target="tpu_custom_call" | custom-call | flops 3623878656 | bytes 9437184 | tf_op jit(solution)/shard_map/pallas_call | solution.py:243
  40.0 0.6 %collective-permute-start.8 = (bf16[384,384]{1,0:T(8,128)(2,1)S(1)}, bf16[384,384]{1,0:T(8,128)(2,1)S(1)}, u32[]{:S(2)}, u32[]{:S(2)}) collective-permute-start(bf16[384,384]{1,0:T(8,128)(2,1)S(1)} %get-tuple-element.23), channel_id=1, source_target_pairs={{0,2},{1,3},{2,0},{3,1},{4,6},{5,7},{6,4},{7,5},{8,10},{9,11},{10,... | collective-permute-start | bytes 884744 | tf_op jit(solution)/shard_map/ppermute | solution.py:258
  40.6 6.9 %shard_map.67 = (f32[192,384]{1,0:T(8,128)S(1)}, f32[192,384]{1,0:T(8,128)S(1)}) custom-call(s32[8]{0:T(128)} %charge.7, s32[8,8]{1,0:T(8,128)} %couple.7, f32[8,8]{1,0:T(8,128)} %amplitude.7, s32[8]{0:T(128)S(1)} %collective-permute-done.2.charge_in, s32[8,8]{1,0:T(8,128)S(1)} %collective-permute-done.3.couple_in, ...), custom_call_target="tpu_custom_call" | custom-call | flops 3623878656 | bytes 9437184 | tf_op jit(solution)/shard_map/pallas_call | solution.py:243
  47.5 1.7 %collective-permute-done.8 = bf16[384,384]{1,0:T(8,128)(2,1)S(1)} collective-permute-done((bf16[384,384]{1,0:T(8,128)(2,1)S(1)}, bf16[384,384]{1,0:T(8,128)(2,1)S(1)}, u32[]{:S(2)}, u32[]{:S(2)}) %collective-permute-start.8) | collective-permute-done | bytes 294944 | tf_op jit(solution)/shard_map/ppermute | solution.py:258
  49.2 0.1 collective-permute-start.9
  49.3 0.0 collective-permute-done.1
  49.3 1.6 %collective-permute-done.9 = f32[192,384]{1,0:T(8,128)S(1)} collective-permute-done((f32[192,384]{1,0:T(8,128)S(1)}, f32[192,384]{1,0:T(8,128)S(1)}, u32[]{:S(2)}, u32[]{:S(2)}) %collective-permute-start.9) | collective-permute-done | bytes 294944 | tf_op jit(solution)/shard_map/ppermute | solution.py:258
  50.9 1.1 %total.1 = f32[8,96,384]{2,1,0:T(8,128)} custom-call(f32[4,96,384]{2,1,0:T(8,128)S(1)} %bitcast.8, f32[4,96,384]{2,1,0:T(8,128)S(1)} %bitcast.9, bf16[8,96,384]{2,1,0:T(8,128)(2,1)S(1)} %bitcast.6, f32[2,96,384]{2,1,0:T(8,128)S(1)} %bitcast.10, bf16[4,96,384]{2,1,0:T(8,128)(2,1)S(1)} %bitcast.7, f32[2,96,384]{2,1,0:T(8,128)S(1)} %bitcast.11), custom_call_target="tpu_custom_call" | custom-call | tf_op jit(solution)/shard_map/total/pallas_call | solution.py:344
  (1 shorter events, 0.0 us)
Async XLA Ops:
  0.0 14.9 %copy-start.8 = (s32[8]{0:T(128)S(1)}, s32[8]{0:T(128)}, u32[]{:S(2)}) copy-start(s32[8]{0:T(128)} %charge.7) | copy-start | bytes 100
  0.0 32.8 %collective-permute-start.5 = (bf16[8,384,384]{2,1,0:T(8,128)(2,1)}, bf16[8,384,384]{2,1,0:T(8,128)(2,1)S(1)}, u32[]{:S(2)}, u32[]{:S(2)}) collective-permute-start(bf16[8,384,384]{2,1,0:T(8,128)(2,1)} %left_far.1), channel_id=1, source_target_pairs={{0,1},{1,0},{2,3},{3,2},{4,5},{5,4},{6,7},{7,6},{8,9},{9,8},{10,11... | collective-permute-start | bytes 7077896 | tf_op jit(solution)/shard_map/ppermute | solution.py:258
  0.5 32.3 %collective-permute-start.6 = (bf16[8,384,384]{2,1,0:T(8,128)(2,1)}, bf16[8,384,384]{2,1,0:T(8,128)(2,1)}, u32[]{:S(2)}, u32[]{:S(2)}) collective-permute-start(bf16[8,384,384]{2,1,0:T(8,128)(2,1)} %right_far.1), channel_id=1, source_target_pairs={{0,1},{1,0},{2,3},{3,2},{4,5},{5,4},{6,7},{7,6},{8,9},{9,8},{10,11... | collective-permute-start | bytes 7077896 | tf_op jit(solution)/shard_map/ppermute | solution.py:258
  7.6 1.4 %copy-start = (bf16[8,384,384]{2,1,0:T(8,128)(2,1)}, bf16[8,384,384]{2,1,0:T(8,128)(2,1)S(1)}, u32[]{:S(2)}) copy-start(bf16[8,384,384]{2,1,0:T(8,128)(2,1)S(1)} %get-tuple-element.15.left) | copy-start | bytes 7077892
  9.0 1.4 %copy-start.2 = (bf16[8,384,384]{2,1,0:T(8,128)(2,1)}, bf16[8,384,384]{2,1,0:T(8,128)(2,1)S(1)}, u32[]{:S(2)}) copy-start(bf16[8,384,384]{2,1,0:T(8,128)(2,1)S(1)} %get-tuple-element.16.right) | copy-start | bytes 7077892
  10.5 1.5 %copy-start.4 = (bf16[8,384,384]{2,1,0:T(8,128)(2,1)}, bf16[8,384,384]{2,1,0:T(8,128)(2,1)S(1)}, u32[]{:S(2)}) copy-start(bf16[8,384,384]{2,1,0:T(8,128)(2,1)S(1)} %get-tuple-element.17.cells) | copy-start | bytes 7077892
  11.9 19.7 %collective-permute-start = (bf16[768,384]{1,0:T(8,128)(2,1)S(1)}, bf16[768,384]{1,0:T(8,128)(2,1)S(1)}, u32[]{:S(2)}, u32[]{:S(2)}) collective-permute-start(bf16[768,384]{1,0:T(8,128)(2,1)S(1)} %get-tuple-element.20), channel_id=1, source_target_pairs={{0,2},{1,3},{2,0},{3,1},{4,6},{5,7},{6,4},{7,5},{8,10},{9,11},{10,... | collective-permute-start | bytes 1769480 | tf_op jit(solution)/shard_map/ppermute | solution.py:258
  14.9 13.3 %collective-permute-start.2 = (s32[8]{0:T(128)S(1)}, s32[8]{0:T(128)S(1)}, u32[]{:S(2)}, u32[]{:S(2)}) collective-permute-start(s32[8]{0:T(128)S(1)} %copy-done.8), channel_id=1, source_target_pairs={{0,1},{1,0},{2,3},{3,2},{4,5},{5,4},{6,7},{7,6},{8,9},{9,8},{10,11... | collective-permute-start | bytes 104 | tf_op jit(solution)/shard_map/ppermute | solution.py:258
  15.9 16.9 %collective-permute-start.7 = (bf16[1,384,384]{2,1,0:T(8,128)(2,1)S(1)}, bf16[1,384,384]{2,1,0:T(8,128)(2,1)S(1)}, u32[]{:S(2)}, u32[]{:S(2)}) collective-permute-start(bf16[1,384,384]{2,1,0:T(8,128)(2,1)S(1)} %constant_dynamic-slice_fusion), channel_id=1, source_target_pairs={{0,4},{1,29},{2,6},{3,31},{4,8},{5,1},{6,10},{7,3},{8,12},{9,5},{1... | collective-permute-start | bytes 884744 | tf_op jit(solution)/shard_map/ppermute | solution.py:270
  17.6 1.7 %copy-start.1 = (bf16[8,384,384]{2,1,0:T(8,128)(2,1)S(1)}, bf16[8,384,384]{2,1,0:T(8,128)(2,1)}, u32[]{:S(2)}) copy-start(bf16[8,384,384]{2,1,0:T(8,128)(2,1)} %copy-done) | copy-start | bytes 7077892
  19.3 1.7 %copy-start.3 = (bf16[8,384,384]{2,1,0:T(8,128)(2,1)S(1)}, bf16[8,384,384]{2,1,0:T(8,128)(2,1)}, u32[]{:S(2)}) copy-start(bf16[8,384,384]{2,1,0:T(8,128)(2,1)} %copy-done.2) | copy-start | bytes 7077892
  21.0 1.7 %copy-start.5 = (bf16[8,384,384]{2,1,0:T(8,128)(2,1)S(1)}, bf16[8,384,384]{2,1,0:T(8,128)(2,1)}, u32[]{:S(2)}) copy-start(bf16[8,384,384]{2,1,0:T(8,128)(2,1)} %copy-done.4) | copy-start | bytes 7077892
  22.6 5.6 %copy-start.6 = (s32[8,8]{1,0:T(8,128)S(1)}, s32[8,8]{1,0:T(8,128)}, u32[]{:S(2)}) copy-start(s32[8,8]{1,0:T(8,128)} %couple.7) | copy-start | bytes 772
  22.6 9.0 %copy-start.7 = (f32[8,8]{1,0:T(8,128)S(1)}, f32[8,8]{1,0:T(8,128)}, u32[]{:S(2)}) copy-start(f32[8,8]{1,0:T(8,128)} %amplitude.7) | copy-start | bytes 772
  28.3 4.2 %collective-permute-start.3 = (s32[8,8]{1,0:T(8,128)S(1)}, s32[8,8]{1,0:T(8,128)S(1)}, u32[]{:S(2)}, u32[]{:S(2)}) collective-permute-start(s32[8,8]{1,0:T(8,128)S(1)} %copy-done.6), channel_id=1, source_target_pairs={{0,1},{1,0},{2,3},{3,2},{4,5},{5,4},{6,7},{7,6},{8,9},{9,8},{10,11... | collective-permute-start | bytes 776 | tf_op jit(solution)/shard_map/ppermute | solution.py:258
  31.6 1.2 %collective-permute-start.4 = (f32[8,8]{1,0:T(8,128)S(1)}, f32[8,8]{1,0:T(8,128)S(1)}, u32[]{:S(2)}, u32[]{:S(2)}) collective-permute-start(f32[8,8]{1,0:T(8,128)S(1)} %copy-done.7), channel_id=1, source_target_pairs={{0,1},{1,0},{2,3},{3,2},{4,5},{5,4},{6,7},{7,6},{8,9},{9,8},{10,11... | collective-permute-start | bytes 776 | tf_op jit(solution)/shard_map/ppermute | solution.py:258
  32.5 16.9 %collective-permute-start.1 = (f32[384,384]{1,0:T(8,128)S(1)}, f32[384,384]{1,0:T(8,128)S(1)}, u32[]{:S(2)}, u32[]{:S(2)}) collective-permute-start(f32[384,384]{1,0:T(8,128)S(1)} %convert_add_fusion), channel_id=1, source_target_pairs={{0,1},{1,0},{2,3},{3,2},{4,5},{5,4},{6,7},{7,6},{8,9},{9,8},{10,11... | collective-permute-start | bytes 1769480 | tf_op jit(solution)/shard_map/ppermute | solution.py:258
  40.0 9.2 %collective-permute-start.8 = (bf16[384,384]{1,0:T(8,128)(2,1)S(1)}, bf16[384,384]{1,0:T(8,128)(2,1)S(1)}, u32[]{:S(2)}, u32[]{:S(2)}) collective-permute-start(bf16[384,384]{1,0:T(8,128)(2,1)S(1)} %get-tuple-element.23), channel_id=1, source_target_pairs={{0,2},{1,3},{2,0},{3,1},{4,6},{5,7},{6,4},{7,5},{8,10},{9,11},{10,... | collective-permute-start | bytes 884744 | tf_op jit(solution)/shard_map/ppermute | solution.py:258
  49.2 1.6 %collective-permute-start.9 = (f32[192,384]{1,0:T(8,128)S(1)}, f32[192,384]{1,0:T(8,128)S(1)}, u32[]{:S(2)}, u32[]{:S(2)}) collective-permute-start(f32[192,384]{1,0:T(8,128)S(1)} %convert_add_fusion.1), channel_id=1, source_target_pairs={{0,1},{1,0},{2,3},{3,2},{4,5},{5,4},{6,7},{7,6},{8,9},{9,8},{10,11... | collective-permute-start | bytes 884744 | tf_op jit(solution)/shard_map/ppermute | solution.py:258

commit v7 on v6

--- a/solution.py
+++ b/solution.py
@@ -132,9 +132,10 @@
         begin(amplitude, amplitude_here, small_sem.at[2]),
     ]
     first = [cell(s) for s in inside]
-    lefts = [begin(*rows(k, 1 - chip), left_sem.at[0, k]) for k in range(operators)]
+    lefts = [begin(*rows(k, 1 - chip), left_sem.at[0, k]) for k in range(AHEAD)]
     for copy in small:
         copy.wait()
+    lefts += [begin(*rows(k, 1 - chip), left_sem.at[0, k]) for k in range(AHEAD, operators)]
     for copy in first + lefts[:AHEAD]:
         copy.wait()
     rights = [begin(right_far.at[k], right.at[k], right_sem.at[k]) for k in range(operators)]
@@ -212,11 +213,12 @@
     edge_products(groups, sources, middles, (keep, send), sectors, chip, core)
 
 
-def sum_kernel(inner_own, inner_chip, inner_far, near_own, edge_far, other, sigma):
+def sum_kernel(inner_own, inner_chip, inner_far, passed_on, near_own, edge_far, other, sigma):
     core = lax.axis_index("op") & (CORES - 1)
     sectors = sigma.shape[0]
     far = sectors - EDGE
-    sigma[EDGE:far] = inner_own[...] + inner_chip[...] + inner_far[: far - EDGE].astype(jnp.float32)
+    received = inner_far[: far - EDGE].astype(jnp.float32) + passed_on[...].astype(jnp.float32)
+    sigma[EDGE:far] = inner_own[...] + inner_chip[...] + received
     sigma[pl.ds(far * core, EDGE)] = near_own[...] + edge_far[:EDGE].astype(jnp.float32)
     sigma[pl.ds(far * (1 - core), EDGE)] = other[...]
 
@@ -327,7 +329,7 @@
         [BLOCK, BLOCK],
         [],
     )
-    inner_chip = over_op(inner_send + inner_far[inner * half :].astype(wide), 1)
+    inner_chip = over_op(inner_send, 1)
     edge_wide = shape(EDGE * half, states)
     near_own, near_mate = run(
         edge_own_kernel,
@@ -340,7 +342,8 @@
         [],
     )
     other = over_op(near_mate + edge_far[EDGE * half :].astype(wide), 1)
-    parts = (inner_own, inner_chip, inner_far, near_own, edge_far, other)
+    passed_on = over_op(inner_far[inner * half :], 1)
+    parts = (inner_own, inner_chip, inner_far, passed_on, near_own, edge_far, other)
     return pl.pallas_call(
         sum_kernel,
         out_shape=shape(sectors, half, states),

time: 52.4 us -> 62.7 us (1.20)
  waiting for transfers between devices: 3.95 us -> 14.2 us
    ppermute x9 -> x10, waiting for transfers between devices: 3.95 us -> 14.2 us  [over_op(): return lax.ppermute(value, 'op', [(i, i ^ flip) for i in range(op)])]
    ppermute x9 -> x10, starting transfers between devices: 7.96 us -> 8.18 us  [over_op(): return lax.ppermute(value, 'op', [(i, i ^ flip) for i in range(op)])]
    unnamed x18 -> x16, local copies, waits for them, and re-layouts: 9.36 us -> 9.36 us
  transfers between devices with their start and end apart: 10 -> 11, of which waited for: 3 -> 3; matrix products, arithmetic and copies ran while one was open for 2% -> 2% of each run, Pallas kernels for 51% -> 43%
where the time goes in v7:
time: 62.7 us; the launch traced here: 62.3 us
  Pallas kernels  27.7 us (44%)
  waiting for transfers between devices  14.2 us (23%)
  local copies, waits for them, and re-layouts  10.4 us (17%)
  starting transfers between devices  9.88 us (16%)
    pallas_call x4, Pallas kernels, run(): pl.pallas_call(kernel, out_shape=outs, in_specs=in_specs, out_specs=out_s...  26.5 us
    ppermute x10, waiting for transfers between devices, over_op(): return lax.ppermute(value, 'op', [(i, i ^ flip) for i in range(op)])  14.2 us
    unnamed x16, local copies, waits for them, and re-layouts  9.36 us
    ppermute x10, starting transfers between devices, over_op(): return lax.ppermute(value, 'op', [(i, i ^ flip) for i in range(op)])  8.18 us
    ppermute x1, starting transfers between devices, shards(): halo = lax.ppermute(border, ('sec', 'op'), ring)  1.71 us
  transfers between devices with their start and end apart: 11, of which 3 were waited for; matrix products, arithmetic and copies ran while one was open for 2% of the time, Pallas kernels for 43%

profile of v7, /device:TPU:0, one launch (start us, length us, event | category | flops | bytes accessed | tf_op | source)
XLA Modules:
  0.0 62.3 jit_solution(1938185064883930021)
XLA Ops:
  0.0 0.0 copy-start.6
  0.0 0.0 copy-start.7
  0.0 0.5 collective-permute-start.6
  0.5 0.1 collective-permute-start.7
  0.6 6.8 %shard_map.64 = (bf16[768,384]{1,0:T(8,128)(2,1)S(1)}, bf16[8,384,384]{2,1,0:T(8,128)(2,1)S(1)}, bf16[8,384,384]{2,1,0:T(8,128)(2,1)S(1)}, bf16[8,384,384]{2,1,0:T(8,128)(2,1)S(1)}) custom-call(s32[8]{0:T(128)} %charge.7, s32[8,8]{1,0:T(8,128)} %couple.7, f32[8,8]{1,0:T(8,128)} %amplitude.7, bf16[8,384,384]{2,1,0:T(8,128)(2,1)} %left_far.1, ...), custom_call_target="tpu_custom_call" | custom-call | flops 3623878656 | bytes 4718592 | tf_op jit(solution)/shard_map/pallas_call | solution.py:245
  7.4 0.0 copy-start
  7.4 1.4 %copy-done = bf16[8,384,384]{2,1,0:T(8,128)(2,1)} copy-done((bf16[8,384,384]{2,1,0:T(8,128)(2,1)}, bf16[8,384,384]{2,1,0:T(8,128)(2,1)S(1)}, u32[]{:S(2)}) %copy-start) | copy-done | bytes 2359320
  8.8 0.0 copy-start.2
  8.8 1.4 %copy-done.2 = bf16[8,384,384]{2,1,0:T(8,128)(2,1)} copy-done((bf16[8,384,384]{2,1,0:T(8,128)(2,1)}, bf16[8,384,384]{2,1,0:T(8,128)(2,1)S(1)}, u32[]{:S(2)}) %copy-start.2) | copy-done | bytes 2359320
  10.3 0.0 copy-start.4
  10.3 1.5 %copy-done.4 = bf16[8,384,384]{2,1,0:T(8,128)(2,1)} copy-done((bf16[8,384,384]{2,1,0:T(8,128)(2,1)}, bf16[8,384,384]{2,1,0:T(8,128)(2,1)S(1)}, u32[]{:S(2)}) %copy-start.4) | copy-done | bytes 2359320
  11.7 2.9 %collective-permute-start.1 = (bf16[768,384]{1,0:T(8,128)(2,1)S(1)}, bf16[768,384]{1,0:T(8,128)(2,1)S(1)}, u32[]{:S(2)}, u32[]{:S(2)}) collective-permute-start(bf16[768,384]{1,0:T(8,128)(2,1)S(1)} %get-tuple-element.20), channel_id=1, source_target_pairs={{0,2},{1,3},{2,0},{3,1},{4,6},{5,7},{6,4},{7,5},{8,10},{9,11},{10,... | collective-permute-start | bytes 1769480 | tf_op jit(solution)/shard_map/ppermute | solution.py:260
  14.7 0.0 copy-done.6
  14.7 0.0 collective-permute-start.4
  14.7 0.5 collective-permute-start.3
  15.2 1.0 %constant_dynamic-slice_fusion = bf16[1,384,384]{2,1,0:T(8,128)(2,1)S(1)} fusion(bf16[8,384,384]{2,1,0:T(8,128)(2,1)} %cells_far.1, s32[]{:T(128)S(6)} %select_n.3), kind=kLoop, calls=%fused_computation.1 | loop fusion | bytes 589828 | tf_op jit(solution)/shard_map/dynamic_slice | solution.py:271
  16.2 0.0 collective-permute-done.3.charge_in
  16.2 0.0 copy-done.7
  16.2 0.3 collective-permute-start.5
  16.5 11.8 %collective-permute-done.1 = bf16[768,384]{1,0:T(8,128)(2,1)S(1)} collective-permute-done((bf16[768,384]{1,0:T(8,128)(2,1)S(1)}, bf16[768,384]{1,0:T(8,128)(2,1)S(1)}, u32[]{:S(2)}, u32[]{:S(2)}) %collective-permute-start.1) | collective-permute-done | bytes 589856 | tf_op jit(solution)/shard_map/ppermute | solution.py:260
  28.3 1.7 %collective-permute-start.8 = (bf16[1,384,384]{2,1,0:T(8,128)(2,1)S(1)}, bf16[1,384,384]{2,1,0:T(8,128)(2,1)S(1)}, u32[]{:S(2)}, u32[]{:S(2)}) collective-permute-start(bf16[1,384,384]{2,1,0:T(8,128)(2,1)S(1)} %constant_dynamic-slice_fusion), channel_id=1, source_target_pairs={{0,4},{1,29},{2,6},{3,31},{4,8},{5,1},{6,10},{7,3},{8,12},{9,5},{1... | collective-permute-start | bytes 884744 | tf_op jit(solution)/shard_map/ppermute | solution.py:272
  30.0 0.0 copy-start.1
  30.0 1.7 %copy-done.1 = bf16[8,384,384]{2,1,0:T(8,128)(2,1)S(1)} copy-done((bf16[8,384,384]{2,1,0:T(8,128)(2,1)S(1)}, bf16[8,384,384]{2,1,0:T(8,128)(2,1)}, u32[]{:S(2)}) %copy-start.1) | copy-done | bytes 2359320
  31.7 0.0 copy-start.3
  31.7 1.7 %copy-done.3 = bf16[8,384,384]{2,1,0:T(8,128)(2,1)S(1)} copy-done((bf16[8,384,384]{2,1,0:T(8,128)(2,1)S(1)}, bf16[8,384,384]{2,1,0:T(8,128)(2,1)}, u32[]{:S(2)}) %copy-start.3) | copy-done | bytes 2359320
  33.3 0.0 copy-start.5
  33.3 1.7 %copy-done.5 = bf16[8,384,384]{2,1,0:T(8,128)(2,1)S(1)} copy-done((bf16[8,384,384]{2,1,0:T(8,128)(2,1)S(1)}, bf16[8,384,384]{2,1,0:T(8,128)(2,1)}, u32[]{:S(2)}) %copy-start.5) | copy-done | bytes 2359320
  35.0 5.5 %shard_map.65 = (f32[384,384]{1,0:T(8,128)S(1)}, f32[384,384]{1,0:T(8,128)S(1)}) custom-call(s32[8]{0:T(128)} %charge.7, s32[8,8]{1,0:T(8,128)} %couple.7, f32[8,8]{1,0:T(8,128)} %amplitude.7, bf16[8,384,384]{2,1,0:T(8,128)(2,1)S(1)} %copy-done.1, bf16[8,384,384]{2,1,0:T(8,128)(2,1)S(1)} %copy-done.3, bf16[8,384,384]{2,1,0:T(8,128)(2,1)S(1)} %copy-done.5), custom_call_target="tpu_custom_call" | custom-call | flops 3623878656 | bytes 4718592 | tf_op jit(solution)/shard_map/pallas_call | solution.py:245
  40.6 0.0 collective-permute-done.4.couple_in
  40.6 2.1 %collective-permute-start = (f32[384,384]{1,0:T(8,128)S(1)}, f32[384,384]{1,0:T(8,128)S(1)}, u32[]{:S(2)}, u32[]{:S(2)}) collective-permute-start(f32[384,384]{1,0:T(8,128)S(1)} %get-tuple-element.19), channel_id=1, source_target_pairs={{0,1},{1,0},{2,3},{3,2},{4,5},{5,4},{6,7},{7,6},{8,9},{9,8},{10,11... | collective-permute-start | bytes 1769480 | tf_op jit(solution)/shard_map/ppermute | solution.py:260
  42.7 0.0 collective-permute-done.5.amplitude_in
  42.7 0.1 collective-permute-start.2
  42.8 0.0 collective-permute-done.8.halo
  42.8 0.0 collective-permute-done.6.left_in
  42.8 0.0 collective-permute-done.7.right_in
  42.8 7.2 %shard_map.66 = (bf16[384,384]{1,0:T(8,128)(2,1)S(1)}, bf16[4,384,384]{2,1,0:T(8,128)(2,1)S(1)}) custom-call(s32[8]{0:T(128)} %charge.7, s32[8,8]{1,0:T(8,128)} %couple.7, f32[8,8]{1,0:T(8,128)} %amplitude.7, s32[8]{0:T(128)S(1)} %collective-permute-done.3.charge_in, s32[8,8]{1,0:T(8,128)S(1)} %collective-permute-done.4.couple_in, ...), custom_call_target="tpu_custom_call" | custom-call | flops 3623878656 | bytes 9437184 | tf_op jit(solution)/shard_map/pallas_call | solution.py:245
  50.0 1.6 %collective-permute-start.9 = (bf16[384,384]{1,0:T(8,128)(2,1)S(1)}, bf16[384,384]{1,0:T(8,128)(2,1)S(1)}, u32[]{:S(2)}, u32[]{:S(2)}) collective-permute-start(bf16[384,384]{1,0:T(8,128)(2,1)S(1)} %get-tuple-element.23), channel_id=1, source_target_pairs={{0,2},{1,3},{2,0},{3,1},{4,6},{5,7},{6,4},{7,5},{8,10},{9,11},{10,... | collective-permute-start | bytes 884744 | tf_op jit(solution)/shard_map/ppermute | solution.py:260
  51.6 7.0 %shard_map.67 = (f32[192,384]{1,0:T(8,128)S(1)}, f32[192,384]{1,0:T(8,128)S(1)}) custom-call(s32[8]{0:T(128)} %charge.7, s32[8,8]{1,0:T(8,128)} %couple.7, f32[8,8]{1,0:T(8,128)} %amplitude.7, s32[8]{0:T(128)S(1)} %collective-permute-done.3.charge_in, s32[8,8]{1,0:T(8,128)S(1)} %collective-permute-done.4.couple_in, ...), custom_call_target="tpu_custom_call" | custom-call | flops 3623878656 | bytes 9437184 | tf_op jit(solution)/shard_map/pallas_call | solution.py:245
  58.6 0.8 %collective-permute-done.9 = bf16[384,384]{1,0:T(8,128)(2,1)S(1)} collective-permute-done((bf16[384,384]{1,0:T(8,128)(2,1)S(1)}, bf16[384,384]{1,0:T(8,128)(2,1)S(1)}, u32[]{:S(2)}, u32[]{:S(2)}) %collective-permute-start.9) | collective-permute-done | bytes 294944 | tf_op jit(solution)/shard_map/ppermute | solution.py:260
  59.5 0.1 collective-permute-start.10
  59.6 0.0 collective-permute-done
  59.6 0.0 collective-permute-done.2
  59.6 1.5 %collective-permute-done.10 = f32[192,384]{1,0:T(8,128)S(1)} collective-permute-done((f32[192,384]{1,0:T(8,128)S(1)}, f32[192,384]{1,0:T(8,128)S(1)}, u32[]{:S(2)}, u32[]{:S(2)}) %collective-permute-start.10) | collective-permute-done | bytes 294944 | tf_op jit(solution)/shard_map/ppermute | solution.py:260
  61.1 1.2 %total.1 = f32[8,96,384]{2,1,0:T(8,128)} custom-call(f32[4,96,384]{2,1,0:T(8,128)S(1)} %bitcast.9, f32[4,96,384]{2,1,0:T(8,128)S(1)} %bitcast.10, bf16[8,96,384]{2,1,0:T(8,128)(2,1)S(1)} %bitcast.7, bf16[4,96,384]{2,1,0:T(8,128)(2,1)S(1)} %bitcast.11, f32[2,96,384]{2,1,0:T(8,128)S(1)} %bitcast.12, bf16[4,96,384]{2,1,0:T(8,128)(2,1)S(1)} %bitcast.8, ...), custom_call_target="tpu_custom_call" | custom-call | tf_op jit(solution)/shard_map/total/pallas_call | solution.py:347
  (2 shorter events, 0.1 us)
Async XLA Ops:
  0.0 14.7 %copy-start.6 = (s32[8,8]{1,0:T(8,128)S(1)}, s32[8,8]{1,0:T(8,128)}, u32[]{:S(2)}) copy-start(s32[8,8]{1,0:T(8,128)} %couple.7) | copy-start | bytes 772
  0.0 16.2 %copy-start.7 = (f32[8,8]{1,0:T(8,128)S(1)}, f32[8,8]{1,0:T(8,128)}, u32[]{:S(2)}) copy-start(f32[8,8]{1,0:T(8,128)} %amplitude.7) | copy-start | bytes 772
  0.0 42.8 %collective-permute-start.6 = (bf16[8,384,384]{2,1,0:T(8,128)(2,1)}, bf16[8,384,384]{2,1,0:T(8,128)(2,1)S(1)}, u32[]{:S(2)}, u32[]{:S(2)}) collective-permute-start(bf16[8,384,384]{2,1,0:T(8,128)(2,1)} %left_far.1), channel_id=1, source_target_pairs={{0,1},{1,0},{2,3},{3,2},{4,5},{5,4},{6,7},{7,6},{8,9},{9,8},{10,11... | collective-permute-start | bytes 7077896 | tf_op jit(solution)/shard_map/ppermute | solution.py:260
  0.5 42.3 %collective-permute-start.7 = (bf16[8,384,384]{2,1,0:T(8,128)(2,1)}, bf16[8,384,384]{2,1,0:T(8,128)(2,1)}, u32[]{:S(2)}, u32[]{:S(2)}) collective-permute-start(bf16[8,384,384]{2,1,0:T(8,128)(2,1)} %right_far.1), channel_id=1, source_target_pairs={{0,1},{1,0},{2,3},{3,2},{4,5},{5,4},{6,7},{7,6},{8,9},{9,8},{10,11... | collective-permute-start | bytes 7077896 | tf_op jit(solution)/shard_map/ppermute | solution.py:260
  7.4 1.4 %copy-start = (bf16[8,384,384]{2,1,0:T(8,128)(2,1)}, bf16[8,384,384]{2,1,0:T(8,128)(2,1)S(1)}, u32[]{:S(2)}) copy-start(bf16[8,384,384]{2,1,0:T(8,128)(2,1)S(1)} %get-tuple-element.15.left) | copy-start | bytes 7077892
  8.8 1.4 %copy-start.2 = (bf16[8,384,384]{2,1,0:T(8,128)(2,1)}, bf16[8,384,384]{2,1,0:T(8,128)(2,1)S(1)}, u32[]{:S(2)}) copy-start(bf16[8,384,384]{2,1,0:T(8,128)(2,1)S(1)} %get-tuple-element.16.right) | copy-start | bytes 7077892
  10.3 1.5 %copy-start.4 = (bf16[8,384,384]{2,1,0:T(8,128)(2,1)}, bf16[8,384,384]{2,1,0:T(8,128)(2,1)S(1)}, u32[]{:S(2)}) copy-start(bf16[8,384,384]{2,1,0:T(8,128)(2,1)S(1)} %get-tuple-element.17.cells) | copy-start | bytes 7077892
  11.7 16.6 %collective-permute-start.1 = (bf16[768,384]{1,0:T(8,128)(2,1)S(1)}, bf16[768,384]{1,0:T(8,128)(2,1)S(1)}, u32[]{:S(2)}, u32[]{:S(2)}) collective-permute-start(bf16[768,384]{1,0:T(8,128)(2,1)S(1)} %get-tuple-element.20), channel_id=1, source_target_pairs={{0,2},{1,3},{2,0},{3,1},{4,6},{5,7},{6,4},{7,5},{8,10},{9,11},{10,... | collective-permute-start | bytes 1769480 | tf_op jit(solution)/shard_map/ppermute | solution.py:260
  14.7 25.9 %collective-permute-start.4 = (s32[8,8]{1,0:T(8,128)S(1)}, s32[8,8]{1,0:T(8,128)S(1)}, u32[]{:S(2)}, u32[]{:S(2)}) collective-permute-start(s32[8,8]{1,0:T(8,128)S(1)} %copy-done.6), channel_id=1, source_target_pairs={{0,1},{1,0},{2,3},{3,2},{4,5},{5,4},{6,7},{7,6},{8,9},{9,8},{10,11... | collective-permute-start | bytes 776 | tf_op jit(solution)/shard_map/ppermute | solution.py:260
  14.7 1.5 %collective-permute-start.3 = (s32[8]{0:T(128)}, s32[8]{0:T(128)S(1)}, u32[]{:S(2)}, u32[]{:S(2)}) collective-permute-start(s32[8]{0:T(128)} %charge.7), channel_id=1, source_target_pairs={{0,1},{1,0},{2,3},{3,2},{4,5},{5,4},{6,7},{7,6},{8,9},{9,8},{10,11... | collective-permute-start | bytes 104 | tf_op jit(solution)/shard_map/ppermute | solution.py:260
  16.2 26.5 %collective-permute-start.5 = (f32[8,8]{1,0:T(8,128)S(1)}, f32[8,8]{1,0:T(8,128)S(1)}, u32[]{:S(2)}, u32[]{:S(2)}) collective-permute-start(f32[8,8]{1,0:T(8,128)S(1)} %copy-done.7), channel_id=1, source_target_pairs={{0,1},{1,0},{2,3},{3,2},{4,5},{5,4},{6,7},{7,6},{8,9},{9,8},{10,11... | collective-permute-start | bytes 776 | tf_op jit(solution)/shard_map/ppermute | solution.py:260
  28.3 14.5 %collective-permute-start.8 = (bf16[1,384,384]{2,1,0:T(8,128)(2,1)S(1)}, bf16[1,384,384]{2,1,0:T(8,128)(2,1)S(1)}, u32[]{:S(2)}, u32[]{:S(2)}) collective-permute-start(bf16[1,384,384]{2,1,0:T(8,128)(2,1)S(1)} %constant_dynamic-slice_fusion), channel_id=1, source_target_pairs={{0,4},{1,29},{2,6},{3,31},{4,8},{5,1},{6,10},{7,3},{8,12},{9,5},{1... | collective-permute-start | bytes 884744 | tf_op jit(solution)/shard_map/ppermute | solution.py:272
  30.0 1.7 %copy-start.1 = (bf16[8,384,384]{2,1,0:T(8,128)(2,1)S(1)}, bf16[8,384,384]{2,1,0:T(8,128)(2,1)}, u32[]{:S(2)}) copy-start(bf16[8,384,384]{2,1,0:T(8,128)(2,1)} %copy-done) | copy-start | bytes 7077892
  31.7 1.7 %copy-start.3 = (bf16[8,384,384]{2,1,0:T(8,128)(2,1)S(1)}, bf16[8,384,384]{2,1,0:T(8,128)(2,1)}, u32[]{:S(2)}) copy-start(bf16[8,384,384]{2,1,0:T(8,128)(2,1)} %copy-done.2) | copy-start | bytes 7077892
  33.3 1.7 %copy-start.5 = (bf16[8,384,384]{2,1,0:T(8,128)(2,1)S(1)}, bf16[8,384,384]{2,1,0:T(8,128)(2,1)}, u32[]{:S(2)}) copy-start(bf16[8,384,384]{2,1,0:T(8,128)(2,1)} %copy-done.4) | copy-start | bytes 7077892
  40.6 19.0 %collective-permute-start = (f32[384,384]{1,0:T(8,128)S(1)}, f32[384,384]{1,0:T(8,128)S(1)}, u32[]{:S(2)}, u32[]{:S(2)}) collective-permute-start(f32[384,384]{1,0:T(8,128)S(1)} %get-tuple-element.19), channel_id=1, source_target_pairs={{0,1},{1,0},{2,3},{3,2},{4,5},{5,4},{6,7},{7,6},{8,9},{9,8},{10,11... | collective-permute-start | bytes 1769480 | tf_op jit(solution)/shard_map/ppermute | solution.py:260
  42.7 16.9 %collective-permute-start.2 = (bf16[384,384]{1,0:T(8,128)(2,1)S(1)}, bf16[384,384]{1,0:T(8,128)(2,1)S(1)}, u32[]{:S(2)}, u32[]{:S(2)}) collective-permute-start(bf16[384,384]{1,0:T(8,128)(2,1)S(1)} %slice.8), channel_id=1, source_target_pairs={{0,1},{1,0},{2,3},{3,2},{4,5},{5,4},{6,7},{7,6},{8,9},{9,8},{10,11... | collective-permute-start | bytes 884744 | tf_op jit(solution)/shard_map/ppermute | solution.py:260
  50.0 9.4 %collective-permute-start.9 = (bf16[384,384]{1,0:T(8,128)(2,1)S(1)}, bf16[384,384]{1,0:T(8,128)(2,1)S(1)}, u32[]{:S(2)}, u32[]{:S(2)}) collective-permute-start(bf16[384,384]{1,0:T(8,128)(2,1)S(1)} %get-tuple-element.23), channel_id=1, source_target_pairs={{0,2},{1,3},{2,0},{3,1},{4,6},{5,7},{6,4},{7,5},{8,10},{9,11},{10,... | collective-permute-start | bytes 884744 | tf_op jit(solution)/shard_map/ppermute | solution.py:260
  59.5 1.6 %collective-permute-start.10 = (f32[192,384]{1,0:T(8,128)S(1)}, f32[192,384]{1,0:T(8,128)S(1)}, u32[]{:S(2)}, u32[]{:S(2)}) collective-permute-start(f32[192,384]{1,0:T(8,128)S(1)} %convert_add_fusion), channel_id=1, source_target_pairs={{0,1},{1,0},{2,3},{3,2},{4,5},{5,4},{6,7},{7,6},{8,9},{9,8},{10,11... | collective-permute-start | bytes 884744 | tf_op jit(solution)/shard_map/ppermute | solution.py:260

commit v8 on v7

--- a/solution.py
+++ b/solution.py
@@ -73,19 +73,20 @@
 
 
 def summed(right, middles, results):
-    width = middles.shape[0] // CORES
+    count = middles.shape[0]
     step = 256
-    for low in range(0, CORES * width, step):
-        high = min(low + step, CORES * width)
+    for low in range(0, count, step):
+        high = min(low + step, count)
         total = lax.dot_general(
             right, middles[low:high, :], (((1,), (1,)), ((), ())), preferred_element_type=jnp.float32
         ).T
-        for part in range(CORES):
-            begin, end = max(low, part * width), min(high, (part + 1) * width)
-            if begin < end:
-                results[part][begin - part * width : end - part * width, :] = total[
-                    begin - low : end - low, :
-                ].astype(results[part].dtype)
+        first = 0
+        for result in results:
+            last = first + result.shape[0]
+            start, end = max(low, first), min(high, last)
+            if start < end:
+                result[start - first : end - first, :] = total[start - low : end - low, :].astype(result.dtype)
+            first = last
 
 
 def halves(results):
@@ -109,14 +110,15 @@
 
 
 def inner_far_kernel(
-    charge, couple, amplitude, left_far, right_far, cells_far, send, left, right, cells, middles,
+    charge, couple, amplitude, left_far, right_far, cells_far,
+    direct, keep, send, left, right, cells, charge_kept, couple_kept, amplitude_kept, middles,
     charge_here, couple_here, amplitude_here, small_sem, cell_sem, left_sem, right_sem,
 ):
     chip, core = position()
     operators = left.shape[0]
     sectors = cells.shape[0]
     targets = sectors - 2 * EDGE
-    chip_rows = send.shape[0] // targets
+    chip_rows = (direct.shape[0] + keep.shape[0] + send.shape[0]) // targets
     inside = range(EDGE - 1, sectors - EDGE + 1)
 
     def rows(k, place):
@@ -141,6 +143,11 @@
     rights = [begin(right_far.at[k], right.at[k], right_sem.at[k]) for k in range(operators)]
     later = [begin(*rows(k, chip), left_sem.at[1, k]) for k in range(operators)]
     later += [cell(s) for s in range(sectors) if s not in inside]
+    later += [
+        begin(charge, charge_kept, small_sem.at[3]),
+        begin(couple, couple_kept, small_sem.at[4]),
+        begin(amplitude, amplitude_kept, small_sem.at[5]),
+    ]
     sources = cells.at[pl.ds(EDGE - 1, targets + 2)]
     here = (charge_here, couple_here, amplitude_here)
     for k in range(operators):
@@ -150,7 +157,8 @@
         middle_of(k, here, k, left, sources, middles, EDGE, targets, 1 - chip, core)
     for copy in rights:
         copy.wait()
-    summed(jnp.concatenate([right[k] for k in range(operators)], axis=1), middles, halves(send))
+    near, far = halves(direct)
+    summed(jnp.concatenate([right[k] for k in range(operators)], axis=1), middles, (near, keep, far, send))
     for copy in later:
         copy.wait()
 
@@ -213,13 +221,15 @@
     edge_products(groups, sources, middles, (keep, send), sectors, chip, core)
 
 
-def sum_kernel(inner_own, inner_chip, inner_far, passed_on, near_own, edge_far, other, sigma):
+def sum_kernel(inner_own, inner_chip, direct_far, later_far, near_own, other, sigma):
     core = lax.axis_index("op") & (CORES - 1)
     sectors = sigma.shape[0]
     far = sectors - EDGE
-    received = inner_far[: far - EDGE].astype(jnp.float32) + passed_on[...].astype(jnp.float32)
-    sigma[EDGE:far] = inner_own[...] + inner_chip[...] + received
-    sigma[pl.ds(far * core, EDGE)] = near_own[...] + edge_far[:EDGE].astype(jnp.float32)
+    split = EDGE + direct_far.shape[0] // CORES
+    direct = split - EDGE
+    sigma[EDGE:split] = inner_own[:direct] + inner_chip[:direct] + direct_far[:direct].astype(jnp.float32)
+    sigma[split:far] = inner_own[direct:] + inner_chip[direct:] + later_far[CORES * EDGE :].astype(jnp.float32)
+    sigma[pl.ds(far * core, EDGE)] = near_own[...] + later_far[:EDGE].astype(jnp.float32)
     sigma[pl.ds(far * (1 - core), EDGE)] = other[...]
 
 
@@ -279,32 +289,37 @@
     def in_hbm(*values):
         return [pltpu.with_memory_space_constraint(value, pltpu.HBM) for value in values]
 
-    far_send, left, right, cells = run(
+    direct_rows = inner // 2 * half
+    reduced = shape(inner * half - direct_rows, states)
+    direct, keep, send, left, right, cells, *here = run(
         inner_far_kernel,
         operators,
         inner,
         in_hbm(*small, left_ops, right_ops, wavefunction),
         [LARGE] * 6,
         [
-            shape(CORES * inner * half, states, dtype=narrow),
+            shape(CORES * direct_rows, states, dtype=narrow),
+            reduced,
+            reduced,
             pltpu.VMEM(left_ops.shape, narrow),
             pltpu.VMEM(right_ops.shape, narrow),
             pltpu.VMEM(wavefunction.shape, narrow),
+            *[pltpu.VMEM(value.shape, value.dtype) for value in small],
         ],
-        [BLOCK] * 4,
+        [BLOCK] * 9,
         [
             pltpu.SMEM(charge.shape, charge.dtype),
             pltpu.SMEM(couple.shape, couple.dtype),
             pltpu.SMEM(amplitude.shape, amplitude.dtype),
-            pltpu.SemaphoreType.DMA((3,)),
+            pltpu.SemaphoreType.DMA((6,)),
             pltpu.SemaphoreType.DMA((sectors,)),
             pltpu.SemaphoreType.DMA((2, operators)),
             pltpu.SemaphoreType.DMA((operators,)),
         ],
     )
-    inner_far = over_op(far_send, CORES)
-
-    here = in_hbm(*small)
+    direct_far = over_op(direct, CORES)
+    send_in = over_op(send, 1)
+
     held = [*here, *small_in, left, right, left_in, right_in]
     held_specs = [SMALL] * 6 + [BLOCK] * 4
     edge_send, sources = run(
@@ -317,7 +332,8 @@
         [BLOCK, BLOCK],
         [pltpu.SemaphoreType.DMA((2,))],
     )
-    edge_far = over_op(edge_send, CORES)
+    later = jnp.concatenate([edge_send, (keep + send_in).astype(narrow)], axis=0)
+    later_far = over_op(later, CORES)
     block = shape(inner * half, states)
     inner_own, inner_send = run(
         inner_own_kernel,
@@ -329,7 +345,8 @@
         [BLOCK, BLOCK],
         [],
     )
-    inner_chip = over_op(inner_send, 1)
+    mate = inner_send[:direct_rows] + direct_far[direct_rows:].astype(wide)
+    inner_chip = over_op(jnp.concatenate([mate, inner_send[direct_rows:]], axis=0), 1)
     edge_wide = shape(EDGE * half, states)
     near_own, near_mate = run(
         edge_own_kernel,
@@ -341,9 +358,9 @@
         [BLOCK, BLOCK],
         [],
     )
-    other = over_op(near_mate + edge_far[EDGE * half :].astype(wide), 1)
-    passed_on = over_op(inner_far[inner * half :], 1)
-    parts = (inner_own, inner_chip, inner_far, passed_on, near_own, edge_far, other)
+    passed = later_far[EDGE * half : CORES * EDGE * half].astype(wide)
+    other = over_op(near_mate + passed, 1)
+    parts = (inner_own, inner_chip, direct_far, later_far, near_own, other)
     return pl.pallas_call(
         sum_kernel,
         out_shape=shape(sectors, half, states),

time: 62.7 us -> 57.2 us (0.912)
  waiting for transfers between devices: 14.2 us -> 8.55 us
  other arithmetic: 0.03 us -> 1.16 us
  starting transfers between devices: 9.88 us -> 9.01 us
    ppermute x10, waiting for transfers between devices: 14.2 us -> 4.47 us  [over_op(): return lax.ppermute(value, 'op', [(i, i ^ flip) for i in range(op)])]
    ppermute x1, waiting for transfers between devices: 0.01 us -> 4.08 us  [shards(): halo = lax.ppermute(border, ('sec', 'op'), ring)]
    convert_element_type x0 -> x1, other arithmetic: none -> 0.99 us  [shards(): (keep + send_in).astype(narrow)]
    ppermute x10, starting transfers between devices: 8.18 us -> 7.28 us  [over_op(): return lax.ppermute(value, 'op', [(i, i ^ flip) for i in range(op)])]
  transfers between devices with their start and end apart: 11 -> 11, of which waited for: 3 -> 4; matrix products, arithmetic and copies ran while one was open for 2% -> 4% of each run, Pallas kernels for 43% -> 34%
where the time goes in v8:
time: 57.2 us; the launch traced here: 56.8 us
  Pallas kernels  27.6 us (48%)
  local copies, waits for them, and re-layouts  10.3 us (18%)
  starting transfers between devices  9.01 us (16%)
  waiting for transfers between devices  8.55 us (15%)
  other arithmetic  1.16 us (2%)
    pallas_call x4, Pallas kernels, run(): pl.pallas_call(kernel, out_shape=outs, in_specs=in_specs, out_specs=out_s...  26.5 us
    unnamed x16, local copies, waits for them, and re-layouts  9.34 us
    ppermute x10, starting transfers between devices, over_op(): return lax.ppermute(value, 'op', [(i, i ^ flip) for i in range(op)])  7.28 us
    ppermute x10, waiting for transfers between devices, over_op(): return lax.ppermute(value, 'op', [(i, i ^ flip) for i in range(op)])  4.47 us
    ppermute x1, waiting for transfers between devices, shards(): halo = lax.ppermute(border, ('sec', 'op'), ring)  4.08 us
    ppermute x1, starting transfers between devices, shards(): halo = lax.ppermute(border, ('sec', 'op'), ring)  1.73 us
  transfers between devices with their start and end apart: 11, of which 4 were waited for; matrix products, arithmetic and copies ran while one was open for 4% of the time, Pallas kernels for 34%

profile of v8, /device:TPU:0, one launch (start us, length us, event | category | flops | bytes accessed | tf_op | source)
XLA Modules:
  0.0 56.8 jit_solution(6866219389536658657)
XLA Ops:
  0.0 0.5 collective-permute-start.5
  0.5 0.0 collective-permute-start.6
  0.5 0.5 collective-permute-start.2
  1.0 6.9 %shard_map.64 = (bf16[384,384]{1,0:T(8,128)(2,1)S(1)}, f32[192,384]{1,0:T(8,128)S(1)}, f32[192,384]{1,0:T(8,128)S(1)}, bf16[8,384,384]{2,1,0:T(8,128)(2,1)S(1)},...) custom-call(s32[8]{0:T(128)} %charge.1, ...), custom_call_target="tpu_custom_call" | custom-call | flops 3623878656 | bytes 4718592 | tf_op jit(solution)/shard_map/pallas_call | solution.py:255
  7.9 0.0 copy-start
  7.9 1.4 %copy-done = bf16[8,384,384]{2,1,0:T(8,128)(2,1)} copy-done((bf16[8,384,384]{2,1,0:T(8,128)(2,1)}, bf16[8,384,384]{2,1,0:T(8,128)(2,1)S(1)}, u32[]{:S(2)}) %copy-start) | copy-done | bytes 2359320
  9.3 0.0 copy-start.2
  9.3 1.4 %copy-done.2 = bf16[8,384,384]{2,1,0:T(8,128)(2,1)} copy-done((bf16[8,384,384]{2,1,0:T(8,128)(2,1)}, bf16[8,384,384]{2,1,0:T(8,128)(2,1)S(1)}, u32[]{:S(2)}) %copy-start.2) | copy-done | bytes 2359320
  10.8 0.0 copy-start.4
  10.8 1.5 %copy-done.4 = bf16[8,384,384]{2,1,0:T(8,128)(2,1)} copy-done((bf16[8,384,384]{2,1,0:T(8,128)(2,1)}, bf16[8,384,384]{2,1,0:T(8,128)(2,1)S(1)}, u32[]{:S(2)}) %copy-start.4) | copy-done | bytes 2359320
  12.2 0.1 collective-permute-start.8
  12.3 3.0 %collective-permute-start = (bf16[384,384]{1,0:T(8,128)(2,1)S(1)}, bf16[384,384]{1,0:T(8,128)(2,1)S(1)}, u32[]{:S(2)}, u32[]{:S(2)}) collective-permute-start(bf16[384,384]{1,0:T(8,128)(2,1)S(1)} %get-tuple-element.28), channel_id=1, source_target_pairs={{0,2},{1,3},{2,0},{3,1},{4,6},{5,7},{6,4},{7,5},{8,10},{9,11},{10,... | collective-permute-start | bytes 884744 | tf_op jit(solution)/shard_map/ppermute | solution.py:270
  15.3 0.0 copy-start.1
  15.3 1.7 %copy-done.1 = bf16[8,384,384]{2,1,0:T(8,128)(2,1)S(1)} copy-done((bf16[8,384,384]{2,1,0:T(8,128)(2,1)S(1)}, bf16[8,384,384]{2,1,0:T(8,128)(2,1)}, u32[]{:S(2)}) %copy-start.1) | copy-done | bytes 2359320
  17.0 0.0 copy-start.3
  17.0 1.7 %copy-done.3 = bf16[8,384,384]{2,1,0:T(8,128)(2,1)S(1)} copy-done((bf16[8,384,384]{2,1,0:T(8,128)(2,1)S(1)}, bf16[8,384,384]{2,1,0:T(8,128)(2,1)}, u32[]{:S(2)}) %copy-start.3) | copy-done | bytes 2359320
  18.6 0.0 copy-start.5
  18.6 1.7 %copy-done.5 = bf16[8,384,384]{2,1,0:T(8,128)(2,1)S(1)} copy-done((bf16[8,384,384]{2,1,0:T(8,128)(2,1)S(1)}, bf16[8,384,384]{2,1,0:T(8,128)(2,1)}, u32[]{:S(2)}) %copy-start.5) | copy-done | bytes 2359320
  20.3 0.0 copy-start.6
  20.3 0.0 copy-start.7
  20.3 5.3 %shard_map.65 = (f32[384,384]{1,0:T(8,128)S(1)}, f32[384,384]{1,0:T(8,128)S(1)}) custom-call(s32[8]{0:T(128)S(1)} %get-tuple-element.20.charge, s32[8,8]{1,0:T(8,128)S(1)} %get-tuple-element.21.couple, f32[8,8]{1,0:T(8,128)S(1)} %get-tuple-element.22.amplitude, bf16[8,384,384]{2,1,0:T(8,128)(2,1)S(1)} %copy-done.1, bf16[8,384,384]{2,1,0:T(8,128)(2,1)S(1)} %copy-done.3, ...), custom_call_target="tpu_custom_call" | custom-call | flops 3623878656 | bytes 4718592 | tf_op jit(solution)/shard_map/pallas_call | solution.py:255
  25.6 1.0 %constant_dynamic-slice_fusion = bf16[1,384,384]{2,1,0:T(8,128)(2,1)S(1)} fusion(bf16[8,384,384]{2,1,0:T(8,128)(2,1)} %cells_far.1, s32[]{:T(128)S(6)} %select_n.3), kind=kLoop, calls=%fused_computation.5 | loop fusion | bytes 589828 | tf_op jit(solution)/shard_map/dynamic_slice | solution.py:281
  26.6 0.0 collective-permute-done
  26.7 1.7 %collective-permute-start.7 = (bf16[1,384,384]{2,1,0:T(8,128)(2,1)S(1)}, bf16[1,384,384]{2,1,0:T(8,128)(2,1)S(1)}, u32[]{:S(2)}, u32[]{:S(2)}) collective-permute-start(bf16[1,384,384]{2,1,0:T(8,128)(2,1)S(1)} %constant_dynamic-slice_fusion), channel_id=1, source_target_pairs={{0,4},{1,29},{2,6},{3,31},{4,8},{5,1},{6,10},{7,3},{8,12},{9,5},{1... | collective-permute-start | bytes 884744 | tf_op jit(solution)/shard_map/ppermute | solution.py:282
  28.4 0.1 convert_add_fusion.1
  28.4 0.0 collective-permute-done.2.charge_in
  28.5 0.0 copy-done.6
  28.5 2.6 %collective-permute-start.3 = (s32[8,8]{1,0:T(8,128)S(1)}, s32[8,8]{1,0:T(8,128)S(1)}, u32[]{:S(2)}, u32[]{:S(2)}) collective-permute-start(s32[8,8]{1,0:T(8,128)S(1)} %copy-done.6), channel_id=1, source_target_pairs={{0,1},{1,0},{2,3},{3,2},{4,5},{5,4},{6,7},{7,6},{8,9},{9,8},{10,11... | collective-permute-start | bytes 776 | tf_op jit(solution)/shard_map/ppermute | solution.py:270
  31.1 0.0 collective-permute-done.8
  31.1 0.0 copy-done.7
  31.1 0.1 collective-permute-start.4
  31.2 1.0 %add_convert_fusion = bf16[192,384]{1,0:T(8,128)(2,1)S(1)} fusion(f32[192,384]{1,0:T(8,128)S(1)} %get-tuple-element.30, f32[192,384]{1,0:T(8,128)} %collective-permute-done.8), kind=kLoop, calls=%fused_computation.3 | loop fusion | flops 147456 | bytes 737280 | tf_op jit(solution)/shard_map/convert_element_type | solution.py:335
  32.1 0.0 collective-permute-done.3.couple_in
  32.2 0.1 collective-permute-done.4.amplitude_in
  32.2 4.1 %collective-permute-done.7.halo = bf16[1,384,384]{2,1,0:T(8,128)(2,1)S(1)} collective-permute-done((bf16[1,384,384]{2,1,0:T(8,128)(2,1)S(1)}, bf16[1,384,384]{2,1,0:T(8,128)(2,1)S(1)}, u32[]{:S(2)}, u32[]{:S(2)}) %collective-permute-start.7) | collective-permute-done | bytes 294944 | tf_op jit(solution)/shard_map/ppermute | solution.py:282
  36.3 0.0 collective-permute-done.5.left_in
  36.3 0.0 collective-permute-done.6.right_in
  36.3 7.2 %shard_map.66 = (bf16[384,384]{1,0:T(8,128)(2,1)S(1)}, bf16[4,384,384]{2,1,0:T(8,128)(2,1)S(1)}) custom-call(s32[8]{0:T(128)S(1)} %get-tuple-element.20.charge, s32[8,8]{1,0:T(8,128)S(1)} %get-tuple-element.21.couple, f32[8,8]{1,0:T(8,128)S(1)} %get-tuple-element.22.amplitude, s32[8]{0:T(128)S(1)} %collective-permute-done.2.charge_in, ...), custom_call_target="tpu_custom_call" | custom-call | flops 3623878656 | bytes 9437184 | tf_op jit(solution)/shard_map/pallas_call | solution.py:255
  43.6 0.4 collective-permute-start.9
  44.1 0.1 collective-permute-start.1
  44.1 7.0 %shard_map.67 = (f32[192,384]{1,0:T(8,128)S(1)}, f32[192,384]{1,0:T(8,128)S(1)}) custom-call(s32[8]{0:T(128)S(1)} %get-tuple-element.20.charge, s32[8,8]{1,0:T(8,128)S(1)} %get-tuple-element.21.couple, f32[8,8]{1,0:T(8,128)S(1)} %get-tuple-element.22.amplitude, s32[8]{0:T(128)S(1)} %collective-permute-done.2.charge_in, ...), custom_call_target="tpu_custom_call" | custom-call | flops 3623878656 | bytes 9437184 | tf_op jit(solution)/shard_map/pallas_call | solution.py:255
  51.1 2.8 %collective-permute-done.9 = bf16[576,384]{1,0:T(8,128)(2,1)S(1)} collective-permute-done((bf16[576,384]{1,0:T(8,128)(2,1)S(1)}, bf16[576,384]{1,0:T(8,128)(2,1)S(1)}, u32[]{:S(2)}, u32[]{:S(2)}) %collective-permute-start.9) | collective-permute-done | bytes 442400 | tf_op jit(solution)/shard_map/ppermute | solution.py:270
  54.0 0.1 collective-permute-start.10
  54.1 0.0 collective-permute-done.1
  54.1 1.6 %collective-permute-done.10 = f32[192,384]{1,0:T(8,128)S(1)} collective-permute-done((f32[192,384]{1,0:T(8,128)S(1)}, f32[192,384]{1,0:T(8,128)S(1)}, u32[]{:S(2)}, u32[]{:S(2)}) %collective-permute-start.10) | collective-permute-done | bytes 294944 | tf_op jit(solution)/shard_map/ppermute | solution.py:270
  55.6 1.1 %total.1 = f32[8,96,384]{2,1,0:T(8,128)} custom-call(f32[4,96,384]{2,1,0:T(8,128)S(1)} %bitcast.8, f32[4,96,384]{2,1,0:T(8,128)S(1)} %bitcast.9, bf16[4,96,384]{2,1,0:T(8,128)(2,1)S(1)} %bitcast.7, bf16[6,96,384]{2,1,0:T(8,128)(2,1)S(1)} %bitcast.6, f32[2,96,384]{2,1,0:T(8,128)S(1)} %bitcast.10, f32[2,96,384]{2,1,0:T(8,128)S(1)} %bitcast.11), custom_call_target="tpu_custom_call" | custom-call | tf_op jit(solution)/shard_map/total/pallas_call | solution.py:364
  (3 shorter events, 0.1 us)
Async XLA Ops:
  0.0 36.3 %collective-permute-start.5 = (bf16[8,384,384]{2,1,0:T(8,128)(2,1)}, bf16[8,384,384]{2,1,0:T(8,128)(2,1)S(1)}, u32[]{:S(2)}, u32[]{:S(2)}) collective-permute-start(bf16[8,384,384]{2,1,0:T(8,128)(2,1)} %left_far.1), channel_id=1, source_target_pairs={{0,1},{1,0},{2,3},{3,2},{4,5},{5,4},{6,7},{7,6},{8,9},{9,8},{10,11... | collective-permute-start | bytes 7077896 | tf_op jit(solution)/shard_map/ppermute | solution.py:270
  0.5 35.8 %collective-permute-start.6 = (bf16[8,384,384]{2,1,0:T(8,128)(2,1)}, bf16[8,384,384]{2,1,0:T(8,128)(2,1)}, u32[]{:S(2)}, u32[]{:S(2)}) collective-permute-start(bf16[8,384,384]{2,1,0:T(8,128)(2,1)} %right_far.1), channel_id=1, source_target_pairs={{0,1},{1,0},{2,3},{3,2},{4,5},{5,4},{6,7},{7,6},{8,9},{9,8},{10,11... | collective-permute-start | bytes 7077896 | tf_op jit(solution)/shard_map/ppermute | solution.py:270
  0.5 27.9 %collective-permute-start.2 = (s32[8]{0:T(128)}, s32[8]{0:T(128)S(1)}, u32[]{:S(2)}, u32[]{:S(2)}) collective-permute-start(s32[8]{0:T(128)} %charge.1), channel_id=1, source_target_pairs={{0,1},{1,0},{2,3},{3,2},{4,5},{5,4},{6,7},{7,6},{8,9},{9,8},{10,11... | collective-permute-start | bytes 104 | tf_op jit(solution)/shard_map/ppermute | solution.py:270
  7.9 1.4 %copy-start = (bf16[8,384,384]{2,1,0:T(8,128)(2,1)}, bf16[8,384,384]{2,1,0:T(8,128)(2,1)S(1)}, u32[]{:S(2)}) copy-start(bf16[8,384,384]{2,1,0:T(8,128)(2,1)S(1)} %get-tuple-element.23.left) | copy-start | bytes 7077892
  9.3 1.4 %copy-start.2 = (bf16[8,384,384]{2,1,0:T(8,128)(2,1)}, bf16[8,384,384]{2,1,0:T(8,128)(2,1)S(1)}, u32[]{:S(2)}) copy-start(bf16[8,384,384]{2,1,0:T(8,128)(2,1)S(1)} %get-tuple-element.24.right) | copy-start | bytes 7077892
  10.8 1.5 %copy-start.4 = (bf16[8,384,384]{2,1,0:T(8,128)(2,1)}, bf16[8,384,384]{2,1,0:T(8,128)(2,1)S(1)}, u32[]{:S(2)}) copy-start(bf16[8,384,384]{2,1,0:T(8,128)(2,1)S(1)} %get-tuple-element.25.cells) | copy-start | bytes 7077892
  12.2 18.8 %collective-permute-start.8 = (f32[192,384]{1,0:T(8,128)S(1)}, f32[192,384]{1,0:T(8,128)}, u32[]{:S(2)}, u32[]{:S(2)}) collective-permute-start(f32[192,384]{1,0:T(8,128)S(1)} %get-tuple-element.31), channel_id=1, source_target_pairs={{0,1},{1,0},{2,3},{3,2},{4,5},{5,4},{6,7},{7,6},{8,9},{9,8},{10,11... | collective-permute-start | bytes 884744 | tf_op jit(solution)/shard_map/ppermute | solution.py:270
  12.3 14.4 %collective-permute-start = (bf16[384,384]{1,0:T(8,128)(2,1)S(1)}, bf16[384,384]{1,0:T(8,128)(2,1)S(1)}, u32[]{:S(2)}, u32[]{:S(2)}) collective-permute-start(bf16[384,384]{1,0:T(8,128)(2,1)S(1)} %get-tuple-element.28), channel_id=1, source_target_pairs={{0,2},{1,3},{2,0},{3,1},{4,6},{5,7},{6,4},{7,5},{8,10},{9,11},{10,... | collective-permute-start | bytes 884744 | tf_op jit(solution)/shard_map/ppermute | solution.py:270
  15.3 1.7 %copy-start.1 = (bf16[8,384,384]{2,1,0:T(8,128)(2,1)S(1)}, bf16[8,384,384]{2,1,0:T(8,128)(2,1)}, u32[]{:S(2)}) copy-start(bf16[8,384,384]{2,1,0:T(8,128)(2,1)} %copy-done) | copy-start | bytes 7077892
  17.0 1.7 %copy-start.3 = (bf16[8,384,384]{2,1,0:T(8,128)(2,1)S(1)}, bf16[8,384,384]{2,1,0:T(8,128)(2,1)}, u32[]{:S(2)}) copy-start(bf16[8,384,384]{2,1,0:T(8,128)(2,1)} %copy-done.2) | copy-start | bytes 7077892
  18.6 1.7 %copy-start.5 = (bf16[8,384,384]{2,1,0:T(8,128)(2,1)S(1)}, bf16[8,384,384]{2,1,0:T(8,128)(2,1)}, u32[]{:S(2)}) copy-start(bf16[8,384,384]{2,1,0:T(8,128)(2,1)} %copy-done.4) | copy-start | bytes 7077892
  20.3 8.2 %copy-start.6 = (s32[8,8]{1,0:T(8,128)S(1)}, s32[8,8]{1,0:T(8,128)}, u32[]{:S(2)}) copy-start(s32[8,8]{1,0:T(8,128)} %couple.1) | copy-start | bytes 772
  20.3 10.8 %copy-start.7 = (f32[8,8]{1,0:T(8,128)S(1)}, f32[8,8]{1,0:T(8,128)}, u32[]{:S(2)}) copy-start(f32[8,8]{1,0:T(8,128)} %amplitude.1) | copy-start | bytes 772
  26.7 9.7 %collective-permute-start.7 = (bf16[1,384,384]{2,1,0:T(8,128)(2,1)S(1)}, bf16[1,384,384]{2,1,0:T(8,128)(2,1)S(1)}, u32[]{:S(2)}, u32[]{:S(2)}) collective-permute-start(bf16[1,384,384]{2,1,0:T(8,128)(2,1)S(1)} %constant_dynamic-slice_fusion), channel_id=1, source_target_pairs={{0,4},{1,29},{2,6},{3,31},{4,8},{5,1},{6,10},{7,3},{8,12},{9,5},{1... | collective-permute-start | bytes 884744 | tf_op jit(solution)/shard_map/ppermute | solution.py:282
  28.5 3.7 %collective-permute-start.3 = (s32[8,8]{1,0:T(8,128)S(1)}, s32[8,8]{1,0:T(8,128)S(1)}, u32[]{:S(2)}, u32[]{:S(2)}) collective-permute-start(s32[8,8]{1,0:T(8,128)S(1)} %copy-done.6), channel_id=1, source_target_pairs={{0,1},{1,0},{2,3},{3,2},{4,5},{5,4},{6,7},{7,6},{8,9},{9,8},{10,11... | collective-permute-start | bytes 776 | tf_op jit(solution)/shard_map/ppermute | solution.py:270
  31.1 1.2 %collective-permute-start.4 = (f32[8,8]{1,0:T(8,128)S(1)}, f32[8,8]{1,0:T(8,128)S(1)}, u32[]{:S(2)}, u32[]{:S(2)}) collective-permute-start(f32[8,8]{1,0:T(8,128)S(1)} %copy-done.7), channel_id=1, source_target_pairs={{0,1},{1,0},{2,3},{3,2},{4,5},{5,4},{6,7},{7,6},{8,9},{9,8},{10,11... | collective-permute-start | bytes 776 | tf_op jit(solution)/shard_map/ppermute | solution.py:270
  43.6 10.3 %collective-permute-start.9 = (bf16[576,384]{1,0:T(8,128)(2,1)S(1)}, bf16[576,384]{1,0:T(8,128)(2,1)S(1)}, u32[]{:S(2)}, u32[]{:S(2)}) collective-permute-start(bf16[576,384]{1,0:T(8,128)(2,1)S(1)} %pad_maximum_fusion.1), channel_id=1, source_target_pairs={{0,2},{1,3},{2,0},{3,1},{4,6},{5,7},{6,4},{7,5},{8,10},{9,11},{10,... | collective-permute-start | bytes 1327112 | tf_op jit(solution)/shard_map/ppermute | solution.py:270
  44.1 10.0 %collective-permute-start.1 = (f32[384,384]{1,0:T(8,128)S(1)}, f32[384,384]{1,0:T(8,128)S(1)}, u32[]{:S(2)}, u32[]{:S(2)}) collective-permute-start(f32[384,384]{1,0:T(8,128)S(1)} %pad_maximum_fusion), channel_id=1, source_target_pairs={{0,1},{1,0},{2,3},{3,2},{4,5},{5,4},{6,7},{7,6},{8,9},{9,8},{10,11... | collective-permute-start | bytes 1769480 | tf_op jit(solution)/shard_map/ppermute | solution.py:270
  54.0 1.6 %collective-permute-start.10 = (f32[192,384]{1,0:T(8,128)S(1)}, f32[192,384]{1,0:T(8,128)S(1)}, u32[]{:S(2)}, u32[]{:S(2)}) collective-permute-start(f32[192,384]{1,0:T(8,128)S(1)} %convert_add_fusion), channel_id=1, source_target_pairs={{0,1},{1,0},{2,3},{3,2},{4,5},{5,4},{6,7},{7,6},{8,9},{9,8},{10,11... | collective-permute-start | bytes 884744 | tf_op jit(solution)/shard_map/ppermute | solution.py:270

commit v9 on v8

--- a/solution.py
+++ b/solution.py
@@ -52,15 +52,17 @@
     return lax.psum_scatter(accumulated, "op", scatter_dimension=1, tiled=True)
 
 
-def middle_of(k, small, own, left, sources, middles, first_target, targets, chip, core):
+def own_rows(left, own, chip, core, half):
+    return [left[own, pl.ds(row_of(chip, owner, half), half)] for owner in (core, 1 - core)]
+
+
+def middle_of(k, small, own, parts, sources, middles, first_target, targets):
     charge, couple, amplitude = small
     states = sources.shape[-1]
     half = middles.shape[0] // (CORES * targets)
     shift = 1 - charge[own]
     wide = jnp.concatenate([sources[shift + t] for t in range(targets)], axis=1)
-    rows = jnp.concatenate(
-        [left[own, pl.ds(row_of(chip, owner, half), half)] for owner in (core, 1 - core)], axis=0
-    )
+    rows = jnp.concatenate(parts, axis=0)
     middle = jnp.dot(rows, wide, preferred_element_type=jnp.float32)
     for t in range(targets):
         at = first_target + t
@@ -103,58 +105,55 @@
     return pl.multiple_of((chip * CORES + core) * half, 32)
 
 
+def rows_of_chip(ops, chip, rows):
+    return ops.at[pl.ds(pl.multiple_of(chip * rows, 64), rows)]
+
+
 def begin(source, target, sem):
     copy = pltpu.make_async_copy(source, target, sem)
     copy.start()
     return copy
 
 
+def first_kernel(left_far, cells_far, border, head, sem):
+    chip, core = position()
+    copies = [begin(cells_far.at[(cells_far.shape[0] - 1) * (1 - core)], border.at[0], sem.at[0])]
+    for k in range(head.shape[0]):
+        rows = rows_of_chip(left_far.at[k], 1 - chip, head.shape[1])
+        copies.append(begin(rows, head.at[k], sem.at[1 + k]))
+    for copy in copies:
+        copy.wait()
+
+
 def inner_far_kernel(
-    charge, couple, amplitude, left_far, right_far, cells_far,
-    direct, keep, send, left, right, cells, charge_kept, couple_kept, amplitude_kept, middles,
-    charge_here, couple_here, amplitude_here, small_sem, cell_sem, left_sem, right_sem,
+    charge, couple, amplitude, left_far, right_far, cells, head,
+    direct, keep, send, left, right, middles, left_sem, right_sem,
 ):
     chip, core = position()
     operators = left.shape[0]
-    sectors = cells.shape[0]
-    targets = sectors - 2 * EDGE
-    chip_rows = (direct.shape[0] + keep.shape[0] + send.shape[0]) // targets
-    inside = range(EDGE - 1, sectors - EDGE + 1)
-
-    def rows(k, place):
-        at = pl.ds(pl.multiple_of(place * chip_rows, 64), chip_rows)
-        return left_far.at[k, at], left.at[k, at]
-
-    def cell(s):
-        return begin(cells_far.at[s], cells.at[s], cell_sem.at[s])
-
-    small = [
-        begin(charge, charge_here, small_sem.at[0]),
-        begin(couple, couple_here, small_sem.at[1]),
-        begin(amplitude, amplitude_here, small_sem.at[2]),
-    ]
-    first = [cell(s) for s in inside]
-    lefts = [begin(*rows(k, 1 - chip), left_sem.at[0, k]) for k in range(AHEAD)]
-    for copy in small:
-        copy.wait()
-    lefts += [begin(*rows(k, 1 - chip), left_sem.at[0, k]) for k in range(AHEAD, operators)]
-    for copy in first + lefts[:AHEAD]:
-        copy.wait()
+    targets = cells.shape[0] - 2 * EDGE
+    ahead, chip_rows = head.shape[:2]
+    half = chip_rows // CORES
+
+    def rows(k, place, which):
+        origin = rows_of_chip(left_far.at[k], place, chip_rows)
+        return begin(origin, rows_of_chip(left.at[k], place, chip_rows), left_sem.at[which, k])
+
+    lefts = [rows(k, 1 - chip, 0) for k in range(ahead, operators)]
     rights = [begin(right_far.at[k], right.at[k], right_sem.at[k]) for k in range(operators)]
-    later = [begin(*rows(k, chip), left_sem.at[1, k]) for k in range(operators)]
-    later += [cell(s) for s in range(sectors) if s not in inside]
-    later += [
-        begin(charge, charge_kept, small_sem.at[3]),
-        begin(couple, couple_kept, small_sem.at[4]),
-        begin(amplitude, amplitude_kept, small_sem.at[5]),
-    ]
-    sources = cells.at[pl.ds(EDGE - 1, targets + 2)]
-    here = (charge_here, couple_here, amplitude_here)
+    inside = cells.at[pl.ds(EDGE - 1, targets + 2)]
+    later = []
     for k in range(operators):
-        if k == AHEAD:
-            for copy in lefts[AHEAD:]:
-                copy.wait()
-        middle_of(k, here, k, left, sources, middles, EDGE, targets, 1 - chip, core)
+        if k < ahead:
+            parts = [head[k, pl.ds(pl.multiple_of(o * half, 32), half)] for o in (core, 1 - core)]
+        else:
+            if k == ahead:
+                for copy in lefts:
+                    copy.wait()
+                later += [rows(own, 1 - chip, 0) for own in range(ahead)]
+                later += [rows(own, chip, 1) for own in range(operators)]
+            parts = own_rows(left, k, 1 - chip, core, half)
+        middle_of(k, (charge, couple, amplitude), k, parts, inside, middles, EDGE, targets)
     for copy in rights:
         copy.wait()
     near, far = halves(direct)
@@ -168,17 +167,21 @@
     operators = left.shape[0]
     targets = cells.shape[0] - 2 * EDGE
     inside = cells.at[pl.ds(EDGE - 1, targets + 2)]
+    half = keep.shape[0] // targets
     for k in range(operators):
-        middle_of(k, (charge, couple, amplitude), k, left, inside, middles, EDGE, targets, chip, core)
+        parts = own_rows(left, k, chip, core, half)
+        middle_of(k, (charge, couple, amplitude), k, parts, inside, middles, EDGE, targets)
     summed(jnp.concatenate([right[k] for k in range(operators)], axis=1), middles, (keep, send))
 
 
 def edge_products(groups, sources, middles, results, sectors, chip, core):
     k = 0
     first_target = (sectors - EDGE) * core
+    half = middles.shape[0] // (CORES * EDGE)
     for small, left, right in groups:
         for own in range(left.shape[0]):
-            middle_of(k, small, own, left, sources, middles, first_target, EDGE, chip, core)
+            parts = own_rows(left, own, chip, core, half)
+            middle_of(k, small, own, parts, sources, middles, first_target, EDGE)
             k += 1
     wide = jnp.concatenate([right[own] for _, _, right in groups for own in range(right.shape[0])], axis=1)
     summed(wide, middles, results)
@@ -277,56 +280,57 @@
     for s in range(sec):
         for o in range(op):
             ring.append((s * op + o, (s + 1 if o % CORES == 0 else s - 1) % sec * op + o))
-    core = lax.axis_index("op") & (CORES - 1)
-    border = lax.dynamic_slice_in_dim(wavefunction, (sectors - 1) * (1 - core), 1, 0)
+
+    def in_hbm(*values):
+        return [pltpu.with_memory_space_constraint(value, pltpu.HBM) for value in values]
+
+    border, head = pl.pallas_call(
+        first_kernel,
+        out_shape=[
+            pltpu.VMEM((1, states, states), narrow),
+            pltpu.VMEM((AHEAD, CORES * half, states), narrow),
+        ],
+        in_specs=[LARGE] * 2,
+        out_specs=[BLOCK] * 2,
+        scratch_shapes=[pltpu.SemaphoreType.DMA((1 + AHEAD,))],
+        compiler_params=pltpu.CompilerParams(vmem_limit_bytes=4 * MIB),
+        name="first_kernel",
+    )(*in_hbm(left_ops, wavefunction))
     halo = lax.ppermute(border, ("sec", "op"), ring)
+    left_far, right_far = in_hbm(left_ops, right_ops)
     left_in = over_op(left_ops, 1)
     right_in = over_op(right_ops, 1)
-
     small = (charge, couple, amplitude)
     small_in = [over_op(value, 1) for value in small]
 
-    def in_hbm(*values):
-        return [pltpu.with_memory_space_constraint(value, pltpu.HBM) for value in values]
-
     direct_rows = inner // 2 * half
     reduced = shape(inner * half - direct_rows, states)
-    direct, keep, send, left, right, cells, *here = run(
+    direct, keep, send, left, right = run(
         inner_far_kernel,
         operators,
         inner,
-        in_hbm(*small, left_ops, right_ops, wavefunction),
-        [LARGE] * 6,
+        (*small, left_far, right_far, wavefunction, head),
+        [SMALL] * 3 + [LARGE] * 2 + [BLOCK] * 2,
         [
             shape(CORES * direct_rows, states, dtype=narrow),
             reduced,
             reduced,
             pltpu.VMEM(left_ops.shape, narrow),
             pltpu.VMEM(right_ops.shape, narrow),
-            pltpu.VMEM(wavefunction.shape, narrow),
-            *[pltpu.VMEM(value.shape, value.dtype) for value in small],
         ],
-        [BLOCK] * 9,
-        [
-            pltpu.SMEM(charge.shape, charge.dtype),
-            pltpu.SMEM(couple.shape, couple.dtype),
-            pltpu.SMEM(amplitude.shape, amplitude.dtype),
-            pltpu.SemaphoreType.DMA((6,)),
-            pltpu.SemaphoreType.DMA((sectors,)),
-            pltpu.SemaphoreType.DMA((2, operators)),
-            pltpu.SemaphoreType.DMA((operators,)),
-        ],
+        [BLOCK] * 5,
+        [pltpu.SemaphoreType.DMA((2, operators)), pltpu.SemaphoreType.DMA((operators,))],
     )
     direct_far = over_op(direct, CORES)
     send_in = over_op(send, 1)
 
-    held = [*here, *small_in, left, right, left_in, right_in]
+    held = [*small, *small_in, left, right, left_in, right_in]
     held_specs = [SMALL] * 6 + [BLOCK] * 4
     edge_send, sources = run(
         edge_far_kernel,
         CORES * operators,
         EDGE,
-        held + [cells, halo],
+        held + [wavefunction, halo],
         held_specs + [BLOCK, BLOCK],
         [shape(CORES * EDGE * half, states, dtype=narrow), shape(EDGE + 2, states, states, dtype=narrow)],
         [BLOCK, BLOCK],
@@ -339,7 +343,7 @@
         inner_own_kernel,
         operators,
         inner,
-        [*here, left, right, cells],
+        [*small, left, right, wavefunction],
         [SMALL] * 3 + [BLOCK] * 3,
         [block, block],
         [BLOCK, BLOCK],

time: 57.2 us -> 49.2 us (0.86)
  local copies, waits for them, and re-layouts: 10.3 us -> 0.01 us
  waiting for transfers between devices: 8.55 us -> 11.2 us
  starting transfers between devices: 9.01 us -> 9.96 us
  other arithmetic: 1.16 us -> 0.21 us
    unnamed x16 -> x8, local copies, waits for them, and re-layouts: 9.34 us -> 0.01 us
    ppermute x10, waiting for transfers between devices: 4.47 us -> 7.08 us  [over_op(): return lax.ppermute(value, 'op', [(i, i ^ flip) for i in range(op)])]
    pallas_call x4, Pallas kernels: 26.5 us -> 25.3 us  [run(): pl.pallas_call(kernel, out_shape=outs, in_specs=in_specs, out_specs=out_s...]
    pallas_call x0 -> x1, Pallas kernels: none -> 1.09 us  [shards(): pl.pallas_call(first_kernel, out_shape=[pltpu.VMEM((1, states, states), n...]
    dynamic_slice x1 -> x0, local copies, waits for them, and re-layouts: 1 us -> none  [shards(): lax.dynamic_slice_in_dim(wavefunction, (sectors - 1) * (1 - core), 1, 0)]
    ppermute x10, starting transfers between devices: 7.28 us -> 8.25 us  [over_op(): return lax.ppermute(value, 'op', [(i, i ^ flip) for i in range(op)])]
    convert_element_type x1, other arithmetic: 0.99 us -> 0.04 us  [shards(): (keep + send_in).astype(narrow)]
  transfers between devices with their start and end apart: 11 -> 11, of which waited for: 4 -> 6; matrix products, arithmetic and copies ran while one was open for 4% -> 0% of each run, Pallas kernels for 34% -> 41%
where the time goes in v9:
time: 49.2 us; the launch traced here: 49.1 us
  Pallas kernels  27.5 us (56%)
  waiting for transfers between devices  11.2 us (23%)
  starting transfers between devices  9.96 us (20%)
    pallas_call x4, Pallas kernels, run(): pl.pallas_call(kernel, out_shape=outs, in_specs=in_specs, out_specs=out_s...  25.3 us
    ppermute x10, starting transfers between devices, over_op(): return lax.ppermute(value, 'op', [(i, i ^ flip) for i in range(op)])  8.25 us
    ppermute x10, waiting for transfers between devices, over_op(): return lax.ppermute(value, 'op', [(i, i ^ flip) for i in range(op)])  7.08 us
    ppermute x1, waiting for transfers between devices, shards(): halo = lax.ppermute(border, ('sec', 'op'), ring)  4.16 us
    ppermute x1, starting transfers between devices, shards(): halo = lax.ppermute(border, ('sec', 'op'), ring)  1.71 us
    pallas_call x1, Pallas kernels, shards(): pl.pallas_call(sum_kernel, out_shape=shape(sectors, half, states), in_spe...  1.13 us
    pallas_call x1, Pallas kernels, shards(): pl.pallas_call(first_kernel, out_shape=[pltpu.VMEM((1, states, states), n...  1.09 us
  transfers between devices with their start and end apart: 11, of which 6 were waited for; matrix products, arithmetic and copies ran while one was open for 0% of the time, Pallas kernels for 41%

profile of v9, /device:TPU:0, one launch (start us, length us, event | category | flops | bytes accessed | tf_op | source)
XLA Modules:
  0.0 49.1 jit_solution(9712735288259762100)
XLA Ops:
  0.0 0.0 copy-start.3
  0.0 0.0 copy-start
  0.0 0.0 copy-start.2
  0.0 0.0 copy-start.1
  0.0 0.6 %collective-permute-start.6 = (bf16[8,384,384]{2,1,0:T(8,128)(2,1)}, bf16[8,384,384]{2,1,0:T(8,128)(2,1)S(1)}, u32[]{:S(2)}, u32[]{:S(2)}) collective-permute-start(bf16[8,384,384]{2,1,0:T(8,128)(2,1)} %right_far.1), channel_id=1, source_target_pairs={{0,1},{1,0},{2,3},{3,2},{4,5},{5,4},{6,7},{7,6},{8,9},{9,8},{10,11... | collective-permute-start | bytes 7077896 | tf_op jit(solution)/shard_map/ppermute | solution.py:273
  0.6 0.1 collective-permute-start.5
  0.7 0.4 collective-permute-start.2
  1.1 1.1 %first_kernel.1 = (bf16[1,384,384]{2,1,0:T(8,128)(2,1)S(1)}, bf16[2,192,384]{2,1,0:T(8,128)(2,1)S(1)}) custom-call(bf16[8,384,384]{2,1,0:T(8,128)(2,1)} %left_far.3, bf16[8,384,384]{2,1,0:T(8,128)(2,1)} %cells.5), custom_call_target="tpu_custom_call" | custom-call | tf_op jit(solution)/shard_map/first_kernel/pallas_call | solution.py:287
  2.2 0.0 copy-done.3
  2.2 0.0 copy-done
  2.2 0.0 copy-done.2
  2.2 0.0 copy-done.1
  2.2 7.5 %shard_map.64 = (bf16[384,384]{1,0:T(8,128)(2,1)S(1)}, f32[192,384]{1,0:T(8,128)S(1)}, f32[192,384]{1,0:T(8,128)S(1)}, bf16[8,384,384]{2,1,0:T(8,128)(2,1)S(1)}, bf16[8,384,384]{2,1,0:T(8,128)(2,1)S(1)}) custom-call(s32[8]{0:T(128)S(1)} %copy-done.3, s32[8,8]{1,0:T(8,128)S(1)} %copy-done.1, f32[8,8]{1,0:T(8,128)S(1)} %copy-done.2, ...), custom_call_target="tpu_custom_call" | custom-call | flops 3623878656 | bytes 4718592 | tf_op jit(solution)/shard_map/pallas_call | solution.py:258
  9.7 2.7 %collective-permute-start = (bf16[384,384]{1,0:T(8,128)(2,1)S(1)}, bf16[384,384]{1,0:T(8,128)(2,1)S(1)}, u32[]{:S(2)}, u32[]{:S(2)}) collective-permute-start(bf16[384,384]{1,0:T(8,128)(2,1)S(1)} %get-tuple-element.23), channel_id=1, source_target_pairs={{0,2},{1,3},{2,0},{3,1},{4,6},{5,7},{6,4},{7,5},{8,10},{9,11},{10,... | collective-permute-start | bytes 884744 | tf_op jit(solution)/shard_map/ppermute | solution.py:273
  12.5 0.1 collective-permute-start.8
  12.6 5.4 %shard_map.65 = (f32[384,384]{1,0:T(8,128)S(1)}, f32[384,384]{1,0:T(8,128)S(1)}) custom-call(s32[8]{0:T(128)S(1)} %copy-done.3, s32[8,8]{1,0:T(8,128)S(1)} %copy-done.1, f32[8,8]{1,0:T(8,128)S(1)} %copy-done.2, bf16[8,384,384]{2,1,0:T(8,128)(2,1)S(1)} %get-tuple-element.19.left, bf16[8,384,384]{2,1,0:T(8,128)(2,1)S(1)} %get-tuple-element.20.right, ...), custom_call_target="tpu_custom_call" | custom-call | flops 3623878656 | bytes 4718592 | tf_op jit(solution)/shard_map/pallas_call | solution.py:258
  18.0 2.1 %collective-permute-done = bf16[384,384]{1,0:T(8,128)(2,1)S(1)} collective-permute-done((bf16[384,384]{1,0:T(8,128)(2,1)S(1)}, bf16[384,384]{1,0:T(8,128)(2,1)S(1)}, u32[]{:S(2)}, u32[]{:S(2)}) %collective-permute-start) | collective-permute-done | bytes 294944 | tf_op jit(solution)/shard_map/ppermute | solution.py:273
  20.0 1.7 %collective-permute-start.7 = (bf16[1,384,384]{2,1,0:T(8,128)(2,1)S(1)}, bf16[1,384,384]{2,1,0:T(8,128)(2,1)S(1)}, u32[]{:S(2)}, u32[]{:S(2)}) collective-permute-start(bf16[1,384,384]{2,1,0:T(8,128)(2,1)S(1)} %get-tuple-element.24), channel_id=1, source_target_pairs={{0,4},{1,29},{2,6},{3,31},{4,8},{5,1},{6,10},{7,3},{8,12},{9,5},{1... | collective-permute-start | bytes 884744 | tf_op jit(solution)/shard_map/ppermute | solution.py:299
  21.7 0.1 convert_add_fusion.1
  21.8 0.0 collective-permute-done.2.charge_in
  21.8 2.3 %collective-permute-start.3 = (s32[8,8]{1,0:T(8,128)S(1)}, s32[8,8]{1,0:T(8,128)S(1)}, u32[]{:S(2)}, u32[]{:S(2)}) collective-permute-start(s32[8,8]{1,0:T(8,128)S(1)} %copy-done.1), channel_id=1, source_target_pairs={{0,1},{1,0},{2,3},{3,2},{4,5},{5,4},{6,7},{7,6},{8,9},{9,8},{10,11... | collective-permute-start | bytes 776 | tf_op jit(solution)/shard_map/ppermute | solution.py:273
  24.1 0.0 collective-permute-done.8
  24.1 0.1 collective-permute-start.4
  24.3 0.7 %collective-permute-done.3.couple_in = s32[8,8]{1,0:T(8,128)S(1)} collective-permute-done((s32[8,8]{1,0:T(8,128)S(1)}, s32[8,8]{1,0:T(8,128)S(1)}, u32[]{:S(2)}, u32[]{:S(2)}) %collective-permute-start.3) | collective-permute-done | bytes 288 | tf_op jit(solution)/shard_map/ppermute | solution.py:273
  24.9 0.3 collective-permute-done.4.amplitude_in
  25.3 4.2 %collective-permute-done.7.halo = bf16[1,384,384]{2,1,0:T(8,128)(2,1)S(1)} collective-permute-done((bf16[1,384,384]{2,1,0:T(8,128)(2,1)S(1)}, bf16[1,384,384]{2,1,0:T(8,128)(2,1)S(1)}, u32[]{:S(2)}, u32[]{:S(2)}) %collective-permute-start.7) | collective-permute-done | bytes 294944 | tf_op jit(solution)/shard_map/ppermute | solution.py:299
  29.5 0.0 collective-permute-done.6.right_in
  29.5 0.0 collective-permute-done.5.left_in
  29.5 6.3 %shard_map.66 = (bf16[384,384]{1,0:T(8,128)(2,1)S(1)}, bf16[4,384,384]{2,1,0:T(8,128)(2,1)S(1)}) custom-call(s32[8]{0:T(128)S(1)} %copy-done.3, s32[8,8]{1,0:T(8,128)S(1)} %copy-done.1, f32[8,8]{1,0:T(8,128)S(1)} %copy-done.2, s32[8]{0:T(128)S(1)} %collective-permute-done.2.charge_in, s32[8,8]{1,0:T(8,128)S(1)} %collective-permute-done.3.couple_in, ...), custom_call_target="tpu_custom_call" | custom-call | flops 3623878656 | bytes 9437184 | tf_op jit(solution)/shard_map/pallas_call | solution.py:258
  35.8 1.8 %collective-permute-start.9 = (bf16[576,384]{1,0:T(8,128)(2,1)S(1)}, bf16[576,384]{1,0:T(8,128)(2,1)S(1)}, u32[]{:S(2)}, u32[]{:S(2)}) collective-permute-start(bf16[576,384]{1,0:T(8,128)(2,1)S(1)} %pad_maximum_fusion.1), channel_id=1, source_target_pairs={{0,2},{1,3},{2,0},{3,1},{4,6},{5,7},{6,4},{7,5},{8,10},{9,11},{10,... | collective-permute-start | bytes 1327112 | tf_op jit(solution)/shard_map/ppermute | solution.py:273
  37.7 0.1 collective-permute-start.1
  37.7 6.1 %shard_map.67 = (f32[192,384]{1,0:T(8,128)S(1)}, f32[192,384]{1,0:T(8,128)S(1)}) custom-call(s32[8]{0:T(128)S(1)} %copy-done.3, s32[8,8]{1,0:T(8,128)S(1)} %copy-done.1, f32[8,8]{1,0:T(8,128)S(1)} %copy-done.2, s32[8]{0:T(128)S(1)} %collective-permute-done.2.charge_in, s32[8,8]{1,0:T(8,128)S(1)} %collective-permute-done.3.couple_in, ...), custom_call_target="tpu_custom_call" | custom-call | flops 3623878656 | bytes 9437184 | tf_op jit(solution)/shard_map/pallas_call | solution.py:258
  43.8 2.4 %collective-permute-done.9 = bf16[576,384]{1,0:T(8,128)(2,1)S(1)} collective-permute-done((bf16[576,384]{1,0:T(8,128)(2,1)S(1)}, bf16[576,384]{1,0:T(8,128)(2,1)S(1)}, u32[]{:S(2)}, u32[]{:S(2)}) %collective-permute-start.9) | collective-permute-done | bytes 442400 | tf_op jit(solution)/shard_map/ppermute | solution.py:273
  46.3 0.1 collective-permute-start.10
  46.4 0.0 collective-permute-done.1
  46.4 1.6 %collective-permute-done.10 = f32[192,384]{1,0:T(8,128)S(1)} collective-permute-done((f32[192,384]{1,0:T(8,128)S(1)}, f32[192,384]{1,0:T(8,128)S(1)}, u32[]{:S(2)}, u32[]{:S(2)}) %collective-permute-start.10) | collective-permute-done | bytes 294944 | tf_op jit(solution)/shard_map/ppermute | solution.py:273
  47.9 1.1 %total.1 = f32[8,96,384]{2,1,0:T(8,128)} custom-call(f32[4,96,384]{2,1,0:T(8,128)S(1)} %bitcast.8, f32[4,96,384]{2,1,0:T(8,128)S(1)} %bitcast.9, bf16[4,96,384]{2,1,0:T(8,128)(2,1)S(1)} %bitcast.7, bf16[6,96,384]{2,1,0:T(8,128)(2,1)S(1)} %bitcast.6, f32[2,96,384]{2,1,0:T(8,128)S(1)} %bitcast.10, f32[2,96,384]{2,1,0:T(8,128)S(1)} %bitcast.11), custom_call_target="tpu_custom_call" | custom-call | tf_op jit(solution)/shard_map/total/pallas_call | solution.py:368
  (4 shorter events, 0.2 us)
Async XLA Ops:
  0.0 2.2 %copy-start.3 = (s32[8]{0:T(128)S(1)}, s32[8]{0:T(128)}, u32[]{:S(2)}) copy-start(s32[8]{0:T(128)} %charge.7) | copy-start | bytes 100
  0.0 2.2 %copy-start = (bf16[8,384,384]{2,1,0:T(8,128)(2,1)S(1)}, bf16[8,384,384]{2,1,0:T(8,128)(2,1)}, u32[]{:S(2)}) copy-start(bf16[8,384,384]{2,1,0:T(8,128)(2,1)} %cells.5) | copy-start | bytes 7077892
  0.0 2.2 %copy-start.2 = (f32[8,8]{1,0:T(8,128)S(1)}, f32[8,8]{1,0:T(8,128)}, u32[]{:S(2)}) copy-start(f32[8,8]{1,0:T(8,128)} %amplitude.7) | copy-start | bytes 772
  0.0 2.2 %copy-start.1 = (s32[8,8]{1,0:T(8,128)S(1)}, s32[8,8]{1,0:T(8,128)}, u32[]{:S(2)}) copy-start(s32[8,8]{1,0:T(8,128)} %couple.7) | copy-start | bytes 772
  0.0 29.4 %collective-permute-start.6 = (bf16[8,384,384]{2,1,0:T(8,128)(2,1)}, bf16[8,384,384]{2,1,0:T(8,128)(2,1)S(1)}, u32[]{:S(2)}, u32[]{:S(2)}) collective-permute-start(bf16[8,384,384]{2,1,0:T(8,128)(2,1)} %right_far.1), channel_id=1, source_target_pairs={{0,1},{1,0},{2,3},{3,2},{4,5},{5,4},{6,7},{7,6},{8,9},{9,8},{10,11... | collective-permute-start | bytes 7077896 | tf_op jit(solution)/shard_map/ppermute | solution.py:273
  0.6 28.9 %collective-permute-start.5 = (bf16[8,384,384]{2,1,0:T(8,128)(2,1)}, bf16[8,384,384]{2,1,0:T(8,128)(2,1)S(1)}, u32[]{:S(2)}, u32[]{:S(2)}) collective-permute-start(bf16[8,384,384]{2,1,0:T(8,128)(2,1)} %left_far.3), channel_id=1, source_target_pairs={{0,1},{1,0},{2,3},{3,2},{4,5},{5,4},{6,7},{7,6},{8,9},{9,8},{10,11... | collective-permute-start | bytes 7077896 | tf_op jit(solution)/shard_map/ppermute | solution.py:273
  0.7 21.1 %collective-permute-start.2 = (s32[8]{0:T(128)}, s32[8]{0:T(128)S(1)}, u32[]{:S(2)}, u32[]{:S(2)}) collective-permute-start(s32[8]{0:T(128)} %charge.7), channel_id=1, source_target_pairs={{0,1},{1,0},{2,3},{3,2},{4,5},{5,4},{6,7},{7,6},{8,9},{9,8},{10,11... | collective-permute-start | bytes 104 | tf_op jit(solution)/shard_map/ppermute | solution.py:273
  9.7 10.3 %collective-permute-start = (bf16[384,384]{1,0:T(8,128)(2,1)S(1)}, bf16[384,384]{1,0:T(8,128)(2,1)S(1)}, u32[]{:S(2)}, u32[]{:S(2)}) collective-permute-start(bf16[384,384]{1,0:T(8,128)(2,1)S(1)} %get-tuple-element.23), channel_id=1, source_target_pairs={{0,2},{1,3},{2,0},{3,1},{4,6},{5,7},{6,4},{7,5},{8,10},{9,11},{10,... | collective-permute-start | bytes 884744 | tf_op jit(solution)/shard_map/ppermute | solution.py:273
  12.5 11.7 %collective-permute-start.8 = (f32[192,384]{1,0:T(8,128)S(1)}, f32[192,384]{1,0:T(8,128)S(1)}, u32[]{:S(2)}, u32[]{:S(2)}) collective-permute-start(f32[192,384]{1,0:T(8,128)S(1)} %get-tuple-element.27), channel_id=1, source_target_pairs={{0,1},{1,0},{2,3},{3,2},{4,5},{5,4},{6,7},{7,6},{8,9},{9,8},{10,11... | collective-permute-start | bytes 884744 | tf_op jit(solution)/shard_map/ppermute | solution.py:273
  20.0 9.4 %collective-permute-start.7 = (bf16[1,384,384]{2,1,0:T(8,128)(2,1)S(1)}, bf16[1,384,384]{2,1,0:T(8,128)(2,1)S(1)}, u32[]{:S(2)}, u32[]{:S(2)}) collective-permute-start(bf16[1,384,384]{2,1,0:T(8,128)(2,1)S(1)} %get-tuple-element.24), channel_id=1, source_target_pairs={{0,4},{1,29},{2,6},{3,31},{4,8},{5,1},{6,10},{7,3},{8,12},{9,5},{1... | collective-permute-start | bytes 884744 | tf_op jit(solution)/shard_map/ppermute | solution.py:299
  21.8 3.2 %collective-permute-start.3 = (s32[8,8]{1,0:T(8,128)S(1)}, s32[8,8]{1,0:T(8,128)S(1)}, u32[]{:S(2)}, u32[]{:S(2)}) collective-permute-start(s32[8,8]{1,0:T(8,128)S(1)} %copy-done.1), channel_id=1, source_target_pairs={{0,1},{1,0},{2,3},{3,2},{4,5},{5,4},{6,7},{7,6},{8,9},{9,8},{10,11... | collective-permute-start | bytes 776 | tf_op jit(solution)/shard_map/ppermute | solution.py:273
  24.1 1.2 %collective-permute-start.4 = (f32[8,8]{1,0:T(8,128)S(1)}, f32[8,8]{1,0:T(8,128)S(1)}, u32[]{:S(2)}, u32[]{:S(2)}) collective-permute-start(f32[8,8]{1,0:T(8,128)S(1)} %copy-done.2), channel_id=1, source_target_pairs={{0,1},{1,0},{2,3},{3,2},{4,5},{5,4},{6,7},{7,6},{8,9},{9,8},{10,11... | collective-permute-start | bytes 776 | tf_op jit(solution)/shard_map/ppermute | solution.py:273
  35.8 10.4 %collective-permute-start.9 = (bf16[576,384]{1,0:T(8,128)(2,1)S(1)}, bf16[576,384]{1,0:T(8,128)(2,1)S(1)}, u32[]{:S(2)}, u32[]{:S(2)}) collective-permute-start(bf16[576,384]{1,0:T(8,128)(2,1)S(1)} %pad_maximum_fusion.1), channel_id=1, source_target_pairs={{0,2},{1,3},{2,0},{3,1},{4,6},{5,7},{6,4},{7,5},{8,10},{9,11},{10,... | collective-permute-start | bytes 1327112 | tf_op jit(solution)/shard_map/ppermute | solution.py:273
  37.7 8.7 %collective-permute-start.1 = (f32[384,384]{1,0:T(8,128)S(1)}, f32[384,384]{1,0:T(8,128)S(1)}, u32[]{:S(2)}, u32[]{:S(2)}) collective-permute-start(f32[384,384]{1,0:T(8,128)S(1)} %pad_maximum_fusion), channel_id=1, source_target_pairs={{0,1},{1,0},{2,3},{3,2},{4,5},{5,4},{6,7},{7,6},{8,9},{9,8},{10,11... | collective-permute-start | bytes 1769480 | tf_op jit(solution)/shard_map/ppermute | solution.py:273
  46.3 1.6 %collective-permute-start.10 = (f32[192,384]{1,0:T(8,128)S(1)}, f32[192,384]{1,0:T(8,128)S(1)}, u32[]{:S(2)}, u32[]{:S(2)}) collective-permute-start(f32[192,384]{1,0:T(8,128)S(1)} %convert_add_fusion), channel_id=1, source_target_pairs={{0,1},{1,0},{2,3},{3,2},{4,5},{5,4},{6,7},{7,6},{8,9},{9,8},{10,11... | collective-permute-start | bytes 884744 | tf_op jit(solution)/shard_map/ppermute | solution.py:273

commit v10 on v8

--- a/solution.py
+++ b/solution.py
@@ -1,3 +1,5 @@
+import functools
+
 import jax
 import jax.numpy as jnp
 from jax import lax
@@ -163,16 +165,6 @@
         copy.wait()
 
 
-def inner_own_kernel(charge, couple, amplitude, left, right, cells, keep, send, middles):
-    chip, core = position()
-    operators = left.shape[0]
-    targets = cells.shape[0] - 2 * EDGE
-    inside = cells.at[pl.ds(EDGE - 1, targets + 2)]
-    for k in range(operators):
-        middle_of(k, (charge, couple, amplitude), k, left, inside, middles, EDGE, targets, chip, core)
-    summed(jnp.concatenate([right[k] for k in range(operators)], axis=1), middles, (keep, send))
-
-
 def edge_products(groups, sources, middles, results, sectors, chip, core):
     k = 0
     first_target = (sectors - EDGE) * core
@@ -208,29 +200,47 @@
     edge_products(groups, sources, middles, halves(send), sectors, 1 - chip, core)
 
 
-def edge_own_kernel(
+def own_kernel(
     charge, couple, amplitude, charge_in, couple_in, amplitude_in, left, right, left_in, right_in,
-    sources, keep, send, middles,
+    cells, sources, inner_keep, edge_keep, send, edge_middles, inner_middles,
 ):
     chip, core = position()
     sectors = couple.shape[1]
-    groups = (
-        ((charge, couple, amplitude), left, right),
-        ((charge_in, couple_in, amplitude_in), left_in, right_in),
-    )
-    edge_products(groups, sources, middles, (keep, send), sectors, chip, core)
-
-
-def sum_kernel(inner_own, inner_chip, direct_far, later_far, near_own, other, sigma):
+    small = (charge, couple, amplitude)
+    inner = sectors - 2 * EDGE
+    inside = cells.at[pl.ds(EDGE - 1, inner + 2)]
+    for k in range(left.shape[0]):
+        middle_of(k, small, k, left, inside, inner_middles, EDGE, inner, chip, core)
+    edge_rows = edge_keep.shape[0]
+    inner_send = send.at[pl.ds(edge_rows, send.shape[0] - edge_rows)]
+    wide = jnp.concatenate([right[k] for k in range(right.shape[0])], axis=1)
+    summed(wide, inner_middles, (inner_keep, inner_send))
+    groups = ((small, left, right), ((charge_in, couple_in, amplitude_in), left_in, right_in))
+    results = (edge_keep, send.at[pl.ds(0, edge_rows)])
+    edge_products(groups, sources, edge_middles, results, sectors, chip, core)
+
+
+def mate_kernel(edge, own, later_far, direct_far, mate):
+    both = edge + direct_far.shape[0] // CORES
+    mate[:edge] = (own[:edge] + later_far[edge : CORES * edge].astype(jnp.float32)).astype(mate.dtype)
+    mate[edge:both] = (own[edge:both] + direct_far[both - edge :].astype(jnp.float32)).astype(mate.dtype)
+    mate[both:] = own[both:].astype(mate.dtype)
+
+
+def sum_kernel(inner_own, near_own, direct_far, later_far, mate, sigma):
     core = lax.axis_index("op") & (CORES - 1)
     sectors = sigma.shape[0]
     far = sectors - EDGE
-    split = EDGE + direct_far.shape[0] // CORES
-    direct = split - EDGE
-    sigma[EDGE:split] = inner_own[:direct] + inner_chip[:direct] + direct_far[:direct].astype(jnp.float32)
-    sigma[split:far] = inner_own[direct:] + inner_chip[direct:] + later_far[CORES * EDGE :].astype(jnp.float32)
-    sigma[pl.ds(far * core, EDGE)] = near_own[...] + later_far[:EDGE].astype(jnp.float32)
-    sigma[pl.ds(far * (1 - core), EDGE)] = other[...]
+    direct = direct_far.shape[0] // CORES
+    split = EDGE + direct
+
+    def wide(value):
+        return value.astype(jnp.float32)
+
+    sigma[EDGE:split] = inner_own[:direct] + wide(direct_far[:direct]) + wide(mate[EDGE:split])
+    sigma[split:far] = inner_own[direct:] + wide(later_far[CORES * EDGE :]) + wide(mate[split:])
+    sigma[pl.ds(far * core, EDGE)] = near_own[...] + wide(later_far[:EDGE])
+    sigma[pl.ds(far * (1 - core), EDGE)] = wide(mate[:EDGE])
 
 
 SMALL = pl.BlockSpec(memory_space=pltpu.SMEM)
@@ -258,7 +268,7 @@
             in_specs=in_specs,
             out_specs=out_specs,
             scratch_shapes=[pltpu.VMEM((targets * CORES * half, ops * states), narrow)] + scratch,
-            compiler_params=pltpu.CompilerParams(vmem_limit_bytes=20 * MIB),
+            compiler_params=pltpu.CompilerParams(vmem_limit_bytes=28 * MIB),
             cost_estimate=pl.CostEstimate(
                 flops=ops * targets * CORES * half * states * states * 4,
                 bytes_accessed=ops * states * states * 4,
@@ -334,33 +344,31 @@
     )
     later = jnp.concatenate([edge_send, (keep + send_in).astype(narrow)], axis=0)
     later_far = over_op(later, CORES)
-    block = shape(inner * half, states)
-    inner_own, inner_send = run(
-        inner_own_kernel,
-        operators,
-        inner,
-        [*here, left, right, cells],
-        [SMALL] * 3 + [BLOCK] * 3,
-        [block, block],
-        [BLOCK, BLOCK],
-        [],
-    )
-    mate = inner_send[:direct_rows] + direct_far[direct_rows:].astype(wide)
-    inner_chip = over_op(jnp.concatenate([mate, inner_send[direct_rows:]], axis=0), 1)
-    edge_wide = shape(EDGE * half, states)
-    near_own, near_mate = run(
-        edge_own_kernel,
+    edge_rows = EDGE * half
+    inner_own, near_own, own_send = run(
+        own_kernel,
         CORES * operators,
         EDGE,
-        held + [sources],
-        held_specs + [BLOCK],
-        [edge_wide, edge_wide],
-        [BLOCK, BLOCK],
-        [],
-    )
-    passed = later_far[EDGE * half : CORES * EDGE * half].astype(wide)
-    other = over_op(near_mate + passed, 1)
-    parts = (inner_own, inner_chip, direct_far, later_far, near_own, other)
+        held + [cells, sources],
+        held_specs + [BLOCK] * 2,
+        [
+            shape(inner * half, states),
+            shape(edge_rows, states),
+            shape(edge_rows + inner * half, states),
+        ],
+        [BLOCK] * 3,
+        [pltpu.VMEM((inner * CORES * half, operators * states), narrow)],
+    )
+    mate = pl.pallas_call(
+        functools.partial(mate_kernel, edge_rows),
+        out_shape=shape(*own_send.shape, dtype=narrow),
+        in_specs=[BLOCK] * 3,
+        out_specs=BLOCK,
+        compiler_params=pltpu.CompilerParams(vmem_limit_bytes=4 * MIB),
+        name="mate_kernel",
+    )(own_send, later_far, direct_far)
+    mate = over_op(mate, 1)
+    parts = (inner_own, near_own, direct_far, later_far, mate)
     return pl.pallas_call(
         sum_kernel,
         out_shape=shape(sectors, half, states),

time: 57.2 us -> 57 us (level)
  waiting for transfers between devices: 8.55 us -> 9.92 us
  other arithmetic: 1.16 us -> 0.08 us
  Pallas kernels: 27.6 us -> 26.9 us
    ppermute x10 -> x9, waiting for transfers between devices: 4.47 us -> 8.01 us  [over_op(): return lax.ppermute(value, 'op', [(i, i ^ flip) for i in range(op)])]
    ppermute x1, waiting for transfers between devices: 4.08 us -> 1.91 us  [shards(): halo = lax.ppermute(border, ('sec', 'op'), ring)]
    convert_element_type x1, other arithmetic: 0.99 us -> 0.03 us  [shards(): (keep + send_in).astype(narrow)]
    ppermute x1, starting transfers between devices: 1.73 us -> 2.59 us  [shards(): halo = lax.ppermute(border, ('sec', 'op'), ring)]
    pallas_call x4 -> x3, Pallas kernels: 26.5 us -> 25.6 us  [run(): pl.pallas_call(kernel, out_shape=outs, in_specs=in_specs, out_specs=out_s...]
    ppermute x10 -> x9, starting transfers between devices: 7.28 us -> 6.88 us  [over_op(): return lax.ppermute(value, 'op', [(i, i ^ flip) for i in range(op)])]
    unnamed x16 -> x14, local copies, waits for them, and re-layouts: 9.34 us -> 9.32 us
  transfers between devices with their start and end apart: 11 -> 10, of which waited for: 4 -> 6; matrix products, arithmetic and copies ran while one was open for 4% -> 2% of each run, Pallas kernels for 34% -> 32%
where the time goes in v10:
time: 57 us; the launch traced here: 56.7 us
  Pallas kernels  26.9 us (47%)
  local copies, waits for them, and re-layouts  10.3 us (18%)
  waiting for transfers between devices  9.92 us (17%)
  starting transfers between devices  9.47 us (17%)
    pallas_call x3, Pallas kernels, run(): pl.pallas_call(kernel, out_shape=outs, in_specs=in_specs, out_specs=out_s...  25.6 us
    unnamed x14, local copies, waits for them, and re-layouts  9.32 us
    ppermute x9, waiting for transfers between devices, over_op(): return lax.ppermute(value, 'op', [(i, i ^ flip) for i in range(op)])  8.01 us
    ppermute x9, starting transfers between devices, over_op(): return lax.ppermute(value, 'op', [(i, i ^ flip) for i in range(op)])  6.88 us
    ppermute x1, starting transfers between devices, shards(): halo = lax.ppermute(border, ('sec', 'op'), ring)  2.59 us
    ppermute x1, waiting for transfers between devices, shards(): halo = lax.ppermute(border, ('sec', 'op'), ring)  1.91 us
    pallas_call x1, Pallas kernels, shards(): pl.pallas_call(sum_kernel, out_shape=shape(sectors, half, states), in_spe...  1.16 us
  transfers between devices with their start and end apart: 10, of which 6 were waited for; matrix products, arithmetic and copies ran while one was open for 2% of the time, Pallas kernels for 32%

profile of v10, /device:TPU:0, one launch (start us, length us, event | category | flops | bytes accessed | tf_op | source)
XLA Modules:
  0.0 56.7 jit_solution(12187598135308461345)
XLA Ops:
  0.0 0.0 copy-start.6
  0.0 0.5 collective-permute-start.3
  0.5 0.1 collective-permute-start.4
  0.6 6.9 %shard_map.64 = (bf16[384,384]{1,0:T(8,128)(2,1)S(1)}, f32[192,384]{1,0:T(8,128)S(1)}, f32[192,384]{1,0:T(8,128)S(1)}, bf16[8,384,384]{2,1,0:T(8,128)(2,1)S(1)},...) custom-call(s32[8]{0:T(128)} %charge.1, ...), custom_call_target="tpu_custom_call" | custom-call | flops 3623878656 | bytes 4718592 | tf_op jit(solution)/shard_map/pallas_call | solution.py:265
  7.5 0.0 copy-start
  7.5 1.4 %copy-done = bf16[8,384,384]{2,1,0:T(8,128)(2,1)} copy-done((bf16[8,384,384]{2,1,0:T(8,128)(2,1)}, bf16[8,384,384]{2,1,0:T(8,128)(2,1)S(1)}, u32[]{:S(2)}) %copy-start) | copy-done | bytes 2359320
  8.9 0.0 copy-start.2
  8.9 1.4 %copy-done.2 = bf16[8,384,384]{2,1,0:T(8,128)(2,1)} copy-done((bf16[8,384,384]{2,1,0:T(8,128)(2,1)}, bf16[8,384,384]{2,1,0:T(8,128)(2,1)S(1)}, u32[]{:S(2)}) %copy-start.2) | copy-done | bytes 2359320
  10.3 0.0 copy-start.4
  10.3 1.5 %copy-done.4 = bf16[8,384,384]{2,1,0:T(8,128)(2,1)} copy-done((bf16[8,384,384]{2,1,0:T(8,128)(2,1)}, bf16[8,384,384]{2,1,0:T(8,128)(2,1)S(1)}, u32[]{:S(2)}) %copy-start.4) | copy-done | bytes 2359320
  11.8 0.5 collective-permute-start.7
  12.3 1.0 %constant_dynamic-slice_fusion = bf16[1,384,384]{2,1,0:T(8,128)(2,1)S(1)} fusion(bf16[8,384,384]{2,1,0:T(8,128)(2,1)} %cells_far.1, s32[]{:T(128)S(6)} %select_n.3), kind=kLoop, calls=%fused_computation.2 | loop fusion | bytes 589828 | tf_op jit(solution)/shard_map/dynamic_slice | solution.py:291
  13.3 2.6 %collective-permute-start.5 = (bf16[1,384,384]{2,1,0:T(8,128)(2,1)S(1)}, bf16[1,384,384]{2,1,0:T(8,128)(2,1)S(1)}, u32[]{:S(2)}, u32[]{:S(2)}) collective-permute-start(bf16[1,384,384]{2,1,0:T(8,128)(2,1)S(1)} %constant_dynamic-slice_fusion), channel_id=1, source_target_pairs={{0,4},{1,29},{2,6},{3,31},{4,8},{5,1},{6,10},{7,3},{8,12},{9,5},{1... | collective-permute-start | bytes 884744 | tf_op jit(solution)/shard_map/ppermute | solution.py:292
  15.9 3.2 %collective-permute-start = (s32[8]{0:T(128)}, s32[8]{0:T(128)S(1)}, u32[]{:S(2)}, u32[]{:S(2)}) collective-permute-start(s32[8]{0:T(128)} %charge.1), channel_id=1, source_target_pairs={{0,1},{1,0},{2,3},{3,2},{4,5},{5,4},{6,7},{7,6},{8,9},{9,8},{10,11... | collective-permute-start | bytes 104 | tf_op jit(solution)/shard_map/ppermute | solution.py:280
  19.0 1.0 %collective-permute-done.charge_in = s32[8]{0:T(128)S(1)} collective-permute-done((s32[8]{0:T(128)}, s32[8]{0:T(128)S(1)}, u32[]{:S(2)}, u32[]{:S(2)}) %collective-permute-start) | collective-permute-done | bytes 64 | tf_op jit(solution)/shard_map/ppermute | solution.py:280
  20.0 0.0 copy-done.6
  20.0 0.3 collective-permute-start.1
  20.3 0.0 collective-permute-done.7
  20.3 0.2 collective-permute-start.2
  20.5 0.6 %collective-permute-done.1.couple_in = s32[8,8]{1,0:T(8,128)S(1)} collective-permute-done((s32[8,8]{1,0:T(8,128)S(1)}, s32[8,8]{1,0:T(8,128)S(1)}, u32[]{:S(2)}, u32[]{:S(2)}) %collective-permute-start.1) | collective-permute-done | bytes 288 | tf_op jit(solution)/shard_map/ppermute | solution.py:280
  21.1 0.6 collective-permute-done.2.amplitude_in
  21.7 1.9 %collective-permute-done.5.halo = bf16[1,384,384]{2,1,0:T(8,128)(2,1)S(1)} collective-permute-done((bf16[1,384,384]{2,1,0:T(8,128)(2,1)S(1)}, bf16[1,384,384]{2,1,0:T(8,128)(2,1)S(1)}, u32[]{:S(2)}, u32[]{:S(2)}) %collective-permute-start.5) | collective-permute-done | bytes 294944 | tf_op jit(solution)/shard_map/ppermute | solution.py:292
  23.6 0.0 collective-permute-done.3.left_in
  23.6 0.0 collective-permute-done.4.right_in
  23.6 0.0 copy-start.1
  23.6 1.7 %copy-done.1 = bf16[8,384,384]{2,1,0:T(8,128)(2,1)S(1)} copy-done((bf16[8,384,384]{2,1,0:T(8,128)(2,1)S(1)}, bf16[8,384,384]{2,1,0:T(8,128)(2,1)}, u32[]{:S(2)}) %copy-start.1) | copy-done | bytes 2359320
  25.3 0.0 copy-start.3
  25.3 1.7 %copy-done.3 = bf16[8,384,384]{2,1,0:T(8,128)(2,1)S(1)} copy-done((bf16[8,384,384]{2,1,0:T(8,128)(2,1)S(1)}, bf16[8,384,384]{2,1,0:T(8,128)(2,1)}, u32[]{:S(2)}) %copy-start.3) | copy-done | bytes 2359320
  27.0 0.0 copy-start.5
  27.0 1.7 %copy-done.5 = bf16[8,384,384]{2,1,0:T(8,128)(2,1)S(1)} copy-done((bf16[8,384,384]{2,1,0:T(8,128)(2,1)S(1)}, bf16[8,384,384]{2,1,0:T(8,128)(2,1)}, u32[]{:S(2)}) %copy-start.5) | copy-done | bytes 2359320
  28.6 7.4 %shard_map.65 = (bf16[384,384]{1,0:T(8,128)(2,1)S(1)}, bf16[4,384,384]{2,1,0:T(8,128)(2,1)S(1)}) custom-call(s32[8]{0:T(128)S(1)} %get-tuple-element.19.charge, s32[8,8]{1,0:T(8,128)S(1)} %get-tuple-element.20.couple, f32[8,8]{1,0:T(8,128)S(1)} %get-tuple-element.21.amplitude, s32[8]{0:T(128)S(1)} %collective-permute-done.charge_in, ...), custom_call_target="tpu_custom_call" | custom-call | flops 3623878656 | bytes 9437184 | tf_op jit(solution)/shard_map/pallas_call | solution.py:265
  36.1 1.8 %collective-permute-start.8 = (bf16[576,384]{1,0:T(8,128)(2,1)S(1)}, bf16[576,384]{1,0:T(8,128)(2,1)S(1)}, u32[]{:S(2)}, u32[]{:S(2)}) collective-permute-start(bf16[576,384]{1,0:T(8,128)(2,1)S(1)} %pad_maximum_fusion), channel_id=1, source_target_pairs={{0,2},{1,3},{2,0},{3,1},{4,6},{5,7},{6,4},{7,5},{8,10},{9,11},{10,... | collective-permute-start | bytes 1327112 | tf_op jit(solution)/shard_map/ppermute | solution.py:280
  37.8 0.3 collective-permute-start.6
  38.2 11.4 %shard_map.66 = (f32[384,384]{1,0:T(8,128)S(1)}, f32[192,384]{1,0:T(8,128)S(1)}, f32[576,384]{1,0:T(8,128)S(1)}) custom-call(s32[8]{0:T(128)S(1)} %get-tuple-element.19.charge, s32[8,8]{1,0:T(8,128)S(1)} %get-tuple-element.20.couple, f32[8,8]{1,0:T(8,128)S(1)} %get-tuple-element.21.amplitude, s32[8]{0:T(128)S(1)} %collective-permute-done.charge_in, ...), custom_call_target="tpu_custom_call" | custom-call | flops 3623878656 | bytes 9437184 | tf_op jit(solution)/shard_map/pallas_call | solution.py:265
  49.5 4.1 %collective-permute-done.6.direct_far = bf16[384,384]{1,0:T(8,128)(2,1)S(1)} collective-permute-done((bf16[384,384]{1,0:T(8,128)(2,1)S(1)}, bf16[384,384]{1,0:T(8,128)(2,1)S(1)}, u32[]{:S(2)}, u32[]{:S(2)}) %collective-permute-start.6) | collective-permute-done | bytes 294944 | tf_op jit(solution)/shard_map/ppermute | solution.py:280
  53.6 0.0 collective-permute-done.8.later_far
  53.6 0.1 mate_kernel.1
  53.7 0.1 collective-permute-start.9
  53.8 1.8 %collective-permute-done.9 = bf16[576,384]{1,0:T(8,128)(2,1)S(1)} collective-permute-done((bf16[576,384]{1,0:T(8,128)(2,1)S(1)}, bf16[576,384]{1,0:T(8,128)(2,1)S(1)}, u32[]{:S(2)}, u32[]{:S(2)}) %collective-permute-start.9) | collective-permute-done | bytes 442400 | tf_op jit(solution)/shard_map/ppermute | solution.py:280
  55.5 1.2 %total.1 = f32[8,96,384]{2,1,0:T(8,128)} custom-call(f32[4,96,384]{2,1,0:T(8,128)S(1)} %bitcast.7, f32[2,96,384]{2,1,0:T(8,128)S(1)} %bitcast.9, bf16[4,96,384]{2,1,0:T(8,128)(2,1)S(1)} %bitcast.6, bf16[6,96,384]{2,1,0:T(8,128)(2,1)S(1)} %bitcast.5, bf16[6,96,384]{2,1,0:T(8,128)(2,1)S(1)} %bitcast.8), custom_call_target="tpu_custom_call" | custom-call | tf_op jit(solution)/shard_map/total/pallas_call | solution.py:372
  (2 shorter events, 0.1 us)
Async XLA Ops:
  0.0 20.0 %copy-start.6 = (s32[8,8]{1,0:T(8,128)S(1)}, s32[8,8]{1,0:T(8,128)}, u32[]{:S(2)}) copy-start(s32[8,8]{1,0:T(8,128)} %couple.1) | copy-start | bytes 772
  0.0 23.6 %collective-permute-start.3 = (bf16[8,384,384]{2,1,0:T(8,128)(2,1)}, bf16[8,384,384]{2,1,0:T(8,128)(2,1)S(1)}, u32[]{:S(2)}, u32[]{:S(2)}) collective-permute-start(bf16[8,384,384]{2,1,0:T(8,128)(2,1)} %left_far.1), channel_id=1, source_target_pairs={{0,1},{1,0},{2,3},{3,2},{4,5},{5,4},{6,7},{7,6},{8,9},{9,8},{10,11... | collective-permute-start | bytes 7077896 | tf_op jit(solution)/shard_map/ppermute | solution.py:280
  0.5 23.1 %collective-permute-start.4 = (bf16[8,384,384]{2,1,0:T(8,128)(2,1)}, bf16[8,384,384]{2,1,0:T(8,128)(2,1)}, u32[]{:S(2)}, u32[]{:S(2)}) collective-permute-start(bf16[8,384,384]{2,1,0:T(8,128)(2,1)} %right_far.1), channel_id=1, source_target_pairs={{0,1},{1,0},{2,3},{3,2},{4,5},{5,4},{6,7},{7,6},{8,9},{9,8},{10,11... | collective-permute-start | bytes 7077896 | tf_op jit(solution)/shard_map/ppermute | solution.py:280
  7.5 1.4 %copy-start = (bf16[8,384,384]{2,1,0:T(8,128)(2,1)}, bf16[8,384,384]{2,1,0:T(8,128)(2,1)S(1)}, u32[]{:S(2)}) copy-start(bf16[8,384,384]{2,1,0:T(8,128)(2,1)S(1)} %get-tuple-element.22.left) | copy-start | bytes 7077892
  8.9 1.4 %copy-start.2 = (bf16[8,384,384]{2,1,0:T(8,128)(2,1)}, bf16[8,384,384]{2,1,0:T(8,128)(2,1)S(1)}, u32[]{:S(2)}) copy-start(bf16[8,384,384]{2,1,0:T(8,128)(2,1)S(1)} %get-tuple-element.23.right) | copy-start | bytes 7077892
  10.3 1.5 %copy-start.4 = (bf16[8,384,384]{2,1,0:T(8,128)(2,1)}, bf16[8,384,384]{2,1,0:T(8,128)(2,1)S(1)}, u32[]{:S(2)}) copy-start(bf16[8,384,384]{2,1,0:T(8,128)(2,1)S(1)} %get-tuple-element.24.cells) | copy-start | bytes 7077892
  11.8 8.5 %collective-permute-start.7 = (f32[192,384]{1,0:T(8,128)S(1)}, f32[192,384]{1,0:T(8,128)S(1)}, u32[]{:S(2)}, u32[]{:S(2)}) collective-permute-start(f32[192,384]{1,0:T(8,128)S(1)} %get-tuple-element.31), channel_id=1, source_target_pairs={{0,1},{1,0},{2,3},{3,2},{4,5},{5,4},{6,7},{7,6},{8,9},{9,8},{10,11... | collective-permute-start | bytes 884744 | tf_op jit(solution)/shard_map/ppermute | solution.py:280
  13.3 10.3 %collective-permute-start.5 = (bf16[1,384,384]{2,1,0:T(8,128)(2,1)S(1)}, bf16[1,384,384]{2,1,0:T(8,128)(2,1)S(1)}, u32[]{:S(2)}, u32[]{:S(2)}) collective-permute-start(bf16[1,384,384]{2,1,0:T(8,128)(2,1)S(1)} %constant_dynamic-slice_fusion), channel_id=1, source_target_pairs={{0,4},{1,29},{2,6},{3,31},{4,8},{5,1},{6,10},{7,3},{8,12},{9,5},{1... | collective-permute-start | bytes 884744 | tf_op jit(solution)/shard_map/ppermute | solution.py:292
  15.9 4.1 %collective-permute-start = (s32[8]{0:T(128)}, s32[8]{0:T(128)S(1)}, u32[]{:S(2)}, u32[]{:S(2)}) collective-permute-start(s32[8]{0:T(128)} %charge.1), channel_id=1, source_target_pairs={{0,1},{1,0},{2,3},{3,2},{4,5},{5,4},{6,7},{7,6},{8,9},{9,8},{10,11... | collective-permute-start | bytes 104 | tf_op jit(solution)/shard_map/ppermute | solution.py:280
  20.0 1.2 %collective-permute-start.1 = (s32[8,8]{1,0:T(8,128)S(1)}, s32[8,8]{1,0:T(8,128)S(1)}, u32[]{:S(2)}, u32[]{:S(2)}) collective-permute-start(s32[8,8]{1,0:T(8,128)S(1)} %copy-done.6), channel_id=1, source_target_pairs={{0,1},{1,0},{2,3},{3,2},{4,5},{5,4},{6,7},{7,6},{8,9},{9,8},{10,11... | collective-permute-start | bytes 776 | tf_op jit(solution)/shard_map/ppermute | solution.py:280
  20.3 1.4 %collective-permute-start.2 = (f32[8,8]{1,0:T(8,128)}, f32[8,8]{1,0:T(8,128)S(1)}, u32[]{:S(2)}, u32[]{:S(2)}) collective-permute-start(f32[8,8]{1,0:T(8,128)} %amplitude.1), channel_id=1, source_target_pairs={{0,1},{1,0},{2,3},{3,2},{4,5},{5,4},{6,7},{7,6},{8,9},{9,8},{10,11... | collective-permute-start | bytes 776 | tf_op jit(solution)/shard_map/ppermute | solution.py:280
  23.6 1.7 %copy-start.1 = (bf16[8,384,384]{2,1,0:T(8,128)(2,1)S(1)}, bf16[8,384,384]{2,1,0:T(8,128)(2,1)}, u32[]{:S(2)}) copy-start(bf16[8,384,384]{2,1,0:T(8,128)(2,1)} %copy-done) | copy-start | bytes 7077892
  25.3 1.7 %copy-start.3 = (bf16[8,384,384]{2,1,0:T(8,128)(2,1)S(1)}, bf16[8,384,384]{2,1,0:T(8,128)(2,1)}, u32[]{:S(2)}) copy-start(bf16[8,384,384]{2,1,0:T(8,128)(2,1)} %copy-done.2) | copy-start | bytes 7077892
  27.0 1.7 %copy-start.5 = (bf16[8,384,384]{2,1,0:T(8,128)(2,1)S(1)}, bf16[8,384,384]{2,1,0:T(8,128)(2,1)}, u32[]{:S(2)}) copy-start(bf16[8,384,384]{2,1,0:T(8,128)(2,1)} %copy-done.4) | copy-start | bytes 7077892
  36.1 17.5 %collective-permute-start.8 = (bf16[576,384]{1,0:T(8,128)(2,1)S(1)}, bf16[576,384]{1,0:T(8,128)(2,1)S(1)}, u32[]{:S(2)}, u32[]{:S(2)}) collective-permute-start(bf16[576,384]{1,0:T(8,128)(2,1)S(1)} %pad_maximum_fusion), channel_id=1, source_target_pairs={{0,2},{1,3},{2,0},{3,1},{4,6},{5,7},{6,4},{7,5},{8,10},{9,11},{10,... | collective-permute-start | bytes 1327112 | tf_op jit(solution)/shard_map/ppermute | solution.py:280
  37.8 15.8 %collective-permute-start.6 = (bf16[384,384]{1,0:T(8,128)(2,1)S(1)}, bf16[384,384]{1,0:T(8,128)(2,1)S(1)}, u32[]{:S(2)}, u32[]{:S(2)}) collective-permute-start(bf16[384,384]{1,0:T(8,128)(2,1)S(1)} %get-tuple-element.28), channel_id=1, source_target_pairs={{0,2},{1,3},{2,0},{3,1},{4,6},{5,7},{6,4},{7,5},{8,10},{9,11},{10,... | collective-permute-start | bytes 884744 | tf_op jit(solution)/shard_map/ppermute | solution.py:280
  53.7 1.9 %collective-permute-start.9 = (bf16[576,384]{1,0:T(8,128)(2,1)S(1)}, bf16[576,384]{1,0:T(8,128)(2,1)S(1)}, u32[]{:S(2)}, u32[]{:S(2)}) collective-permute-start(bf16[576,384]{1,0:T(8,128)(2,1)S(1)} %mate_kernel.1), channel_id=1, source_target_pairs={{0,1},{1,0},{2,3},{3,2},{4,5},{5,4},{6,7},{7,6},{8,9},{9,8},{10,11... | collective-permute-start | bytes 1327112 | tf_op jit(solution)/shard_map/ppermute | solution.py:280

commit v11 on v10

--- a/solution.py
+++ b/solution.py
@@ -220,14 +220,14 @@
     edge_products(groups, sources, edge_middles, results, sectors, chip, core)
 
 
-def mate_kernel(edge, own, later_far, direct_far, mate):
+def mate_kernel(edge, own, direct_far, mate):
     both = edge + direct_far.shape[0] // CORES
-    mate[:edge] = (own[:edge] + later_far[edge : CORES * edge].astype(jnp.float32)).astype(mate.dtype)
+    mate[:edge] = own[:edge].astype(mate.dtype)
     mate[edge:both] = (own[edge:both] + direct_far[both - edge :].astype(jnp.float32)).astype(mate.dtype)
     mate[both:] = own[both:].astype(mate.dtype)
 
 
-def sum_kernel(inner_own, near_own, direct_far, later_far, mate, sigma):
+def sum_kernel(inner_own, near_own, direct_far, later_far, mate, passed, sigma):
     core = lax.axis_index("op") & (CORES - 1)
     sectors = sigma.shape[0]
     far = sectors - EDGE
@@ -240,7 +240,7 @@
     sigma[EDGE:split] = inner_own[:direct] + wide(direct_far[:direct]) + wide(mate[EDGE:split])
     sigma[split:far] = inner_own[direct:] + wide(later_far[CORES * EDGE :]) + wide(mate[split:])
     sigma[pl.ds(far * core, EDGE)] = near_own[...] + wide(later_far[:EDGE])
-    sigma[pl.ds(far * (1 - core), EDGE)] = wide(mate[:EDGE])
+    sigma[pl.ds(far * (1 - core), EDGE)] = wide(mate[:EDGE]) + wide(passed[...])
 
 
 SMALL = pl.BlockSpec(memory_space=pltpu.SMEM)
@@ -362,13 +362,14 @@
     mate = pl.pallas_call(
         functools.partial(mate_kernel, edge_rows),
         out_shape=shape(*own_send.shape, dtype=narrow),
-        in_specs=[BLOCK] * 3,
+        in_specs=[BLOCK] * 2,
         out_specs=BLOCK,
         compiler_params=pltpu.CompilerParams(vmem_limit_bytes=4 * MIB),
         name="mate_kernel",
-    )(own_send, later_far, direct_far)
+    )(own_send, direct_far)
     mate = over_op(mate, 1)
-    parts = (inner_own, near_own, direct_far, later_far, mate)
+    passed = over_op(later_far[edge_rows : CORES * edge_rows], 1)
+    parts = (inner_own, near_own, direct_far, later_far, mate, passed)
     return pl.pallas_call(
         sum_kernel,
         out_shape=shape(sectors, half, states),

time: 57 us -> 52.9 us (0.928)
  waiting for transfers between devices: 9.92 us -> 3.93 us
  starting transfers between devices: 9.47 us -> 11.4 us
    ppermute x9 -> x10, waiting for transfers between devices: 8.01 us -> 2.99 us  [over_op(): return lax.ppermute(value, 'op', [(i, i ^ flip) for i in range(op)])]
    ppermute x9 -> x10, starting transfers between devices: 6.88 us -> 8.62 us  [over_op(): return lax.ppermute(value, 'op', [(i, i ^ flip) for i in range(op)])]
    ppermute x1, waiting for transfers between devices: 1.91 us -> 0.94 us  [shards(): halo = lax.ppermute(border, ('sec', 'op'), ring)]
  transfers between devices with their start and end apart: 10 -> 11, of which waited for: 6 -> 5; matrix products, arithmetic and copies ran while one was open for 2% -> 2% of each run, Pallas kernels for 32% -> 49%
where the time goes in v11:
time: 52.9 us; the launch traced here: 52.6 us
  Pallas kernels  26.7 us (50%)
  starting transfers between devices  11.4 us (22%)
  local copies, waits for them, and re-layouts  10.4 us (20%)
  waiting for transfers between devices  3.93 us (7%)
    pallas_call x3, Pallas kernels, run(): pl.pallas_call(kernel, out_shape=outs, in_specs=in_specs, out_specs=out_s...  25.5 us
    unnamed x14, local copies, waits for them, and re-layouts  9.35 us
    ppermute x10, starting transfers between devices, over_op(): return lax.ppermute(value, 'op', [(i, i ^ flip) for i in range(op)])  8.62 us
    ppermute x10, waiting for transfers between devices, over_op(): return lax.ppermute(value, 'op', [(i, i ^ flip) for i in range(op)])  2.99 us
    ppermute x1, starting transfers between devices, shards(): halo = lax.ppermute(border, ('sec', 'op'), ring)  2.76 us
    pallas_call x1, Pallas kernels, shards(): pl.pallas_call(sum_kernel, out_shape=shape(sectors, half, states), in_spe...  1.17 us
  transfers between devices with their start and end apart: 11, of which 5 were waited for; matrix products, arithmetic and copies ran while one was open for 2% of the time, Pallas kernels for 49%

profile of v11, /device:TPU:0, one launch (start us, length us, event | category | flops | bytes accessed | tf_op | source)
XLA Modules:
  0.0 52.6 jit_solution(11056008883705326753)
XLA Ops:
  0.0 0.0 copy-start.6
  0.0 0.5 collective-permute-start.3
  0.5 0.1 collective-permute-start.4
  0.6 6.9 %shard_map.64 = (bf16[384,384]{1,0:T(8,128)(2,1)S(1)}, f32[192,384]{1,0:T(8,128)S(1)}, f32[192,384]{1,0:T(8,128)S(1)}, bf16[8,384,384]{2,1,0:T(8,128)(2,1)S(1)},...) custom-call(s32[8]{0:T(128)} %charge.1, ...), custom_call_target="tpu_custom_call" | custom-call | flops 3623878656 | bytes 4718592 | tf_op jit(solution)/shard_map/pallas_call | solution.py:265
  7.4 0.0 copy-start
  7.5 1.4 %copy-done = bf16[8,384,384]{2,1,0:T(8,128)(2,1)} copy-done((bf16[8,384,384]{2,1,0:T(8,128)(2,1)}, bf16[8,384,384]{2,1,0:T(8,128)(2,1)S(1)}, u32[]{:S(2)}) %copy-start) | copy-done | bytes 2359320
  8.9 0.0 copy-start.2
  8.9 1.5 %copy-done.2 = bf16[8,384,384]{2,1,0:T(8,128)(2,1)} copy-done((bf16[8,384,384]{2,1,0:T(8,128)(2,1)}, bf16[8,384,384]{2,1,0:T(8,128)(2,1)S(1)}, u32[]{:S(2)}) %copy-start.2) | copy-done | bytes 2359320
  10.3 0.0 copy-start.4
  10.3 1.5 %copy-done.4 = bf16[8,384,384]{2,1,0:T(8,128)(2,1)} copy-done((bf16[8,384,384]{2,1,0:T(8,128)(2,1)}, bf16[8,384,384]{2,1,0:T(8,128)(2,1)S(1)}, u32[]{:S(2)}) %copy-start.4) | copy-done | bytes 2359320
  11.8 0.5 collective-permute-start.7
  12.3 1.0 %constant_dynamic-slice_fusion = bf16[1,384,384]{2,1,0:T(8,128)(2,1)S(1)} fusion(bf16[8,384,384]{2,1,0:T(8,128)(2,1)} %cells_far.1, s32[]{:T(128)S(6)} %select_n.3), kind=kLoop, calls=%fused_computation.2 | loop fusion | bytes 589828 | tf_op jit(solution)/shard_map/dynamic_slice | solution.py:291
  13.3 2.8 %collective-permute-start.5 = (bf16[1,384,384]{2,1,0:T(8,128)(2,1)S(1)}, bf16[1,384,384]{2,1,0:T(8,128)(2,1)S(1)}, u32[]{:S(2)}, u32[]{:S(2)}) collective-permute-start(bf16[1,384,384]{2,1,0:T(8,128)(2,1)S(1)} %constant_dynamic-slice_fusion), channel_id=1, source_target_pairs={{0,4},{1,29},{2,6},{3,31},{4,8},{5,1},{6,10},{7,3},{8,12},{9,5},{1... | collective-permute-start | bytes 884744 | tf_op jit(solution)/shard_map/ppermute | solution.py:292
  16.1 3.2 %collective-permute-start = (s32[8]{0:T(128)}, s32[8]{0:T(128)S(1)}, u32[]{:S(2)}, u32[]{:S(2)}) collective-permute-start(s32[8]{0:T(128)} %charge.1), channel_id=1, source_target_pairs={{0,1},{1,0},{2,3},{3,2},{4,5},{5,4},{6,7},{7,6},{8,9},{9,8},{10,11... | collective-permute-start | bytes 104 | tf_op jit(solution)/shard_map/ppermute | solution.py:280
  19.2 1.0 %collective-permute-done.charge_in = s32[8]{0:T(128)S(1)} collective-permute-done((s32[8]{0:T(128)}, s32[8]{0:T(128)S(1)}, u32[]{:S(2)}, u32[]{:S(2)}) %collective-permute-start) | collective-permute-done | bytes 64 | tf_op jit(solution)/shard_map/ppermute | solution.py:280
  20.2 0.0 copy-done.6
  20.2 0.3 collective-permute-start.1
  20.5 0.0 collective-permute-done.7
  20.5 0.2 collective-permute-start.2
  20.7 0.6 %collective-permute-done.1.couple_in = s32[8,8]{1,0:T(8,128)S(1)} collective-permute-done((s32[8,8]{1,0:T(8,128)S(1)}, s32[8,8]{1,0:T(8,128)S(1)}, u32[]{:S(2)}, u32[]{:S(2)}) %collective-permute-start.1) | collective-permute-done | bytes 288 | tf_op jit(solution)/shard_map/ppermute | solution.py:280
  21.3 1.5 %collective-permute-start.6 = (bf16[384,384]{1,0:T(8,128)(2,1)S(1)}, bf16[384,384]{1,0:T(8,128)(2,1)S(1)}, u32[]{:S(2)}, u32[]{:S(2)}) collective-permute-start(bf16[384,384]{1,0:T(8,128)(2,1)S(1)} %get-tuple-element.28), channel_id=1, source_target_pairs={{0,2},{1,3},{2,0},{3,1},{4,6},{5,7},{6,4},{7,5},{8,10},{9,11},{10,... | collective-permute-start | bytes 884744 | tf_op jit(solution)/shard_map/ppermute | solution.py:280
  22.9 0.0 collective-permute-done.2.amplitude_in
  22.9 0.9 %collective-permute-done.5.halo = bf16[1,384,384]{2,1,0:T(8,128)(2,1)S(1)} collective-permute-done((bf16[1,384,384]{2,1,0:T(8,128)(2,1)S(1)}, bf16[1,384,384]{2,1,0:T(8,128)(2,1)S(1)}, u32[]{:S(2)}, u32[]{:S(2)}) %collective-permute-start.5) | collective-permute-done | bytes 294944 | tf_op jit(solution)/shard_map/ppermute | solution.py:292
  23.8 0.0 collective-permute-done.3.left_in
  23.8 0.0 collective-permute-done.4.right_in
  23.8 0.0 copy-start.1
  23.8 1.7 %copy-done.1 = bf16[8,384,384]{2,1,0:T(8,128)(2,1)S(1)} copy-done((bf16[8,384,384]{2,1,0:T(8,128)(2,1)S(1)}, bf16[8,384,384]{2,1,0:T(8,128)(2,1)}, u32[]{:S(2)}) %copy-start.1) | copy-done | bytes 2359320
  25.5 0.0 copy-start.3
  25.5 1.7 %copy-done.3 = bf16[8,384,384]{2,1,0:T(8,128)(2,1)S(1)} copy-done((bf16[8,384,384]{2,1,0:T(8,128)(2,1)S(1)}, bf16[8,384,384]{2,1,0:T(8,128)(2,1)}, u32[]{:S(2)}) %copy-start.3) | copy-done | bytes 2359320
  27.1 0.0 copy-start.5
  27.2 1.7 %copy-done.5 = bf16[8,384,384]{2,1,0:T(8,128)(2,1)S(1)} copy-done((bf16[8,384,384]{2,1,0:T(8,128)(2,1)S(1)}, bf16[8,384,384]{2,1,0:T(8,128)(2,1)}, u32[]{:S(2)}) %copy-start.5) | copy-done | bytes 2359320
  28.8 7.2 %shard_map.65 = (bf16[384,384]{1,0:T(8,128)(2,1)S(1)}, bf16[4,384,384]{2,1,0:T(8,128)(2,1)S(1)}) custom-call(s32[8]{0:T(128)S(1)} %get-tuple-element.19.charge, s32[8,8]{1,0:T(8,128)S(1)} %get-tuple-element.20.couple, f32[8,8]{1,0:T(8,128)S(1)} %get-tuple-element.21.amplitude, s32[8]{0:T(128)S(1)} %collective-permute-done.charge_in, ...), custom_call_target="tpu_custom_call" | custom-call | flops 3623878656 | bytes 9437184 | tf_op jit(solution)/shard_map/pallas_call | solution.py:265
  36.1 1.7 %collective-permute-start.8 = (bf16[576,384]{1,0:T(8,128)(2,1)S(1)}, bf16[576,384]{1,0:T(8,128)(2,1)S(1)}, u32[]{:S(2)}, u32[]{:S(2)}) collective-permute-start(bf16[576,384]{1,0:T(8,128)(2,1)S(1)} %pad_maximum_fusion), channel_id=1, source_target_pairs={{0,2},{1,3},{2,0},{3,1},{4,6},{5,7},{6,4},{7,5},{8,10},{9,11},{10,... | collective-permute-start | bytes 1327112 | tf_op jit(solution)/shard_map/ppermute | solution.py:280
  37.9 11.4 %shard_map.66 = (f32[384,384]{1,0:T(8,128)S(1)}, f32[192,384]{1,0:T(8,128)S(1)}, f32[576,384]{1,0:T(8,128)S(1)}) custom-call(s32[8]{0:T(128)S(1)} %get-tuple-element.19.charge, s32[8,8]{1,0:T(8,128)S(1)} %get-tuple-element.20.couple, f32[8,8]{1,0:T(8,128)S(1)} %get-tuple-element.21.amplitude, s32[8]{0:T(128)S(1)} %collective-permute-done.charge_in, ...), custom_call_target="tpu_custom_call" | custom-call | flops 3623878656 | bytes 9437184 | tf_op jit(solution)/shard_map/pallas_call | solution.py:265
  49.3 0.0 collective-permute-done.6.direct_far
  49.3 0.1 mate_kernel.1
  49.3 0.1 collective-permute-start.9
  49.4 0.0 collective-permute-done.8
  49.5 0.6 %collective-permute-start.10 = (bf16[192,384]{1,0:T(8,128)(2,1)S(1)}, bf16[192,384]{1,0:T(8,128)(2,1)S(1)}, u32[]{:S(2)}, u32[]{:S(2)}) collective-permute-start(bf16[192,384]{1,0:T(8,128)(2,1)S(1)} %slice.4), channel_id=1, source_target_pairs={{0,1},{1,0},{2,3},{3,2},{4,5},{5,4},{6,7},{7,6},{8,9},{9,8},{10,11... | collective-permute-start | bytes 442376 | tf_op jit(solution)/shard_map/ppermute | solution.py:280
  50.0 1.2 %collective-permute-done.9 = bf16[576,384]{1,0:T(8,128)(2,1)S(1)} collective-permute-done((bf16[576,384]{1,0:T(8,128)(2,1)S(1)}, bf16[576,384]{1,0:T(8,128)(2,1)S(1)}, u32[]{:S(2)}, u32[]{:S(2)}) %collective-permute-start.9) | collective-permute-done | bytes 442400 | tf_op jit(solution)/shard_map/ppermute | solution.py:280
  51.2 0.2 collective-permute-done.10
  51.4 1.2 %total.1 = f32[8,96,384]{2,1,0:T(8,128)} custom-call(f32[4,96,384]{2,1,0:T(8,128)S(1)} %bitcast.8, f32[2,96,384]{2,1,0:T(8,128)S(1)} %bitcast.10, bf16[4,96,384]{2,1,0:T(8,128)(2,1)S(1)} %bitcast.6, bf16[6,96,384]{2,1,0:T(8,128)(2,1)S(1)} %bitcast.7, bf16[6,96,384]{2,1,0:T(8,128)(2,1)S(1)} %bitcast.9, bf16[2,96,384]{2,1,0:T(8,128)(2,1)S(1)} %bitcast.11), custom_call_target="tpu_custom_call" | custom-call | tf_op jit(solution)/shard_map/total/pallas_call | solution.py:373
  (3 shorter events, 0.1 us)
Async XLA Ops:
  0.0 20.2 %copy-start.6 = (s32[8,8]{1,0:T(8,128)S(1)}, s32[8,8]{1,0:T(8,128)}, u32[]{:S(2)}) copy-start(s32[8,8]{1,0:T(8,128)} %couple.1) | copy-start | bytes 772
  0.0 23.8 %collective-permute-start.3 = (bf16[8,384,384]{2,1,0:T(8,128)(2,1)}, bf16[8,384,384]{2,1,0:T(8,128)(2,1)S(1)}, u32[]{:S(2)}, u32[]{:S(2)}) collective-permute-start(bf16[8,384,384]{2,1,0:T(8,128)(2,1)} %left_far.1), channel_id=1, source_target_pairs={{0,1},{1,0},{2,3},{3,2},{4,5},{5,4},{6,7},{7,6},{8,9},{9,8},{10,11... | collective-permute-start | bytes 7077896 | tf_op jit(solution)/shard_map/ppermute | solution.py:280
  0.5 23.3 %collective-permute-start.4 = (bf16[8,384,384]{2,1,0:T(8,128)(2,1)}, bf16[8,384,384]{2,1,0:T(8,128)(2,1)}, u32[]{:S(2)}, u32[]{:S(2)}) collective-permute-start(bf16[8,384,384]{2,1,0:T(8,128)(2,1)} %right_far.1), channel_id=1, source_target_pairs={{0,1},{1,0},{2,3},{3,2},{4,5},{5,4},{6,7},{7,6},{8,9},{9,8},{10,11... | collective-permute-start | bytes 7077896 | tf_op jit(solution)/shard_map/ppermute | solution.py:280
  7.4 1.4 %copy-start = (bf16[8,384,384]{2,1,0:T(8,128)(2,1)}, bf16[8,384,384]{2,1,0:T(8,128)(2,1)S(1)}, u32[]{:S(2)}) copy-start(bf16[8,384,384]{2,1,0:T(8,128)(2,1)S(1)} %get-tuple-element.22.left) | copy-start | bytes 7077892
  8.9 1.5 %copy-start.2 = (bf16[8,384,384]{2,1,0:T(8,128)(2,1)}, bf16[8,384,384]{2,1,0:T(8,128)(2,1)S(1)}, u32[]{:S(2)}) copy-start(bf16[8,384,384]{2,1,0:T(8,128)(2,1)S(1)} %get-tuple-element.23.right) | copy-start | bytes 7077892
  10.3 1.5 %copy-start.4 = (bf16[8,384,384]{2,1,0:T(8,128)(2,1)}, bf16[8,384,384]{2,1,0:T(8,128)(2,1)S(1)}, u32[]{:S(2)}) copy-start(bf16[8,384,384]{2,1,0:T(8,128)(2,1)S(1)} %get-tuple-element.24.cells) | copy-start | bytes 7077892
  11.8 8.7 %collective-permute-start.7 = (f32[192,384]{1,0:T(8,128)S(1)}, f32[192,384]{1,0:T(8,128)S(1)}, u32[]{:S(2)}, u32[]{:S(2)}) collective-permute-start(f32[192,384]{1,0:T(8,128)S(1)} %get-tuple-element.31), channel_id=1, source_target_pairs={{0,1},{1,0},{2,3},{3,2},{4,5},{5,4},{6,7},{7,6},{8,9},{9,8},{10,11... | collective-permute-start | bytes 884744 | tf_op jit(solution)/shard_map/ppermute | solution.py:280
  13.3 10.5 %collective-permute-start.5 = (bf16[1,384,384]{2,1,0:T(8,128)(2,1)S(1)}, bf16[1,384,384]{2,1,0:T(8,128)(2,1)S(1)}, u32[]{:S(2)}, u32[]{:S(2)}) collective-permute-start(bf16[1,384,384]{2,1,0:T(8,128)(2,1)S(1)} %constant_dynamic-slice_fusion), channel_id=1, source_target_pairs={{0,4},{1,29},{2,6},{3,31},{4,8},{5,1},{6,10},{7,3},{8,12},{9,5},{1... | collective-permute-start | bytes 884744 | tf_op jit(solution)/shard_map/ppermute | solution.py:292
  16.1 4.1 %collective-permute-start = (s32[8]{0:T(128)}, s32[8]{0:T(128)S(1)}, u32[]{:S(2)}, u32[]{:S(2)}) collective-permute-start(s32[8]{0:T(128)} %charge.1), channel_id=1, source_target_pairs={{0,1},{1,0},{2,3},{3,2},{4,5},{5,4},{6,7},{7,6},{8,9},{9,8},{10,11... | collective-permute-start | bytes 104 | tf_op jit(solution)/shard_map/ppermute | solution.py:280
  20.2 1.2 %collective-permute-start.1 = (s32[8,8]{1,0:T(8,128)S(1)}, s32[8,8]{1,0:T(8,128)S(1)}, u32[]{:S(2)}, u32[]{:S(2)}) collective-permute-start(s32[8,8]{1,0:T(8,128)S(1)} %copy-done.6), channel_id=1, source_target_pairs={{0,1},{1,0},{2,3},{3,2},{4,5},{5,4},{6,7},{7,6},{8,9},{9,8},{10,11... | collective-permute-start | bytes 776 | tf_op jit(solution)/shard_map/ppermute | solution.py:280
  20.5 2.3 %collective-permute-start.2 = (f32[8,8]{1,0:T(8,128)}, f32[8,8]{1,0:T(8,128)S(1)}, u32[]{:S(2)}, u32[]{:S(2)}) collective-permute-start(f32[8,8]{1,0:T(8,128)} %amplitude.1), channel_id=1, source_target_pairs={{0,1},{1,0},{2,3},{3,2},{4,5},{5,4},{6,7},{7,6},{8,9},{9,8},{10,11... | collective-permute-start | bytes 776 | tf_op jit(solution)/shard_map/ppermute | solution.py:280
  21.3 27.9 %collective-permute-start.6 = (bf16[384,384]{1,0:T(8,128)(2,1)S(1)}, bf16[384,384]{1,0:T(8,128)(2,1)S(1)}, u32[]{:S(2)}, u32[]{:S(2)}) collective-permute-start(bf16[384,384]{1,0:T(8,128)(2,1)S(1)} %get-tuple-element.28), channel_id=1, source_target_pairs={{0,2},{1,3},{2,0},{3,1},{4,6},{5,7},{6,4},{7,5},{8,10},{9,11},{10,... | collective-permute-start | bytes 884744 | tf_op jit(solution)/shard_map/ppermute | solution.py:280
  23.8 1.7 %copy-start.1 = (bf16[8,384,384]{2,1,0:T(8,128)(2,1)S(1)}, bf16[8,384,384]{2,1,0:T(8,128)(2,1)}, u32[]{:S(2)}) copy-start(bf16[8,384,384]{2,1,0:T(8,128)(2,1)} %copy-done) | copy-start | bytes 7077892
  25.5 1.7 %copy-start.3 = (bf16[8,384,384]{2,1,0:T(8,128)(2,1)S(1)}, bf16[8,384,384]{2,1,0:T(8,128)(2,1)}, u32[]{:S(2)}) copy-start(bf16[8,384,384]{2,1,0:T(8,128)(2,1)} %copy-done.2) | copy-start | bytes 7077892
  27.1 1.7 %copy-start.5 = (bf16[8,384,384]{2,1,0:T(8,128)(2,1)S(1)}, bf16[8,384,384]{2,1,0:T(8,128)(2,1)}, u32[]{:S(2)}) copy-start(bf16[8,384,384]{2,1,0:T(8,128)(2,1)} %copy-done.4) | copy-start | bytes 7077892
  36.1 13.3 %collective-permute-start.8 = (bf16[576,384]{1,0:T(8,128)(2,1)S(1)}, bf16[576,384]{1,0:T(8,128)(2,1)S(1)}, u32[]{:S(2)}, u32[]{:S(2)}) collective-permute-start(bf16[576,384]{1,0:T(8,128)(2,1)S(1)} %pad_maximum_fusion), channel_id=1, source_target_pairs={{0,2},{1,3},{2,0},{3,1},{4,6},{5,7},{6,4},{7,5},{8,10},{9,11},{10,... | collective-permute-start | bytes 1327112 | tf_op jit(solution)/shard_map/ppermute | solution.py:280
  49.3 1.9 %collective-permute-start.9 = (bf16[576,384]{1,0:T(8,128)(2,1)S(1)}, bf16[576,384]{1,0:T(8,128)(2,1)S(1)}, u32[]{:S(2)}, u32[]{:S(2)}) collective-permute-start(bf16[576,384]{1,0:T(8,128)(2,1)S(1)} %mate_kernel.1), channel_id=1, source_target_pairs={{0,1},{1,0},{2,3},{3,2},{4,5},{5,4},{6,7},{7,6},{8,9},{9,8},{10,11... | collective-permute-start | bytes 1327112 | tf_op jit(solution)/shard_map/ppermute | solution.py:280
  49.5 2.0 %collective-permute-start.10 = (bf16[192,384]{1,0:T(8,128)(2,1)S(1)}, bf16[192,384]{1,0:T(8,128)(2,1)S(1)}, u32[]{:S(2)}, u32[]{:S(2)}) collective-permute-start(bf16[192,384]{1,0:T(8,128)(2,1)S(1)} %slice.4), channel_id=1, source_target_pairs={{0,1},{1,0},{2,3},{3,2},{4,5},{5,4},{6,7},{7,6},{8,9},{9,8},{10,11... | collective-permute-start | bytes 442376 | tf_op jit(solution)/shard_map/ppermute | solution.py:280

commit v12 on v8

--- a/solution.py
+++ b/solution.py
@@ -52,19 +52,17 @@
     return lax.psum_scatter(accumulated, "op", scatter_dimension=1, tiled=True)
 
 
-def middle_of(k, small, own, left, sources, middles, first_target, targets, chip, core):
-    charge, couple, amplitude = small
+def middle_of(k, table, own, left, sources, middles, first_target, targets, chip, core):
     states = sources.shape[-1]
     half = middles.shape[0] // (CORES * targets)
-    shift = 1 - charge[own]
+    shift = 1 - table[table.shape[0] - 1, own].astype(jnp.int32)
     wide = jnp.concatenate([sources[shift + t] for t in range(targets)], axis=1)
     rows = jnp.concatenate(
         [left[own, pl.ds(row_of(chip, owner, half), half)] for owner in (core, 1 - core)], axis=0
     )
     middle = jnp.dot(rows, wide, preferred_element_type=jnp.float32)
     for t in range(targets):
-        at = first_target + t
-        factor = amplitude[own, at] * couple[own, at].astype(jnp.float32)
+        factor = table[own, first_target + t]
         block = middle[:, t * states : (t + 1) * states].astype(jnp.bfloat16)
         block = (block.astype(jnp.float32) * factor).astype(jnp.bfloat16)
         for part in range(CORES):
@@ -109,10 +107,26 @@
     return copy
 
 
+def first_kernel(
+    charge, couple, amplitude, cells_far, border, table, charge_here, couple_here, amplitude_here, sem
+):
+    _, core = position()
+    operators, sectors = couple.shape
+    copies = [
+        begin(charge, charge_here.at[0], sem.at[0]),
+        begin(couple, couple_here, sem.at[1]),
+        begin(amplitude, amplitude_here, sem.at[2]),
+        begin(cells_far.at[(sectors - 1) * (1 - core)], border.at[0], sem.at[3]),
+    ]
+    for copy in copies:
+        copy.wait()
+    table[:operators, :sectors] = amplitude_here[...] * couple_here[...].astype(jnp.float32)
+    table[operators:, :operators] = charge_here[...].astype(jnp.float32)
+
+
 def inner_far_kernel(
-    charge, couple, amplitude, left_far, right_far, cells_far,
-    direct, keep, send, left, right, cells, charge_kept, couple_kept, amplitude_kept, middles,
-    charge_here, couple_here, amplitude_here, small_sem, cell_sem, left_sem, right_sem,
+    table, left_far, right_far, cells_far, direct, keep, send, left, right, cells, middles,
+    cell_sem, left_sem, right_sem,
 ):
     chip, core = position()
     operators = left.shape[0]
@@ -128,33 +142,19 @@
     def cell(s):
         return begin(cells_far.at[s], cells.at[s], cell_sem.at[s])
 
-    small = [
-        begin(charge, charge_here, small_sem.at[0]),
-        begin(couple, couple_here, small_sem.at[1]),
-        begin(amplitude, amplitude_here, small_sem.at[2]),
-    ]
     first = [cell(s) for s in inside]
-    lefts = [begin(*rows(k, 1 - chip), left_sem.at[0, k]) for k in range(AHEAD)]
-    for copy in small:
-        copy.wait()
-    lefts += [begin(*rows(k, 1 - chip), left_sem.at[0, k]) for k in range(AHEAD, operators)]
+    lefts = [begin(*rows(k, 1 - chip), left_sem.at[0, k]) for k in range(operators)]
     for copy in first + lefts[:AHEAD]:
         copy.wait()
     rights = [begin(right_far.at[k], right.at[k], right_sem.at[k]) for k in range(operators)]
     later = [begin(*rows(k, chip), left_sem.at[1, k]) for k in range(operators)]
     later += [cell(s) for s in range(sectors) if s not in inside]
-    later += [
-        begin(charge, charge_kept, small_sem.at[3]),
-        begin(couple, couple_kept, small_sem.at[4]),
-        begin(amplitude, amplitude_kept, small_sem.at[5]),
-    ]
     sources = cells.at[pl.ds(EDGE - 1, targets + 2)]
-    here = (charge_here, couple_here, amplitude_here)
     for k in range(operators):
         if k == AHEAD:
             for copy in lefts[AHEAD:]:
                 copy.wait()
-        middle_of(k, here, k, left, sources, middles, EDGE, targets, 1 - chip, core)
+        middle_of(k, table, k, left, sources, middles, EDGE, targets, 1 - chip, core)
     for copy in rights:
         copy.wait()
     near, far = halves(direct)
@@ -163,30 +163,29 @@
         copy.wait()
 
 
-def inner_own_kernel(charge, couple, amplitude, left, right, cells, keep, send, middles):
+def inner_own_kernel(table, left, right, cells, keep, send, middles):
     chip, core = position()
     operators = left.shape[0]
     targets = cells.shape[0] - 2 * EDGE
     inside = cells.at[pl.ds(EDGE - 1, targets + 2)]
     for k in range(operators):
-        middle_of(k, (charge, couple, amplitude), k, left, inside, middles, EDGE, targets, chip, core)
+        middle_of(k, table, k, left, inside, middles, EDGE, targets, chip, core)
     summed(jnp.concatenate([right[k] for k in range(operators)], axis=1), middles, (keep, send))
 
 
 def edge_products(groups, sources, middles, results, sectors, chip, core):
     k = 0
     first_target = (sectors - EDGE) * core
-    for small, left, right in groups:
+    for table, left, right in groups:
         for own in range(left.shape[0]):
-            middle_of(k, small, own, left, sources, middles, first_target, EDGE, chip, core)
+            middle_of(k, table, own, left, sources, middles, first_target, EDGE, chip, core)
             k += 1
     wide = jnp.concatenate([right[own] for _, _, right in groups for own in range(right.shape[0])], axis=1)
     summed(wide, middles, results)
 
 
 def edge_far_kernel(
-    charge, couple, amplitude, charge_in, couple_in, amplitude_in, left, right, left_in, right_in,
-    cells, halo, send, sources, middles, sem,
+    table, table_in, left, right, left_in, right_in, cells, halo, send, sources, middles, sem,
 ):
     chip, core = position()
     sectors = cells.shape[0]
@@ -201,23 +200,15 @@
         copy.start()
     for copy in copies:
         copy.wait()
-    groups = (
-        ((charge, couple, amplitude), left, right),
-        ((charge_in, couple_in, amplitude_in), left_in, right_in),
-    )
+    groups = ((table, left, right), (table_in, left_in, right_in))
     edge_products(groups, sources, middles, halves(send), sectors, 1 - chip, core)
 
 
-def edge_own_kernel(
-    charge, couple, amplitude, charge_in, couple_in, amplitude_in, left, right, left_in, right_in,
-    sources, keep, send, middles,
+def edge_own(
+    sectors, table, table_in, left, right, left_in, right_in, sources, keep, send, middles
 ):
     chip, core = position()
-    sectors = couple.shape[1]
-    groups = (
-        ((charge, couple, amplitude), left, right),
-        ((charge_in, couple_in, amplitude_in), left_in, right_in),
-    )
+    groups = ((table, left, right), (table_in, left_in, right_in))
     edge_products(groups, sources, middles, (keep, send), sectors, chip, core)
 
 
@@ -277,26 +268,41 @@
     for s in range(sec):
         for o in range(op):
             ring.append((s * op + o, (s + 1 if o % CORES == 0 else s - 1) % sec * op + o))
-    core = lax.axis_index("op") & (CORES - 1)
-    border = lax.dynamic_slice_in_dim(wavefunction, (sectors - 1) * (1 - core), 1, 0)
+
+    def in_hbm(*values):
+        return [pltpu.with_memory_space_constraint(value, pltpu.HBM) for value in values]
+
+    border, table = pl.pallas_call(
+        first_kernel,
+        out_shape=[
+            pltpu.VMEM((1, states, states), narrow),
+            pltpu.VMEM((operators + 1, max(operators, sectors)), wide),
+        ],
+        in_specs=[LARGE] * 4,
+        out_specs=[BLOCK] * 2,
+        scratch_shapes=[
+            pltpu.VMEM((1, operators), charge.dtype),
+            pltpu.VMEM(couple.shape, couple.dtype),
+            pltpu.VMEM(amplitude.shape, amplitude.dtype),
+            pltpu.SemaphoreType.DMA((4,)),
+        ],
+        compiler_params=pltpu.CompilerParams(vmem_limit_bytes=4 * MIB),
+        name="first_kernel",
+    )(*in_hbm(charge, couple, amplitude, wavefunction))
     halo = lax.ppermute(border, ("sec", "op"), ring)
     left_in = over_op(left_ops, 1)
     right_in = over_op(right_ops, 1)
 
-    small = (charge, couple, amplitude)
-    small_in = [over_op(value, 1) for value in small]
-
-    def in_hbm(*values):
-        return [pltpu.with_memory_space_constraint(value, pltpu.HBM) for value in values]
+    table_in = over_op(table, 1)
 
     direct_rows = inner // 2 * half
     reduced = shape(inner * half - direct_rows, states)
-    direct, keep, send, left, right, cells, *here = run(
+    direct, keep, send, left, right, cells = run(
         inner_far_kernel,
         operators,
         inner,
-        in_hbm(*small, left_ops, right_ops, wavefunction),
-        [LARGE] * 6,
+        [table, *in_hbm(left_ops, right_ops, wavefunction)],
+        [SMALL] + [LARGE] * 3,
         [
             shape(CORES * direct_rows, states, dtype=narrow),
             reduced,
@@ -304,14 +310,9 @@
             pltpu.VMEM(left_ops.shape, narrow),
             pltpu.VMEM(right_ops.shape, narrow),
             pltpu.VMEM(wavefunction.shape, narrow),
-            *[pltpu.VMEM(value.shape, value.dtype) for value in small],
         ],
-        [BLOCK] * 9,
+        [BLOCK] * 6,
         [
-            pltpu.SMEM(charge.shape, charge.dtype),
-            pltpu.SMEM(couple.shape, couple.dtype),
-            pltpu.SMEM(amplitude.shape, amplitude.dtype),
-            pltpu.SemaphoreType.DMA((6,)),
             pltpu.SemaphoreType.DMA((sectors,)),
             pltpu.SemaphoreType.DMA((2, operators)),
             pltpu.SemaphoreType.DMA((operators,)),
@@ -320,8 +321,8 @@
     direct_far = over_op(direct, CORES)
     send_in = over_op(send, 1)
 
-    held = [*here, *small_in, left, right, left_in, right_in]
-    held_specs = [SMALL] * 6 + [BLOCK] * 4
+    held = [table, table_in, left, right, left_in, right_in]
+    held_specs = [SMALL] * 2 + [BLOCK] * 4
     edge_send, sources = run(
         edge_far_kernel,
         CORES * operators,
@@ -339,8 +340,8 @@
         inner_own_kernel,
         operators,
         inner,
-        [*here, left, right, cells],
-        [SMALL] * 3 + [BLOCK] * 3,
+        [table, left, right, cells],
+        [SMALL] + [BLOCK] * 3,
         [block, block],
         [BLOCK, BLOCK],
         [],
@@ -348,6 +349,10 @@
     mate = inner_send[:direct_rows] + direct_far[direct_rows:].astype(wide)
     inner_chip = over_op(jnp.concatenate([mate, inner_send[direct_rows:]], axis=0), 1)
     edge_wide = shape(EDGE * half, states)
+
+    def edge_own_kernel(*refs):
+        edge_own(sectors, *refs)
+
     near_own, near_mate = run(
         edge_own_kernel,
         CORES * operators,

time: 57.2 us -> 49 us (0.86)
  local copies, waits for them, and re-layouts: 10.3 us -> 0 us
  waiting for transfers between devices: 8.55 us -> 13 us
  starting transfers between devices: 9.01 us -> 7.71 us
  other arithmetic: 1.16 us -> 0.21 us
    unnamed x16 -> x0, local copies, waits for them, and re-layouts: 9.34 us -> none
    ppermute x1, waiting for transfers between devices: 4.08 us -> 7.62 us  [shards(): halo = lax.ppermute(border, ('sec', 'op'), ring)]
    ppermute x10 -> x8, starting transfers between devices: 7.28 us -> 6 us  [over_op(): return lax.ppermute(value, 'op', [(i, i ^ flip) for i in range(op)])]
    pallas_call x0 -> x1, Pallas kernels: none -> 1.05 us  [shards(): pl.pallas_call(first_kernel, out_shape=[pltpu.VMEM((1, states, states), n...]
    dynamic_slice x1 -> x0, local copies, waits for them, and re-layouts: 1 us -> none  [shards(): lax.dynamic_slice_in_dim(wavefunction, (sectors - 1) * (1 - core), 1, 0)]
    convert_element_type x1, other arithmetic: 0.99 us -> 0.04 us  [shards(): (keep + send_in).astype(narrow)]
    ppermute x10 -> x8, waiting for transfers between devices: 4.47 us -> 5.35 us  [over_op(): return lax.ppermute(value, 'op', [(i, i ^ flip) for i in range(op)])]
    pallas_call x4, Pallas kernels: 26.5 us -> 25.7 us  [run(): pl.pallas_call(kernel, out_shape=outs, in_specs=in_specs, out_specs=out_s...]
  transfers between devices with their start and end apart: 11 -> 9, of which waited for: 4 -> 4; matrix products, arithmetic and copies ran while one was open for 4% -> 0% of each run, Pallas kernels for 34% -> 42%
where the time goes in v12:
time: 49 us; the launch traced here: 48.9 us
  Pallas kernels  27.9 us (57%)
  waiting for transfers between devices  13 us (27%)
  starting transfers between devices  7.71 us (16%)
    pallas_call x4, Pallas kernels, run(): pl.pallas_call(kernel, out_shape=outs, in_specs=in_specs, out_specs=out_s...  25.7 us
    ppermute x1, waiting for transfers between devices, shards(): halo = lax.ppermute(border, ('sec', 'op'), ring)  7.62 us
    ppermute x8, starting transfers between devices, over_op(): return lax.ppermute(value, 'op', [(i, i ^ flip) for i in range(op)])  6 us
    ppermute x8, waiting for transfers between devices, over_op(): return lax.ppermute(value, 'op', [(i, i ^ flip) for i in range(op)])  5.35 us
    ppermute x1, starting transfers between devices, shards(): halo = lax.ppermute(border, ('sec', 'op'), ring)  1.71 us
    pallas_call x1, Pallas kernels, shards(): pl.pallas_call(sum_kernel, out_shape=shape(sectors, half, states), in_spe...  1.13 us
    pallas_call x1, Pallas kernels, shards(): pl.pallas_call(first_kernel, out_shape=[pltpu.VMEM((1, states, states), n...  1.05 us
  transfers between devices with their start and end apart: 9, of which 4 were waited for; matrix products, arithmetic and copies ran while one was open for 0% of the time, Pallas kernels for 42%

profile of v12, /device:TPU:0, one launch (start us, length us, event | category | flops | bytes accessed | tf_op | source)
XLA Modules:
  0.0 48.9 jit_solution(10005714649689440556)
XLA Ops:
  0.0 0.5 %collective-permute-start.3 = (bf16[8,384,384]{2,1,0:T(8,128)(2,1)}, bf16[8,384,384]{2,1,0:T(8,128)(2,1)S(1)}, u32[]{:S(2)}, u32[]{:S(2)}) collective-permute-start(bf16[8,384,384]{2,1,0:T(8,128)(2,1)} %left_far.1), channel_id=1, source_target_pairs={{0,1},{1,0},{2,3},{3,2},{4,5},{5,4},{6,7},{7,6},{8,9},{9,8},{10,11... | collective-permute-start | bytes 7077896 | tf_op jit(solution)/shard_map/ppermute | solution.py:261
  0.5 0.0 collective-permute-start.4
  0.5 1.0 %first_kernel.1 = (bf16[1,384,384]{2,1,0:T(8,128)(2,1)S(1)}, f32[9,8]{1,0:T(8,128)S(1)}) custom-call(s32[8]{0:T(128)} %charge.1, s32[8,8]{1,0:T(8,128)} %couple.1, f32[8,8]{1,0:T(8,128)} %amplitude.1, bf16[8,384,384]{2,1,0:T(8,128)(2,1)} %cells_far.3), custom_call_target="tpu_custom_call" | custom-call | tf_op jit(solution)/shard_map/first_kernel/pallas_call | solution.py:275
  1.6 0.6 %collective-permute-start.2 = (f32[9,8]{1,0:T(8,128)S(1)}, f32[9,8]{1,0:T(8,128)S(1)}, u32[]{:S(2)}, u32[]{:S(2)}) collective-permute-start(f32[9,8]{1,0:T(8,128)S(1)} %get-tuple-element.19.table.refs_0_), channel_id=1, source_target_pairs={{0,1},{1,0},{2,3},{3,2},{4,5},{5,4},{6,7},{7,6},{8,9},{9,8},{10,11... | collective-permute-start | bytes 872 | tf_op jit(solution)/shard_map/ppermute | solution.py:261
  2.1 7.8 %shard_map.64 = (bf16[384,384]{1,0:T(8,128)(2,1)S(1)}, f32[192,384]{1,0:T(8,128)S(1)}, f32[192,384]{1,0:T(8,128)S(1)}, bf16[8,384,384]{2,1,0:T(8,128)(2,1)S(1)},...) custom-call(f32[9,8]{1,0:T(8,128)S(1)} %get-tuple-element.19.table.refs_0_, ...), custom_call_target="tpu_custom_call" | custom-call | flops 3623878656 | bytes 4718592 | tf_op jit(solution)/shard_map/pallas_call | solution.py:246
  9.9 0.1 collective-permute-start.6
  10.0 2.9 %collective-permute-start = (bf16[384,384]{1,0:T(8,128)(2,1)S(1)}, bf16[384,384]{1,0:T(8,128)(2,1)S(1)}, u32[]{:S(2)}, u32[]{:S(2)}) collective-permute-start(bf16[384,384]{1,0:T(8,128)(2,1)S(1)} %get-tuple-element.25), channel_id=1, source_target_pairs={{0,2},{1,3},{2,0},{3,1},{4,6},{5,7},{6,4},{7,5},{8,10},{9,11},{10,... | collective-permute-start | bytes 884744 | tf_op jit(solution)/shard_map/ppermute | solution.py:261
  12.9 5.4 %shard_map.65 = (f32[384,384]{1,0:T(8,128)S(1)}, f32[384,384]{1,0:T(8,128)S(1)}) custom-call(f32[9,8]{1,0:T(8,128)S(1)} %get-tuple-element.19.table.refs_0_, bf16[8,384,384]{2,1,0:T(8,128)(2,1)S(1)} %get-tuple-element.20.left.refs_2_, bf16[8,384,384]{2,1,0:T(8,128)(2,1)S(1)} %get-tuple-element.21.right.refs_3_, bf16[8,384,384]{2,1,0:T(8,128)(2,1)S(1)} %get-tuple-element.22.cells), custom_call_target="tpu_custom_call" | custom-call | flops 3623878656 | bytes 4718592 | tf_op jit(solution)/shard_map/pallas_call | solution.py:246
  18.4 1.8 %collective-permute-done = bf16[384,384]{1,0:T(8,128)(2,1)S(1)} collective-permute-done((bf16[384,384]{1,0:T(8,128)(2,1)S(1)}, bf16[384,384]{1,0:T(8,128)(2,1)S(1)}, u32[]{:S(2)}, u32[]{:S(2)}) %collective-permute-start) | collective-permute-done | bytes 294944 | tf_op jit(solution)/shard_map/ppermute | solution.py:261
  20.2 1.7 %collective-permute-start.5 = (bf16[1,384,384]{2,1,0:T(8,128)(2,1)S(1)}, bf16[1,384,384]{2,1,0:T(8,128)(2,1)S(1)}, u32[]{:S(2)}, u32[]{:S(2)}) collective-permute-start(bf16[1,384,384]{2,1,0:T(8,128)(2,1)S(1)} %get-tuple-element.26), channel_id=1, source_target_pairs={{0,4},{1,29},{2,6},{3,31},{4,8},{5,1},{6,10},{7,3},{8,12},{9,5},{1... | collective-permute-start | bytes 884744 | tf_op jit(solution)/shard_map/ppermute | solution.py:292
  21.9 0.1 convert_add_fusion.1
  22.0 0.0 collective-permute-done.6
  22.0 0.0 collective-permute-done.2.table_in.refs_1_
  22.0 7.6 %collective-permute-done.5.halo = bf16[1,384,384]{2,1,0:T(8,128)(2,1)S(1)} collective-permute-done((bf16[1,384,384]{2,1,0:T(8,128)(2,1)S(1)}, bf16[1,384,384]{2,1,0:T(8,128)(2,1)S(1)}, u32[]{:S(2)}, u32[]{:S(2)}) %collective-permute-start.5) | collective-permute-done | bytes 294944 | tf_op jit(solution)/shard_map/ppermute | solution.py:292
  29.6 0.0 collective-permute-done.3.left_in.refs_4_
  29.6 0.0 collective-permute-done.4.right_in.refs_5_
  29.6 6.4 %shard_map.66 = (bf16[384,384]{1,0:T(8,128)(2,1)S(1)}, bf16[4,384,384]{2,1,0:T(8,128)(2,1)S(1)}) custom-call(f32[9,8]{1,0:T(8,128)S(1)} %get-tuple-element.19.table.refs_0_, f32[9,8]{1,0:T(8,128)S(1)} %collective-permute-done.2.table_in.refs_1_, bf16[8,384,384]{2,1,0:T(8,128)(2,1)S(1)} %get-tuple-element.20.left.refs_2_, ...), custom_call_target="tpu_custom_call" | custom-call | flops 3623878656 | bytes 9437184 | tf_op jit(solution)/shard_map/pallas_call | solution.py:246
  36.1 1.8 %collective-permute-start.7 = (bf16[576,384]{1,0:T(8,128)(2,1)S(1)}, bf16[576,384]{1,0:T(8,128)(2,1)S(1)}, u32[]{:S(2)}, u32[]{:S(2)}) collective-permute-start(bf16[576,384]{1,0:T(8,128)(2,1)S(1)} %pad_maximum_fusion.1), channel_id=1, source_target_pairs={{0,2},{1,3},{2,0},{3,1},{4,6},{5,7},{6,4},{7,5},{8,10},{9,11},{10,... | collective-permute-start | bytes 1327112 | tf_op jit(solution)/shard_map/ppermute | solution.py:261
  37.9 0.1 collective-permute-start.1
  38.0 6.1 %shard_map.67 = (f32[192,384]{1,0:T(8,128)S(1)}, f32[192,384]{1,0:T(8,128)S(1)}) custom-call(f32[9,8]{1,0:T(8,128)S(1)} %get-tuple-element.19.table.refs_0_, f32[9,8]{1,0:T(8,128)S(1)} %collective-permute-done.2.table_in.refs_1_, bf16[8,384,384]{2,1,0:T(8,128)(2,1)S(1)} %get-tuple-element.20.left.refs_2_, ...), custom_call_target="tpu_custom_call" | custom-call | flops 3623878656 | bytes 9437184 | tf_op jit(solution)/shard_map/pallas_call | solution.py:246
  44.1 2.0 %collective-permute-done.7 = bf16[576,384]{1,0:T(8,128)(2,1)S(1)} collective-permute-done((bf16[576,384]{1,0:T(8,128)(2,1)S(1)}, bf16[576,384]{1,0:T(8,128)(2,1)S(1)}, u32[]{:S(2)}, u32[]{:S(2)}) %collective-permute-start.7) | collective-permute-done | bytes 442400 | tf_op jit(solution)/shard_map/ppermute | solution.py:261
  46.1 0.1 collective-permute-start.8
  46.2 0.0 collective-permute-done.1
  46.2 1.6 %collective-permute-done.8 = f32[192,384]{1,0:T(8,128)S(1)} collective-permute-done((f32[192,384]{1,0:T(8,128)S(1)}, f32[192,384]{1,0:T(8,128)S(1)}, u32[]{:S(2)}, u32[]{:S(2)}) %collective-permute-start.8) | collective-permute-done | bytes 294944 | tf_op jit(solution)/shard_map/ppermute | solution.py:261
  47.7 1.1 %total.1 = f32[8,96,384]{2,1,0:T(8,128)} custom-call(f32[4,96,384]{2,1,0:T(8,128)S(1)} %bitcast.8, f32[4,96,384]{2,1,0:T(8,128)S(1)} %bitcast.9, bf16[4,96,384]{2,1,0:T(8,128)(2,1)S(1)} %bitcast.7, bf16[6,96,384]{2,1,0:T(8,128)(2,1)S(1)} %bitcast.6, f32[2,96,384]{2,1,0:T(8,128)S(1)} %bitcast.10, f32[2,96,384]{2,1,0:T(8,128)S(1)} %bitcast.11), custom_call_target="tpu_custom_call" | custom-call | tf_op jit(solution)/shard_map/total/pallas_call | solution.py:369
  (4 shorter events, 0.2 us)
Async XLA Ops:
  0.0 29.6 %collective-permute-start.3 = (bf16[8,384,384]{2,1,0:T(8,128)(2,1)}, bf16[8,384,384]{2,1,0:T(8,128)(2,1)S(1)}, u32[]{:S(2)}, u32[]{:S(2)}) collective-permute-start(bf16[8,384,384]{2,1,0:T(8,128)(2,1)} %left_far.1), channel_id=1, source_target_pairs={{0,1},{1,0},{2,3},{3,2},{4,5},{5,4},{6,7},{7,6},{8,9},{9,8},{10,11... | collective-permute-start | bytes 7077896 | tf_op jit(solution)/shard_map/ppermute | solution.py:261
  0.5 29.2 %collective-permute-start.4 = (bf16[8,384,384]{2,1,0:T(8,128)(2,1)}, bf16[8,384,384]{2,1,0:T(8,128)(2,1)S(1)}, u32[]{:S(2)}, u32[]{:S(2)}) collective-permute-start(bf16[8,384,384]{2,1,0:T(8,128)(2,1)} %right_far.1), channel_id=1, source_target_pairs={{0,1},{1,0},{2,3},{3,2},{4,5},{5,4},{6,7},{7,6},{8,9},{9,8},{10,11... | collective-permute-start | bytes 7077896 | tf_op jit(solution)/shard_map/ppermute | solution.py:261
  1.6 20.4 %collective-permute-start.2 = (f32[9,8]{1,0:T(8,128)S(1)}, f32[9,8]{1,0:T(8,128)S(1)}, u32[]{:S(2)}, u32[]{:S(2)}) collective-permute-start(f32[9,8]{1,0:T(8,128)S(1)} %get-tuple-element.19.table.refs_0_), channel_id=1, source_target_pairs={{0,1},{1,0},{2,3},{3,2},{4,5},{5,4},{6,7},{7,6},{8,9},{9,8},{10,11... | collective-permute-start | bytes 872 | tf_op jit(solution)/shard_map/ppermute | solution.py:261
  9.9 12.0 %collective-permute-start.6 = (f32[192,384]{1,0:T(8,128)S(1)}, f32[192,384]{1,0:T(8,128)S(1)}, u32[]{:S(2)}, u32[]{:S(2)}) collective-permute-start(f32[192,384]{1,0:T(8,128)S(1)} %get-tuple-element.29), channel_id=1, source_target_pairs={{0,1},{1,0},{2,3},{3,2},{4,5},{5,4},{6,7},{7,6},{8,9},{9,8},{10,11... | collective-permute-start | bytes 884744 | tf_op jit(solution)/shard_map/ppermute | solution.py:261
  10.0 10.2 %collective-permute-start = (bf16[384,384]{1,0:T(8,128)(2,1)S(1)}, bf16[384,384]{1,0:T(8,128)(2,1)S(1)}, u32[]{:S(2)}, u32[]{:S(2)}) collective-permute-start(bf16[384,384]{1,0:T(8,128)(2,1)S(1)} %get-tuple-element.25), channel_id=1, source_target_pairs={{0,2},{1,3},{2,0},{3,1},{4,6},{5,7},{6,4},{7,5},{8,10},{9,11},{10,... | collective-permute-start | bytes 884744 | tf_op jit(solution)/shard_map/ppermute | solution.py:261
  20.2 9.4 %collective-permute-start.5 = (bf16[1,384,384]{2,1,0:T(8,128)(2,1)S(1)}, bf16[1,384,384]{2,1,0:T(8,128)(2,1)S(1)}, u32[]{:S(2)}, u32[]{:S(2)}) collective-permute-start(bf16[1,384,384]{2,1,0:T(8,128)(2,1)S(1)} %get-tuple-element.26), channel_id=1, source_target_pairs={{0,4},{1,29},{2,6},{3,31},{4,8},{5,1},{6,10},{7,3},{8,12},{9,5},{1... | collective-permute-start | bytes 884744 | tf_op jit(solution)/shard_map/ppermute | solution.py:292
  36.1 10.0 %collective-permute-start.7 = (bf16[576,384]{1,0:T(8,128)(2,1)S(1)}, bf16[576,384]{1,0:T(8,128)(2,1)S(1)}, u32[]{:S(2)}, u32[]{:S(2)}) collective-permute-start(bf16[576,384]{1,0:T(8,128)(2,1)S(1)} %pad_maximum_fusion.1), channel_id=1, source_target_pairs={{0,2},{1,3},{2,0},{3,1},{4,6},{5,7},{6,4},{7,5},{8,10},{9,11},{10,... | collective-permute-start | bytes 1327112 | tf_op jit(solution)/shard_map/ppermute | solution.py:261
  37.9 8.3 %collective-permute-start.1 = (f32[384,384]{1,0:T(8,128)S(1)}, f32[384,384]{1,0:T(8,128)S(1)}, u32[]{:S(2)}, u32[]{:S(2)}) collective-permute-start(f32[384,384]{1,0:T(8,128)S(1)} %pad_maximum_fusion), channel_id=1, source_target_pairs={{0,1},{1,0},{2,3},{3,2},{4,5},{5,4},{6,7},{7,6},{8,9},{9,8},{10,11... | collective-permute-start | bytes 1769480 | tf_op jit(solution)/shard_map/ppermute | solution.py:261
  46.1 1.6 %collective-permute-start.8 = (f32[192,384]{1,0:T(8,128)S(1)}, f32[192,384]{1,0:T(8,128)S(1)}, u32[]{:S(2)}, u32[]{:S(2)}) collective-permute-start(f32[192,384]{1,0:T(8,128)S(1)} %convert_add_fusion), channel_id=1, source_target_pairs={{0,1},{1,0},{2,3},{3,2},{4,5},{5,4},{6,7},{7,6},{8,9},{9,8},{10,11... | collective-permute-start | bytes 884744 | tf_op jit(solution)/shard_map/ppermute | solution.py:261

commit v13 on v12

--- a/solution.py
+++ b/solution.py
@@ -125,8 +125,8 @@
 
 
 def inner_far_kernel(
-    table, left_far, right_far, cells_far, direct, keep, send, left, right, cells, middles,
-    cell_sem, left_sem, right_sem,
+    table_kept, left_far, right_far, cells_far, direct, keep, send, left, right, cells, middles,
+    table, table_sem, cell_sem, left_sem, right_sem,
 ):
     chip, core = position()
     operators = left.shape[0]
@@ -143,8 +143,13 @@
         return begin(cells_far.at[s], cells.at[s], cell_sem.at[s])
 
     first = [cell(s) for s in inside]
-    lefts = [begin(*rows(k, 1 - chip), left_sem.at[0, k]) for k in range(operators)]
-    for copy in first + lefts[:AHEAD]:
+    lefts = [begin(*rows(k, 1 - chip), left_sem.at[0, k]) for k in range(AHEAD)]
+    begin(table_kept, table, table_sem).wait()
+    most = len(first) // 2 + 1
+    for copy in first[:most]:
+        copy.wait()
+    lefts += [begin(*rows(k, 1 - chip), left_sem.at[0, k]) for k in range(AHEAD, operators)]
+    for copy in first[most:] + lefts[:AHEAD]:
         copy.wait()
     rights = [begin(right_far.at[k], right.at[k], right_sem.at[k]) for k in range(operators)]
     later = [begin(*rows(k, chip), left_sem.at[1, k]) for k in range(operators)]
@@ -302,7 +307,7 @@
         operators,
         inner,
         [table, *in_hbm(left_ops, right_ops, wavefunction)],
-        [SMALL] + [LARGE] * 3,
+        [BLOCK] + [LARGE] * 3,
         [
             shape(CORES * direct_rows, states, dtype=narrow),
             reduced,
@@ -313,6 +318,8 @@
         ],
         [BLOCK] * 6,
         [
+            pltpu.SMEM(table.shape, table.dtype),
+            pltpu.SemaphoreType.DMA,
             pltpu.SemaphoreType.DMA((sectors,)),
             pltpu.SemaphoreType.DMA((2, operators)),
             pltpu.SemaphoreType.DMA((operators,)),

time: 49 us -> 48.3 us (0.986)
  Pallas kernels: 27.9 us -> 27.1 us
    pallas_call x4, Pallas kernels: 25.7 us -> 24.9 us  [run(): pl.pallas_call(kernel, out_shape=outs, in_specs=in_specs, out_specs=out_s...]
  transfers between devices with their start and end apart: 9 -> 9, of which waited for: 4 -> 4; matrix products, arithmetic and copies ran while one was open for 0% -> 0% of each run, Pallas kernels for 42% -> 41%
where the time goes in v13:
time: 48.3 us; the launch traced here: 48.1 us
  Pallas kernels  27.1 us (56%)
  waiting for transfers between devices  13 us (27%)
  starting transfers between devices  7.72 us (16%)
    pallas_call x4, Pallas kernels, run(): pl.pallas_call(kernel, out_shape=outs, in_specs=in_specs, out_specs=out_s...  24.9 us
    ppermute x1, waiting for transfers between devices, shards(): halo = lax.ppermute(border, ('sec', 'op'), ring)  7.62 us
    ppermute x8, starting transfers between devices, over_op(): return lax.ppermute(value, 'op', [(i, i ^ flip) for i in range(op)])  6.01 us
    ppermute x8, waiting for transfers between devices, over_op(): return lax.ppermute(value, 'op', [(i, i ^ flip) for i in range(op)])  5.35 us
    ppermute x1, starting transfers between devices, shards(): halo = lax.ppermute(border, ('sec', 'op'), ring)  1.71 us
    pallas_call x1, Pallas kernels, shards(): pl.pallas_call(sum_kernel, out_shape=shape(sectors, half, states), in_spe...  1.13 us
    pallas_call x1, Pallas kernels, shards(): pl.pallas_call(first_kernel, out_shape=[pltpu.VMEM((1, states, states), n...  1.05 us
  transfers between devices with their start and end apart: 9, of which 4 were waited for; matrix products, arithmetic and copies ran while one was open for 0% of the time, Pallas kernels for 41%

profile of v13, /device:TPU:0, one launch (start us, length us, event | category | flops | bytes accessed | tf_op | source)
XLA Modules:
  0.0 48.1 jit_solution(18169343257168476235)
XLA Ops:
  0.0 0.5 %collective-permute-start.3 = (bf16[8,384,384]{2,1,0:T(8,128)(2,1)}, bf16[8,384,384]{2,1,0:T(8,128)(2,1)S(1)}, u32[]{:S(2)}, u32[]{:S(2)}) collective-permute-start(bf16[8,384,384]{2,1,0:T(8,128)(2,1)} %left_far.1), channel_id=1, source_target_pairs={{0,1},{1,0},{2,3},{3,2},{4,5},{5,4},{6,7},{7,6},{8,9},{9,8},{10,11... | collective-permute-start | bytes 7077896 | tf_op jit(solution)/shard_map/ppermute | solution.py:266
  0.5 0.0 collective-permute-start.4
  0.5 1.0 %first_kernel.1 = (bf16[1,384,384]{2,1,0:T(8,128)(2,1)S(1)}, f32[9,8]{1,0:T(8,128)S(1)}) custom-call(s32[8]{0:T(128)} %charge.1, s32[8,8]{1,0:T(8,128)} %couple.1, f32[8,8]{1,0:T(8,128)} %amplitude.1, bf16[8,384,384]{2,1,0:T(8,128)(2,1)} %cells_far.3), custom_call_target="tpu_custom_call" | custom-call | tf_op jit(solution)/shard_map/first_kernel/pallas_call | solution.py:280
  1.6 0.6 %collective-permute-start.2 = (f32[9,8]{1,0:T(8,128)S(1)}, f32[9,8]{1,0:T(8,128)S(1)}, u32[]{:S(2)}, u32[]{:S(2)}) collective-permute-start(f32[9,8]{1,0:T(8,128)S(1)} %get-tuple-element.19.table_kept.table.refs_0_), channel_id=1, source_target_pairs={{0,1},{1,0},{2,3},{3,2},{4,5},{5,4},{6,7},{7,6},{8,9},{9,8},{10,11... | collective-permute-start | bytes 872 | tf_op jit(solution)/shard_map/ppermute | solution.py:266
  2.1 7.0 %shard_map.64 = (bf16[384,384]{1,0:T(8,128)(2,1)S(1)}, f32[192,384]{1,0:T(8,128)S(1)}, f32[192,384]{1,0:T(8,128)S(1)}, bf16[8,384,384]{2,1,0:T(8,128)(2,1)S(1)},...) custom-call(f32[9,8]{1,0:T(8,128)S(1)} %get-tuple-element.19.table_kept.table.refs_0_, ...), custom_call_target="tpu_custom_call" | custom-call | flops 3623878656 | bytes 4718592 | tf_op jit(solution)/shard_map/pallas_call | solution.py:251
  9.1 0.1 collective-permute-start.6
  9.2 3.0 %collective-permute-start = (bf16[384,384]{1,0:T(8,128)(2,1)S(1)}, bf16[384,384]{1,0:T(8,128)(2,1)S(1)}, u32[]{:S(2)}, u32[]{:S(2)}) collective-permute-start(bf16[384,384]{1,0:T(8,128)(2,1)S(1)} %get-tuple-element.25), channel_id=1, source_target_pairs={{0,2},{1,3},{2,0},{3,1},{4,6},{5,7},{6,4},{7,5},{8,10},{9,11},{10,... | collective-permute-start | bytes 884744 | tf_op jit(solution)/shard_map/ppermute | solution.py:266
  12.2 5.4 %shard_map.65 = (f32[384,384]{1,0:T(8,128)S(1)}, f32[384,384]{1,0:T(8,128)S(1)}) custom-call(f32[9,8]{1,0:T(8,128)S(1)} %get-tuple-element.19.table_kept.table.refs_0_, bf16[8,384,384]{2,1,0:T(8,128)(2,1)S(1)} %get-tuple-element.20.left.refs_2_, bf16[8,384,384]{2,1,0:T(8,128)(2,1)S(1)} %get-tuple-element.21.right.refs_3_, ...), custom_call_target="tpu_custom_call" | custom-call | flops 3623878656 | bytes 4718592 | tf_op jit(solution)/shard_map/pallas_call | solution.py:251
  17.6 1.8 %collective-permute-done = bf16[384,384]{1,0:T(8,128)(2,1)S(1)} collective-permute-done((bf16[384,384]{1,0:T(8,128)(2,1)S(1)}, bf16[384,384]{1,0:T(8,128)(2,1)S(1)}, u32[]{:S(2)}, u32[]{:S(2)}) %collective-permute-start) | collective-permute-done | bytes 294944 | tf_op jit(solution)/shard_map/ppermute | solution.py:266
  19.4 1.7 %collective-permute-start.5 = (bf16[1,384,384]{2,1,0:T(8,128)(2,1)S(1)}, bf16[1,384,384]{2,1,0:T(8,128)(2,1)S(1)}, u32[]{:S(2)}, u32[]{:S(2)}) collective-permute-start(bf16[1,384,384]{2,1,0:T(8,128)(2,1)S(1)} %get-tuple-element.26), channel_id=1, source_target_pairs={{0,4},{1,29},{2,6},{3,31},{4,8},{5,1},{6,10},{7,3},{8,12},{9,5},{1... | collective-permute-start | bytes 884744 | tf_op jit(solution)/shard_map/ppermute | solution.py:297
  21.1 0.1 convert_add_fusion.1
  21.2 0.0 collective-permute-done.6
  21.3 0.0 collective-permute-done.2.table_in.refs_1_
  21.3 7.6 %collective-permute-done.5.halo = bf16[1,384,384]{2,1,0:T(8,128)(2,1)S(1)} collective-permute-done((bf16[1,384,384]{2,1,0:T(8,128)(2,1)S(1)}, bf16[1,384,384]{2,1,0:T(8,128)(2,1)S(1)}, u32[]{:S(2)}, u32[]{:S(2)}) %collective-permute-start.5) | collective-permute-done | bytes 294944 | tf_op jit(solution)/shard_map/ppermute | solution.py:297
  28.9 0.0 collective-permute-done.3.left_in.refs_4_
  28.9 0.0 collective-permute-done.4.right_in.refs_5_
  28.9 6.4 %shard_map.66 = (bf16[384,384]{1,0:T(8,128)(2,1)S(1)}, bf16[4,384,384]{2,1,0:T(8,128)(2,1)S(1)}) custom-call(f32[9,8]{1,0:T(8,128)S(1)} %get-tuple-element.19.table_kept.table.refs_0_, f32[9,8]{1,0:T(8,128)S(1)} %collective-permute-done.2.table_in.refs_1_, bf16[8,384,384]{2,1,0:T(8,128)(2,1)S(1)} %get-tuple-element.20.left.refs_2_, ...), custom_call_target="tpu_custom_call" | custom-call | flops 3623878656 | bytes 9437184 | tf_op jit(solution)/shard_map/pallas_call | solution.py:251
  35.3 1.8 %collective-permute-start.7 = (bf16[576,384]{1,0:T(8,128)(2,1)S(1)}, bf16[576,384]{1,0:T(8,128)(2,1)S(1)}, u32[]{:S(2)}, u32[]{:S(2)}) collective-permute-start(bf16[576,384]{1,0:T(8,128)(2,1)S(1)} %pad_maximum_fusion.1), channel_id=1, source_target_pairs={{0,2},{1,3},{2,0},{3,1},{4,6},{5,7},{6,4},{7,5},{8,10},{9,11},{10,... | collective-permute-start | bytes 1327112 | tf_op jit(solution)/shard_map/ppermute | solution.py:266
  37.1 0.1 collective-permute-start.1
  37.2 6.1 %shard_map.67 = (f32[192,384]{1,0:T(8,128)S(1)}, f32[192,384]{1,0:T(8,128)S(1)}) custom-call(f32[9,8]{1,0:T(8,128)S(1)} %get-tuple-element.19.table_kept.table.refs_0_, f32[9,8]{1,0:T(8,128)S(1)} %collective-permute-done.2.table_in.refs_1_, bf16[8,384,384]{2,1,0:T(8,128)(2,1)S(1)} %get-tuple-element.20.left.refs_2_, ...), custom_call_target="tpu_custom_call" | custom-call | flops 3623878656 | bytes 9437184 | tf_op jit(solution)/shard_map/pallas_call | solution.py:251
  43.3 2.0 %collective-permute-done.7 = bf16[576,384]{1,0:T(8,128)(2,1)S(1)} collective-permute-done((bf16[576,384]{1,0:T(8,128)(2,1)S(1)}, bf16[576,384]{1,0:T(8,128)(2,1)S(1)}, u32[]{:S(2)}, u32[]{:S(2)}) %collective-permute-start.7) | collective-permute-done | bytes 442400 | tf_op jit(solution)/shard_map/ppermute | solution.py:266
  45.3 0.1 collective-permute-start.8
  45.4 0.0 collective-permute-done.1
  45.4 1.6 %collective-permute-done.8 = f32[192,384]{1,0:T(8,128)S(1)} collective-permute-done((f32[192,384]{1,0:T(8,128)S(1)}, f32[192,384]{1,0:T(8,128)S(1)}, u32[]{:S(2)}, u32[]{:S(2)}) %collective-permute-start.8) | collective-permute-done | bytes 294944 | tf_op jit(solution)/shard_map/ppermute | solution.py:266
  47.0 1.1 %total.1 = f32[8,96,384]{2,1,0:T(8,128)} custom-call(f32[4,96,384]{2,1,0:T(8,128)S(1)} %bitcast.8, f32[4,96,384]{2,1,0:T(8,128)S(1)} %bitcast.9, bf16[4,96,384]{2,1,0:T(8,128)(2,1)S(1)} %bitcast.7, bf16[6,96,384]{2,1,0:T(8,128)(2,1)S(1)} %bitcast.6, f32[2,96,384]{2,1,0:T(8,128)S(1)} %bitcast.10, f32[2,96,384]{2,1,0:T(8,128)S(1)} %bitcast.11), custom_call_target="tpu_custom_call" | custom-call | tf_op jit(solution)/shard_map/total/pallas_call | solution.py:376
  (4 shorter events, 0.2 us)
Async XLA Ops:
  0.0 28.9 %collective-permute-start.3 = (bf16[8,384,384]{2,1,0:T(8,128)(2,1)}, bf16[8,384,384]{2,1,0:T(8,128)(2,1)S(1)}, u32[]{:S(2)}, u32[]{:S(2)}) collective-permute-start(bf16[8,384,384]{2,1,0:T(8,128)(2,1)} %left_far.1), channel_id=1, source_target_pairs={{0,1},{1,0},{2,3},{3,2},{4,5},{5,4},{6,7},{7,6},{8,9},{9,8},{10,11... | collective-permute-start | bytes 7077896 | tf_op jit(solution)/shard_map/ppermute | solution.py:266
  0.5 28.4 %collective-permute-start.4 = (bf16[8,384,384]{2,1,0:T(8,128)(2,1)}, bf16[8,384,384]{2,1,0:T(8,128)(2,1)S(1)}, u32[]{:S(2)}, u32[]{:S(2)}) collective-permute-start(bf16[8,384,384]{2,1,0:T(8,128)(2,1)} %right_far.1), channel_id=1, source_target_pairs={{0,1},{1,0},{2,3},{3,2},{4,5},{5,4},{6,7},{7,6},{8,9},{9,8},{10,11... | collective-permute-start | bytes 7077896 | tf_op jit(solution)/shard_map/ppermute | solution.py:266
  1.6 19.7 %collective-permute-start.2 = (f32[9,8]{1,0:T(8,128)S(1)}, f32[9,8]{1,0:T(8,128)S(1)}, u32[]{:S(2)}, u32[]{:S(2)}) collective-permute-start(f32[9,8]{1,0:T(8,128)S(1)} %get-tuple-element.19.table_kept.table.refs_0_), channel_id=1, source_target_pairs={{0,1},{1,0},{2,3},{3,2},{4,5},{5,4},{6,7},{7,6},{8,9},{9,8},{10,11... | collective-permute-start | bytes 872 | tf_op jit(solution)/shard_map/ppermute | solution.py:266
  9.1 12.1 %collective-permute-start.6 = (f32[192,384]{1,0:T(8,128)S(1)}, f32[192,384]{1,0:T(8,128)S(1)}, u32[]{:S(2)}, u32[]{:S(2)}) collective-permute-start(f32[192,384]{1,0:T(8,128)S(1)} %get-tuple-element.29), channel_id=1, source_target_pairs={{0,1},{1,0},{2,3},{3,2},{4,5},{5,4},{6,7},{7,6},{8,9},{9,8},{10,11... | collective-permute-start | bytes 884744 | tf_op jit(solution)/shard_map/ppermute | solution.py:266
  9.2 10.2 %collective-permute-start = (bf16[384,384]{1,0:T(8,128)(2,1)S(1)}, bf16[384,384]{1,0:T(8,128)(2,1)S(1)}, u32[]{:S(2)}, u32[]{:S(2)}) collective-permute-start(bf16[384,384]{1,0:T(8,128)(2,1)S(1)} %get-tuple-element.25), channel_id=1, source_target_pairs={{0,2},{1,3},{2,0},{3,1},{4,6},{5,7},{6,4},{7,5},{8,10},{9,11},{10,... | collective-permute-start | bytes 884744 | tf_op jit(solution)/shard_map/ppermute | solution.py:266
  19.4 9.5 %collective-permute-start.5 = (bf16[1,384,384]{2,1,0:T(8,128)(2,1)S(1)}, bf16[1,384,384]{2,1,0:T(8,128)(2,1)S(1)}, u32[]{:S(2)}, u32[]{:S(2)}) collective-permute-start(bf16[1,384,384]{2,1,0:T(8,128)(2,1)S(1)} %get-tuple-element.26), channel_id=1, source_target_pairs={{0,4},{1,29},{2,6},{3,31},{4,8},{5,1},{6,10},{7,3},{8,12},{9,5},{1... | collective-permute-start | bytes 884744 | tf_op jit(solution)/shard_map/ppermute | solution.py:297
  35.3 10.0 %collective-permute-start.7 = (bf16[576,384]{1,0:T(8,128)(2,1)S(1)}, bf16[576,384]{1,0:T(8,128)(2,1)S(1)}, u32[]{:S(2)}, u32[]{:S(2)}) collective-permute-start(bf16[576,384]{1,0:T(8,128)(2,1)S(1)} %pad_maximum_fusion.1), channel_id=1, source_target_pairs={{0,2},{1,3},{2,0},{3,1},{4,6},{5,7},{6,4},{7,5},{8,10},{9,11},{10,... | collective-permute-start | bytes 1327112 | tf_op jit(solution)/shard_map/ppermute | solution.py:266
  37.1 8.3 %collective-permute-start.1 = (f32[384,384]{1,0:T(8,128)S(1)}, f32[384,384]{1,0:T(8,128)S(1)}, u32[]{:S(2)}, u32[]{:S(2)}) collective-permute-start(f32[384,384]{1,0:T(8,128)S(1)} %pad_maximum_fusion), channel_id=1, source_target_pairs={{0,1},{1,0},{2,3},{3,2},{4,5},{5,4},{6,7},{7,6},{8,9},{9,8},{10,11... | collective-permute-start | bytes 1769480 | tf_op jit(solution)/shard_map/ppermute | solution.py:266
  45.3 1.6 %collective-permute-start.8 = (f32[192,384]{1,0:T(8,128)S(1)}, f32[192,384]{1,0:T(8,128)S(1)}, u32[]{:S(2)}, u32[]{:S(2)}) collective-permute-start(f32[192,384]{1,0:T(8,128)S(1)} %convert_add_fusion), channel_id=1, source_target_pairs={{0,1},{1,0},{2,3},{3,2},{4,5},{5,4},{6,7},{7,6},{8,9},{9,8},{10,11... | collective-permute-start | bytes 884744 | tf_op jit(solution)/shard_map/ppermute | solution.py:266

commit v14 on v12

--- a/solution.py
+++ b/solution.py
@@ -7,7 +7,6 @@
 
 
 CORES = 2
-AHEAD = 2
 EDGE = 2
 
 
@@ -125,35 +124,27 @@
 
 
 def inner_far_kernel(
-    table, left_far, right_far, cells_far, direct, keep, send, left, right, cells, middles,
-    cell_sem, left_sem, right_sem,
+    table_kept, left, right_far, cells_far, direct, keep, send, right, cells, middles,
+    table, table_sem, cell_sem, right_sem,
 ):
     chip, core = position()
     operators = left.shape[0]
     sectors = cells.shape[0]
     targets = sectors - 2 * EDGE
-    chip_rows = (direct.shape[0] + keep.shape[0] + send.shape[0]) // targets
     inside = range(EDGE - 1, sectors - EDGE + 1)
-
-    def rows(k, place):
-        at = pl.ds(pl.multiple_of(place * chip_rows, 64), chip_rows)
-        return left_far.at[k, at], left.at[k, at]
 
     def cell(s):
         return begin(cells_far.at[s], cells.at[s], cell_sem.at[s])
 
     first = [cell(s) for s in inside]
-    lefts = [begin(*rows(k, 1 - chip), left_sem.at[0, k]) for k in range(operators)]
-    for copy in first + lefts[:AHEAD]:
+    begin(table_kept, table, table_sem).wait()
+    for copy in first[:-1]:
         copy.wait()
     rights = [begin(right_far.at[k], right.at[k], right_sem.at[k]) for k in range(operators)]
-    later = [begin(*rows(k, chip), left_sem.at[1, k]) for k in range(operators)]
-    later += [cell(s) for s in range(sectors) if s not in inside]
+    later = [cell(s) for s in range(sectors) if s not in inside]
+    first[-1].wait()
     sources = cells.at[pl.ds(EDGE - 1, targets + 2)]
     for k in range(operators):
-        if k == AHEAD:
-            for copy in lefts[AHEAD:]:
-                copy.wait()
         middle_of(k, table, k, left, sources, middles, EDGE, targets, 1 - chip, core)
     for copy in rights:
         copy.wait()
@@ -297,31 +288,31 @@
 
     direct_rows = inner // 2 * half
     reduced = shape(inner * half - direct_rows, states)
-    direct, keep, send, left, right, cells = run(
+    direct, keep, send, right, cells = run(
         inner_far_kernel,
         operators,
         inner,
-        [table, *in_hbm(left_ops, right_ops, wavefunction)],
-        [SMALL] + [LARGE] * 3,
+        [table, left_ops, *in_hbm(right_ops, wavefunction)],
+        [BLOCK] * 2 + [LARGE] * 2,
         [
             shape(CORES * direct_rows, states, dtype=narrow),
             reduced,
             reduced,
-            pltpu.VMEM(left_ops.shape, narrow),
             pltpu.VMEM(right_ops.shape, narrow),
             pltpu.VMEM(wavefunction.shape, narrow),
         ],
-        [BLOCK] * 6,
+        [BLOCK] * 5,
         [
+            pltpu.SMEM(table.shape, table.dtype),
+            pltpu.SemaphoreType.DMA,
             pltpu.SemaphoreType.DMA((sectors,)),
-            pltpu.SemaphoreType.DMA((2, operators)),
             pltpu.SemaphoreType.DMA((operators,)),
         ],
     )
     direct_far = over_op(direct, CORES)
     send_in = over_op(send, 1)
 
-    held = [table, table_in, left, right, left_in, right_in]
+    held = [table, table_in, left_ops, right, left_in, right_in]
     held_specs = [SMALL] * 2 + [BLOCK] * 4
     edge_send, sources = run(
         edge_far_kernel,
@@ -340,7 +331,7 @@
         inner_own_kernel,
         operators,
         inner,
-        [table, left, right, cells],
+        [table, left_ops, right, cells],
         [SMALL] + [BLOCK] * 3,
         [block, block],
         [BLOCK, BLOCK],

time: 49 us -> 47.9 us (0.978)
  Pallas kernels: 27.9 us -> 26.6 us
    pallas_call x4, Pallas kernels: 25.7 us -> 24.3 us  [run(): pl.pallas_call(kernel, out_shape=outs, in_specs=in_specs, out_specs=out_s...]
  transfers between devices with their start and end apart: 9 -> 9, of which waited for: 4 -> 4; matrix products, arithmetic and copies ran while one was open for 0% -> 0% of each run, Pallas kernels for 42% -> 40%
where the time goes in v14:
time: 47.9 us; the launch traced here: 47.8 us
  Pallas kernels  26.6 us (56%)
  waiting for transfers between devices  13.1 us (27%)
  starting transfers between devices  7.77 us (16%)
    pallas_call x4, Pallas kernels, run(): pl.pallas_call(kernel, out_shape=outs, in_specs=in_specs, out_specs=out_s...  24.3 us
    ppermute x1, waiting for transfers between devices, shards(): halo = lax.ppermute(border, ('sec', 'op'), ring)  7.62 us
    ppermute x8, starting transfers between devices, over_op(): return lax.ppermute(value, 'op', [(i, i ^ flip) for i in range(op)])  6.06 us
    ppermute x8, waiting for transfers between devices, over_op(): return lax.ppermute(value, 'op', [(i, i ^ flip) for i in range(op)])  5.49 us
    ppermute x1, starting transfers between devices, shards(): halo = lax.ppermute(border, ('sec', 'op'), ring)  1.71 us
    pallas_call x1, Pallas kernels, shards(): pl.pallas_call(first_kernel, out_shape=[pltpu.VMEM((1, states, states), n...  1.2 us
    pallas_call x1, Pallas kernels, shards(): pl.pallas_call(sum_kernel, out_shape=shape(sectors, half, states), in_spe...  1.13 us
  transfers between devices with their start and end apart: 9, of which 4 were waited for; matrix products, arithmetic and copies ran while one was open for 0% of the time, Pallas kernels for 40%

profile of v14, /device:TPU:0, one launch (start us, length us, event | category | flops | bytes accessed | tf_op | source)
XLA Modules:
  0.0 47.8 jit_solution(6769658146451968163)
XLA Ops:
  0.0 0.0 copy-start
  0.0 0.5 %collective-permute-start.3 = (bf16[8,384,384]{2,1,0:T(8,128)(2,1)}, bf16[8,384,384]{2,1,0:T(8,128)(2,1)S(1)}, u32[]{:S(2)}, u32[]{:S(2)}) collective-permute-start(bf16[8,384,384]{2,1,0:T(8,128)(2,1)} %refs_2_.1), channel_id=1, source_target_pairs={{0,1},{1,0},{2,3},{3,2},{4,5},{5,4},{6,7},{7,6},{8,9},{9,8},{10,11... | collective-permute-start | bytes 7077896 | tf_op jit(solution)/shard_map/ppermute | solution.py:252
  0.5 0.1 collective-permute-start.4
  0.6 1.2 %first_kernel.1 = (bf16[1,384,384]{2,1,0:T(8,128)(2,1)S(1)}, f32[9,8]{1,0:T(8,128)S(1)}) custom-call(s32[8]{0:T(128)} %charge.1, s32[8,8]{1,0:T(8,128)} %couple.1, f32[8,8]{1,0:T(8,128)} %amplitude.1, bf16[8,384,384]{2,1,0:T(8,128)(2,1)} %cells_far.3), custom_call_target="tpu_custom_call" | custom-call | tf_op jit(solution)/shard_map/first_kernel/pallas_call | solution.py:266
  1.8 0.6 %collective-permute-start.2 = (f32[9,8]{1,0:T(8,128)S(1)}, f32[9,8]{1,0:T(8,128)S(1)}, u32[]{:S(2)}, u32[]{:S(2)}) collective-permute-start(f32[9,8]{1,0:T(8,128)S(1)} %get-tuple-element.18.table_kept.table.refs_0_), channel_id=1, source_target_pairs={{0,1},{1,0},{2,3},{3,2},{4,5},{5,4},{6,7},{7,6},{8,9},{9,8},{10,11... | collective-permute-start | bytes 872 | tf_op jit(solution)/shard_map/ppermute | solution.py:252
  2.3 0.0 copy-done
  2.3 6.5 %shard_map.64 = (bf16[384,384]{1,0:T(8,128)(2,1)S(1)}, f32[192,384]{1,0:T(8,128)S(1)}, f32[192,384]{1,0:T(8,128)S(1)}, bf16[8,384,384]{2,1,0:T(8,128)(2,1)S(1)}, bf16[8,384,384]{2,1,0:T(8,128)(2,1)S(1)}) custom-call(f32[9,8]{1,0:T(8,128)S(1)} %get-tuple-element.18.table_kept.table.refs_0_, bf16[8,384,384]{2,1,0:T(8,128)(2,1)S(1)} %copy-done, ...), custom_call_target="tpu_custom_call" | custom-call | flops 3623878656 | bytes 4718592 | tf_op jit(solution)/shard_map/pallas_call | solution.py:237
  8.8 0.1 collective-permute-start.6
  8.9 3.0 %collective-permute-start = (bf16[384,384]{1,0:T(8,128)(2,1)S(1)}, bf16[384,384]{1,0:T(8,128)(2,1)S(1)}, u32[]{:S(2)}, u32[]{:S(2)}) collective-permute-start(bf16[384,384]{1,0:T(8,128)(2,1)S(1)} %get-tuple-element.23), channel_id=1, source_target_pairs={{0,2},{1,3},{2,0},{3,1},{4,6},{5,7},{6,4},{7,5},{8,10},{9,11},{10,... | collective-permute-start | bytes 884744 | tf_op jit(solution)/shard_map/ppermute | solution.py:252
  11.8 5.4 %shard_map.65 = (f32[384,384]{1,0:T(8,128)S(1)}, f32[384,384]{1,0:T(8,128)S(1)}) custom-call(f32[9,8]{1,0:T(8,128)S(1)} %get-tuple-element.18.table_kept.table.refs_0_, bf16[8,384,384]{2,1,0:T(8,128)(2,1)S(1)} %copy-done, bf16[8,384,384]{2,1,0:T(8,128)(2,1)S(1)} %get-tuple-element.19.right.refs_3_, bf16[8,384,384]{2,1,0:T(8,128)(2,1)S(1)} %get-tuple-element.20.cells), custom_call_target="tpu_custom_call" | custom-call | flops 3623878656 | bytes 4718592 | tf_op jit(solution)/shard_map/pallas_call | solution.py:237
  17.2 1.8 %collective-permute-done = bf16[384,384]{1,0:T(8,128)(2,1)S(1)} collective-permute-done((bf16[384,384]{1,0:T(8,128)(2,1)S(1)}, bf16[384,384]{1,0:T(8,128)(2,1)S(1)}, u32[]{:S(2)}, u32[]{:S(2)}) %collective-permute-start) | collective-permute-done | bytes 294944 | tf_op jit(solution)/shard_map/ppermute | solution.py:252
  19.1 1.7 %collective-permute-start.5 = (bf16[1,384,384]{2,1,0:T(8,128)(2,1)S(1)}, bf16[1,384,384]{2,1,0:T(8,128)(2,1)S(1)}, u32[]{:S(2)}, u32[]{:S(2)}) collective-permute-start(bf16[1,384,384]{2,1,0:T(8,128)(2,1)S(1)} %get-tuple-element.24), channel_id=1, source_target_pairs={{0,4},{1,29},{2,6},{3,31},{4,8},{5,1},{6,10},{7,3},{8,12},{9,5},{1... | collective-permute-start | bytes 884744 | tf_op jit(solution)/shard_map/ppermute | solution.py:283
  20.8 0.1 convert_add_fusion.1
  20.8 0.0 collective-permute-done.6
  20.9 0.0 collective-permute-done.2.table_in.refs_1_
  20.9 7.6 %collective-permute-done.5.halo = bf16[1,384,384]{2,1,0:T(8,128)(2,1)S(1)} collective-permute-done((bf16[1,384,384]{2,1,0:T(8,128)(2,1)S(1)}, bf16[1,384,384]{2,1,0:T(8,128)(2,1)S(1)}, u32[]{:S(2)}, u32[]{:S(2)}) %collective-permute-start.5) | collective-permute-done | bytes 294944 | tf_op jit(solution)/shard_map/ppermute | solution.py:283
  28.5 0.0 collective-permute-done.3.left_in.refs_4_
  28.5 0.0 collective-permute-done.4.right_in.refs_5_
  28.5 6.3 %shard_map.66 = (bf16[384,384]{1,0:T(8,128)(2,1)S(1)}, bf16[4,384,384]{2,1,0:T(8,128)(2,1)S(1)}) custom-call(f32[9,8]{1,0:T(8,128)S(1)} %get-tuple-element.18.table_kept.table.refs_0_, f32[9,8]{1,0:T(8,128)S(1)} %collective-permute-done.2.table_in.refs_1_, bf16[8,384,384]{2,1,0:T(8,128)(2,1)S(1)} %copy-done, ...), custom_call_target="tpu_custom_call" | custom-call | flops 3623878656 | bytes 9437184 | tf_op jit(solution)/shard_map/pallas_call | solution.py:237
  34.9 1.8 %collective-permute-start.7 = (bf16[576,384]{1,0:T(8,128)(2,1)S(1)}, bf16[576,384]{1,0:T(8,128)(2,1)S(1)}, u32[]{:S(2)}, u32[]{:S(2)}) collective-permute-start(bf16[576,384]{1,0:T(8,128)(2,1)S(1)} %pad_maximum_fusion.1), channel_id=1, source_target_pairs={{0,2},{1,3},{2,0},{3,1},{4,6},{5,7},{6,4},{7,5},{8,10},{9,11},{10,... | collective-permute-start | bytes 1327112 | tf_op jit(solution)/shard_map/ppermute | solution.py:252
  36.7 0.1 collective-permute-start.1
  36.8 6.1 %shard_map.67 = (f32[192,384]{1,0:T(8,128)S(1)}, f32[192,384]{1,0:T(8,128)S(1)}) custom-call(f32[9,8]{1,0:T(8,128)S(1)} %get-tuple-element.18.table_kept.table.refs_0_, f32[9,8]{1,0:T(8,128)S(1)} %collective-permute-done.2.table_in.refs_1_, bf16[8,384,384]{2,1,0:T(8,128)(2,1)S(1)} %copy-done, bf16[8,384,384]{2,1,0:T(8,128)(2,1)S(1)} %get-tuple-element.19.right.refs_3_, ...), custom_call_target="tpu_custom_call" | custom-call | flops 3623878656 | bytes 9437184 | tf_op jit(solution)/shard_map/pallas_call | solution.py:237
  42.9 2.1 %collective-permute-done.7 = bf16[576,384]{1,0:T(8,128)(2,1)S(1)} collective-permute-done((bf16[576,384]{1,0:T(8,128)(2,1)S(1)}, bf16[576,384]{1,0:T(8,128)(2,1)S(1)}, u32[]{:S(2)}, u32[]{:S(2)}) %collective-permute-start.7) | collective-permute-done | bytes 442400 | tf_op jit(solution)/shard_map/ppermute | solution.py:252
  45.0 0.1 collective-permute-start.8
  45.1 0.0 collective-permute-done.1
  45.1 1.6 %collective-permute-done.8 = f32[192,384]{1,0:T(8,128)S(1)} collective-permute-done((f32[192,384]{1,0:T(8,128)S(1)}, f32[192,384]{1,0:T(8,128)S(1)}, u32[]{:S(2)}, u32[]{:S(2)}) %collective-permute-start.8) | collective-permute-done | bytes 294944 | tf_op jit(solution)/shard_map/ppermute | solution.py:252
  46.6 1.1 %total.1 = f32[8,96,384]{2,1,0:T(8,128)} custom-call(f32[4,96,384]{2,1,0:T(8,128)S(1)} %bitcast.8, f32[4,96,384]{2,1,0:T(8,128)S(1)} %bitcast.9, bf16[4,96,384]{2,1,0:T(8,128)(2,1)S(1)} %bitcast.7, bf16[6,96,384]{2,1,0:T(8,128)(2,1)S(1)} %bitcast.6, f32[2,96,384]{2,1,0:T(8,128)S(1)} %bitcast.10, f32[2,96,384]{2,1,0:T(8,128)S(1)} %bitcast.11), custom_call_target="tpu_custom_call" | custom-call | tf_op jit(solution)/shard_map/total/pallas_call | solution.py:360
  (4 shorter events, 0.2 us)
Async XLA Ops:
  0.0 2.3 %copy-start = (bf16[8,384,384]{2,1,0:T(8,128)(2,1)S(1)}, bf16[8,384,384]{2,1,0:T(8,128)(2,1)}, u32[]{:S(2)}) copy-start(bf16[8,384,384]{2,1,0:T(8,128)(2,1)} %refs_2_.1) | copy-start | bytes 7077892
  0.0 28.5 %collective-permute-start.3 = (bf16[8,384,384]{2,1,0:T(8,128)(2,1)}, bf16[8,384,384]{2,1,0:T(8,128)(2,1)S(1)}, u32[]{:S(2)}, u32[]{:S(2)}) collective-permute-start(bf16[8,384,384]{2,1,0:T(8,128)(2,1)} %refs_2_.1), channel_id=1, source_target_pairs={{0,1},{1,0},{2,3},{3,2},{4,5},{5,4},{6,7},{7,6},{8,9},{9,8},{10,11... | collective-permute-start | bytes 7077896 | tf_op jit(solution)/shard_map/ppermute | solution.py:252
  0.5 28.0 %collective-permute-start.4 = (bf16[8,384,384]{2,1,0:T(8,128)(2,1)}, bf16[8,384,384]{2,1,0:T(8,128)(2,1)S(1)}, u32[]{:S(2)}, u32[]{:S(2)}) collective-permute-start(bf16[8,384,384]{2,1,0:T(8,128)(2,1)} %right_far.1), channel_id=1, source_target_pairs={{0,1},{1,0},{2,3},{3,2},{4,5},{5,4},{6,7},{7,6},{8,9},{9,8},{10,11... | collective-permute-start | bytes 7077896 | tf_op jit(solution)/shard_map/ppermute | solution.py:252
  1.8 19.1 %collective-permute-start.2 = (f32[9,8]{1,0:T(8,128)S(1)}, f32[9,8]{1,0:T(8,128)S(1)}, u32[]{:S(2)}, u32[]{:S(2)}) collective-permute-start(f32[9,8]{1,0:T(8,128)S(1)} %get-tuple-element.18.table_kept.table.refs_0_), channel_id=1, source_target_pairs={{0,1},{1,0},{2,3},{3,2},{4,5},{5,4},{6,7},{7,6},{8,9},{9,8},{10,11... | collective-permute-start | bytes 872 | tf_op jit(solution)/shard_map/ppermute | solution.py:252
  8.8 12.1 %collective-permute-start.6 = (f32[192,384]{1,0:T(8,128)S(1)}, f32[192,384]{1,0:T(8,128)S(1)}, u32[]{:S(2)}, u32[]{:S(2)}) collective-permute-start(f32[192,384]{1,0:T(8,128)S(1)} %get-tuple-element.27), channel_id=1, source_target_pairs={{0,1},{1,0},{2,3},{3,2},{4,5},{5,4},{6,7},{7,6},{8,9},{9,8},{10,11... | collective-permute-start | bytes 884744 | tf_op jit(solution)/shard_map/ppermute | solution.py:252
  8.9 10.2 %collective-permute-start = (bf16[384,384]{1,0:T(8,128)(2,1)S(1)}, bf16[384,384]{1,0:T(8,128)(2,1)S(1)}, u32[]{:S(2)}, u32[]{:S(2)}) collective-permute-start(bf16[384,384]{1,0:T(8,128)(2,1)S(1)} %get-tuple-element.23), channel_id=1, source_target_pairs={{0,2},{1,3},{2,0},{3,1},{4,6},{5,7},{6,4},{7,5},{8,10},{9,11},{10,... | collective-permute-start | bytes 884744 | tf_op jit(solution)/shard_map/ppermute | solution.py:252
  19.1 9.4 %collective-permute-start.5 = (bf16[1,384,384]{2,1,0:T(8,128)(2,1)S(1)}, bf16[1,384,384]{2,1,0:T(8,128)(2,1)S(1)}, u32[]{:S(2)}, u32[]{:S(2)}) collective-permute-start(bf16[1,384,384]{2,1,0:T(8,128)(2,1)S(1)} %get-tuple-element.24), channel_id=1, source_target_pairs={{0,4},{1,29},{2,6},{3,31},{4,8},{5,1},{6,10},{7,3},{8,12},{9,5},{1... | collective-permute-start | bytes 884744 | tf_op jit(solution)/shard_map/ppermute | solution.py:283
  34.9 10.0 %collective-permute-start.7 = (bf16[576,384]{1,0:T(8,128)(2,1)S(1)}, bf16[576,384]{1,0:T(8,128)(2,1)S(1)}, u32[]{:S(2)}, u32[]{:S(2)}) collective-permute-start(bf16[576,384]{1,0:T(8,128)(2,1)S(1)} %pad_maximum_fusion.1), channel_id=1, source_target_pairs={{0,2},{1,3},{2,0},{3,1},{4,6},{5,7},{6,4},{7,5},{8,10},{9,11},{10,... | collective-permute-start | bytes 1327112 | tf_op jit(solution)/shard_map/ppermute | solution.py:252
  36.7 8.3 %collective-permute-start.1 = (f32[384,384]{1,0:T(8,128)S(1)}, f32[384,384]{1,0:T(8,128)S(1)}, u32[]{:S(2)}, u32[]{:S(2)}) collective-permute-start(f32[384,384]{1,0:T(8,128)S(1)} %pad_maximum_fusion), channel_id=1, source_target_pairs={{0,1},{1,0},{2,3},{3,2},{4,5},{5,4},{6,7},{7,6},{8,9},{9,8},{10,11... | collective-permute-start | bytes 1769480 | tf_op jit(solution)/shard_map/ppermute | solution.py:252
  45.0 1.6 %collective-permute-start.8 = (f32[192,384]{1,0:T(8,128)S(1)}, f32[192,384]{1,0:T(8,128)S(1)}, u32[]{:S(2)}, u32[]{:S(2)}) collective-permute-start(f32[192,384]{1,0:T(8,128)S(1)} %convert_add_fusion), channel_id=1, source_target_pairs={{0,1},{1,0},{2,3},{3,2},{4,5},{5,4},{6,7},{7,6},{8,9},{9,8},{10,11... | collective-permute-start | bytes 884744 | tf_op jit(solution)/shard_map/ppermute | solution.py:252

commit v15 on v14

--- a/solution.py
+++ b/solution.py
@@ -138,11 +138,12 @@
 
     first = [cell(s) for s in inside]
     begin(table_kept, table, table_sem).wait()
-    for copy in first[:-1]:
+    for copy in first[: len(first) // 2]:
         copy.wait()
     rights = [begin(right_far.at[k], right.at[k], right_sem.at[k]) for k in range(operators)]
     later = [cell(s) for s in range(sectors) if s not in inside]
-    first[-1].wait()
+    for copy in first[len(first) // 2 :]:
+        copy.wait()
     sources = cells.at[pl.ds(EDGE - 1, targets + 2)]
     for k in range(operators):
         middle_of(k, table, k, left, sources, middles, EDGE, targets, 1 - chip, core)

time: 47.9 us -> 47.9 us (level)
  no operation moved by 1% of the time
where the time goes in v15:
time: 47.9 us; the launch traced here: 47.8 us
  Pallas kernels  26.6 us (56%)
  waiting for transfers between devices  13.1 us (27%)
  starting transfers between devices  7.77 us (16%)
    pallas_call x4, Pallas kernels, run(): pl.pallas_call(kernel, out_shape=outs, in_specs=in_specs, out_specs=out_s...  24.3 us
    ppermute x1, waiting for transfers between devices, shards(): halo = lax.ppermute(border, ('sec', 'op'), ring)  7.62 us
    ppermute x8, starting transfers between devices, over_op(): return lax.ppermute(value, 'op', [(i, i ^ flip) for i in range(op)])  6.06 us
    ppermute x8, waiting for transfers between devices, over_op(): return lax.ppermute(value, 'op', [(i, i ^ flip) for i in range(op)])  5.49 us
    ppermute x1, starting transfers between devices, shards(): halo = lax.ppermute(border, ('sec', 'op'), ring)  1.71 us
    pallas_call x1, Pallas kernels, shards(): pl.pallas_call(first_kernel, out_shape=[pltpu.VMEM((1, states, states), n...  1.2 us
    pallas_call x1, Pallas kernels, shards(): pl.pallas_call(sum_kernel, out_shape=shape(sectors, half, states), in_spe...  1.13 us
  transfers between devices with their start and end apart: 9, of which 4 were waited for; matrix products, arithmetic and copies ran while one was open for 0% of the time, Pallas kernels for 40%

profile of v15, /device:TPU:0, one launch (start us, length us, event | category | flops | bytes accessed | tf_op | source)
XLA Modules:
  0.0 47.8 jit_solution(6709525828882379027)
XLA Ops:
  0.0 0.0 copy-start
  0.0 0.5 %collective-permute-start.3 = (bf16[8,384,384]{2,1,0:T(8,128)(2,1)}, bf16[8,384,384]{2,1,0:T(8,128)(2,1)S(1)}, u32[]{:S(2)}, u32[]{:S(2)}) collective-permute-start(bf16[8,384,384]{2,1,0:T(8,128)(2,1)} %refs_2_.1), channel_id=1, source_target_pairs={{0,1},{1,0},{2,3},{3,2},{4,5},{5,4},{6,7},{7,6},{8,9},{9,8},{10,11... | collective-permute-start | bytes 7077896 | tf_op jit(solution)/shard_map/ppermute | solution.py:253
  0.5 0.1 collective-permute-start.4
  0.6 1.2 %first_kernel.1 = (bf16[1,384,384]{2,1,0:T(8,128)(2,1)S(1)}, f32[9,8]{1,0:T(8,128)S(1)}) custom-call(s32[8]{0:T(128)} %charge.1, s32[8,8]{1,0:T(8,128)} %couple.1, f32[8,8]{1,0:T(8,128)} %amplitude.1, bf16[8,384,384]{2,1,0:T(8,128)(2,1)} %cells_far.3), custom_call_target="tpu_custom_call" | custom-call | tf_op jit(solution)/shard_map/first_kernel/pallas_call | solution.py:267
  1.8 0.6 %collective-permute-start.2 = (f32[9,8]{1,0:T(8,128)S(1)}, f32[9,8]{1,0:T(8,128)S(1)}, u32[]{:S(2)}, u32[]{:S(2)}) collective-permute-start(f32[9,8]{1,0:T(8,128)S(1)} %get-tuple-element.18.table_kept.table.refs_0_), channel_id=1, source_target_pairs={{0,1},{1,0},{2,3},{3,2},{4,5},{5,4},{6,7},{7,6},{8,9},{9,8},{10,11... | collective-permute-start | bytes 872 | tf_op jit(solution)/shard_map/ppermute | solution.py:253
  2.3 0.0 copy-done
  2.3 6.5 %shard_map.64 = (bf16[384,384]{1,0:T(8,128)(2,1)S(1)}, f32[192,384]{1,0:T(8,128)S(1)}, f32[192,384]{1,0:T(8,128)S(1)}, bf16[8,384,384]{2,1,0:T(8,128)(2,1)S(1)}, bf16[8,384,384]{2,1,0:T(8,128)(2,1)S(1)}) custom-call(f32[9,8]{1,0:T(8,128)S(1)} %get-tuple-element.18.table_kept.table.refs_0_, bf16[8,384,384]{2,1,0:T(8,128)(2,1)S(1)} %copy-done, ...), custom_call_target="tpu_custom_call" | custom-call | flops 3623878656 | bytes 4718592 | tf_op jit(solution)/shard_map/pallas_call | solution.py:238
  8.8 0.1 collective-permute-start.6
  8.9 3.0 %collective-permute-start = (bf16[384,384]{1,0:T(8,128)(2,1)S(1)}, bf16[384,384]{1,0:T(8,128)(2,1)S(1)}, u32[]{:S(2)}, u32[]{:S(2)}) collective-permute-start(bf16[384,384]{1,0:T(8,128)(2,1)S(1)} %get-tuple-element.23), channel_id=1, source_target_pairs={{0,2},{1,3},{2,0},{3,1},{4,6},{5,7},{6,4},{7,5},{8,10},{9,11},{10,... | collective-permute-start | bytes 884744 | tf_op jit(solution)/shard_map/ppermute | solution.py:253
  11.8 5.4 %shard_map.65 = (f32[384,384]{1,0:T(8,128)S(1)}, f32[384,384]{1,0:T(8,128)S(1)}) custom-call(f32[9,8]{1,0:T(8,128)S(1)} %get-tuple-element.18.table_kept.table.refs_0_, bf16[8,384,384]{2,1,0:T(8,128)(2,1)S(1)} %copy-done, bf16[8,384,384]{2,1,0:T(8,128)(2,1)S(1)} %get-tuple-element.19.right.refs_3_, bf16[8,384,384]{2,1,0:T(8,128)(2,1)S(1)} %get-tuple-element.20.cells), custom_call_target="tpu_custom_call" | custom-call | flops 3623878656 | bytes 4718592 | tf_op jit(solution)/shard_map/pallas_call | solution.py:238
  17.2 1.8 %collective-permute-done = bf16[384,384]{1,0:T(8,128)(2,1)S(1)} collective-permute-done((bf16[384,384]{1,0:T(8,128)(2,1)S(1)}, bf16[384,384]{1,0:T(8,128)(2,1)S(1)}, u32[]{:S(2)}, u32[]{:S(2)}) %collective-permute-start) | collective-permute-done | bytes 294944 | tf_op jit(solution)/shard_map/ppermute | solution.py:253
  19.1 1.7 %collective-permute-start.5 = (bf16[1,384,384]{2,1,0:T(8,128)(2,1)S(1)}, bf16[1,384,384]{2,1,0:T(8,128)(2,1)S(1)}, u32[]{:S(2)}, u32[]{:S(2)}) collective-permute-start(bf16[1,384,384]{2,1,0:T(8,128)(2,1)S(1)} %get-tuple-element.24), channel_id=1, source_target_pairs={{0,4},{1,29},{2,6},{3,31},{4,8},{5,1},{6,10},{7,3},{8,12},{9,5},{1... | collective-permute-start | bytes 884744 | tf_op jit(solution)/shard_map/ppermute | solution.py:284
  20.8 0.1 convert_add_fusion.1
  20.8 0.0 collective-permute-done.6
  20.9 0.0 collective-permute-done.2.table_in.refs_1_
  20.9 7.6 %collective-permute-done.5.halo = bf16[1,384,384]{2,1,0:T(8,128)(2,1)S(1)} collective-permute-done((bf16[1,384,384]{2,1,0:T(8,128)(2,1)S(1)}, bf16[1,384,384]{2,1,0:T(8,128)(2,1)S(1)}, u32[]{:S(2)}, u32[]{:S(2)}) %collective-permute-start.5) | collective-permute-done | bytes 294944 | tf_op jit(solution)/shard_map/ppermute | solution.py:284
  28.5 0.0 collective-permute-done.3.left_in.refs_4_
  28.5 0.0 collective-permute-done.4.right_in.refs_5_
  28.5 6.3 %shard_map.66 = (bf16[384,384]{1,0:T(8,128)(2,1)S(1)}, bf16[4,384,384]{2,1,0:T(8,128)(2,1)S(1)}) custom-call(f32[9,8]{1,0:T(8,128)S(1)} %get-tuple-element.18.table_kept.table.refs_0_, f32[9,8]{1,0:T(8,128)S(1)} %collective-permute-done.2.table_in.refs_1_, bf16[8,384,384]{2,1,0:T(8,128)(2,1)S(1)} %copy-done, ...), custom_call_target="tpu_custom_call" | custom-call | flops 3623878656 | bytes 9437184 | tf_op jit(solution)/shard_map/pallas_call | solution.py:238
  34.9 1.8 %collective-permute-start.7 = (bf16[576,384]{1,0:T(8,128)(2,1)S(1)}, bf16[576,384]{1,0:T(8,128)(2,1)S(1)}, u32[]{:S(2)}, u32[]{:S(2)}) collective-permute-start(bf16[576,384]{1,0:T(8,128)(2,1)S(1)} %pad_maximum_fusion.1), channel_id=1, source_target_pairs={{0,2},{1,3},{2,0},{3,1},{4,6},{5,7},{6,4},{7,5},{8,10},{9,11},{10,... | collective-permute-start | bytes 1327112 | tf_op jit(solution)/shard_map/ppermute | solution.py:253
  36.7 0.1 collective-permute-start.1
  36.8 6.1 %shard_map.67 = (f32[192,384]{1,0:T(8,128)S(1)}, f32[192,384]{1,0:T(8,128)S(1)}) custom-call(f32[9,8]{1,0:T(8,128)S(1)} %get-tuple-element.18.table_kept.table.refs_0_, f32[9,8]{1,0:T(8,128)S(1)} %collective-permute-done.2.table_in.refs_1_, bf16[8,384,384]{2,1,0:T(8,128)(2,1)S(1)} %copy-done, bf16[8,384,384]{2,1,0:T(8,128)(2,1)S(1)} %get-tuple-element.19.right.refs_3_, ...), custom_call_target="tpu_custom_call" | custom-call | flops 3623878656 | bytes 9437184 | tf_op jit(solution)/shard_map/pallas_call | solution.py:238
  42.9 2.1 %collective-permute-done.7 = bf16[576,384]{1,0:T(8,128)(2,1)S(1)} collective-permute-done((bf16[576,384]{1,0:T(8,128)(2,1)S(1)}, bf16[576,384]{1,0:T(8,128)(2,1)S(1)}, u32[]{:S(2)}, u32[]{:S(2)}) %collective-permute-start.7) | collective-permute-done | bytes 442400 | tf_op jit(solution)/shard_map/ppermute | solution.py:253
  45.0 0.1 collective-permute-start.8
  45.1 0.0 collective-permute-done.1
  45.1 1.6 %collective-permute-done.8 = f32[192,384]{1,0:T(8,128)S(1)} collective-permute-done((f32[192,384]{1,0:T(8,128)S(1)}, f32[192,384]{1,0:T(8,128)S(1)}, u32[]{:S(2)}, u32[]{:S(2)}) %collective-permute-start.8) | collective-permute-done | bytes 294944 | tf_op jit(solution)/shard_map/ppermute | solution.py:253
  46.6 1.1 %total.1 = f32[8,96,384]{2,1,0:T(8,128)} custom-call(f32[4,96,384]{2,1,0:T(8,128)S(1)} %bitcast.8, f32[4,96,384]{2,1,0:T(8,128)S(1)} %bitcast.9, bf16[4,96,384]{2,1,0:T(8,128)(2,1)S(1)} %bitcast.7, bf16[6,96,384]{2,1,0:T(8,128)(2,1)S(1)} %bitcast.6, f32[2,96,384]{2,1,0:T(8,128)S(1)} %bitcast.10, f32[2,96,384]{2,1,0:T(8,128)S(1)} %bitcast.11), custom_call_target="tpu_custom_call" | custom-call | tf_op jit(solution)/shard_map/total/pallas_call | solution.py:361
  (4 shorter events, 0.2 us)
Async XLA Ops:
  0.0 2.3 %copy-start = (bf16[8,384,384]{2,1,0:T(8,128)(2,1)S(1)}, bf16[8,384,384]{2,1,0:T(8,128)(2,1)}, u32[]{:S(2)}) copy-start(bf16[8,384,384]{2,1,0:T(8,128)(2,1)} %refs_2_.1) | copy-start | bytes 7077892
  0.0 28.5 %collective-permute-start.3 = (bf16[8,384,384]{2,1,0:T(8,128)(2,1)}, bf16[8,384,384]{2,1,0:T(8,128)(2,1)S(1)}, u32[]{:S(2)}, u32[]{:S(2)}) collective-permute-start(bf16[8,384,384]{2,1,0:T(8,128)(2,1)} %refs_2_.1), channel_id=1, source_target_pairs={{0,1},{1,0},{2,3},{3,2},{4,5},{5,4},{6,7},{7,6},{8,9},{9,8},{10,11... | collective-permute-start | bytes 7077896 | tf_op jit(solution)/shard_map/ppermute | solution.py:253
  0.5 28.0 %collective-permute-start.4 = (bf16[8,384,384]{2,1,0:T(8,128)(2,1)}, bf16[8,384,384]{2,1,0:T(8,128)(2,1)S(1)}, u32[]{:S(2)}, u32[]{:S(2)}) collective-permute-start(bf16[8,384,384]{2,1,0:T(8,128)(2,1)} %right_far.1), channel_id=1, source_target_pairs={{0,1},{1,0},{2,3},{3,2},{4,5},{5,4},{6,7},{7,6},{8,9},{9,8},{10,11... | collective-permute-start | bytes 7077896 | tf_op jit(solution)/shard_map/ppermute | solution.py:253
  1.8 19.1 %collective-permute-start.2 = (f32[9,8]{1,0:T(8,128)S(1)}, f32[9,8]{1,0:T(8,128)S(1)}, u32[]{:S(2)}, u32[]{:S(2)}) collective-permute-start(f32[9,8]{1,0:T(8,128)S(1)} %get-tuple-element.18.table_kept.table.refs_0_), channel_id=1, source_target_pairs={{0,1},{1,0},{2,3},{3,2},{4,5},{5,4},{6,7},{7,6},{8,9},{9,8},{10,11... | collective-permute-start | bytes 872 | tf_op jit(solution)/shard_map/ppermute | solution.py:253
  8.8 12.1 %collective-permute-start.6 = (f32[192,384]{1,0:T(8,128)S(1)}, f32[192,384]{1,0:T(8,128)S(1)}, u32[]{:S(2)}, u32[]{:S(2)}) collective-permute-start(f32[192,384]{1,0:T(8,128)S(1)} %get-tuple-element.27), channel_id=1, source_target_pairs={{0,1},{1,0},{2,3},{3,2},{4,5},{5,4},{6,7},{7,6},{8,9},{9,8},{10,11... | collective-permute-start | bytes 884744 | tf_op jit(solution)/shard_map/ppermute | solution.py:253
  8.9 10.2 %collective-permute-start = (bf16[384,384]{1,0:T(8,128)(2,1)S(1)}, bf16[384,384]{1,0:T(8,128)(2,1)S(1)}, u32[]{:S(2)}, u32[]{:S(2)}) collective-permute-start(bf16[384,384]{1,0:T(8,128)(2,1)S(1)} %get-tuple-element.23), channel_id=1, source_target_pairs={{0,2},{1,3},{2,0},{3,1},{4,6},{5,7},{6,4},{7,5},{8,10},{9,11},{10,... | collective-permute-start | bytes 884744 | tf_op jit(solution)/shard_map/ppermute | solution.py:253
  19.1 9.4 %collective-permute-start.5 = (bf16[1,384,384]{2,1,0:T(8,128)(2,1)S(1)}, bf16[1,384,384]{2,1,0:T(8,128)(2,1)S(1)}, u32[]{:S(2)}, u32[]{:S(2)}) collective-permute-start(bf16[1,384,384]{2,1,0:T(8,128)(2,1)S(1)} %get-tuple-element.24), channel_id=1, source_target_pairs={{0,4},{1,29},{2,6},{3,31},{4,8},{5,1},{6,10},{7,3},{8,12},{9,5},{1... | collective-permute-start | bytes 884744 | tf_op jit(solution)/shard_map/ppermute | solution.py:284
  34.9 10.0 %collective-permute-start.7 = (bf16[576,384]{1,0:T(8,128)(2,1)S(1)}, bf16[576,384]{1,0:T(8,128)(2,1)S(1)}, u32[]{:S(2)}, u32[]{:S(2)}) collective-permute-start(bf16[576,384]{1,0:T(8,128)(2,1)S(1)} %pad_maximum_fusion.1), channel_id=1, source_target_pairs={{0,2},{1,3},{2,0},{3,1},{4,6},{5,7},{6,4},{7,5},{8,10},{9,11},{10,... | collective-permute-start | bytes 1327112 | tf_op jit(solution)/shard_map/ppermute | solution.py:253
  36.7 8.3 %collective-permute-start.1 = (f32[384,384]{1,0:T(8,128)S(1)}, f32[384,384]{1,0:T(8,128)S(1)}, u32[]{:S(2)}, u32[]{:S(2)}) collective-permute-start(f32[384,384]{1,0:T(8,128)S(1)} %pad_maximum_fusion), channel_id=1, source_target_pairs={{0,1},{1,0},{2,3},{3,2},{4,5},{5,4},{6,7},{7,6},{8,9},{9,8},{10,11... | collective-permute-start | bytes 1769480 | tf_op jit(solution)/shard_map/ppermute | solution.py:253
  45.0 1.6 %collective-permute-start.8 = (f32[192,384]{1,0:T(8,128)S(1)}, f32[192,384]{1,0:T(8,128)S(1)}, u32[]{:S(2)}, u32[]{:S(2)}) collective-permute-start(f32[192,384]{1,0:T(8,128)S(1)} %convert_add_fusion), channel_id=1, source_target_pairs={{0,1},{1,0},{2,3},{3,2},{4,5},{5,4},{6,7},{7,6},{8,9},{9,8},{10,11... | collective-permute-start | bytes 884744 | tf_op jit(solution)/shard_map/ppermute | solution.py:253
